TPU v7x, 32 devices: a whole 2x2x4 slice. The times are simulated.
32 devices in a mesh: dp: 8 (over y, x, core), tensor: 4 (over z).
Axes of the slice: x: 2, y: 2, z: 4, core: 2. Of those that a mesh axis runs over, the one named last changes fastest.
Arguments:
- tokens: bfloat16 [4096, 1024], P(('dp', 'tensor')), may hold values from -6 to 6
- attn_gain: bfloat16 [1024], replicated, may hold values from 0.099609375 to 1.8984375
- ffn_gain: bfloat16 [1024], replicated, may hold values from 0.099609375 to 1.8984375
- w_qkv: bfloat16 [3, 1024, 1024], P(None, None, 'tensor'), may hold values from -0.1875 to 0.1875
- w_out: bfloat16 [1024, 1024], P('tensor'), may hold values from -0.1875 to 0.1875
- w_gateup: bfloat16 [2, 1024, 4096], P(None, None, 'tensor'), may hold values from -0.1875 to 0.1875
- w_down: bfloat16 [4096, 1024], P('tensor'), may hold values from -0.09375 to 0.09375
- variate_bias: float32 [2, 16], P(None, 'tensor'), may hold values from -4 to 4
- adapter_down: bfloat16 [16, 2, 16, 1024], P('dp'), may hold values from -0.1875 to 0.1875
- adapter_up: bfloat16 [16, 2, 16, 1024], P('dp', None, None, 'tensor'), may hold values from -1.5 to 1.5
- owner_table: int32 [16], replicated, may hold values from 0 to 15, each once
- lengths: int32 [8, 4], P('dp'), may hold values from 1 to 256, 512 in all within a row
- adapter_ids: int32 [8, 4], P('dp'), may hold values from 0 to 15
- page_counts: int32 [8, 4], P('dp'), may hold values from 1 to 8, 20 in all within a row
- page_table: int32 [8, 32], P('dp'), may hold values from 0 to 255, as said below
- cache_pool: bfloat16 [256, 128, 2, 1024], P('dp', None, None, 'tensor'), may hold values from -500 to 500
Outputs:
- output: bfloat16 [4096, 1024], P(('dp', 'tensor'))
Inputs may be any that keep to these rules, and one draw needn't show every extreme that they name: owner_table is a permutation: adapter a is row owner_table[a] of adapter_down and adapter_up. `page_table`: every pool page is named exactly once; page p lies on home p // 32; the 32 pages of one row lie 4 to a home on 8 distinct homes.
All inputs are finite; a program needn't handle non-finite values.
Results may differ from a plain program's by a relative error of at most 0.0085.
The roundings to bfloat16 on the way count: a program that leaves them out, or rounds other values in their place, can miss the bound.
Values may be sent and summed in bfloat16 or wider, within the bound.
No kernel may reach another device: no remote copies, remote signals or barrier semaphores. Data moves between devices by JAX's collectives and lax.ppermute only.
A program may use at most 192 MiB of HBM per device.

v0:
```python
import functools

import jax
import jax.numpy as jnp
from jax import lax
from jax.experimental import pallas as pl
from jax.experimental.pallas import tpu as pltpu
from jax.sharding import PartitionSpec as P

HD = 64
PAGES_REQ = 8
VARLEN = 160
TILE = 128
KCH = 128
BLK = 4
CHUNK = 64
BF = jnp.bfloat16
F32 = jnp.float32
NEG = -1e30


def normalize(values, gain):
    values = values.astype(F32)
    inv_scale = lax.rsqrt(jnp.mean(values * values, axis=-1, keepdims=True) + 1e-05)
    return values * inv_scale * gain.astype(F32)


def rotary(values, time_pos):
    half_dim = values.shape[-1] // 2
    frequency = 10000.0 ** (-2.0 * jnp.arange(half_dim, dtype=F32) / values.shape[-1])
    angles = time_pos.astype(F32)[:, None] * frequency[None, :]
    cosine = jnp.cos(angles)[:, None, :]
    sine_part = jnp.sin(angles)[:, None, :]
    first_half = values[..., :half_dim]
    second_half = values[..., half_dim:]
    return jnp.concatenate(
        [
            first_half * cosine - second_half * sine_part,
            first_half * sine_part + second_half * cosine,
        ],
        axis=-1,
    )


def token_layout(req_lens, live_counts, page_len, tok_total):
    end_pos = jnp.cumsum(req_lens, dtype=jnp.int32)
    starts = end_pos - req_lens
    tok_index = jnp.arange(tok_total, dtype=jnp.int32)
    request = jnp.sum(
        (tok_index[:, None] >= end_pos[None, :]).astype(jnp.int32), axis=1, dtype=jnp.int32
    )
    onehot = request[:, None] == jnp.arange(req_lens.shape[0], dtype=jnp.int32)[None, :]
    first_pos = jnp.sum(jnp.where(onehot, starts[None, :], 0), axis=1, dtype=jnp.int32)
    cached = jnp.sum(jnp.where(onehot, live_counts[None, :], 0), axis=1, dtype=jnp.int32)
    return (onehot, cached * page_len + tok_index - first_pos)


def want_kernel(n_dp, cap, pool_dev, me_ref, table_ref, want_ref, pos_ref, count):
    me = me_ref[0]
    slots = table_ref.shape[1]

    def clear(g, carry):
        count[g] = 0
        for j in range(n_dp * cap):
            want_ref[g, j] = 0
        return carry

    lax.fori_loop(0, n_dp, clear, 0)

    def place(p, carry):
        page = table_ref[0, p]
        home = page // pool_dev
        rank = count[home]
        count[home] = rank + 1
        want_ref[me, home * cap + rank] = page - home * pool_dev
        pos_ref[p] = home * cap + rank
        return carry

    lax.fori_loop(0, slots, place, 0)


def want(me, page_table, n_dp, cap, pool_dev):
    smem = pl.BlockSpec(memory_space=pltpu.SMEM)
    return pl.pallas_call(
        functools.partial(want_kernel, n_dp, cap, pool_dev),
        out_shape=(
            jax.ShapeDtypeStruct((n_dp, n_dp * cap), jnp.int32),
            jax.ShapeDtypeStruct((page_table.shape[1],), jnp.int32),
        ),
        in_specs=[smem, smem],
        out_specs=(smem, smem),
        scratch_shapes=[pltpu.SMEM((n_dp,), jnp.int32)],
        name="want_pages",
    )(me, page_table)


def pick_kernel(n_dp, cap, me_ref, asked_ref, pool_ref, *rest):
    n_out = len(rest) - 3
    outs, (buf, sem_in, sem_out) = rest[:n_out], rest[n_out:]
    lanes = outs[0].shape[-1]
    me = me_ref[0]
    copies = []
    for g in range(n_dp):
        for k in range(cap):
            page = asked_ref[g, me * cap + k]
            copy = pltpu.make_async_copy(pool_ref.at[page], buf.at[g, k], sem_in.at[g, k])
            copy.start()
            copies.append(copy)
    done = []
    for g in range(n_dp):
        for k in range(cap):
            copies[g * cap + k].wait()
        for a in range(n_out):
            copy = pltpu.make_async_copy(
                buf.at[g, :, :, :, pl.ds(a * lanes, lanes)], outs[a].at[g], sem_out.at[a, g]
            )
            copy.start()
            done.append(copy)
    for copy in done:
        copy.wait()


def pick(me, asked, pool, n_dp, cap, lanes):
    smem = pl.BlockSpec(memory_space=pltpu.SMEM)
    hbm = pl.BlockSpec(memory_space=pl.ANY)
    n_out = pool.shape[-1] // lanes
    shape = (n_dp, cap) + pool.shape[1:-1]
    return pl.pallas_call(
        functools.partial(pick_kernel, n_dp, cap),
        out_shape=[jax.ShapeDtypeStruct(shape + (lanes,), pool.dtype)] * n_out,
        in_specs=[smem, smem, hbm],
        out_specs=[hbm] * n_out,
        scratch_shapes=[
            pltpu.VMEM(shape + pool.shape[-1:], pool.dtype),
            pltpu.SemaphoreType.DMA((n_dp, cap)),
            pltpu.SemaphoreType.DMA((n_out, n_dp)),
        ],
        name="pick_pages",
    )(me, asked, pool)


def attend_kernel(
    group, per, lens_ref, counts_ref, pos_ref, bias_ref,
    q_ref, kn_ref, vn_ref, raw_ref, out_ref,
    kc, vc, knp, vnp, qbd, info, sbuf, wbuf, obuf,
):
    page_len = kc.shape[1]
    width = q_ref.shape[1]
    rows = q_ref.shape[0]
    n_req = lens_ref.shape[1]
    back = knp.shape[0] - rows
    n_page = PAGES_REQ
    n_new = (back + TILE) // KCH

    row = lax.broadcasted_iota(jnp.int32, (2 * page_len, 2 * page_len), 0)
    col = lax.broadcasted_iota(jnp.int32, (2 * page_len, 2 * page_len), 1)
    src = jnp.where(row < page_len, 2 * row, 2 * row - (2 * page_len - 1))
    choose = (col == src).astype(F32).astype(BF)

    def unpack(slot):
        pages = [raw_ref[pos_ref[slot + i]] for i in range(BLK)]
        both = jnp.dot(
            choose, jnp.concatenate(pages, axis=1), preferred_element_type=F32
        ).astype(BF)
        for i in range(BLK):
            kc[slot + i] = both[:page_len, i * width : (i + 1) * width]
            vc[slot + i] = both[page_len:, i * width : (i + 1) * width]

    for r in range(n_req):
        unpack(r * n_page)
    for r in range(n_req):
        for b in range(1, n_page // BLK):
            @pl.when(counts_ref[0, r] > b * BLK)
            def _():
                unpack(r * n_page + b * BLK)

    knp[:back, :] = jnp.zeros((back, width), BF)
    vnp[:back, :] = jnp.zeros((back, width), BF)
    knp[back:, :] = kn_ref[...]
    vnp[back:, :] = vn_ref[...]

    lane = lax.broadcasted_iota(jnp.int32, (1, width), 1)
    lane_f = lax.broadcasted_iota(jnp.int32, (1, KCH), 1).astype(F32)
    delta = [bias_ref[0, group * per + a] - bias_ref[1, group * per + a] for a in range(per)]
    starts = [jnp.int32(0)]
    for r in range(n_req):
        starts.append(starts[-1] + lens_ref[0, r])

    def tile_body(t, carry):
        row0 = pl.multiple_of(t * TILE, TILE)
        qt = q_ref[pl.ds(row0, TILE), :].astype(F32)
        for a in range(per):
            mine = (lane >= a * HD) & (lane < (a + 1) * HD)
            qbd[a * TILE : (a + 1) * TILE, :] = jnp.where(mine, qt, 0.0).astype(BF)

        row = (row0 + lax.broadcasted_iota(jnp.int32, (TILE, KCH), 0)).astype(F32)
        start_row = jnp.zeros((TILE, KCH), F32)
        offset = jnp.zeros((TILE, KCH), F32)
        blocks = jnp.int32(1)
        for r in range(n_req):
            start, end, live = starts[r], starts[r + 1], counts_ref[0, r]
            inside = (row >= start.astype(F32)) & (row < end.astype(F32))
            start_row = jnp.where(inside, start.astype(F32), start_row)
            offset = jnp.where(inside, (live * page_len - start).astype(F32), offset)
            here = (start < row0 + TILE) & (end > row0)
            blocks = jnp.maximum(blocks, jnp.where(here, (live + BLK - 1) // BLK, 0))
        var_first = jnp.floor((row + offset + 0.5) * (1.0 / VARLEN)) * VARLEN
        info[0] = row
        info[1] = start_row
        info[2] = var_first
        info[3] = var_first - offset

        for b in range(n_page // BLK):
            @pl.when(b < blocks)
            def _():
                for i in range(BLK):
                    sbuf[b * BLK + i] = jnp.full((per * TILE, KCH), NEG, F32)

        def scores(keys):
            return lax.dot_general(
                qbd[...], keys, (((1,), (1,)), ((), ())), preferred_element_type=F32
            )

        for r in range(n_req):
            start, end, live = starts[r], starts[r + 1], counts_ref[0, r]
            here = (start < row0 + TILE) & (end > row0)
            for b in range(n_page // BLK):
                @pl.when(here & (live > b * BLK))
                def _():
                    s_all = scores(
                        kc[r * n_page + b * BLK : r * n_page + (b + 1) * BLK].reshape(
                            BLK * page_len, width
                        )
                    )
                    row = info[0]
                    inside = (row >= start.astype(F32)) & (row < end.astype(F32))
                    for i in range(BLK):
                        page = b * BLK + i
                        dead = jnp.where(page < live, 0.0, NEG)
                        same = info[2] <= lane_f + page * page_len
                        for a in range(per):
                            part = slice(a * TILE, (a + 1) * TILE)
                            s = s_all[part, i * KCH : (i + 1) * KCH]
                            s = s + jnp.where(same, delta[a] + dead, dead)
                            sbuf[page, part, :] = jnp.where(inside, s, sbuf[page, part, :])

        s_all = scores(knp[pl.ds(row0, back + TILE), :])
        for i in range(n_new):
            key_row = lane_f + (row0 - back + i * KCH).astype(F32)
            allowed = (key_row >= info[1]) & (key_row <= info[0])
            same = info[3] <= key_row
            for a in range(per):
                part = slice(a * TILE, (a + 1) * TILE)
                s = s_all[part, i * KCH : (i + 1) * KCH]
                s = jnp.where(allowed, s + jnp.where(same, delta[a], 0.0), NEG)
                sbuf[n_page + i, part, :] = s

        for a in range(per):
            part = slice(a * TILE, (a + 1) * TILE)

            def top_block(b, top):
                for i in range(BLK):
                    top = jnp.maximum(top, sbuf[b * BLK + i, part, :])
                return top

            top = sbuf[n_page, part, :]
            for i in range(1, n_new):
                top = jnp.maximum(top, sbuf[n_page + i, part, :])
            top = lax.fori_loop(0, blocks, top_block, top)
            peak = jnp.broadcast_to(jnp.max(top, axis=1, keepdims=True), (TILE, KCH))

            def weigh(c, total):
                p = jnp.exp(sbuf[c, part, :] - peak)
                sbuf[c, part, :] = p
                return total + p

            def weigh_block(b, total):
                for i in range(BLK):
                    total = weigh(b * BLK + i, total)
                return total

            total = jnp.zeros((TILE, KCH), F32)
            for i in range(n_new):
                total = weigh(n_page + i, total)
            total = lax.fori_loop(0, blocks, weigh_block, total)
            inverse = jnp.broadcast_to(
                1.0 / jnp.sum(total, axis=1, keepdims=True), (TILE, KCH)
            )
            for i in range(n_new):
                c = n_page + i
                wbuf[part, c * KCH : (c + 1) * KCH] = (sbuf[c, part, :] * inverse).astype(BF)
            for b in range(n_page // BLK):
                @pl.when(b < blocks)
                def _():
                    for i in range(BLK):
                        c = b * BLK + i
                        wbuf[part, c * KCH : (c + 1) * KCH] = (
                            sbuf[c, part, :] * inverse
                        ).astype(BF)

        obuf[...] = jnp.dot(
            wbuf[:, n_page * KCH :], vnp[pl.ds(row0, back + TILE), :],
            preferred_element_type=F32,
        )
        for r in range(n_req):
            start, end, live = starts[r], starts[r + 1], counts_ref[0, r]
            here = (start < row0 + TILE) & (end > row0)
            for b in range(n_page // BLK):
                @pl.when(here & (live > b * BLK))
                def _():
                    o = jnp.dot(
                        wbuf[:, b * BLK * KCH : (b + 1) * BLK * KCH],
                        vc[r * n_page + b * BLK : r * n_page + (b + 1) * BLK].reshape(
                            BLK * page_len, width
                        ),
                        preferred_element_type=F32,
                    )
                    row = info[0]
                    inside = (row >= start.astype(F32)) & (row < end.astype(F32))
                    for a in range(per):
                        part = slice(a * TILE, (a + 1) * TILE)
                        before = obuf[part, :]
                        obuf[part, :] = jnp.where(inside[:, :width], before + o[part], before)
        o = obuf[:TILE, :]
        for a in range(1, per):
            o = jnp.where(lane >= a * HD, obuf[a * TILE : (a + 1) * TILE, :], o)
        out_ref[pl.ds(row0, TILE), :] = o.astype(BF)
        return carry

    lax.fori_loop(0, rows // TILE, tile_body, 0)


def attend(group, lanes, most, lens, counts, pos, bias, q, kn, vn, raw):
    rows = q.shape[0]
    per = lanes // HD
    page_len = raw.shape[1] // 2
    slots = raw.shape[0]
    back = -(-most // KCH) * KCH
    n_all = PAGES_REQ + (back + TILE) // KCH
    smem = pl.BlockSpec(memory_space=pltpu.SMEM)
    part = pl.BlockSpec((rows, lanes), lambda i: (0, group))
    return pl.pallas_call(
        functools.partial(attend_kernel, group, per),
        grid=(1,),
        out_shape=jax.ShapeDtypeStruct((rows, lanes), BF),
        in_specs=[smem] * 4
        + [part] * 3
        + [pl.BlockSpec(raw.shape, lambda i: (0, 0, 0), pipeline_mode=pl.Buffered(1))],
        out_specs=pl.BlockSpec((rows, lanes), lambda i: (0, 0)),
        scratch_shapes=[
            pltpu.VMEM((slots, page_len, lanes), BF),
            pltpu.VMEM((slots, page_len, lanes), BF),
            pltpu.VMEM((back + rows, lanes), BF),
            pltpu.VMEM((back + rows, lanes), BF),
            pltpu.VMEM((per * TILE, lanes), BF),
            pltpu.VMEM((4, TILE, KCH), F32),
            pltpu.VMEM((n_all, per * TILE, KCH), F32),
            pltpu.VMEM((per * TILE, n_all * KCH), BF),
            pltpu.VMEM((per * TILE, lanes), F32),
        ],
        compiler_params=pltpu.CompilerParams(vmem_limit_bytes=32 << 20),
        cost_estimate=pl.CostEstimate(
            flops=4 * rows * per * 1408 * lanes, bytes_accessed=raw.size * 2, transcendentals=0
        ),
        name="attend",
    )(lens, counts, pos, bias, q, kn, vn, raw)


def shift(value, axis, n, k):
    return lax.ppermute(value, axis, [(i, (i + k) % n) for i in range(n)])


def per_device(
    tokens,
    attn_gain,
    ffn_gain,
    w_qkv,
    w_out,
    w_gateup,
    w_down,
    variate_bias,
    adapter_down,
    adapter_up,
    owner_table,
    lengths,
    adapter_ids,
    page_counts,
    page_table,
    cache_pool,
):
    n_tp = lax.axis_size("tensor")
    n_dp = lax.axis_size("dp")
    tp = lax.axis_index("tensor")
    dp = lax.axis_index("dp")
    me = dp.astype(jnp.int32).reshape(1)
    row_count, d_model = tokens.shape
    tok_total = row_count * n_tp
    width = w_out.shape[0]
    heads = width // HD
    page_len = cache_pool.shape[1]
    cap = max(1, page_table.shape[1] // n_dp)
    far_first = [k for k in range(1, n_tp)]

    lanes = min(width, 2 * HD)
    n_group = width // lanes
    slots = n_dp * cap
    wanted, buffer_pos = want(me, page_table, n_dp, cap, cache_pool.shape[0])
    asked = lax.psum(wanted, "dp")
    picked = pick(me, asked, cache_pool, n_dp, cap, lanes)
    own_half = lax.dynamic_slice_in_dim(w_out, (dp % 2) * (width // 2), width // 2, 0)
    picked, own_half, lengths, adapter_ids, page_counts = lax.optimization_barrier(
        (picked, own_half, lengths, adapter_ids, page_counts)
    )
    fetched = []
    for a in range(n_group):
        send = picked[a]
        if fetched:
            send, _ = lax.optimization_barrier((send, fetched[-1]))
        got = lax.all_to_all(send, "dp", split_axis=0, concat_axis=0, tiled=True)
        fetched.append(got.reshape(slots, 2 * page_len, lanes))

    all_tokens = lax.all_gather(tokens, "tensor", axis=0, tiled=True)
    normed = normalize(all_tokens, attn_gain).astype(BF)

    dd = d_model // n_tp
    down_part = lax.dynamic_slice_in_dim(adapter_down, tp * dd, dd, 3)
    both_parts = jnp.concatenate([down_part, adapter_up], axis=3)
    both_all = lax.all_gather(both_parts, "dp", axis=0, tiled=True)
    slot_ids = jnp.take(owner_table, adapter_ids[0])
    select = (
        slot_ids[:, None] == jnp.arange(both_all.shape[0], dtype=jnp.int32)[None, :]
    ).astype(BF)
    both_sel = jnp.einsum("rn,nkce->rkce", select, both_all, preferred_element_type=F32).astype(BF)
    down_named, up_sel = both_sel[..., :dd], both_sel[..., dd:]
    down_blocks = [down_named] + [shift(down_named, "tensor", n_tp, k) for k in far_first]

    halves = jnp.stack([shift(own_half, "tensor", n_tp, k) for k in far_first])
    twins = lax.ppermute(halves, "dp", [(i, i ^ 1) for i in range(n_dp)])
    w_rest = jnp.where(
        dp % 2 == 0,
        jnp.concatenate([halves, twins], axis=1),
        jnp.concatenate([twins, halves], axis=1),
    )
    w_whole = jnp.concatenate([w_out[None], w_rest], axis=0)

    live_counts = page_counts[0]
    onehot, position = token_layout(lengths[0], live_counts, page_len, tok_total)
    member = onehot.astype(F32)
    projected = jnp.einsum("td,kde->kte", normed, w_qkv, preferred_element_type=F32)
    n_req = member.shape[1]
    rank = down_named.shape[2]
    down_sel = jnp.zeros((n_req, 2, rank, n_tp, dd), BF)
    for k, block in enumerate(down_blocks):
        down_sel = lax.dynamic_update_index_in_dim(down_sel, block, (tp - k) % n_tp, 3)
    down_sel = down_sel.reshape(n_req, 2, rank, d_model)
    lowall = jnp.einsum("td,rkcd->rtkc", normed, down_sel, preferred_element_type=F32)
    low_rank = jnp.sum(
        lowall * jnp.transpose(member)[:, :, None, None], axis=0
    ).astype(BF)
    spread = (jnp.transpose(member)[:, :, None, None] * low_rank.astype(F32)).astype(BF)
    delta_proj = jnp.einsum("rtkc,rkce->kte", spread, up_sel, preferred_element_type=F32)
    time_pos = position % VARLEN
    query = rotary((projected[0] + delta_proj[0]).reshape(tok_total, heads, HD), time_pos)
    query = (query.astype(BF) * BF(HD ** -0.5)).reshape(tok_total, width)
    new_keys = rotary(projected[1].reshape(tok_total, heads, HD), time_pos)
    new_keys = new_keys.astype(BF).reshape(tok_total, width)
    new_values = (projected[2] + delta_proj[1]).astype(BF)

    n_chunk = max(1, row_count // CHUNK)
    sub = row_count // n_chunk
    mixes = [[] for _ in range(n_chunk)]
    for a in range(n_group):
        mix = attend(
            a, lanes, 2 * TILE, lengths, page_counts, buffer_pos, variate_bias,
            query, new_keys, new_values, fetched[a],
        ).reshape(n_tp, n_chunk, sub, lanes)
        for c in range(n_chunk):
            own = mix[:, c].reshape(n_tp * sub, lanes)
            mixes[c].append([own] + [shift(own, "tensor", n_tp, k) for k in far_first])

    base = all_tokens.reshape(n_tp, n_chunk, sub, d_model)
    w_parts = w_whole.reshape(n_tp, n_group, lanes, d_model)
    outs = []
    for c in range(n_chunk):
        residual = base[:, c].reshape(n_tp * sub, d_model).astype(F32)
        for a in range(n_group):
            residual = residual + jnp.dot(
                jnp.concatenate(mixes[c][a], axis=1),
                w_parts[:, a].reshape(n_tp * lanes, d_model),
                preferred_element_type=F32,
            )
        ffn_in = normalize(residual, ffn_gain).astype(BF)
        gate_up = jnp.einsum("td,kdf->ktf", ffn_in, w_gateup, preferred_element_type=F32)
        hidden = (jax.nn.silu(gate_up[0]) * gate_up[1]).astype(BF)
        down = jnp.dot(hidden, w_down, preferred_element_type=F32).reshape(n_tp, sub, d_model)
        total = lax.dynamic_index_in_dim(down, tp, 0, False)
        total = total + lax.dynamic_index_in_dim(
            residual.reshape(n_tp, sub, d_model), tp, 0, False
        )
        down = down.astype(BF)
        for k in far_first:
            piece = lax.dynamic_index_in_dim(down, (tp + k) % n_tp, 0, False)
            total = total + shift(piece, "tensor", n_tp, k).astype(F32)
        outs.append(total.astype(BF))
    return jnp.concatenate(outs, axis=0)


def solution(mesh):
    return jax.shard_map(
        per_device,
        mesh=mesh,
        in_specs=(
            P(("dp", "tensor"), None),
            P(),
            P(),
            P(None, None, "tensor"),
            P("tensor", None),
            P(None, None, "tensor"),
            P("tensor", None),
            P(None, "tensor"),
            P("dp", None, None, None),
            P("dp", None, None, "tensor"),
            P(),
            P("dp", None),
            P("dp", None),
            P("dp", None),
            P("dp", None),
            P("dp", None, None, "tensor"),
        ),
        out_specs=P(("dp", "tensor"), None),
        check_vma=False,
    )
```

profile of v0, /device:TPU:0, one launch (start us, length us, event | category | flops | bytes accessed | tf_op | source)
XLA Modules:
  0.0 200.9 jit_solution(13600243505836143695)
XLA Ops:
  6.5 2.1 %want_pages.1 = (s32[8,32]{1,0:T(8,128)}, s32[32]{0:T(128)}) custom-call(s32[1]{0:T(128)} %bitcast.2.me_ref, s32[1,32]{1,0:T(1,128)} %table_ref.1), custom_call_target="tpu_custom_call" | custom-call | tf_op jit(solution)/shard_map/want_pages/pallas_call | solution.py:84
  8.7 10.2 %psum.7.asked_ref = s32[8,32]{1,0:T(8,128)} all-reduce(s32[8,32]{1,0:T(8,128)} %get-tuple-element.16), channel_id=1, replica_groups=mesh['dp'=8,'tensor'=4] {'dp'}, use_global_device_ids=true, to_apply=%region_0.0 | all-reduce | flops 256 | bytes 2048 | tf_op jit(solution)/shard_map/psum | solution.py:408
  18.9 1.0 constant_dynamic-slice_fusion.1
  19.9 4.9 %pick_pages.1 = (bf16[8,4,128,2,128]{4,3,2,1,0:T(2,128)(2,1)}, bf16[8,4,128,2,128]{4,3,2,1,0:T(2,128)(2,1)}) custom-call(s32[1]{0:T(128)} %bitcast.2.me_ref, s32[8,32]{1,0:T(8,128)} %psum.7.asked_ref, bf16[32,128,2,256]{3,2,1,0:T(2,128)(2,1)} %pool_ref.1), custom_call_target="tpu_custom_call" | custom-call | tf_op jit(solution)/shard_map/pick_pages/pallas_call | solution.py:128
  24.8 0.6 gather_fusion
  25.5 0.8 constant_dynamic-slice_fusion
  26.3 9.2 %all_gather.7 = bf16[16,2,16,512]{3,2,1,0:T(8,128)(2,1)S(1)} all-gather(bf16[2,2,16,512]{3,2,1,0:T(8,128)(2,1)S(1)} %pad_maximum_fusion.4), channel_id=1, replica_groups=mesh['dp'=8,'tensor'=4] {'dp'}, dimensions={0}, use_global_device_ids=true | all-gather | bytes 589824 | tf_op jit(solution)/shard_map/all_gather | solution.py:428
  35.9 0.7 fusion.85
  36.6 1.6 collective-permute-start
  38.2 2.6 %collective-permute-start.1 = (bf16[4,2,16,256]{3,0,2,1:T(4,128)(2,1)}, bf16[4,2,16,256]{3,0,2,1:T(4,128)(2,1)S(1)}, u32[]{:S(2)}, u32[]{:S(2)}) collective-permute-start(bf16[4,2,16,256]{3,0,2,1:T(4,128)(2,1)} %get-tuple-element.58), channel_id=1, source_target_pairs={{0,2},{1,3},{2,0},{3,1},{4,6},{5,7},{6,4},{7,5},{8,10},{9,11},{10,... | collective-permute-start | bytes 196616 | tf_op jit(solution)/shard_map/ppermute | solution.py:370
  41.0 1.7 collective-permute-start.7
  42.7 1.9 collective-permute-start.8
  44.7 4.4 %all-to-all-start = ((bf16[8,4,128,2,128]{4,3,2,1,0:T(2,128)(2,1)}), bf16[8,4,128,2,128]{4,3,2,1,0:T(2,128)(2,1)}, u32[]{:S(2)}, u32[]{:S(2)}) async-start(bf16[8,4,128,2,128]{4,3,2,1,0:T(2,128)(2,1)} %get-tuple-element.23), calls=%async_computation | async-start | bytes 4194304 | tf_op jit(solution)/shard_map/all_to_all | solution.py:419
  49.4 2.4 %collective-permute-done.6 = bf16[128,1024]{1,0:T(8,128)(2,1)S(1)} collective-permute-done((bf16[128,1024]{1,0:T(8,128)(2,1)S(1)}, bf16[128,1024]{1,0:T(8,128)(2,1)S(1)}, u32[]{:S(2)}, u32[]{:S(2)}) %collective-permute-start.6) | collective-permute-done | bytes 262176 | tf_op jit(solution)/shard_map/ppermute | solution.py:370
  51.8 22.4 %collective-permute-done.7 = bf16[128,1024]{1,0:T(8,128)(2,1)S(1)} collective-permute-done((bf16[128,1024]{1,0:T(8,128)(2,1)S(1)}, bf16[128,1024]{1,0:T(8,128)(2,1)S(1)}, u32[]{:S(2)}, u32[]{:S(2)}) %collective-permute-start.7) | collective-permute-done | bytes 262176 | tf_op jit(solution)/shard_map/ppermute | solution.py:370
  74.3 1.0 pad_maximum_fusion.1
  75.3 1.0 multiply_cosine_fusion
  76.4 0.6 convert_element_type.129
  77.0 0.6 convert_element_type.142
  77.7 1.6 dynamic_update_slice.13
  79.4 0.6 copy-done.18
  80.0 0.9 copy.69
  81.0 1.6 copy.70
  82.6 1.6 dynamic_update_slice.14
  84.2 1.6 dynamic_update_slice.15
  85.7 2.6 %dynamic_update_slice.16 = bf16[4,2,16,4,256]{4,3,2,1,0:T(4,128)(2,1)S(1)} dynamic-update-slice(bf16[4,2,16,4,256]{4,3,2,1,0:T(4,128)(2,1)S(1)} %dynamic_update_slice.15, bf16[4,2,16,1,256]{4,3,2,1,0:T(2,128)(2,1)} %copy.70, s32[]{:T(128)} %constant.145.clone.1, s32[]{:T(128)} %constant.145.clone.1, s32[]{:T(128)} %constant.145.clone.1, s32[]{:T(128)S(6)} %select_n.151, s32[]{:T(128)} %constant.145.clone.1) | dynamic-update-slice | bytes 131076 | tf_op jit(solution)/shard_map/jit(dynamic_update_index_in_dim)/dynamic_update_slice | solution.py:454
  88.4 0.9 reshape.241
  89.3 1.9 maximum_select_fusion
  91.1 1.6 fusion.10
  92.7 1.5 fusion
  94.3 4.5 %all-to-all-start.1 = ((bf16[8,4,128,2,128]{4,3,2,1,0:T(2,128)(2,1)}), bf16[8,4,128,2,128]{4,3,2,1,0:T(2,128)(2,1)}, u32[]{:S(2)}, u32[]{:S(2)}) async-start(bf16[8,4,128,2,128]{4,3,2,1,0:T(2,128)(2,1)} %get-tuple-element.26), calls=%async_computation.1 | async-start | bytes 4194304 | tf_op jit(solution)/shard_map/all_to_all | solution.py:419
  98.8 0.6 fusion.9
  100.3 1.0 convolution_bitcast_fusion.2
  101.5 1.0 copy.73
  102.8 1.2 subtract_convert_fusion
  104.3 2.1 %fusion.82 = (bf16[4,1,64,1024]{3,2,1,0:T(8,128)(2,1)}, bf16[4,1,64,1024]{3,2,1,0:T(8,128)(2,1)S(1)}) fusion(bf16[4,2,64,1024]{3,2,1,0:T(8,128)(2,1)} %bitcast.144), kind=kLoop, calls=%fused_computation.142 | loop fusion | bytes 2097152 | tf_op jit(solution)/shard_map/slice | solution.py:485
  106.5 13.8 %attend.2 = bf16[512,128]{1,0:T(8,128)(2,1)S(1)} custom-call(s32[1,4]{1,0:T(1,128)S(1)} %copy-done.3, s32[1,4]{1,0:T(1,128)S(1)} %copy-done.1, s32[32]{0:T(128)S(1)} %copy-done.4, f32[2,4]{1,0:T(2,128)S(1)} %copy-done.2, bf16[512,256]{1,0:T(8,128)(2,1)S(1)} %copy.76.q_ref, bf16[512,256]{1,0:T(8,128)(2,1)S(1)} %copy.77.kn_ref, ...), custom_call_target="tpu_custom_call" | custom-call | flops 738197504 | bytes 2097152 | tf_op jit(solution)/shard_map/attend/pallas_call | solution.py:342
  120.3 5.1 %all-to-all-done.1 = bf16[8,4,128,2,128]{4,3,2,1,0:T(2,128)(2,1)} async-done(((bf16[8,4,128,2,128]{4,3,2,1,0:T(2,128)(2,1)}), bf16[8,4,128,2,128]{4,3,2,1,0:T(2,128)(2,1)}, u32[]{:S(2)}, u32[]{:S(2)}) %all-to-all-start.1) | async-done | bytes 2097184 | tf_op jit(solution)/shard_map/all_to_all | solution.py:419
  125.4 13.7 %attend.3 = bf16[512,128]{1,0:T(8,128)(2,1)S(1)} custom-call(s32[1,4]{1,0:T(1,128)S(1)} %copy-done.3, s32[1,4]{1,0:T(1,128)S(1)} %copy-done.1, s32[32]{0:T(128)S(1)} %copy-done.4, f32[2,4]{1,0:T(2,128)S(1)} %copy-done.2, bf16[512,256]{1,0:T(8,128)(2,1)S(1)} %copy.76.q_ref, bf16[512,256]{1,0:T(8,128)(2,1)S(1)} %copy.77.kn_ref, ...), custom_call_target="tpu_custom_call" | custom-call | flops 738197504 | bytes 2097152 | tf_op jit(solution)/shard_map/attend/pallas_call | solution.py:342
  139.2 11.0 %collective-permute-start.10 = (bf16[256,128]{1,0:T(8,128)(2,1)S(1)}, bf16[256,128]{1,0:T(8,128)(2,1)S(1)}, u32[]{:S(2)}, u32[]{:S(2)}) collective-permute-start(bf16[256,128]{1,0:T(8,128)(2,1)S(1)} %bitcast.174), channel_id=1, source_target_pairs={{0,1},{1,2},{2,3},{3,0},{4,5},{5,6},{6,7},{7,4},{8,9},{9,10},{10,1... | collective-permute-start | bytes 196616 | tf_op jit(solution)/shard_map/ppermute | solution.py:370
  150.2 1.6 collective-permute-start.11
  151.8 0.9 collective-permute-start.12
  152.7 1.2 collective-permute-start.3
  153.9 1.4 collective-permute-start.4
  155.2 1.3 collective-permute-start.5
  156.6 4.6 %collective-permute-done.11 = bf16[256,128]{1,0:T(8,128)(2,1)S(1)} collective-permute-done((bf16[256,128]{1,0:T(8,128)(2,1)S(1)}, bf16[256,128]{1,0:T(8,128)(2,1)S(1)}, u32[]{:S(2)}, u32[]{:S(2)}) %collective-permute-start.11) | collective-permute-done | bytes 65568 | tf_op jit(solution)/shard_map/ppermute | solution.py:370
  161.2 0.9 collective-permute-start.17
  162.6 3.5 %collective-permute-start.19 = (bf16[256,128]{1,0:T(8,128)(2,1)S(1)}, bf16[256,128]{1,0:T(8,128)(2,1)S(1)}, u32[]{:S(2)}, u32[]{:S(2)}) collective-permute-start(bf16[256,128]{1,0:T(8,128)(2,1)S(1)} %bitcast.170), channel_id=1, source_target_pairs={{0,1},{1,2},{2,3},{3,0},{4,5},{5,6},{6,7},{7,4},{8,9},{9,10},{10,1... | collective-permute-start | bytes 196616 | tf_op jit(solution)/shard_map/ppermute | solution.py:370
  166.6 2.0 collective-permute-start.21
  168.6 0.6 multiply_reduce_fusion.1
  169.2 1.3 convolution_bitcast_fusion.1
  170.7 0.8 fusion.87
  171.6 2.0 collective-permute-start.18
  173.6 1.0 collective-permute-done.20
  174.6 0.7 collective-permute-start.13
  175.3 3.4 %collective-permute-start.14 = (bf16[64,1024]{1,0:T(8,128)(2,1)S(1)}, bf16[64,1024]{1,0:T(8,128)(2,1)S(1)}, u32[]{:S(2)}, u32[]{:S(2)}) collective-permute-start(bf16[64,1024]{1,0:T(8,128)(2,1)S(1)} %get-tuple-element.46), channel_id=1, source_target_pairs={{0,2},{1,3},{2,0},{3,1},{4,6},{5,7},{6,4},{7,5},{8,10},{9,11},{10,... | collective-permute-start | bytes 393224 | tf_op jit(solution)/shard_map/ppermute | solution.py:370
  179.7 0.6 multiply_reduce_fusion
  180.3 1.3 convolution_bitcast_fusion
  181.9 0.8 fusion.86
  182.7 1.9 collective-permute-start.22
  184.6 2.6 %collective-permute-start.24 = (bf16[64,1024]{1,0:T(8,128)(2,1)S(1)}, bf16[64,1024]{1,0:T(8,128)(2,1)S(1)}, u32[]{:S(2)}, u32[]{:S(2)}) collective-permute-start(bf16[64,1024]{1,0:T(8,128)(2,1)S(1)} %get-tuple-element.48), channel_id=1, source_target_pairs={{0,3},{1,0},{2,1},{3,2},{4,7},{5,4},{6,5},{7,6},{8,11},{9,8},{10,9... | collective-permute-start | bytes 393224 | tf_op jit(solution)/shard_map/ppermute | solution.py:370
  187.3 2.4 %collective-permute-done.22 = bf16[64,1024]{1,0:T(8,128)(2,1)S(1)} collective-permute-done((bf16[64,1024]{1,0:T(8,128)(2,1)S(1)}, bf16[64,1024]{1,0:T(8,128)(2,1)S(1)}, u32[]{:S(2)}, u32[]{:S(2)}) %collective-permute-start.22) | collective-permute-done | bytes 131104 | tf_op jit(solution)/shard_map/ppermute | solution.py:370
  189.8 3.5 %collective-permute-done.23 = bf16[64,1024]{1,0:T(8,128)(2,1)S(1)} collective-permute-done((bf16[64,1024]{1,0:T(8,128)(2,1)S(1)}, bf16[64,1024]{1,0:T(8,128)(2,1)S(1)}, u32[]{:S(2)}, u32[]{:S(2)}) %collective-permute-start.23) | collective-permute-done | bytes 131104 | tf_op jit(solution)/shard_map/ppermute | solution.py:370
  193.3 0.7 pad_maximum_fusion.3
  (114 shorter events, 5.7 us)
Async XLA Ops:
  6.5 164.2 %copy-start = (bf16[1024,1024]{1,0:T(8,128)(2,1)S(1)}, bf16[1024,1024]{1,0:T(8,128)(2,1)}, u32[]{:S(2)}) copy-start(bf16[1024,1024]{1,0:T(8,128)(2,1)} %param.22) | copy-start | bytes 6291460
  6.5 86.2 %all-gather.2.cloned.1.call-start = ((), (), s32[]{:S(2)}) async-start(), calls=%async_computation.2 | async-start | bytes 1310720 | tf_op jit(solution)/shard_map/all_gather | solution.py:422
  19.9 4.9 %copy-start.24 = (s32[1,4]{1,0:T(1,128)S(1)}, s32[1,4]{1,0:T(1,128)}, u32[]{:S(2)}) copy-start(s32[1,4]{1,0:T(1,128)} %param.28) | copy-start | bytes 52
  19.9 5.0 %copy-start.5 = (s32[16]{0:T(128)S(1)}, s32[16]{0:T(128)}, u32[]{:S(2)}) copy-start(s32[16]{0:T(128)} %param.26) | copy-start | bytes 196
  19.9 6.4 %copy-start.19 = (bf16[2,2,16,256]{3,2,1,0:T(8,128)(2,1)S(1)}, bf16[2,2,16,256]{3,2,1,0:T(8,128)(2,1)}, u32[]{:S(2)}) copy-start(bf16[2,2,16,256]{3,2,1,0:T(8,128)(2,1)} %param.25) | copy-start | bytes 98308
  36.6 42.6 %collective-permute-start = (bf16[4,2,16,256]{3,0,2,1:T(4,128)(2,1)}, bf16[4,2,16,256]{3,0,2,1:T(4,128)(2,1)S(1)}, u32[]{:S(2)}, u32[]{:S(2)}) collective-permute-start(bf16[4,2,16,256]{3,0,2,1:T(4,128)(2,1)} %get-tuple-element.58), channel_id=1, source_target_pairs={{0,1},{1,2},{2,3},{3,0},{4,5},{5,6},{6,7},{7,4},{8,9},{9,10},{10,1... | collective-permute-start | bytes 196616 | tf_op jit(solution)/shard_map/ppermute | solution.py:370
  38.2 41.2 %collective-permute-start.1 = (bf16[4,2,16,256]{3,0,2,1:T(4,128)(2,1)}, bf16[4,2,16,256]{3,0,2,1:T(4,128)(2,1)S(1)}, u32[]{:S(2)}, u32[]{:S(2)}) collective-permute-start(bf16[4,2,16,256]{3,0,2,1:T(4,128)(2,1)} %get-tuple-element.58), channel_id=1, source_target_pairs={{0,2},{1,3},{2,0},{3,1},{4,6},{5,7},{6,4},{7,5},{8,10},{9,11},{10,... | collective-permute-start | bytes 196616 | tf_op jit(solution)/shard_map/ppermute | solution.py:370
  40.8 11.0 %collective-permute-start.6 = (bf16[128,1024]{1,0:T(8,128)(2,1)S(1)}, bf16[128,1024]{1,0:T(8,128)(2,1)S(1)}, u32[]{:S(2)}, u32[]{:S(2)}) collective-permute-start(bf16[128,1024]{1,0:T(8,128)(2,1)S(1)} %constant_dynamic-slice_fusion.1), channel_id=1, source_target_pairs={{0,1},{1,2},{2,3},{3,0},{4,5},{5,6},{6,7},{7,4},{8,9},{9,10},{10,1... | collective-permute-start | bytes 786440 | tf_op jit(solution)/shard_map/ppermute | solution.py:370
  41.0 33.2 %collective-permute-start.7 = (bf16[128,1024]{1,0:T(8,128)(2,1)S(1)}, bf16[128,1024]{1,0:T(8,128)(2,1)S(1)}, u32[]{:S(2)}, u32[]{:S(2)}) collective-permute-start(bf16[128,1024]{1,0:T(8,128)(2,1)S(1)} %constant_dynamic-slice_fusion.1), channel_id=1, source_target_pairs={{0,2},{1,3},{2,0},{3,1},{4,6},{5,7},{6,4},{7,5},{8,10},{9,11},{10,... | collective-permute-start | bytes 786440 | tf_op jit(solution)/shard_map/ppermute | solution.py:370
  42.7 31.6 %collective-permute-start.8 = (bf16[128,1024]{1,0:T(8,128)(2,1)S(1)}, bf16[128,1024]{1,0:T(8,128)(2,1)S(1)}, u32[]{:S(2)}, u32[]{:S(2)}) collective-permute-start(bf16[128,1024]{1,0:T(8,128)(2,1)S(1)} %constant_dynamic-slice_fusion.1), channel_id=1, source_target_pairs={{0,3},{1,0},{2,1},{3,2},{4,7},{5,4},{6,5},{7,6},{8,11},{9,8},{10,9... | collective-permute-start | bytes 786440 | tf_op jit(solution)/shard_map/ppermute | solution.py:370
  44.6 4.4 %copy-start.3 = (s32[1,4]{1,0:T(1,128)S(1)}, s32[1,4]{1,0:T(1,128)}, u32[]{:S(2)}) copy-start(s32[1,4]{1,0:T(1,128)} %lens_ref.1) | copy-start | bytes 52
  44.6 4.7 %copy-start.1 = (s32[1,4]{1,0:T(1,128)S(1)}, s32[1,4]{1,0:T(1,128)}, u32[]{:S(2)}) copy-start(s32[1,4]{1,0:T(1,128)} %counts_ref.1) | copy-start | bytes 52
  44.7 49.6 %all-to-all-start = ((bf16[8,4,128,2,128]{4,3,2,1,0:T(2,128)(2,1)}), bf16[8,4,128,2,128]{4,3,2,1,0:T(2,128)(2,1)}, u32[]{:S(2)}, u32[]{:S(2)}) async-start(bf16[8,4,128,2,128]{4,3,2,1,0:T(2,128)(2,1)} %get-tuple-element.23), calls=%async_computation | async-start | bytes 4194304 | tf_op jit(solution)/shard_map/all_to_all | solution.py:419
  49.0 27.4 %copy-start.21 = (bf16[1024]{0:T(1024)(128)(2,1)S(1)}, bf16[1024]{0:T(1024)(128)(2,1)}, u32[]{:S(2)}) copy-start(bf16[1024]{0:T(1024)(128)(2,1)} %param.17) | copy-start | bytes 6148
  49.1 28.0 %copy-start.22 = (bf16[1024]{0:T(1024)(128)(2,1)S(1)}, bf16[1024]{0:T(1024)(128)(2,1)}, u32[]{:S(2)}) copy-start(bf16[1024]{0:T(1024)(128)(2,1)} %param.18) | copy-start | bytes 6148
  51.8 29.2 %collective-permute-start.2 = (bf16[4,2,16,256]{3,0,2,1:T(4,128)(2,1)}, bf16[4,2,16,256]{3,0,2,1:T(4,128)(2,1)}, u32[]{:S(2)}, u32[]{:S(2)}) collective-permute-start(bf16[4,2,16,256]{3,0,2,1:T(4,128)(2,1)} %get-tuple-element.58), channel_id=1, source_target_pairs={{0,3},{1,0},{2,1},{3,2},{4,7},{5,4},{6,5},{7,6},{8,11},{9,8},{10,9... | collective-permute-start | bytes 196616 | tf_op jit(solution)/shard_map/ppermute | solution.py:370
  74.3 8.3 %copy-start.12 = (bf16[128,1024]{1,0:T(8,128)(2,1)}, bf16[128,1024]{1,0:T(8,128)(2,1)S(1)}, u32[]{:S(2)}) copy-start(bf16[128,1024]{1,0:T(8,128)(2,1)S(1)} %collective-permute-done.8) | copy-start | bytes 786436
  75.3 14.0 %collective-permute-start.9 = (bf16[3,128,1024]{2,1,0:T(8,128)(2,1)}, bf16[3,128,1024]{2,1,0:T(8,128)(2,1)}, u32[]{:S(2)}, u32[]{:S(2)}) collective-permute-start(bf16[3,128,1024]{2,1,0:T(8,128)(2,1)} %pad_maximum_fusion.1), channel_id=1, source_target_pairs={{0,4},{4,0},{8,12},{12,8},{16,20},{20,16},{24,28},{28,24},{1,5},{5... | collective-permute-start | bytes 2359304 | tf_op jit(solution)/shard_map/ppermute | solution.py:438
  79.4 0.6 copy-start.18
  84.1 7.0 %copy-start.11 = (bf16[256,1024]{1,0:T(8,128)(2,1)S(1)}, bf16[256,1024]{1,0:T(8,128)(2,1)}, u32[]{:S(2)}) copy-start(bf16[256,1024]{1,0:T(8,128)(2,1)} %param.20) | copy-start | bytes 1572868
  94.3 4.5 %copy-start.9 = (bf16[512,1024]{1,0:T(8,128)(2,1)S(1)}, bf16[512,1024]{1,0:T(8,128)(2,1)}, u32[]{:S(2)}) copy-start(bf16[512,1024]{1,0:T(8,128)(2,1)} %all-gather.2.cloned.1.call-done) | copy-start | bytes 3145732
  94.3 4.5 %copy-start.13 = (bf16[4,2,16,1024]{3,2,1,0:T(8,128)(2,1)S(1)}, bf16[4,2,16,1024]{3,2,1,0:T(8,128)(2,1)}, u32[]{:S(2)}) copy-start(bf16[4,2,16,1024]{3,2,1,0:T(8,128)(2,1)} %reshape.241) | copy-start | bytes 786436
  94.3 4.5 %copy-start.20 = (f32[1024]{0:T(1024)S(1)}, f32[1024]{0:T(1024)}, u32[]{:S(2)}) copy-start(f32[1024]{0:T(1024)} %convert_element_type.129) | copy-start | bytes 12292
  94.3 31.2 %all-to-all-start.1 = ((bf16[8,4,128,2,128]{4,3,2,1,0:T(2,128)(2,1)}), bf16[8,4,128,2,128]{4,3,2,1,0:T(2,128)(2,1)}, u32[]{:S(2)}, u32[]{:S(2)}) async-start(bf16[8,4,128,2,128]{4,3,2,1,0:T(2,128)(2,1)} %get-tuple-element.26), calls=%async_computation.1 | async-start | bytes 4194304 | tf_op jit(solution)/shard_map/all_to_all | solution.py:419
  98.8 0.8 copy-start.17
  98.8 1.4 copy-start.23
  101.3 1.4 copy-start.14
  101.3 1.4 copy-start.15
  104.0 2.5 %copy-start.2 = (f32[2,4]{1,0:T(2,128)S(1)}, f32[2,4]{1,0:T(2,128)}, u32[]{:S(2)}) copy-start(f32[2,4]{1,0:T(2,128)} %bias_ref.3) | copy-start | bytes 100
  104.0 2.5 %copy-start.4 = (s32[32]{0:T(128)S(1)}, s32[32]{0:T(128)}, u32[]{:S(2)}) copy-start(s32[32]{0:T(128)} %get-tuple-element.21.pos_ref) | copy-start | bytes 388
  125.4 36.7 %copy-start.8 = (bf16[4,1,128,1024]{3,2,1,0:T(8,128)(2,1)S(1)}, bf16[4,1,128,1024]{3,2,1,0:T(8,128)(2,1)}, u32[]{:S(2)}) copy-start(bf16[4,1,128,1024]{3,2,1,0:T(8,128)(2,1)} %get-tuple-element.36) | copy-start | bytes 3145732
  139.2 29.4 %copy-start.7 = (bf16[4,1,128,1024]{3,2,1,0:T(8,128)(2,1)S(1)}, bf16[4,1,128,1024]{3,2,1,0:T(8,128)(2,1)}, u32[]{:S(2)}) copy-start(bf16[4,1,128,1024]{3,2,1,0:T(8,128)(2,1)} %get-tuple-element.35) | copy-start | bytes 3145732
  139.2 29.4 %copy-start.10 = (bf16[4,1,64,1024]{3,2,1,0:T(8,128)(2,1)S(1)}, bf16[4,1,64,1024]{3,2,1,0:T(8,128)(2,1)}, u32[]{:S(2)}) copy-start(bf16[4,1,64,1024]{3,2,1,0:T(8,128)(2,1)} %get-tuple-element.38) | copy-start | bytes 1572868
  139.2 16.0 %collective-permute-start.10 = (bf16[256,128]{1,0:T(8,128)(2,1)S(1)}, bf16[256,128]{1,0:T(8,128)(2,1)S(1)}, u32[]{:S(2)}, u32[]{:S(2)}) collective-permute-start(bf16[256,128]{1,0:T(8,128)(2,1)S(1)} %bitcast.174), channel_id=1, source_target_pairs={{0,1},{1,2},{2,3},{3,0},{4,5},{5,6},{6,7},{7,4},{8,9},{9,10},{10,1... | collective-permute-start | bytes 196616 | tf_op jit(solution)/shard_map/ppermute | solution.py:370
  150.2 10.9 %collective-permute-start.11 = (bf16[256,128]{1,0:T(8,128)(2,1)S(1)}, bf16[256,128]{1,0:T(8,128)(2,1)S(1)}, u32[]{:S(2)}, u32[]{:S(2)}) collective-permute-start(bf16[256,128]{1,0:T(8,128)(2,1)S(1)} %bitcast.175), channel_id=1, source_target_pairs={{0,2},{1,3},{2,0},{3,1},{4,6},{5,7},{6,4},{7,5},{8,10},{9,11},{10,... | collective-permute-start | bytes 196616 | tf_op jit(solution)/shard_map/ppermute | solution.py:370
  151.8 9.4 %collective-permute-start.12 = (bf16[256,128]{1,0:T(8,128)(2,1)S(1)}, bf16[256,128]{1,0:T(8,128)(2,1)S(1)}, u32[]{:S(2)}, u32[]{:S(2)}) collective-permute-start(bf16[256,128]{1,0:T(8,128)(2,1)S(1)} %bitcast.176), channel_id=1, source_target_pairs={{0,3},{1,0},{2,1},{3,2},{4,7},{5,4},{6,5},{7,6},{8,11},{9,8},{10,9... | collective-permute-start | bytes 196616 | tf_op jit(solution)/shard_map/ppermute | solution.py:370
  152.7 9.9 %collective-permute-start.3 = (bf16[256,128]{1,0:T(8,128)(2,1)S(1)}, bf16[256,128]{1,0:T(8,128)(2,1)S(1)}, u32[]{:S(2)}, u32[]{:S(2)}) collective-permute-start(bf16[256,128]{1,0:T(8,128)(2,1)S(1)} %bitcast.166), channel_id=1, source_target_pairs={{0,1},{1,2},{2,3},{3,0},{4,5},{5,6},{6,7},{7,4},{8,9},{9,10},{10,1... | collective-permute-start | bytes 196616 | tf_op jit(solution)/shard_map/ppermute | solution.py:370
  153.9 12.2 %collective-permute-start.4 = (bf16[256,128]{1,0:T(8,128)(2,1)S(1)}, bf16[256,128]{1,0:T(8,128)(2,1)S(1)}, u32[]{:S(2)}, u32[]{:S(2)}) collective-permute-start(bf16[256,128]{1,0:T(8,128)(2,1)S(1)} %bitcast.167), channel_id=1, source_target_pairs={{0,2},{1,3},{2,0},{3,1},{4,6},{5,7},{6,4},{7,5},{8,10},{9,11},{10,... | collective-permute-start | bytes 196616 | tf_op jit(solution)/shard_map/ppermute | solution.py:370
  155.2 11.4 %collective-permute-start.5 = (bf16[256,128]{1,0:T(8,128)(2,1)S(1)}, bf16[256,128]{1,0:T(8,128)(2,1)S(1)}, u32[]{:S(2)}, u32[]{:S(2)}) collective-permute-start(bf16[256,128]{1,0:T(8,128)(2,1)S(1)} %bitcast.168), channel_id=1, source_target_pairs={{0,3},{1,0},{2,1},{3,2},{4,7},{5,4},{6,5},{7,6},{8,11},{9,8},{10,9... | collective-permute-start | bytes 196616 | tf_op jit(solution)/shard_map/ppermute | solution.py:370
  161.2 18.1 %collective-permute-start.16 = (bf16[256,128]{1,0:T(8,128)(2,1)S(1)}, bf16[256,128]{1,0:T(8,128)(2,1)S(1)}, u32[]{:S(2)}, u32[]{:S(2)}) collective-permute-start(bf16[256,128]{1,0:T(8,128)(2,1)S(1)} %bitcast.162), channel_id=1, source_target_pairs={{0,1},{1,2},{2,3},{3,0},{4,5},{5,6},{6,7},{7,4},{8,9},{9,10},{10,1... | collective-permute-start | bytes 196616 | tf_op jit(solution)/shard_map/ppermute | solution.py:370
  161.2 18.5 %collective-permute-start.17 = (bf16[256,128]{1,0:T(8,128)(2,1)S(1)}, bf16[256,128]{1,0:T(8,128)(2,1)S(1)}, u32[]{:S(2)}, u32[]{:S(2)}) collective-permute-start(bf16[256,128]{1,0:T(8,128)(2,1)S(1)} %bitcast.163), channel_id=1, source_target_pairs={{0,2},{1,3},{2,0},{3,1},{4,6},{5,7},{6,4},{7,5},{8,10},{9,11},{10,... | collective-permute-start | bytes 196616 | tf_op jit(solution)/shard_map/ppermute | solution.py:370
  162.1 7.0 %copy-start.6 = (bf16[2,1024,1024]{2,1,0:T(8,128)(2,1)S(1)}, bf16[2,1024,1024]{2,1,0:T(8,128)(2,1)}, u32[]{:S(2)}) copy-start(bf16[2,1024,1024]{2,1,0:T(8,128)(2,1)} %param.21) | copy-start | bytes 12582916
  162.6 6.6 %copy-start.16 = (f32[1024]{0:T(1024)S(1)}, f32[1024]{0:T(1024)}, u32[]{:S(2)}) copy-start(f32[1024]{0:T(1024)} %convert_element_type.142) | copy-start | bytes 12292
  162.6 9.0 %collective-permute-start.19 = (bf16[256,128]{1,0:T(8,128)(2,1)S(1)}, bf16[256,128]{1,0:T(8,128)(2,1)S(1)}, u32[]{:S(2)}, u32[]{:S(2)}) collective-permute-start(bf16[256,128]{1,0:T(8,128)(2,1)S(1)} %bitcast.170), channel_id=1, source_target_pairs={{0,1},{1,2},{2,3},{3,0},{4,5},{5,6},{6,7},{7,4},{8,9},{9,10},{10,1... | collective-permute-start | bytes 196616 | tf_op jit(solution)/shard_map/ppermute | solution.py:370
  166.1 8.5 %collective-permute-start.20 = (bf16[256,128]{1,0:T(8,128)(2,1)S(1)}, bf16[256,128]{1,0:T(8,128)(2,1)S(1)}, u32[]{:S(2)}, u32[]{:S(2)}) collective-permute-start(bf16[256,128]{1,0:T(8,128)(2,1)S(1)} %bitcast.171), channel_id=1, source_target_pairs={{0,2},{1,3},{2,0},{3,1},{4,6},{5,7},{6,4},{7,5},{8,10},{9,11},{10,... | collective-permute-start | bytes 196616 | tf_op jit(solution)/shard_map/ppermute | solution.py:370
  166.6 8.7 %collective-permute-start.21 = (bf16[256,128]{1,0:T(8,128)(2,1)S(1)}, bf16[256,128]{1,0:T(8,128)(2,1)S(1)}, u32[]{:S(2)}, u32[]{:S(2)}) collective-permute-start(bf16[256,128]{1,0:T(8,128)(2,1)S(1)} %bitcast.172), channel_id=1, source_target_pairs={{0,3},{1,0},{2,1},{3,2},{4,7},{5,4},{6,5},{7,6},{8,11},{9,8},{10,9... | collective-permute-start | bytes 196616 | tf_op jit(solution)/shard_map/ppermute | solution.py:370
  171.6 8.1 %collective-permute-start.18 = (bf16[256,128]{1,0:T(8,128)(2,1)S(1)}, bf16[256,128]{1,0:T(8,128)(2,1)S(1)}, u32[]{:S(2)}, u32[]{:S(2)}) collective-permute-start(bf16[256,128]{1,0:T(8,128)(2,1)S(1)} %bitcast.164), channel_id=1, source_target_pairs={{0,3},{1,0},{2,1},{3,2},{4,7},{5,4},{6,5},{7,6},{8,11},{9,8},{10,9... | collective-permute-start | bytes 196616 | tf_op jit(solution)/shard_map/ppermute | solution.py:370
  174.6 10.0 %collective-permute-start.13 = (bf16[64,1024]{1,0:T(8,128)(2,1)S(1)}, bf16[64,1024]{1,0:T(8,128)(2,1)S(1)}, u32[]{:S(2)}, u32[]{:S(2)}) collective-permute-start(bf16[64,1024]{1,0:T(8,128)(2,1)S(1)} %get-tuple-element.44), channel_id=1, source_target_pairs={{0,1},{1,2},{2,3},{3,0},{4,5},{5,6},{6,7},{7,4},{8,9},{9,10},{10,1... | collective-permute-start | bytes 393224 | tf_op jit(solution)/shard_map/ppermute | solution.py:370
  175.3 11.9 %collective-permute-start.14 = (bf16[64,1024]{1,0:T(8,128)(2,1)S(1)}, bf16[64,1024]{1,0:T(8,128)(2,1)S(1)}, u32[]{:S(2)}, u32[]{:S(2)}) collective-permute-start(bf16[64,1024]{1,0:T(8,128)(2,1)S(1)} %get-tuple-element.46), channel_id=1, source_target_pairs={{0,2},{1,3},{2,0},{3,1},{4,6},{5,7},{6,4},{7,5},{8,10},{9,11},{10,... | collective-permute-start | bytes 393224 | tf_op jit(solution)/shard_map/ppermute | solution.py:370
  179.2 8.0 %collective-permute-start.15 = (bf16[64,1024]{1,0:T(8,128)(2,1)S(1)}, bf16[64,1024]{1,0:T(8,128)(2,1)S(1)}, u32[]{:S(2)}, u32[]{:S(2)}) collective-permute-start(bf16[64,1024]{1,0:T(8,128)(2,1)S(1)} %get-tuple-element.45), channel_id=1, source_target_pairs={{0,3},{1,0},{2,1},{3,2},{4,7},{5,4},{6,5},{7,6},{8,11},{9,8},{10,9... | collective-permute-start | bytes 393224 | tf_op jit(solution)/shard_map/ppermute | solution.py:370
  182.7 7.0 %collective-permute-start.22 = (bf16[64,1024]{1,0:T(8,128)(2,1)S(1)}, bf16[64,1024]{1,0:T(8,128)(2,1)S(1)}, u32[]{:S(2)}, u32[]{:S(2)}) collective-permute-start(bf16[64,1024]{1,0:T(8,128)(2,1)S(1)} %get-tuple-element.47), channel_id=1, source_target_pairs={{0,1},{1,2},{2,3},{3,0},{4,5},{5,6},{6,7},{7,4},{8,9},{9,10},{10,1... | collective-permute-start | bytes 393224 | tf_op jit(solution)/shard_map/ppermute | solution.py:370
  184.6 8.6 %collective-permute-start.23 = (bf16[64,1024]{1,0:T(8,128)(2,1)S(1)}, bf16[64,1024]{1,0:T(8,128)(2,1)S(1)}, u32[]{:S(2)}, u32[]{:S(2)}) collective-permute-start(bf16[64,1024]{1,0:T(8,128)(2,1)S(1)} %get-tuple-element.49), channel_id=1, source_target_pairs={{0,2},{1,3},{2,0},{3,1},{4,6},{5,7},{6,4},{7,5},{8,10},{9,11},{10,... | collective-permute-start | bytes 393224 | tf_op jit(solution)/shard_map/ppermute | solution.py:370
  184.6 8.6 %collective-permute-start.24 = (bf16[64,1024]{1,0:T(8,128)(2,1)S(1)}, bf16[64,1024]{1,0:T(8,128)(2,1)S(1)}, u32[]{:S(2)}, u32[]{:S(2)}) collective-permute-start(bf16[64,1024]{1,0:T(8,128)(2,1)S(1)} %get-tuple-element.48), channel_id=1, source_target_pairs={{0,3},{1,0},{2,1},{3,2},{4,7},{5,4},{6,5},{7,6},{8,11},{9,8},{10,9... | collective-permute-start | bytes 393224 | tf_op jit(solution)/shard_map/ppermute | solution.py:370
Sparse Core Ops, SparseCore 0:
  44.8 38.7 all-gather.1
where the time goes:
time: 204 us; the launch traced here: 201 us
  starting transfers between devices  52.2 us (26%)
  waiting for transfers between devices  41.6 us (20%)
  Pallas kernels  34.6 us (17%)
  local copies, waits for them, and re-layouts  19.5 us (10%)
  blocking collectives  19.4 us (10%)
  between operations  14 us (7%)
  other arithmetic  10.9 us (5%)
  matrix products  8.67 us (4%)
    ppermute x24, starting transfers between devices, shift(): return lax.ppermute(value, axis, [(i, (i + k) % n) for i in range(n)])  43.3 us
    ppermute x24, waiting for transfers between devices, shift(): return lax.ppermute(value, axis, [(i, (i + k) % n) for i in range(n)])  36.4 us
    pallas_call x2, Pallas kernels, attend(): pl.pallas_call(functools.partial(attend_kernel, group, per), grid=(1,), o...  27.6 us
    psum x1, blocking collectives, per_device(): asked = lax.psum(wanted, 'dp')  10.2 us
    all_gather x1, blocking collectives, per_device(): both_all = lax.all_gather(both_parts, 'dp', axis=0, tiled=True)  9.21 us
    all_to_all x2, starting transfers between devices, per_device(): got = lax.all_to_all(send, 'dp', split_axis=0, concat_axis=0, tiled=True)  8.88 us
    dynamic_update_slice x4, local copies, waits for them, and re-layouts, per_device(): lax.dynamic_update_index_in_dim(down_sel, block, (tp - k) % n_tp, 3)  7.36 us
    all_to_all x2, waiting for transfers between devices, per_device(): got = lax.all_to_all(send, 'dp', split_axis=0, concat_axis=0, tiled=True)  5.15 us
  transfers between devices with their start and end apart: 28, of which 7 were waited for; matrix products, arithmetic and copies ran while one was open for 17% of the time, Pallas kernels for 7%

commit v1 on v0

--- a/solution.py
+++ b/solution.py
@@ -23,23 +23,6 @@
     values = values.astype(F32)
     inv_scale = lax.rsqrt(jnp.mean(values * values, axis=-1, keepdims=True) + 1e-05)
     return values * inv_scale * gain.astype(F32)
-
-
-def rotary(values, time_pos):
-    half_dim = values.shape[-1] // 2
-    frequency = 10000.0 ** (-2.0 * jnp.arange(half_dim, dtype=F32) / values.shape[-1])
-    angles = time_pos.astype(F32)[:, None] * frequency[None, :]
-    cosine = jnp.cos(angles)[:, None, :]
-    sine_part = jnp.sin(angles)[:, None, :]
-    first_half = values[..., :half_dim]
-    second_half = values[..., half_dim:]
-    return jnp.concatenate(
-        [
-            first_half * cosine - second_half * sine_part,
-            first_half * sine_part + second_half * cosine,
-        ],
-        axis=-1,
-    )
 
 
 def token_layout(req_lens, live_counts, page_len, tok_total):
@@ -55,61 +38,31 @@
     return (onehot, cached * page_len + tok_index - first_pos)
 
 
-def want_kernel(n_dp, cap, pool_dev, me_ref, table_ref, want_ref, pos_ref, count):
-    me = me_ref[0]
-    slots = table_ref.shape[1]
-
-    def clear(g, carry):
-        count[g] = 0
-        for j in range(n_dp * cap):
-            want_ref[g, j] = 0
-        return carry
-
-    lax.fori_loop(0, n_dp, clear, 0)
-
-    def place(p, carry):
-        page = table_ref[0, p]
-        home = page // pool_dev
-        rank = count[home]
-        count[home] = rank + 1
-        want_ref[me, home * cap + rank] = page - home * pool_dev
-        pos_ref[p] = home * cap + rank
-        return carry
-
-    lax.fori_loop(0, slots, place, 0)
-
-
-def want(me, page_table, n_dp, cap, pool_dev):
-    smem = pl.BlockSpec(memory_space=pltpu.SMEM)
-    return pl.pallas_call(
-        functools.partial(want_kernel, n_dp, cap, pool_dev),
-        out_shape=(
-            jax.ShapeDtypeStruct((n_dp, n_dp * cap), jnp.int32),
-            jax.ShapeDtypeStruct((page_table.shape[1],), jnp.int32),
-        ),
-        in_specs=[smem, smem],
-        out_specs=(smem, smem),
-        scratch_shapes=[pltpu.SMEM((n_dp,), jnp.int32)],
-        name="want_pages",
-    )(me, page_table)
-
-
 def pick_kernel(n_dp, cap, me_ref, asked_ref, pool_ref, *rest):
     n_out = len(rest) - 3
     outs, (buf, sem_in, sem_out) = rest[:n_out], rest[n_out:]
     lanes = outs[0].shape[-1]
     me = me_ref[0]
-    copies = []
-    for g in range(n_dp):
-        for k in range(cap):
-            page = asked_ref[g, me * cap + k]
-            copy = pltpu.make_async_copy(pool_ref.at[page], buf.at[g, k], sem_in.at[g, k])
-            copy.start()
-            copies.append(copy)
+    slots = asked_ref.shape[2]
+
+    def find(g, carry):
+        count = jnp.int32(0)
+        for p in range(slots):
+            hit = asked_ref[g, 0, p] == me
+
+            @pl.when(hit)
+            def _():
+                pltpu.make_async_copy(
+                    pool_ref.at[asked_ref[g, 1, p]], buf.at[g, count], sem_in.at[g]
+                ).start()
+
+            count = count + hit.astype(jnp.int32)
+        return carry
+
+    lax.fori_loop(0, n_dp, find, 0)
     done = []
     for g in range(n_dp):
-        for k in range(cap):
-            copies[g * cap + k].wait()
+        pltpu.make_async_copy(pool_ref.at[pl.ds(0, cap)], buf.at[g], sem_in.at[g]).wait()
         for a in range(n_out):
             copy = pltpu.make_async_copy(
                 buf.at[g, :, :, :, pl.ds(a * lanes, lanes)], outs[a].at[g], sem_out.at[a, g]
@@ -132,11 +85,145 @@
         out_specs=[hbm] * n_out,
         scratch_shapes=[
             pltpu.VMEM(shape + pool.shape[-1:], pool.dtype),
-            pltpu.SemaphoreType.DMA((n_dp, cap)),
+            pltpu.SemaphoreType.DMA((n_dp,)),
             pltpu.SemaphoreType.DMA((n_out, n_dp)),
         ],
+        cost_estimate=pl.CostEstimate(flops=0, bytes_accessed=4 * pool.size, transcendentals=0),
         name="pick_pages",
     )(me, asked, pool)
+
+
+def named_kernel(n_loc, span, table_ref, ids_ref, all_ref, down_ref, up_ref, sem):
+    copies = []
+    for r in range(ids_ref.shape[1]):
+        slot = table_ref[ids_ref[0, r]]
+        home, inner = slot // n_loc, slot % n_loc
+        for half, out in ((0, down_ref), (1, up_ref)):
+            base = pl.multiple_of((half * n_loc + inner) * span, span)
+            copy = pltpu.make_async_copy(
+                all_ref.at[home, pl.ds(base, span)], out.at[pl.ds(r * span, span)], sem.at[r, half]
+            )
+            copy.start()
+            copies.append(copy)
+    for copy in copies:
+        copy.wait()
+
+
+def named(owner_table, adapter_ids, gathered, n_loc, span):
+    n_req = adapter_ids.shape[1]
+    smem = pl.BlockSpec(memory_space=pltpu.SMEM)
+    vmem = pl.BlockSpec(memory_space=pltpu.VMEM)
+    out = jax.ShapeDtypeStruct((n_req * span, gathered.shape[-1]), BF)
+    return pl.pallas_call(
+        functools.partial(named_kernel, n_loc, span),
+        out_shape=(out, out),
+        in_specs=[smem, smem, pl.BlockSpec(memory_space=pl.ANY)],
+        out_specs=(vmem, vmem),
+        scratch_shapes=[pltpu.SemaphoreType.DMA((n_req, 2))],
+        name="named_adapters",
+    )(owner_table, adapter_ids, gathered)
+
+
+def project_kernel(
+    n_tp, cap, pool_dev, tp_ref, lens_ref, table_ref, gain_ref, w_ref, up_ref, cos_ref, sin_ref, *rest
+):
+    tok_refs, down_refs = rest[:n_tp], rest[n_tp : 2 * n_tp]
+    q_ref, k_ref, v_ref, pos_ref, down, count = rest[2 * n_tp :]
+    tp = tp_ref[0]
+    rows, _ = tok_refs[0].shape
+    width = q_ref.shape[1]
+    dd = down_refs[0].shape[1]
+    n_low = down_refs[0].shape[0]
+    n_req = lens_ref.shape[1]
+    rank = n_low // n_req // 2
+
+    for g in range(count.shape[0]):
+        count[g] = 0
+
+    def place(p, carry):
+        home = table_ref[0, p] // pool_dev
+        seen = count[home]
+        count[home] = seen + 1
+        pos_ref[p] = home * cap + seen
+        return carry
+
+    lax.fori_loop(0, table_ref.shape[1], place, 0)
+
+    for k in range(n_tp):
+        at = lax.rem(tp - k + n_tp, n_tp)
+        down[at] = down_refs[k][...]
+    lane = lax.broadcasted_iota(jnp.int32, (1, 128), 1)
+    first = jnp.bitwise_and(lane, HD - 1) < HD // 2
+
+    def rope(u, cos, sin):
+        parts = []
+        for a in range(width // 128):
+            part = u[:, a * 128 : (a + 1) * 128]
+            other = jnp.where(
+                first, pltpu.roll(part, 128 - HD // 2, 1), pltpu.roll(part, HD // 2, 1)
+            )
+            parts.append(part * cos + other * sin)
+        return parts
+
+    for k in range(n_tp):
+        row0 = pl.multiple_of(lax.rem(tp - k + n_tp, n_tp) * rows, rows)
+        x = tok_refs[k][...].astype(F32)
+        inv = lax.rsqrt(jnp.mean(x * x, axis=1, keepdims=True) + 1e-05)
+        normed = (x * inv * gain_ref[...].astype(F32)).astype(BF)
+        low = jnp.zeros((rows, n_low), F32)
+        for j in range(n_tp):
+            low = low + lax.dot_general(
+                normed[:, j * dd : (j + 1) * dd], down[j], (((1,), (1,)), ((), ())),
+                preferred_element_type=F32,
+            )
+        row = row0 + lax.broadcasted_iota(jnp.int32, (rows, n_low), 0)
+        col = lax.broadcasted_iota(jnp.int32, (rows, n_low), 1)
+        request = jnp.zeros((rows, n_low), jnp.int32)
+        end = jnp.int32(0)
+        for r in range(n_req - 1):
+            end = end + lens_ref[0, r]
+            request = request + (row >= end).astype(jnp.int32)
+        own = col // (2 * rank) == request
+        kind = (col // rank) % 2
+        deltas = []
+        for kk in range(2):
+            part = jnp.where(own & (kind == kk), low, 0.0).astype(BF)
+            deltas.append(jnp.dot(part, up_ref[...], preferred_element_type=F32))
+        cos = cos_ref[pl.ds(row0, rows), :]
+        sin = sin_ref[pl.ds(row0, rows), :]
+        q = jnp.dot(normed, w_ref[0], preferred_element_type=F32) + deltas[0]
+        for a, part in enumerate(rope(q, cos, sin)):
+            part = part.astype(BF).astype(F32) * (HD ** -0.5)
+            q_ref[pl.ds(row0, rows), a * 128 : (a + 1) * 128] = part.astype(BF)
+        kk = jnp.dot(normed, w_ref[1], preferred_element_type=F32)
+        for a, part in enumerate(rope(kk, cos, sin)):
+            k_ref[pl.ds(row0, rows), a * 128 : (a + 1) * 128] = part.astype(BF)
+        v = jnp.dot(normed, w_ref[2], preferred_element_type=F32) + deltas[1]
+        v_ref[pl.ds(row0, rows), :] = v.astype(BF)
+
+
+def project(tp, lens, table, gain, w_qkv, up, cos, sin, toks, downs, n_dp, cap, pool_dev):
+    n_tp = len(toks)
+    rows = toks[0].shape[0] * n_tp
+    width = w_qkv.shape[2]
+    smem = pl.BlockSpec(memory_space=pltpu.SMEM)
+    vmem = pl.BlockSpec(memory_space=pltpu.VMEM)
+    out = jax.ShapeDtypeStruct((rows, width), BF)
+    return pl.pallas_call(
+        functools.partial(project_kernel, n_tp, cap, pool_dev),
+        out_shape=(out, out, out, jax.ShapeDtypeStruct((table.shape[1],), jnp.int32)),
+        in_specs=[smem] * 3 + [vmem] * (5 + 2 * n_tp),
+        out_specs=(vmem, vmem, vmem, smem),
+        scratch_shapes=[
+            pltpu.VMEM((n_tp,) + downs[0].shape, BF),
+            pltpu.SMEM((n_dp,), jnp.int32),
+        ],
+        compiler_params=pltpu.CompilerParams(vmem_limit_bytes=32 << 20),
+        cost_estimate=pl.CostEstimate(
+            flops=8 * rows * w_qkv.size // 3, bytes_accessed=4 * w_qkv.size, transcendentals=0
+        ),
+        name="project",
+    )(tp, lens, table, gain, w_qkv, up, cos, sin, *toks, *downs)
 
 
 def attend_kernel(
@@ -393,47 +480,40 @@
     tp = lax.axis_index("tensor")
     dp = lax.axis_index("dp")
     me = dp.astype(jnp.int32).reshape(1)
+    tp_id = tp.astype(jnp.int32).reshape(1)
     row_count, d_model = tokens.shape
     tok_total = row_count * n_tp
     width = w_out.shape[0]
-    heads = width // HD
     page_len = cache_pool.shape[1]
+    pool_dev = cache_pool.shape[0]
     cap = max(1, page_table.shape[1] // n_dp)
     far_first = [k for k in range(1, n_tp)]
-
     lanes = min(width, 2 * HD)
     n_group = width // lanes
     slots = n_dp * cap
-    wanted, buffer_pos = want(me, page_table, n_dp, cap, cache_pool.shape[0])
-    asked = lax.psum(wanted, "dp")
-    picked = pick(me, asked, cache_pool, n_dp, cap, lanes)
+    dd = d_model // n_tp
+    n_loc, _, rank, _ = adapter_down.shape
+    span = 2 * rank
+
+    toks = [tokens] + [shift(tokens, "tensor", n_tp, k) for k in far_first]
+
+    down_part = lax.dynamic_slice_in_dim(adapter_down, tp * dd, dd, 3).reshape(n_loc * span, dd)
+    names = jnp.concatenate([page_table // pool_dev, page_table % pool_dev], axis=0).astype(BF)
+    names = jnp.pad(names, ((0, 14), (0, dd - names.shape[1])))
+    payload = jnp.concatenate([down_part, adapter_up.reshape(n_loc * span, width), names], axis=0)
+    gathered = lax.all_gather(payload, "dp", axis=0)
+    asked = gathered[:, 2 * n_loc * span : 2 * n_loc * span + 2, : page_table.shape[1]]
+    picked = pick(me, asked.astype(jnp.int32), cache_pool, n_dp, cap, lanes)
+    fetched = [
+        lax.all_to_all(picked[0], "dp", split_axis=0, concat_axis=0, tiled=True)
+    ]
+
     own_half = lax.dynamic_slice_in_dim(w_out, (dp % 2) * (width // 2), width // 2, 0)
-    picked, own_half, lengths, adapter_ids, page_counts = lax.optimization_barrier(
-        (picked, own_half, lengths, adapter_ids, page_counts)
-    )
-    fetched = []
-    for a in range(n_group):
-        send = picked[a]
-        if fetched:
-            send, _ = lax.optimization_barrier((send, fetched[-1]))
-        got = lax.all_to_all(send, "dp", split_axis=0, concat_axis=0, tiled=True)
-        fetched.append(got.reshape(slots, 2 * page_len, lanes))
-
-    all_tokens = lax.all_gather(tokens, "tensor", axis=0, tiled=True)
-    normed = normalize(all_tokens, attn_gain).astype(BF)
-
-    dd = d_model // n_tp
-    down_part = lax.dynamic_slice_in_dim(adapter_down, tp * dd, dd, 3)
-    both_parts = jnp.concatenate([down_part, adapter_up], axis=3)
-    both_all = lax.all_gather(both_parts, "dp", axis=0, tiled=True)
-    slot_ids = jnp.take(owner_table, adapter_ids[0])
-    select = (
-        slot_ids[:, None] == jnp.arange(both_all.shape[0], dtype=jnp.int32)[None, :]
-    ).astype(BF)
-    both_sel = jnp.einsum("rn,nkce->rkce", select, both_all, preferred_element_type=F32).astype(BF)
-    down_named, up_sel = both_sel[..., :dd], both_sel[..., dd:]
-    down_blocks = [down_named] + [shift(down_named, "tensor", n_tp, k) for k in far_first]
-
+    gathered, lengths_b = lax.optimization_barrier((gathered, lengths, picked))[:2]
+    down_named, up_named = named(owner_table, adapter_ids, gathered, n_loc, span)
+    downs = [down_named] + [shift(down_named, "tensor", n_tp, k) for k in far_first]
+
+    own_half = lax.optimization_barrier((own_half, toks[1:], downs[1:]))[0]
     halves = jnp.stack([shift(own_half, "tensor", n_tp, k) for k in far_first])
     twins = lax.ppermute(halves, "dp", [(i, i ^ 1) for i in range(n_dp)])
     w_rest = jnp.where(
@@ -443,52 +523,56 @@
     )
     w_whole = jnp.concatenate([w_out[None], w_rest], axis=0)
 
-    live_counts = page_counts[0]
-    onehot, position = token_layout(lengths[0], live_counts, page_len, tok_total)
-    member = onehot.astype(F32)
-    projected = jnp.einsum("td,kde->kte", normed, w_qkv, preferred_element_type=F32)
-    n_req = member.shape[1]
-    rank = down_named.shape[2]
-    down_sel = jnp.zeros((n_req, 2, rank, n_tp, dd), BF)
-    for k, block in enumerate(down_blocks):
-        down_sel = lax.dynamic_update_index_in_dim(down_sel, block, (tp - k) % n_tp, 3)
-    down_sel = down_sel.reshape(n_req, 2, rank, d_model)
-    lowall = jnp.einsum("td,rkcd->rtkc", normed, down_sel, preferred_element_type=F32)
-    low_rank = jnp.sum(
-        lowall * jnp.transpose(member)[:, :, None, None], axis=0
-    ).astype(BF)
-    spread = (jnp.transpose(member)[:, :, None, None] * low_rank.astype(F32)).astype(BF)
-    delta_proj = jnp.einsum("rtkc,rkce->kte", spread, up_sel, preferred_element_type=F32)
-    time_pos = position % VARLEN
-    query = rotary((projected[0] + delta_proj[0]).reshape(tok_total, heads, HD), time_pos)
-    query = (query.astype(BF) * BF(HD ** -0.5)).reshape(tok_total, width)
-    new_keys = rotary(projected[1].reshape(tok_total, heads, HD), time_pos)
-    new_keys = new_keys.astype(BF).reshape(tok_total, width)
-    new_values = (projected[2] + delta_proj[1]).astype(BF)
+    _, position = token_layout(lengths_b[0], page_counts[0], page_len, tok_total)
+    index = jnp.arange(2 * HD, dtype=jnp.int32)
+    frequency = 10000.0 ** (-2.0 * (index % (HD // 2)).astype(F32) / HD)
+    angles = (position % VARLEN).astype(F32)[:, None] * frequency[None, :]
+    sign = jnp.where(index % HD < HD // 2, -1.0, 1.0).astype(F32)
+    query, new_keys, new_values, buffer_pos = project(
+        tp_id, lengths, page_table, attn_gain.reshape(1, d_model), w_qkv, up_named,
+        jnp.cos(angles), jnp.sin(angles) * sign[None, :], toks, downs, n_dp, cap, pool_dev,
+    )
+    for a in range(1, n_group):
+        send, _ = lax.optimization_barrier((picked[a], fetched[-1]))
+        fetched.append(lax.all_to_all(send, "dp", split_axis=0, concat_axis=0, tiled=True))
+    fetched = [f.reshape(slots, 2 * page_len, lanes) for f in fetched]
+
+    all_tokens = jnp.zeros((n_tp, row_count, d_model), BF)
+    for k, block in enumerate(toks):
+        all_tokens = lax.dynamic_update_index_in_dim(all_tokens, block, (tp - k) % n_tp, 0)
 
     n_chunk = max(1, row_count // CHUNK)
     sub = row_count // n_chunk
-    mixes = [[] for _ in range(n_chunk)]
-    for a in range(n_group):
-        mix = attend(
+    w_parts = w_whole.reshape(n_tp, n_group, lanes, d_model)
+    base = all_tokens.astype(F32).reshape(tok_total, d_model)
+
+    def mixed(blocks, a):
+        return jnp.dot(
+            jnp.concatenate(blocks, axis=1),
+            w_parts[:, a].reshape(n_tp * lanes, d_model),
+            preferred_element_type=F32,
+        )
+
+    def attended(a, q):
+        return attend(
             a, lanes, 2 * TILE, lengths, page_counts, buffer_pos, variate_bias,
-            query, new_keys, new_values, fetched[a],
-        ).reshape(n_tp, n_chunk, sub, lanes)
-        for c in range(n_chunk):
-            own = mix[:, c].reshape(n_tp * sub, lanes)
-            mixes[c].append([own] + [shift(own, "tensor", n_tp, k) for k in far_first])
-
-    base = all_tokens.reshape(n_tp, n_chunk, sub, d_model)
-    w_parts = w_whole.reshape(n_tp, n_group, lanes, d_model)
+            q, new_keys, new_values, fetched[a],
+        )
+
+    for a in range(n_group - 1):
+        mix = attended(a, query)
+        blocks = [mix] + [shift(mix, "tensor", n_tp, k) for k in far_first]
+        base = base + mixed(blocks, a)
+        query, base = lax.optimization_barrier((query, base))
+    mix = attended(n_group - 1, query).reshape(n_tp, n_chunk, sub, lanes)
+    base = base.reshape(n_tp, n_chunk, sub, d_model)
+    gathered_mix = []
+    for c in range(n_chunk):
+        own = mix[:, c].reshape(n_tp * sub, lanes)
+        gathered_mix.append([own] + [shift(own, "tensor", n_tp, k) for k in far_first])
     outs = []
     for c in range(n_chunk):
-        residual = base[:, c].reshape(n_tp * sub, d_model).astype(F32)
-        for a in range(n_group):
-            residual = residual + jnp.dot(
-                jnp.concatenate(mixes[c][a], axis=1),
-                w_parts[:, a].reshape(n_tp * lanes, d_model),
-                preferred_element_type=F32,
-            )
+        residual = base[:, c].reshape(n_tp * sub, d_model) + mixed(gathered_mix[c], n_group - 1)
         ffn_in = normalize(residual, ffn_gain).astype(BF)
         gate_up = jnp.einsum("td,kdf->ktf", ffn_in, w_gateup, preferred_element_type=F32)
         hidden = (jax.nn.silu(gate_up[0]) * gate_up[1]).astype(BF)

time: 204 us -> 188 us (0.922); the launches traced: 201 us -> 187 us
  between operations: 14 us -> 0.45 us
  waiting for transfers between devices: 41.6 us -> 54.4 us
  blocking collectives: 19.4 us -> 11.4 us
  local copies, waits for them, and re-layouts: 19.5 us -> 16.6 us
    ppermute x24, waiting for transfers between devices: 36.4 us -> 54.4 us  [shift(): return lax.ppermute(value, axis, [(i, (i + k) % n) for i in range(n)])]
    psum x1 -> x0, blocking collectives: 10.2 us -> none  [per_device(): asked = lax.psum(wanted, 'dp')]
    unnamed x50 -> x58, local copies, waits for them, and re-layouts: 1.23 us -> 9.27 us
    all_to_all x2, waiting for transfers between devices: 5.15 us -> 0.01 us  [the longest x1 0.01 us: per_device(): lax.all_to_all(picked[0], 'dp', split_axis=0, concat_axis=0, tiled=True)]
    dynamic_update_slice x4, local copies, waits for them, and re-layouts: 7.36 us -> 3 us  [per_device(): lax.dynamic_update_index_in_dim(all_tokens, block, (tp - k) % n_tp, 0)]
    pallas_call x1 -> x2, Pallas kernels: 2.15 us -> 5.83 us  [the longest x1 3.59 us: project(): pl.pallas_call(functools.partial(project_kernel, n_tp, cap, pool_dev), ou...]
    pallas_call x2, Pallas kernels: 27.6 us -> 24.2 us  [attend(): pl.pallas_call(functools.partial(attend_kernel, group, per), grid=(1,), o...]
    slice x3 -> x1, local copies, waits for them, and re-layouts: 3.04 us -> 0.14 us  [per_device(): base[:, c].reshape(n_tp * sub, d_model)]
  transfers between devices with their start and end apart: 28 -> 27, of which waited for: 7 -> 11; matrix products, arithmetic and copies ran while one was open for 17% -> 10% of each run, Pallas kernels for 7% -> 10%
where the time goes in v1:
time: 188 us; the launch traced here: 187 us
  waiting for transfers between devices  54.4 us (29%)
  starting transfers between devices  51 us (27%)
  Pallas kernels  34.6 us (18%)
  local copies, waits for them, and re-layouts  16.6 us (9%)
  blocking collectives  11.4 us (6%)
  other arithmetic  10.1 us (5%)
  matrix products  8.67 us (5%)
    ppermute x24, waiting for transfers between devices, shift(): return lax.ppermute(value, axis, [(i, (i + k) % n) for i in range(n)])  54.4 us
    ppermute x24, starting transfers between devices, shift(): return lax.ppermute(value, axis, [(i, (i + k) % n) for i in range(n)])  42.1 us
    pallas_call x2, Pallas kernels, attend(): pl.pallas_call(functools.partial(attend_kernel, group, per), grid=(1,), o...  24.2 us
    all_gather x1, blocking collectives, per_device(): gathered = lax.all_gather(payload, 'dp', axis=0)  11.4 us
    unnamed x58, local copies, waits for them, and re-layouts  9.27 us
    pallas_call x1, Pallas kernels, pick(): pl.pallas_call(functools.partial(pick_kernel, n_dp, cap), out_shape=[jax....  4.6 us
    all_to_all x1, starting transfers between devices, per_device(): lax.all_to_all(picked[0], 'dp', split_axis=0, concat_axis=0, tiled=True)  4.5 us
    dot_general x3, matrix products, mixed(): jnp.dot(jnp.concatenate(blocks, axis=1), w_parts[:, a].reshape(n_tp * lan...  4.38 us
  transfers between devices with their start and end apart: 27, of which 11 were waited for; matrix products, arithmetic and copies ran while one was open for 10% of the time, Pallas kernels for 10%

profile of v1, /device:TPU:0, one launch (start us, length us, event | category | flops | bytes accessed | tf_op | source)
XLA Modules:
  0.0 187.3 jit_solution(3581774176069254807)
XLA Ops:
  0.0 0.8 fusion.58
  0.8 0.8 constant_dynamic-slice_fusion.1
  1.6 0.8 pad_maximum_fusion.3
  2.4 11.4 %all-gather = bf16[1152,256]{1,0:T(8,128)(2,1)S(1)} all-gather(bf16[144,256]{1,0:T(8,128)(2,1)S(1)} %pad_maximum_fusion.3), channel_id=2, replica_groups=mesh['dp'=8,'tensor'=4] {'dp'}, dimensions={0}, use_global_device_ids=true | all-gather | bytes 663552 | tf_op jit(solution)/shard_map/all_gather | solution.py:504
  13.8 0.8 copy-done.23
  15.2 4.6 %pick_pages.1 = (bf16[8,4,128,2,128]{4,3,2,1,0:T(2,128)(2,1)}, bf16[8,4,128,2,128]{4,3,2,1,0:T(2,128)(2,1)}) custom-call(s32[1]{0:T(128)} %bitcast.4.me_ref, s32[8,2,32]{2,1,0:T(2,128)} %slice_convert_fusion.asked_ref, bf16[32,128,2,256]{3,2,1,0:T(2,128)(2,1)} %pool_ref.1), custom_call_target="tpu_custom_call" | custom-call | bytes 8388608 | tf_op jit(solution)/shard_map/pick_pages/pallas_call | solution.py:81
  19.9 4.5 %all-to-all-start = ((bf16[8,4,128,2,128]{4,3,2,1,0:T(2,128)(2,1)}), bf16[8,4,128,2,128]{4,3,2,1,0:T(2,128)(2,1)}, u32[]{:S(2)}, u32[]{:S(2)}) async-start(bf16[8,4,128,2,128]{4,3,2,1,0:T(2,128)(2,1)} %get-tuple-element.19), calls=%async_computation | async-start | bytes 4194304 | tf_op jit(solution)/shard_map/all_to_all | solution.py:508
  24.4 3.7 %collective-permute-start.2 = (bf16[128,1024]{1,0:T(8,128)(2,1)S(1)}, bf16[128,1024]{1,0:T(8,128)(2,1)S(1)}, u32[]{:S(2)}, u32[]{:S(2)}) collective-permute-start(bf16[128,1024]{1,0:T(8,128)(2,1)S(1)} %copy-done.1), channel_id=1, source_target_pairs={{0,3},{1,0},{2,1},{3,2},{4,7},{5,4},{6,5},{7,6},{8,11},{9,8},{10,9... | collective-permute-start | bytes 786440 | tf_op jit(solution)/shard_map/ppermute | solution.py:457
  28.0 1.0 collective-permute-start
  29.0 2.2 %named_adapters.1 = (bf16[128,256]{1,0:T(8,128)(2,1)}, bf16[128,256]{1,0:T(8,128)(2,1)}) custom-call(s32[16]{0:T(128)} %table_ref.2, s32[1,4]{1,0:T(1,128)} %ids_ref.1, bf16[8,144,256]{2,1,0:T(8,128)(2,1)} %bitcast.109), custom_call_target="tpu_custom_call" | custom-call | tf_op jit(solution)/shard_map/named_adapters/pallas_call | solution.py:117
  31.3 2.9 %collective-permute-start.5 = (bf16[128,256]{1,0:T(8,128)(2,1)}, bf16[128,256]{1,0:T(8,128)(2,1)S(1)}, u32[]{:S(2)}, u32[]{:S(2)}) collective-permute-start(bf16[128,256]{1,0:T(8,128)(2,1)} %get-tuple-element.24.rest_4_), channel_id=1, source_target_pairs={{0,3},{1,0},{2,1},{3,2},{4,7},{5,4},{6,5},{7,6},{8,11},{9,8},{10,9... | collective-permute-start | bytes 196616 | tf_op jit(solution)/shard_map/ppermute | solution.py:457
  34.2 1.1 collective-permute-start.4
  35.7 1.7 constant_dynamic-slice_fusion
  37.4 10.2 %collective-permute-done.5.rest_7_ = bf16[128,256]{1,0:T(8,128)(2,1)S(1)} collective-permute-done((bf16[128,256]{1,0:T(8,128)(2,1)}, bf16[128,256]{1,0:T(8,128)(2,1)S(1)}, u32[]{:S(2)}, u32[]{:S(2)}) %collective-permute-start.5) | collective-permute-done | bytes 65568 | tf_op jit(solution)/shard_map/ppermute | solution.py:457
  47.6 8.6 %collective-permute-start.3 = (bf16[128,256]{1,0:T(8,128)(2,1)}, bf16[128,256]{1,0:T(8,128)(2,1)S(1)}, u32[]{:S(2)}, u32[]{:S(2)}) collective-permute-start(bf16[128,256]{1,0:T(8,128)(2,1)} %get-tuple-element.24.rest_4_), channel_id=1, source_target_pairs={{0,1},{1,2},{2,3},{3,0},{4,5},{5,6},{6,7},{7,4},{8,9},{9,10},{10,1... | collective-permute-start | bytes 196616 | tf_op jit(solution)/shard_map/ppermute | solution.py:457
  56.4 2.0 %collective-permute-done.3.rest_5_ = bf16[128,256]{1,0:T(8,128)(2,1)S(1)} collective-permute-done((bf16[128,256]{1,0:T(8,128)(2,1)}, bf16[128,256]{1,0:T(8,128)(2,1)S(1)}, u32[]{:S(2)}, u32[]{:S(2)}) %collective-permute-start.3) | collective-permute-done | bytes 65568 | tf_op jit(solution)/shard_map/ppermute | solution.py:457
  58.5 1.1 collective-permute-start.11
  59.5 2.8 %collective-permute-start.10 = (bf16[128,1024]{1,0:T(8,128)(2,1)}, bf16[128,1024]{1,0:T(8,128)(2,1)}, u32[]{:S(2)}, u32[]{:S(2)}) collective-permute-start(bf16[128,1024]{1,0:T(8,128)(2,1)} %constant_dynamic-slice_fusion), channel_id=1, source_target_pairs={{0,2},{1,3},{2,0},{3,1},{4,6},{5,7},{6,4},{7,5},{8,10},{9,11},{10,... | collective-permute-start | bytes 786440 | tf_op jit(solution)/shard_map/ppermute | solution.py:457
  62.3 1.8 fusion.25
  64.2 4.4 %all-to-all-start.1 = ((bf16[8,4,128,2,128]{4,3,2,1,0:T(2,128)(2,1)}), bf16[8,4,128,2,128]{4,3,2,1,0:T(2,128)(2,1)}, u32[]{:S(2)}, u32[]{:S(2)}) async-start(bf16[8,4,128,2,128]{4,3,2,1,0:T(2,128)(2,1)} %get-tuple-element.32), calls=%async_computation.1 | async-start | bytes 4194304 | tf_op jit(solution)/shard_map/all_to_all | solution.py:537
  68.6 1.2 broadcast_in_dim.66
  69.8 0.8 bitcast_dynamic-update-slice_fusion.3
  71.1 12.2 %collective-permute-done.10 = bf16[128,1024]{1,0:T(8,128)(2,1)} collective-permute-done((bf16[128,1024]{1,0:T(8,128)(2,1)}, bf16[128,1024]{1,0:T(8,128)(2,1)}, u32[]{:S(2)}, u32[]{:S(2)}) %collective-permute-start.10) | collective-permute-done | bytes 262176 | tf_op jit(solution)/shard_map/ppermute | solution.py:457
  83.4 1.2 pad_maximum_fusion.1
  84.7 0.9 copy-done.3
  85.6 0.9 copy-done.5
  86.6 0.9 copy-done.6
  87.5 0.9 copy-done.7
  88.5 1.4 copy-done.11
  89.9 0.8 copy-done.15
  90.7 0.8 copy-done.17
  91.5 0.8 copy-done.19
  92.4 0.7 copy-done.20
  93.0 3.6 %project.1 = (bf16[512,256]{1,0:T(8,128)(2,1)S(1)}, bf16[512,256]{1,0:T(8,128)(2,1)S(1)}, bf16[512,256]{1,0:T(8,128)(2,1)S(1)}, s32[32]{0:T(128)S(1)}) custom-call(s32[1]{0:T(128)} %bitcast.tp_ref, s32[1,4]{1,0:T(1,128)S(1)} %copy-done.10, s32[1,32]{1,0:T(1,128)S(1)} %copy-done.20, bf16[1,1024]{1,0:T(2,128)(2,1)S(1)} %reshape.126.gain_ref, ...), custom_call_target="tpu_custom_call" | custom-call | flops 1073741824 | bytes 3145728 | tf_op jit(solution)/shard_map/project/pallas_call | solution.py:212
  96.6 0.7 bitcast_dynamic-update-slice_fusion.2
  97.4 0.7 bitcast_dynamic-update-slice_fusion.1
  98.1 0.8 bitcast_dynamic-update-slice_fusion
  98.9 1.9 maximum_select_fusion
  100.8 12.0 %attend.2 = bf16[512,128]{1,0:T(8,128)(2,1)S(1)} custom-call(s32[1,4]{1,0:T(1,128)S(1)} %copy-done.10, s32[1,4]{1,0:T(1,128)S(1)} %copy-done.8, s32[32]{0:T(128)S(1)} %get-tuple-element.26.pos_ref, f32[2,4]{1,0:T(2,128)S(1)} %copy-done.9, bf16[512,256]{1,0:T(8,128)(2,1)S(1)} %get-tuple-element.31.q_ref, bf16[512,256]{1,0:T(8,128)(2,1)S(1)} %get-tuple-element.27.kn_ref, ...), custom_call_target="tpu_custom_call" | custom-call | flops 738197504 | bytes 2097152 | tf_op jit(solution)/shard_map/attend/pallas_call | solution.py:429
  112.8 0.9 collective-permute-start.7
  113.8 1.9 %collective-permute-start.6 = (bf16[512,128]{1,0:T(8,128)(2,1)S(1)}, bf16[512,128]{1,0:T(8,128)(2,1)S(1)}, u32[]{:S(2)}, u32[]{:S(2)}) collective-permute-start(bf16[512,128]{1,0:T(8,128)(2,1)S(1)} %attend.2), channel_id=1, source_target_pairs={{0,1},{1,2},{2,3},{3,0},{4,5},{5,6},{6,7},{7,4},{8,9},{9,10},{10,1... | collective-permute-start | bytes 393224 | tf_op jit(solution)/shard_map/ppermute | solution.py:457
  115.7 1.2 pad_maximum_fusion
  116.9 3.3 %collective-permute-done.8 = bf16[512,128]{1,0:T(8,128)(2,1)S(1)} collective-permute-done((bf16[512,128]{1,0:T(8,128)(2,1)S(1)}, bf16[512,128]{1,0:T(8,128)(2,1)S(1)}, u32[]{:S(2)}, u32[]{:S(2)}) %collective-permute-start.8) | collective-permute-done | bytes 131104 | tf_op jit(solution)/shard_map/ppermute | solution.py:457
  120.2 5.6 %collective-permute-done.7 = bf16[512,128]{1,0:T(8,128)(2,1)S(1)} collective-permute-done((bf16[512,128]{1,0:T(8,128)(2,1)S(1)}, bf16[512,128]{1,0:T(8,128)(2,1)S(1)}, u32[]{:S(2)}, u32[]{:S(2)}) %collective-permute-start.7) | collective-permute-done | bytes 131104 | tf_op jit(solution)/shard_map/ppermute | solution.py:457
  125.8 3.3 %convert_add_fusion = f32[512,1024]{1,0:T(8,128)} fusion(bf16[4,128,1024]{2,1,0:T(8,128)(2,1)} %bitcast_dynamic-update-slice_fusion, bf16[512,1024]{1,0:T(8,128)(2,1)S(1)} %bitcast.112, bf16[512,128]{1,0:T(8,128)(2,1)S(1)} %collective-permute-done.8, bf16[512,128]{1,0:T(8,128)(2,1)S(1)} %collective-permute-done.7, ...), kind=kOutput, calls=%fused_computation.2 | convolution fusion | flops 540016640 | bytes 4718592 | tf_op jit(solution)/shard_map/dot_general | solution.py:550
  129.1 12.2 %attend.3 = bf16[512,128]{1,0:T(8,128)(2,1)S(1)} custom-call(s32[1,4]{1,0:T(1,128)S(1)} %copy-done.10, s32[1,4]{1,0:T(1,128)S(1)} %copy-done.8, s32[32]{0:T(128)S(1)} %get-tuple-element.26.pos_ref, f32[2,4]{1,0:T(2,128)S(1)} %copy-done.9, bf16[512,256]{1,0:T(8,128)(2,1)S(1)} %get-tuple-element.31.q_ref, bf16[512,256]{1,0:T(8,128)(2,1)S(1)} %get-tuple-element.27.kn_ref, ...), custom_call_target="tpu_custom_call" | custom-call | flops 738197504 | bytes 2097152 | tf_op jit(solution)/shard_map/attend/pallas_call | solution.py:429
  141.4 1.1 collective-permute-start.21
  142.5 1.8 collective-permute-start.20
  144.2 1.9 %collective-permute-start.19 = (bf16[256,128]{1,0:T(8,128)(2,1)S(1)}, bf16[256,128]{1,0:T(8,128)(2,1)S(1)}, u32[]{:S(2)}, u32[]{:S(2)}) collective-permute-start(bf16[256,128]{1,0:T(8,128)(2,1)S(1)} %bitcast.123), channel_id=1, source_target_pairs={{0,1},{1,2},{2,3},{3,0},{4,5},{5,6},{6,7},{7,4},{8,9},{9,10},{10,1... | collective-permute-start | bytes 196616 | tf_op jit(solution)/shard_map/ppermute | solution.py:457
  146.3 1.9 %collective-permute-start.15 = (bf16[256,128]{1,0:T(8,128)(2,1)S(1)}, bf16[256,128]{1,0:T(8,128)(2,1)S(1)}, u32[]{:S(2)}, u32[]{:S(2)}) collective-permute-start(bf16[256,128]{1,0:T(8,128)(2,1)S(1)} %bitcast.117), channel_id=1, source_target_pairs={{0,3},{1,0},{2,1},{3,2},{4,7},{5,4},{6,5},{7,6},{8,11},{9,8},{10,9... | collective-permute-start | bytes 196616 | tf_op jit(solution)/shard_map/ppermute | solution.py:457
  148.2 0.6 collective-permute-start.13
  148.9 2.4 %collective-permute-done.19 = bf16[256,128]{1,0:T(8,128)(2,1)S(1)} collective-permute-done((bf16[256,128]{1,0:T(8,128)(2,1)S(1)}, bf16[256,128]{1,0:T(8,128)(2,1)S(1)}, u32[]{:S(2)}, u32[]{:S(2)}) %collective-permute-start.19) | collective-permute-done | bytes 65568 | tf_op jit(solution)/shard_map/ppermute | solution.py:457
  152.1 4.9 %collective-permute-done.14 = bf16[256,128]{1,0:T(8,128)(2,1)S(1)} collective-permute-done((bf16[256,128]{1,0:T(8,128)(2,1)S(1)}, bf16[256,128]{1,0:T(8,128)(2,1)S(1)}, u32[]{:S(2)}, u32[]{:S(2)}) %collective-permute-start.14) | collective-permute-done | bytes 65568 | tf_op jit(solution)/shard_map/ppermute | solution.py:457
  157.5 1.3 convolution_bitcast_fusion.1
  159.1 0.8 fusion.69
  160.1 3.8 %collective-permute-start.18 = (bf16[64,1024]{1,0:T(8,128)(2,1)S(1)}, bf16[64,1024]{1,0:T(8,128)(2,1)S(1)}, u32[]{:S(2)}, u32[]{:S(2)}) collective-permute-start(bf16[64,1024]{1,0:T(8,128)(2,1)S(1)} %get-tuple-element.44), channel_id=1, source_target_pairs={{0,3},{1,0},{2,1},{3,2},{4,7},{5,4},{6,5},{7,6},{8,11},{9,8},{10,9... | collective-permute-start | bytes 393224 | tf_op jit(solution)/shard_map/ppermute | solution.py:457
  163.9 1.3 convolution_bitcast_fusion
  165.5 0.8 fusion.68
  166.3 0.6 collective-permute-start.22
  167.0 3.3 %collective-permute-start.24 = (bf16[64,1024]{1,0:T(8,128)(2,1)S(1)}, bf16[64,1024]{1,0:T(8,128)(2,1)S(1)}, u32[]{:S(2)}, u32[]{:S(2)}) collective-permute-start(bf16[64,1024]{1,0:T(8,128)(2,1)S(1)} %get-tuple-element.47), channel_id=1, source_target_pairs={{0,3},{1,0},{2,1},{3,2},{4,7},{5,4},{6,5},{7,6},{8,11},{9,8},{10,9... | collective-permute-start | bytes 393224 | tf_op jit(solution)/shard_map/ppermute | solution.py:457
  170.2 2.9 %collective-permute-start.23 = (bf16[64,1024]{1,0:T(8,128)(2,1)S(1)}, bf16[64,1024]{1,0:T(8,128)(2,1)S(1)}, u32[]{:S(2)}, u32[]{:S(2)}) collective-permute-start(bf16[64,1024]{1,0:T(8,128)(2,1)S(1)} %get-tuple-element.48), channel_id=1, source_target_pairs={{0,2},{1,3},{2,0},{3,1},{4,6},{5,7},{6,4},{7,5},{8,10},{9,11},{10,... | collective-permute-start | bytes 393224 | tf_op jit(solution)/shard_map/ppermute | solution.py:457
  173.1 6.5 %collective-permute-done.17 = bf16[64,1024]{1,0:T(8,128)(2,1)S(1)} collective-permute-done((bf16[64,1024]{1,0:T(8,128)(2,1)S(1)}, bf16[64,1024]{1,0:T(8,128)(2,1)S(1)}, u32[]{:S(2)}, u32[]{:S(2)}) %collective-permute-start.17) | collective-permute-done | bytes 131104 | tf_op jit(solution)/shard_map/ppermute | solution.py:457
  179.7 6.8 %collective-permute-done.23 = bf16[64,1024]{1,0:T(8,128)(2,1)S(1)} collective-permute-done((bf16[64,1024]{1,0:T(8,128)(2,1)S(1)}, bf16[64,1024]{1,0:T(8,128)(2,1)S(1)}, u32[]{:S(2)}, u32[]{:S(2)}) %collective-permute-start.23) | collective-permute-done | bytes 131104 | tf_op jit(solution)/shard_map/ppermute | solution.py:457
  186.6 0.7 pad_maximum_fusion.2
  (95 shorter events, 4.3 us)
Async XLA Ops:
  0.0 159.1 %copy-start = (bf16[1024,1024]{1,0:T(8,128)(2,1)S(1)}, bf16[1024,1024]{1,0:T(8,128)(2,1)}, u32[]{:S(2)}) copy-start(bf16[1024,1024]{1,0:T(8,128)(2,1)} %param.22) | copy-start | bytes 6291460
  13.8 0.8 copy-start.23
  19.8 4.5 %copy-start.1 = (bf16[128,1024]{1,0:T(8,128)(2,1)S(1)}, bf16[128,1024]{1,0:T(8,128)(2,1)}, u32[]{:S(2)}) copy-start(bf16[128,1024]{1,0:T(8,128)(2,1)} %rest_0_.1) | copy-start | bytes 786436
  19.8 15.5 %copy-start.10 = (s32[1,4]{1,0:T(1,128)S(1)}, s32[1,4]{1,0:T(1,128)}, u32[]{:S(2)}) copy-start(s32[1,4]{1,0:T(1,128)} %lens_ref.5) | copy-start | bytes 52
  19.9 15.7 %copy-start.8 = (s32[1,4]{1,0:T(1,128)S(1)}, s32[1,4]{1,0:T(1,128)}, u32[]{:S(2)}) copy-start(s32[1,4]{1,0:T(1,128)} %counts_ref.3) | copy-start | bytes 52
  19.9 44.3 %all-to-all-start = ((bf16[8,4,128,2,128]{4,3,2,1,0:T(2,128)(2,1)}), bf16[8,4,128,2,128]{4,3,2,1,0:T(2,128)(2,1)}, u32[]{:S(2)}, u32[]{:S(2)}) async-start(bf16[8,4,128,2,128]{4,3,2,1,0:T(2,128)(2,1)} %get-tuple-element.19), calls=%async_computation | async-start | bytes 4194304 | tf_op jit(solution)/shard_map/all_to_all | solution.py:508
  24.4 34.1 %collective-permute-start.2 = (bf16[128,1024]{1,0:T(8,128)(2,1)S(1)}, bf16[128,1024]{1,0:T(8,128)(2,1)S(1)}, u32[]{:S(2)}, u32[]{:S(2)}) collective-permute-start(bf16[128,1024]{1,0:T(8,128)(2,1)S(1)} %copy-done.1), channel_id=1, source_target_pairs={{0,3},{1,0},{2,1},{3,2},{4,7},{5,4},{6,5},{7,6},{8,11},{9,8},{10,9... | collective-permute-start | bytes 786440 | tf_op jit(solution)/shard_map/ppermute | solution.py:457
  28.0 30.4 %collective-permute-start.1 = (bf16[128,1024]{1,0:T(8,128)(2,1)S(1)}, bf16[128,1024]{1,0:T(8,128)(2,1)S(1)}, u32[]{:S(2)}, u32[]{:S(2)}) collective-permute-start(bf16[128,1024]{1,0:T(8,128)(2,1)S(1)} %copy-done.1), channel_id=1, source_target_pairs={{0,2},{1,3},{2,0},{3,1},{4,6},{5,7},{6,4},{7,5},{8,10},{9,11},{10,... | collective-permute-start | bytes 786440 | tf_op jit(solution)/shard_map/ppermute | solution.py:457
  28.0 30.4 %collective-permute-start = (bf16[128,1024]{1,0:T(8,128)(2,1)S(1)}, bf16[128,1024]{1,0:T(8,128)(2,1)S(1)}, u32[]{:S(2)}, u32[]{:S(2)}) collective-permute-start(bf16[128,1024]{1,0:T(8,128)(2,1)S(1)} %copy-done.1), channel_id=1, source_target_pairs={{0,1},{1,2},{2,3},{3,0},{4,5},{5,6},{6,7},{7,4},{8,9},{9,10},{10,1... | collective-permute-start | bytes 786440 | tf_op jit(solution)/shard_map/ppermute | solution.py:457
  31.3 16.3 %collective-permute-start.5 = (bf16[128,256]{1,0:T(8,128)(2,1)}, bf16[128,256]{1,0:T(8,128)(2,1)S(1)}, u32[]{:S(2)}, u32[]{:S(2)}) collective-permute-start(bf16[128,256]{1,0:T(8,128)(2,1)} %get-tuple-element.24.rest_4_), channel_id=1, source_target_pairs={{0,3},{1,0},{2,1},{3,2},{4,7},{5,4},{6,5},{7,6},{8,11},{9,8},{10,9... | collective-permute-start | bytes 196616 | tf_op jit(solution)/shard_map/ppermute | solution.py:457
  34.2 22.3 %collective-permute-start.4 = (bf16[128,256]{1,0:T(8,128)(2,1)}, bf16[128,256]{1,0:T(8,128)(2,1)S(1)}, u32[]{:S(2)}, u32[]{:S(2)}) collective-permute-start(bf16[128,256]{1,0:T(8,128)(2,1)} %get-tuple-element.24.rest_4_), channel_id=1, source_target_pairs={{0,2},{1,3},{2,0},{3,1},{4,6},{5,7},{6,4},{7,5},{8,10},{9,11},{10,... | collective-permute-start | bytes 196616 | tf_op jit(solution)/shard_map/ppermute | solution.py:457
  47.6 16.6 %copy-start.14 = (bf16[128,256]{1,0:T(8,128)(2,1)}, bf16[128,256]{1,0:T(8,128)(2,1)S(1)}, u32[]{:S(2)}) copy-start(bf16[128,256]{1,0:T(8,128)(2,1)S(1)} %collective-permute-done.5.rest_7_) | copy-start | bytes 196612
  47.6 10.9 %collective-permute-start.3 = (bf16[128,256]{1,0:T(8,128)(2,1)}, bf16[128,256]{1,0:T(8,128)(2,1)S(1)}, u32[]{:S(2)}, u32[]{:S(2)}) collective-permute-start(bf16[128,256]{1,0:T(8,128)(2,1)} %get-tuple-element.24.rest_4_), channel_id=1, source_target_pairs={{0,1},{1,2},{2,3},{3,0},{4,5},{5,6},{6,7},{7,4},{8,9},{9,10},{10,1... | collective-permute-start | bytes 196616 | tf_op jit(solution)/shard_map/ppermute | solution.py:457
  56.4 7.7 %copy-start.16 = (bf16[128,256]{1,0:T(8,128)(2,1)}, bf16[128,256]{1,0:T(8,128)(2,1)S(1)}, u32[]{:S(2)}) copy-start(bf16[128,256]{1,0:T(8,128)(2,1)S(1)} %collective-permute-done.4.rest_6_) | copy-start | bytes 196612
  58.4 5.7 %copy-start.18 = (bf16[128,256]{1,0:T(8,128)(2,1)}, bf16[128,256]{1,0:T(8,128)(2,1)S(1)}, u32[]{:S(2)}) copy-start(bf16[128,256]{1,0:T(8,128)(2,1)S(1)} %collective-permute-done.3.rest_5_) | copy-start | bytes 196612
  58.4 5.7 %copy-start.2 = (bf16[128,1024]{1,0:T(8,128)(2,1)}, bf16[128,1024]{1,0:T(8,128)(2,1)S(1)}, u32[]{:S(2)}) copy-start(bf16[128,1024]{1,0:T(8,128)(2,1)S(1)} %collective-permute-done.1.rest_2_) | copy-start | bytes 786436
  58.5 5.7 %copy-start.4 = (bf16[128,1024]{1,0:T(8,128)(2,1)}, bf16[128,1024]{1,0:T(8,128)(2,1)S(1)}, u32[]{:S(2)}) copy-start(bf16[128,1024]{1,0:T(8,128)(2,1)S(1)} %collective-permute-done.rest_1_) | copy-start | bytes 786436
  58.5 12.7 %collective-permute-start.11 = (bf16[128,1024]{1,0:T(8,128)(2,1)}, bf16[128,1024]{1,0:T(8,128)(2,1)}, u32[]{:S(2)}, u32[]{:S(2)}) collective-permute-start(bf16[128,1024]{1,0:T(8,128)(2,1)} %constant_dynamic-slice_fusion), channel_id=1, source_target_pairs={{0,3},{1,0},{2,1},{3,2},{4,7},{5,4},{6,5},{7,6},{8,11},{9,8},{10,9... | collective-permute-start | bytes 786440 | tf_op jit(solution)/shard_map/ppermute | solution.py:457
  59.5 23.8 %collective-permute-start.10 = (bf16[128,1024]{1,0:T(8,128)(2,1)}, bf16[128,1024]{1,0:T(8,128)(2,1)}, u32[]{:S(2)}, u32[]{:S(2)}) collective-permute-start(bf16[128,1024]{1,0:T(8,128)(2,1)} %constant_dynamic-slice_fusion), channel_id=1, source_target_pairs={{0,2},{1,3},{2,0},{3,1},{4,6},{5,7},{6,4},{7,5},{8,10},{9,11},{10,... | collective-permute-start | bytes 786440 | tf_op jit(solution)/shard_map/ppermute | solution.py:457
  62.3 21.0 %collective-permute-start.9 = (bf16[128,1024]{1,0:T(8,128)(2,1)}, bf16[128,1024]{1,0:T(8,128)(2,1)}, u32[]{:S(2)}, u32[]{:S(2)}) collective-permute-start(bf16[128,1024]{1,0:T(8,128)(2,1)} %constant_dynamic-slice_fusion), channel_id=1, source_target_pairs={{0,1},{1,2},{2,3},{3,0},{4,5},{5,6},{6,7},{7,4},{8,9},{9,10},{10,1... | collective-permute-start | bytes 786440 | tf_op jit(solution)/shard_map/ppermute | solution.py:457
  64.1 6.4 %copy-start.27 = (bf16[1024]{0:T(1024)(128)(2,1)S(1)}, bf16[1024]{0:T(1024)(128)(2,1)}, u32[]{:S(2)}) copy-start(bf16[1024]{0:T(1024)(128)(2,1)} %param.18) | copy-start | bytes 6148
  64.1 7.0 %copy-start.28 = (bf16[1024]{0:T(1024)(128)(2,1)S(1)}, bf16[1024]{0:T(1024)(128)(2,1)}, u32[]{:S(2)}) copy-start(bf16[1024]{0:T(1024)(128)(2,1)} %param.17) | copy-start | bytes 6148
  64.2 64.9 %all-to-all-start.1 = ((bf16[8,4,128,2,128]{4,3,2,1,0:T(2,128)(2,1)}), bf16[8,4,128,2,128]{4,3,2,1,0:T(2,128)(2,1)}, u32[]{:S(2)}, u32[]{:S(2)}) async-start(bf16[8,4,128,2,128]{4,3,2,1,0:T(2,128)(2,1)} %get-tuple-element.32), calls=%async_computation.1 | async-start | bytes 4194304 | tf_op jit(solution)/shard_map/all_to_all | solution.py:537
  68.6 16.1 %copy-start.12 = (bf16[128,256]{1,0:T(8,128)(2,1)S(1)}, bf16[128,256]{1,0:T(8,128)(2,1)}, u32[]{:S(2)}) copy-start(bf16[128,256]{1,0:T(8,128)(2,1)} %get-tuple-element.24.rest_4_) | copy-start | bytes 196612
  68.6 16.1 %copy-start.13 = (bf16[128,256]{1,0:T(8,128)(2,1)S(1)}, bf16[128,256]{1,0:T(8,128)(2,1)}, u32[]{:S(2)}) copy-start(bf16[128,256]{1,0:T(8,128)(2,1)} %get-tuple-element.22.up_ref) | copy-start | bytes 196612
  84.6 14.3 %collective-permute-start.12 = (bf16[3,128,1024]{2,1,0:T(8,128)(2,1)S(1)}, bf16[3,128,1024]{2,1,0:T(8,128)(2,1)S(1)}, u32[]{:S(2)}, u32[]{:S(2)}) collective-permute-start(bf16[3,128,1024]{2,1,0:T(8,128)(2,1)S(1)} %pad_maximum_fusion.1), channel_id=1, source_target_pairs={{0,4},{4,0},{8,12},{12,8},{16,20},{20,16},{24,28},{28,24},{1,5},{5... | collective-permute-start | bytes 2359304 | tf_op jit(solution)/shard_map/ppermute | solution.py:518
  84.7 1.0 copy-start.3
  85.6 0.9 copy-start.5
  86.6 0.9 copy-start.6
  87.5 0.9 copy-start.7
  88.5 1.4 copy-start.11
  89.9 0.8 copy-start.15
  90.7 0.8 copy-start.17
  91.5 0.8 copy-start.19
  92.4 0.7 copy-start.20
  97.4 3.4 %copy-start.9 = (f32[2,4]{1,0:T(2,128)S(1)}, f32[2,4]{1,0:T(2,128)}, u32[]{:S(2)}) copy-start(f32[2,4]{1,0:T(2,128)} %bias_ref.3) | copy-start | bytes 100
  100.7 15.0 %copy-start.25 = (bf16[256,1024]{1,0:T(8,128)(2,1)S(1)}, bf16[256,1024]{1,0:T(8,128)(2,1)}, u32[]{:S(2)}) copy-start(bf16[256,1024]{1,0:T(8,128)(2,1)} %param.20) | copy-start | bytes 1572868
  112.7 7.5 %collective-permute-start.8 = (bf16[512,128]{1,0:T(8,128)(2,1)S(1)}, bf16[512,128]{1,0:T(8,128)(2,1)S(1)}, u32[]{:S(2)}, u32[]{:S(2)}) collective-permute-start(bf16[512,128]{1,0:T(8,128)(2,1)S(1)} %attend.2), channel_id=1, source_target_pairs={{0,3},{1,0},{2,1},{3,2},{4,7},{5,4},{6,5},{7,6},{8,11},{9,8},{10,9... | collective-permute-start | bytes 393224 | tf_op jit(solution)/shard_map/ppermute | solution.py:457
  112.8 13.0 %collective-permute-start.7 = (bf16[512,128]{1,0:T(8,128)(2,1)S(1)}, bf16[512,128]{1,0:T(8,128)(2,1)S(1)}, u32[]{:S(2)}, u32[]{:S(2)}) collective-permute-start(bf16[512,128]{1,0:T(8,128)(2,1)S(1)} %attend.2), channel_id=1, source_target_pairs={{0,2},{1,3},{2,0},{3,1},{4,6},{5,7},{6,4},{7,5},{8,10},{9,11},{10,... | collective-permute-start | bytes 393224 | tf_op jit(solution)/shard_map/ppermute | solution.py:457
  113.8 12.0 %collective-permute-start.6 = (bf16[512,128]{1,0:T(8,128)(2,1)S(1)}, bf16[512,128]{1,0:T(8,128)(2,1)S(1)}, u32[]{:S(2)}, u32[]{:S(2)}) collective-permute-start(bf16[512,128]{1,0:T(8,128)(2,1)S(1)} %attend.2), channel_id=1, source_target_pairs={{0,1},{1,2},{2,3},{3,0},{4,5},{5,6},{6,7},{7,4},{8,9},{9,10},{10,1... | collective-permute-start | bytes 393224 | tf_op jit(solution)/shard_map/ppermute | solution.py:457
  129.1 17.1 %copy-start.24 = (f32[512,1024]{1,0:T(8,128)S(1)}, f32[512,1024]{1,0:T(8,128)}, u32[]{:S(2)}) copy-start(f32[512,1024]{1,0:T(8,128)} %convert_add_fusion) | copy-start | bytes 6291460
  141.4 6.9 %collective-permute-start.21 = (bf16[256,128]{1,0:T(8,128)(2,1)S(1)}, bf16[256,128]{1,0:T(8,128)(2,1)S(1)}, u32[]{:S(2)}, u32[]{:S(2)}) collective-permute-start(bf16[256,128]{1,0:T(8,128)(2,1)S(1)} %bitcast.121), channel_id=1, source_target_pairs={{0,3},{1,0},{2,1},{3,2},{4,7},{5,4},{6,5},{7,6},{8,11},{9,8},{10,9... | collective-permute-start | bytes 196616 | tf_op jit(solution)/shard_map/ppermute | solution.py:457
  142.5 6.4 %collective-permute-start.20 = (bf16[256,128]{1,0:T(8,128)(2,1)S(1)}, bf16[256,128]{1,0:T(8,128)(2,1)S(1)}, u32[]{:S(2)}, u32[]{:S(2)}) collective-permute-start(bf16[256,128]{1,0:T(8,128)(2,1)S(1)} %bitcast.122), channel_id=1, source_target_pairs={{0,2},{1,3},{2,0},{3,1},{4,6},{5,7},{6,4},{7,5},{8,10},{9,11},{10,... | collective-permute-start | bytes 196616 | tf_op jit(solution)/shard_map/ppermute | solution.py:457
  144.2 7.1 %collective-permute-start.19 = (bf16[256,128]{1,0:T(8,128)(2,1)S(1)}, bf16[256,128]{1,0:T(8,128)(2,1)S(1)}, u32[]{:S(2)}, u32[]{:S(2)}) collective-permute-start(bf16[256,128]{1,0:T(8,128)(2,1)S(1)} %bitcast.123), channel_id=1, source_target_pairs={{0,1},{1,2},{2,3},{3,0},{4,5},{5,6},{6,7},{7,4},{8,9},{9,10},{10,1... | collective-permute-start | bytes 196616 | tf_op jit(solution)/shard_map/ppermute | solution.py:457
  146.2 5.2 %copy-start.22 = (bf16[4,1,128,1024]{3,2,1,0:T(8,128)(2,1)S(1)}, bf16[4,1,128,1024]{3,2,1,0:T(8,128)(2,1)}, u32[]{:S(2)}) copy-start(bf16[4,1,128,1024]{3,2,1,0:T(8,128)(2,1)} %get-tuple-element.41) | copy-start | bytes 3145732
  146.3 5.8 %collective-permute-start.15 = (bf16[256,128]{1,0:T(8,128)(2,1)S(1)}, bf16[256,128]{1,0:T(8,128)(2,1)S(1)}, u32[]{:S(2)}, u32[]{:S(2)}) collective-permute-start(bf16[256,128]{1,0:T(8,128)(2,1)S(1)} %bitcast.117), channel_id=1, source_target_pairs={{0,3},{1,0},{2,1},{3,2},{4,7},{5,4},{6,5},{7,6},{8,11},{9,8},{10,9... | collective-permute-start | bytes 196616 | tf_op jit(solution)/shard_map/ppermute | solution.py:457
  148.2 8.7 %collective-permute-start.14 = (bf16[256,128]{1,0:T(8,128)(2,1)S(1)}, bf16[256,128]{1,0:T(8,128)(2,1)S(1)}, u32[]{:S(2)}, u32[]{:S(2)}) collective-permute-start(bf16[256,128]{1,0:T(8,128)(2,1)S(1)} %bitcast.118), channel_id=1, source_target_pairs={{0,2},{1,3},{2,0},{3,1},{4,6},{5,7},{6,4},{7,5},{8,10},{9,11},{10,... | collective-permute-start | bytes 196616 | tf_op jit(solution)/shard_map/ppermute | solution.py:457
  148.2 8.7 %collective-permute-start.13 = (bf16[256,128]{1,0:T(8,128)(2,1)S(1)}, bf16[256,128]{1,0:T(8,128)(2,1)S(1)}, u32[]{:S(2)}, u32[]{:S(2)}) collective-permute-start(bf16[256,128]{1,0:T(8,128)(2,1)S(1)} %bitcast.119), channel_id=1, source_target_pairs={{0,1},{1,2},{2,3},{3,0},{4,5},{5,6},{6,7},{7,4},{8,9},{9,10},{10,1... | collective-permute-start | bytes 196616 | tf_op jit(solution)/shard_map/ppermute | solution.py:457
  151.3 6.2 %copy-start.21 = (bf16[2,1024,1024]{2,1,0:T(8,128)(2,1)S(1)}, bf16[2,1024,1024]{2,1,0:T(8,128)(2,1)}, u32[]{:S(2)}) copy-start(bf16[2,1024,1024]{2,1,0:T(8,128)(2,1)} %param.21) | copy-start | bytes 12582916
  151.9 5.7 %copy-start.26 = (f32[1024]{0:T(1024)S(1)}, f32[1024]{0:T(1024)}, u32[]{:S(2)}) copy-start(f32[1024]{0:T(1024)} %convert_element_type.76) | copy-start | bytes 12292
  160.0 10.2 %collective-permute-start.16 = (bf16[64,1024]{1,0:T(8,128)(2,1)S(1)}, bf16[64,1024]{1,0:T(8,128)(2,1)S(1)}, u32[]{:S(2)}, u32[]{:S(2)}) collective-permute-start(bf16[64,1024]{1,0:T(8,128)(2,1)S(1)} %get-tuple-element.43), channel_id=1, source_target_pairs={{0,1},{1,2},{2,3},{3,0},{4,5},{5,6},{6,7},{7,4},{8,9},{9,10},{10,1... | collective-permute-start | bytes 393224 | tf_op jit(solution)/shard_map/ppermute | solution.py:457
  160.1 13.0 %collective-permute-start.18 = (bf16[64,1024]{1,0:T(8,128)(2,1)S(1)}, bf16[64,1024]{1,0:T(8,128)(2,1)S(1)}, u32[]{:S(2)}, u32[]{:S(2)}) collective-permute-start(bf16[64,1024]{1,0:T(8,128)(2,1)S(1)} %get-tuple-element.44), channel_id=1, source_target_pairs={{0,3},{1,0},{2,1},{3,2},{4,7},{5,4},{6,5},{7,6},{8,11},{9,8},{10,9... | collective-permute-start | bytes 393224 | tf_op jit(solution)/shard_map/ppermute | solution.py:457
  163.9 15.7 %collective-permute-start.17 = (bf16[64,1024]{1,0:T(8,128)(2,1)S(1)}, bf16[64,1024]{1,0:T(8,128)(2,1)S(1)}, u32[]{:S(2)}, u32[]{:S(2)}) collective-permute-start(bf16[64,1024]{1,0:T(8,128)(2,1)S(1)} %get-tuple-element.45), channel_id=1, source_target_pairs={{0,2},{1,3},{2,0},{3,1},{4,6},{5,7},{6,4},{7,5},{8,10},{9,11},{10,... | collective-permute-start | bytes 393224 | tf_op jit(solution)/shard_map/ppermute | solution.py:457
  166.3 13.3 %collective-permute-start.22 = (bf16[64,1024]{1,0:T(8,128)(2,1)S(1)}, bf16[64,1024]{1,0:T(8,128)(2,1)S(1)}, u32[]{:S(2)}, u32[]{:S(2)}) collective-permute-start(bf16[64,1024]{1,0:T(8,128)(2,1)S(1)} %get-tuple-element.46), channel_id=1, source_target_pairs={{0,1},{1,2},{2,3},{3,0},{4,5},{5,6},{6,7},{7,4},{8,9},{9,10},{10,1... | collective-permute-start | bytes 393224 | tf_op jit(solution)/shard_map/ppermute | solution.py:457
  167.0 12.7 %collective-permute-start.24 = (bf16[64,1024]{1,0:T(8,128)(2,1)S(1)}, bf16[64,1024]{1,0:T(8,128)(2,1)S(1)}, u32[]{:S(2)}, u32[]{:S(2)}) collective-permute-start(bf16[64,1024]{1,0:T(8,128)(2,1)S(1)} %get-tuple-element.47), channel_id=1, source_target_pairs={{0,3},{1,0},{2,1},{3,2},{4,7},{5,4},{6,5},{7,6},{8,11},{9,8},{10,9... | collective-permute-start | bytes 393224 | tf_op jit(solution)/shard_map/ppermute | solution.py:457
  170.2 16.3 %collective-permute-start.23 = (bf16[64,1024]{1,0:T(8,128)(2,1)S(1)}, bf16[64,1024]{1,0:T(8,128)(2,1)S(1)}, u32[]{:S(2)}, u32[]{:S(2)}) collective-permute-start(bf16[64,1024]{1,0:T(8,128)(2,1)S(1)} %get-tuple-element.48), channel_id=1, source_target_pairs={{0,2},{1,3},{2,0},{3,1},{4,6},{5,7},{6,4},{7,5},{8,10},{9,11},{10,... | collective-permute-start | bytes 393224 | tf_op jit(solution)/shard_map/ppermute | solution.py:457

commit v2 on v1

--- a/solution.py
+++ b/solution.py
@@ -93,7 +93,7 @@
     )(me, asked, pool)
 
 
-def named_kernel(n_loc, span, table_ref, ids_ref, all_ref, down_ref, up_ref, sem):
+def named_kernel(n_loc, span, table_ref, ids_ref, all_ref, down_out, up_out, down_ref, up_ref, sem):
     copies = []
     for r in range(ids_ref.shape[1]):
         slot = table_ref[ids_ref[0, r]]
@@ -107,33 +107,52 @@
             copies.append(copy)
     for copy in copies:
         copy.wait()
+    last = [
+        pltpu.make_async_copy(down_ref, down_out, sem.at[0, 0]),
+        pltpu.make_async_copy(up_ref, up_out, sem.at[0, 1]),
+    ]
+    for copy in last:
+        copy.start()
+    for copy in last:
+        copy.wait()
 
 
 def named(owner_table, adapter_ids, gathered, n_loc, span):
     n_req = adapter_ids.shape[1]
     smem = pl.BlockSpec(memory_space=pltpu.SMEM)
-    vmem = pl.BlockSpec(memory_space=pltpu.VMEM)
+    hbm = pl.BlockSpec(memory_space=pltpu.HBM)
     out = jax.ShapeDtypeStruct((n_req * span, gathered.shape[-1]), BF)
     return pl.pallas_call(
         functools.partial(named_kernel, n_loc, span),
         out_shape=(out, out),
-        in_specs=[smem, smem, pl.BlockSpec(memory_space=pl.ANY)],
-        out_specs=(vmem, vmem),
-        scratch_shapes=[pltpu.SemaphoreType.DMA((n_req, 2))],
+        in_specs=[smem, smem, hbm],
+        out_specs=(hbm, hbm),
+        scratch_shapes=[
+            pltpu.VMEM(out.shape, BF),
+            pltpu.VMEM(out.shape, BF),
+            pltpu.SemaphoreType.DMA((n_req, 2)),
+        ],
         name="named_adapters",
     )(owner_table, adapter_ids, gathered)
 
 
-def project_kernel(
-    n_tp, cap, pool_dev, tp_ref, lens_ref, table_ref, gain_ref, w_ref, up_ref, cos_ref, sin_ref, *rest
-):
-    tok_refs, down_refs = rest[:n_tp], rest[n_tp : 2 * n_tp]
-    q_ref, k_ref, v_ref, pos_ref, down, count = rest[2 * n_tp :]
+def project_kernel(n_tp, cap, pool_dev, tp_ref, lens_ref, table_ref, *rest):
+    hbm_refs, rest = rest[: 5 + 2 * n_tp], rest[5 + 2 * n_tp :]
+    q_ref, k_ref, v_ref, pos_ref, down, count, *held = rest
+    held, sem = held[:-1], held[-1]
+    gain_ref, w_ref, up_ref, cos_ref, sin_ref, tok_ref = held
     tp = tp_ref[0]
-    rows, _ = tok_refs[0].shape
+    copies = []
+    targets = list(held[:5]) + [tok_ref.at[k] for k in range(n_tp)]
+    for k in range(n_tp):
+        targets.append(down.at[lax.rem(tp - k + n_tp, n_tp)])
+    for i in list(range(5, 5 + 2 * n_tp)) + list(range(5)):
+        copy = pltpu.make_async_copy(hbm_refs[i], targets[i], sem.at[i])
+        copy.start()
+        copies.append(copy)
+    _, rows, _ = tok_ref.shape
     width = q_ref.shape[1]
-    dd = down_refs[0].shape[1]
-    n_low = down_refs[0].shape[0]
+    n_low, dd = down.shape[1:]
     n_req = lens_ref.shape[1]
     rank = n_low // n_req // 2
 
@@ -149,9 +168,8 @@
 
     lax.fori_loop(0, table_ref.shape[1], place, 0)
 
-    for k in range(n_tp):
-        at = lax.rem(tp - k + n_tp, n_tp)
-        down[at] = down_refs[k][...]
+    for copy in copies:
+        copy.wait()
     lane = lax.broadcasted_iota(jnp.int32, (1, 128), 1)
     first = jnp.bitwise_and(lane, HD - 1) < HD // 2
 
@@ -167,7 +185,7 @@
 
     for k in range(n_tp):
         row0 = pl.multiple_of(lax.rem(tp - k + n_tp, n_tp) * rows, rows)
-        x = tok_refs[k][...].astype(F32)
+        x = tok_ref[k].astype(F32)
         inv = lax.rsqrt(jnp.mean(x * x, axis=1, keepdims=True) + 1e-05)
         normed = (x * inv * gain_ref[...].astype(F32)).astype(BF)
         low = jnp.zeros((rows, n_low), F32)
@@ -212,11 +230,16 @@
     return pl.pallas_call(
         functools.partial(project_kernel, n_tp, cap, pool_dev),
         out_shape=(out, out, out, jax.ShapeDtypeStruct((table.shape[1],), jnp.int32)),
-        in_specs=[smem] * 3 + [vmem] * (5 + 2 * n_tp),
+        in_specs=[smem] * 3 + [pl.BlockSpec(memory_space=pltpu.HBM)] * (5 + 2 * n_tp),
         out_specs=(vmem, vmem, vmem, smem),
         scratch_shapes=[
             pltpu.VMEM((n_tp,) + downs[0].shape, BF),
             pltpu.SMEM((n_dp,), jnp.int32),
+        ]
+        + [pltpu.VMEM(x.shape, x.dtype) for x in (gain, w_qkv, up, cos, sin)]
+        + [
+            pltpu.VMEM((n_tp,) + toks[0].shape, BF),
+            pltpu.SemaphoreType.DMA((5 + 2 * n_tp,)),
         ],
         compiler_params=pltpu.CompilerParams(vmem_limit_bytes=32 << 20),
         cost_estimate=pl.CostEstimate(
@@ -455,6 +478,17 @@
 
 def shift(value, axis, n, k):
     return lax.ppermute(value, axis, [(i, (i + k) % n) for i in range(n)])
+
+
+def whole_weight(own, halves, dp, n_dp):
+    halves = jnp.stack(halves)
+    twins = lax.ppermute(halves, "dp", [(i, i ^ 1) for i in range(n_dp)])
+    rest = jnp.where(
+        dp % 2 == 0,
+        jnp.concatenate([halves, twins], axis=1),
+        jnp.concatenate([twins, halves], axis=1),
+    )
+    return jnp.concatenate([own[None], rest], axis=0)
 
 
 def per_device(
@@ -504,24 +538,13 @@
     gathered = lax.all_gather(payload, "dp", axis=0)
     asked = gathered[:, 2 * n_loc * span : 2 * n_loc * span + 2, : page_table.shape[1]]
     picked = pick(me, asked.astype(jnp.int32), cache_pool, n_dp, cap, lanes)
-    fetched = [
-        lax.all_to_all(picked[0], "dp", split_axis=0, concat_axis=0, tiled=True)
-    ]
+    send = lax.optimization_barrier((picked[0], toks[1:]))[0]
+    fetched = [lax.all_to_all(send, "dp", split_axis=0, concat_axis=0, tiled=True)]
 
     own_half = lax.dynamic_slice_in_dim(w_out, (dp % 2) * (width // 2), width // 2, 0)
     gathered, lengths_b = lax.optimization_barrier((gathered, lengths, picked))[:2]
     down_named, up_named = named(owner_table, adapter_ids, gathered, n_loc, span)
     downs = [down_named] + [shift(down_named, "tensor", n_tp, k) for k in far_first]
-
-    own_half = lax.optimization_barrier((own_half, toks[1:], downs[1:]))[0]
-    halves = jnp.stack([shift(own_half, "tensor", n_tp, k) for k in far_first])
-    twins = lax.ppermute(halves, "dp", [(i, i ^ 1) for i in range(n_dp)])
-    w_rest = jnp.where(
-        dp % 2 == 0,
-        jnp.concatenate([halves, twins], axis=1),
-        jnp.concatenate([twins, halves], axis=1),
-    )
-    w_whole = jnp.concatenate([w_out[None], w_rest], axis=0)
 
     _, position = token_layout(lengths_b[0], page_counts[0], page_len, tok_total)
     index = jnp.arange(2 * HD, dtype=jnp.int32)
@@ -532,6 +555,8 @@
         tp_id, lengths, page_table, attn_gain.reshape(1, d_model), w_qkv, up_named,
         jnp.cos(angles), jnp.sin(angles) * sign[None, :], toks, downs, n_dp, cap, pool_dev,
     )
+    own_half = lax.optimization_barrier((own_half, query))[0]
+    halves = [shift(own_half, "tensor", n_tp, k) for k in far_first]
     for a in range(1, n_group):
         send, _ = lax.optimization_barrier((picked[a], fetched[-1]))
         fetched.append(lax.all_to_all(send, "dp", split_axis=0, concat_axis=0, tiled=True))
@@ -543,10 +568,10 @@
 
     n_chunk = max(1, row_count // CHUNK)
     sub = row_count // n_chunk
-    w_parts = w_whole.reshape(n_tp, n_group, lanes, d_model)
     base = all_tokens.astype(F32).reshape(tok_total, d_model)
 
     def mixed(blocks, a):
+        w_parts = w_whole.reshape(n_tp, n_group, lanes, d_model)
         return jnp.dot(
             jnp.concatenate(blocks, axis=1),
             w_parts[:, a].reshape(n_tp * lanes, d_model),
@@ -559,11 +584,17 @@
             q, new_keys, new_values, fetched[a],
         )
 
+    w_whole = None
     for a in range(n_group - 1):
         mix = attended(a, query)
+        if w_whole is None:
+            mix, halves = lax.optimization_barrier((mix, halves))
+            w_whole = whole_weight(w_out, halves, dp, n_dp)
         blocks = [mix] + [shift(mix, "tensor", n_tp, k) for k in far_first]
         base = base + mixed(blocks, a)
         query, base = lax.optimization_barrier((query, base))
+    if w_whole is None:
+        w_whole = whole_weight(w_out, halves, dp, n_dp)
     mix = attended(n_group - 1, query).reshape(n_tp, n_chunk, sub, lanes)
     base = base.reshape(n_tp, n_chunk, sub, d_model)
     gathered_mix = []
@@ -571,8 +602,12 @@
         own = mix[:, c].reshape(n_tp * sub, lanes)
         gathered_mix.append([own] + [shift(own, "tensor", n_tp, k) for k in far_first])
     outs = []
+    pieces = None
     for c in range(n_chunk):
-        residual = base[:, c].reshape(n_tp * sub, d_model) + mixed(gathered_mix[c], n_group - 1)
+        blocks = gathered_mix[c]
+        if pieces is not None:
+            blocks = lax.optimization_barrier((blocks, pieces))[0]
+        residual = base[:, c].reshape(n_tp * sub, d_model) + mixed(blocks, n_group - 1)
         ffn_in = normalize(residual, ffn_gain).astype(BF)
         gate_up = jnp.einsum("td,kdf->ktf", ffn_in, w_gateup, preferred_element_type=F32)
         hidden = (jax.nn.silu(gate_up[0]) * gate_up[1]).astype(BF)
@@ -582,8 +617,8 @@
             residual.reshape(n_tp, sub, d_model), tp, 0, False
         )
         down = down.astype(BF)
-        for k in far_first:
-            piece = lax.dynamic_index_in_dim(down, (tp + k) % n_tp, 0, False)
+        pieces = [lax.dynamic_index_in_dim(down, (tp + k) % n_tp, 0, False) for k in far_first]
+        for k, piece in zip(far_first, pieces):
             total = total + shift(piece, "tensor", n_tp, k).astype(F32)
         outs.append(total.astype(BF))
     return jnp.concatenate(outs, axis=0)

time: 188 us -> 161 us (0.86)
  waiting for transfers between devices: 54.4 us -> 36.4 us
  starting transfers between devices: 51 us -> 41.6 us
    ppermute x24, waiting for transfers between devices: 54.4 us -> 36.3 us  [shift(): return lax.ppermute(value, axis, [(i, (i + k) % n) for i in range(n)])]
    ppermute x24, starting transfers between devices: 42.1 us -> 32.9 us  [shift(): return lax.ppermute(value, axis, [(i, (i + k) % n) for i in range(n)])]
    all_to_all x1 -> x0, starting transfers between devices: 4.5 us -> none  [per_device(): lax.all_to_all(picked[0], 'dp', split_axis=0, concat_axis=0, tiled=True)]
    all_to_all x1 -> x2, starting transfers between devices: 4.36 us -> 8.74 us  [per_device(): lax.all_to_all(send, 'dp', split_axis=0, concat_axis=0, tiled=True)]
    dynamic_update_slice x4, local copies, waits for them, and re-layouts: 3 us -> 4.92 us  [per_device(): lax.dynamic_update_index_in_dim(all_tokens, block, (tp - k) % n_tp, 0)]
    unnamed x58 -> x46, local copies, waits for them, and re-layouts: 9.27 us -> 8.7 us
  transfers between devices with their start and end apart: 27 -> 27, of which waited for: 11 -> 10; matrix products, arithmetic and copies ran while one was open for 10% -> 17% of each run, Pallas kernels for 10% -> 14%
where the time goes in v2:
time: 161 us; the launch traced here: 160 us
  starting transfers between devices  41.6 us (26%)
  waiting for transfers between devices  36.4 us (23%)
  Pallas kernels  34.9 us (22%)
  local copies, waits for them, and re-layouts  17.9 us (11%)
  other arithmetic  10.4 us (6%)
  blocking collectives  9.99 us (6%)
  matrix products  8.76 us (5%)
    ppermute x24, waiting for transfers between devices, shift(): return lax.ppermute(value, axis, [(i, (i + k) % n) for i in range(n)])  36.3 us
    ppermute x24, starting transfers between devices, shift(): return lax.ppermute(value, axis, [(i, (i + k) % n) for i in range(n)])  32.9 us
    pallas_call x2, Pallas kernels, attend(): pl.pallas_call(functools.partial(attend_kernel, group, per), grid=(1,), o...  24.3 us
    all_gather x1, blocking collectives, per_device(): gathered = lax.all_gather(payload, 'dp', axis=0)  9.99 us
    all_to_all x2, starting transfers between devices, per_device(): lax.all_to_all(send, 'dp', split_axis=0, concat_axis=0, tiled=True)  8.74 us
    unnamed x46, local copies, waits for them, and re-layouts  8.7 us
    dynamic_update_slice x4, local copies, waits for them, and re-layouts, per_device(): lax.dynamic_update_index_in_dim(all_tokens, block, (tp - k) % n_tp, 0)  4.92 us
    pallas_call x1, Pallas kernels, pick(): pl.pallas_call(functools.partial(pick_kernel, n_dp, cap), out_shape=[jax....  4.51 us
  transfers between devices with their start and end apart: 27, of which 10 were waited for; matrix products, arithmetic and copies ran while one was open for 17% of the time, Pallas kernels for 14%

profile of v2, /device:TPU:0, one launch (start us, length us, event | category | flops | bytes accessed | tf_op | source)
XLA Modules:
  0.0 160.3 jit_solution(15755575206698035152)
XLA Ops:
  0.0 5.0 %collective-permute-start.2 = (bf16[128,1024]{1,0:T(8,128)(2,1)}, bf16[128,1024]{1,0:T(8,128)(2,1)S(1)}, u32[]{:S(2)}, u32[]{:S(2)}) collective-permute-start(bf16[128,1024]{1,0:T(8,128)(2,1)} %rest_5_.1), channel_id=1, source_target_pairs={{0,3},{1,0},{2,1},{3,2},{4,7},{5,4},{6,5},{7,6},{8,11},{9,8},{10,9... | collective-permute-start | bytes 786440 | tf_op jit(solution)/shard_map/ppermute | solution.py:480
  5.1 1.0 collective-permute-start
  6.1 0.7 fusion.58
  6.7 0.8 constant_dynamic-slice_fusion.1
  7.5 0.8 pad_maximum_fusion.3
  8.3 10.0 %all-gather = bf16[1152,256]{1,0:T(8,128)(2,1)S(1)} all-gather(bf16[144,256]{1,0:T(8,128)(2,1)S(1)} %pad_maximum_fusion.3), channel_id=2, replica_groups=mesh['dp'=8,'tensor'=4] {'dp'}, dimensions={0}, use_global_device_ids=true | all-gather | bytes 663552 | tf_op jit(solution)/shard_map/all_gather | solution.py:538
  18.3 0.6 slice_convert_fusion.asked_ref
  18.9 4.5 %pick_pages.1 = (bf16[8,4,128,2,128]{4,3,2,1,0:T(2,128)(2,1)}, bf16[8,4,128,2,128]{4,3,2,1,0:T(2,128)(2,1)}) custom-call(s32[1]{0:T(128)} %bitcast.4.me_ref, s32[8,2,32]{2,1,0:T(2,128)} %slice_convert_fusion.asked_ref, bf16[32,128,2,256]{3,2,1,0:T(2,128)(2,1)} %pool_ref.1), custom_call_target="tpu_custom_call" | custom-call | bytes 8388608 | tf_op jit(solution)/shard_map/pick_pages/pallas_call | solution.py:81
  23.5 4.1 %collective-permute-done.1.rest_7_ = bf16[128,1024]{1,0:T(8,128)(2,1)S(1)} collective-permute-done((bf16[128,1024]{1,0:T(8,128)(2,1)}, bf16[128,1024]{1,0:T(8,128)(2,1)S(1)}, u32[]{:S(2)}, u32[]{:S(2)}) %collective-permute-start.1) | collective-permute-done | bytes 262176 | tf_op jit(solution)/shard_map/ppermute | solution.py:480
  27.6 0.6 copy-done.2
  28.4 4.4 %all-to-all-start = ((bf16[8,4,128,2,128]{4,3,2,1,0:T(2,128)(2,1)}), bf16[8,4,128,2,128]{4,3,2,1,0:T(2,128)(2,1)}, u32[]{:S(2)}, u32[]{:S(2)}) async-start(bf16[8,4,128,2,128]{4,3,2,1,0:T(2,128)(2,1)} %get-tuple-element.38), calls=%async_computation | async-start | bytes 4194304 | tf_op jit(solution)/shard_map/all_to_all | solution.py:542
  32.7 2.3 %named_adapters.1 = (bf16[128,256]{1,0:T(8,128)(2,1)}, bf16[128,256]{1,0:T(8,128)(2,1)}) custom-call(s32[16]{0:T(128)} %table_ref.2, s32[1,4]{1,0:T(1,128)} %ids_ref.1, bf16[8,144,256]{2,1,0:T(8,128)(2,1)} %bitcast.109), custom_call_target="tpu_custom_call" | custom-call | tf_op jit(solution)/shard_map/named_adapters/pallas_call | solution.py:125
  35.1 2.8 %collective-permute-start.4 = (bf16[128,256]{1,0:T(8,128)(2,1)}, bf16[128,256]{1,0:T(8,128)(2,1)S(1)}, u32[]{:S(2)}, u32[]{:S(2)}) collective-permute-start(bf16[128,256]{1,0:T(8,128)(2,1)} %get-tuple-element.33.rest_9_), channel_id=1, source_target_pairs={{0,2},{1,3},{2,0},{3,1},{4,6},{5,7},{6,4},{7,5},{8,10},{9,11},{10,... | collective-permute-start | bytes 196616 | tf_op jit(solution)/shard_map/ppermute | solution.py:480
  37.9 1.9 %collective-permute-start.3 = (bf16[128,256]{1,0:T(8,128)(2,1)}, bf16[128,256]{1,0:T(8,128)(2,1)S(1)}, u32[]{:S(2)}, u32[]{:S(2)}) collective-permute-start(bf16[128,256]{1,0:T(8,128)(2,1)} %get-tuple-element.33.rest_9_), channel_id=1, source_target_pairs={{0,1},{1,2},{2,3},{3,0},{4,5},{5,6},{6,7},{7,4},{8,9},{9,10},{10,1... | collective-permute-start | bytes 196616 | tf_op jit(solution)/shard_map/ppermute | solution.py:480
  40.3 1.0 fusion.25
  41.3 1.7 %constant_dynamic-slice_fusion = bf16[128,1024]{1,0:T(8,128)(2,1)} fusion(bf16[256,1024]{1,0:T(8,128)(2,1)} %param.20, s32[]{:T(128)S(6)} %select_n.166), kind=kLoop, calls=%fused_computation.88 | loop fusion | bytes 524292 | tf_op jit(solution)/shard_map/dynamic_slice | solution.py:544
  42.9 1.9 %collective-permute-done.4.rest_11_ = bf16[128,256]{1,0:T(8,128)(2,1)S(1)} collective-permute-done((bf16[128,256]{1,0:T(8,128)(2,1)}, bf16[128,256]{1,0:T(8,128)(2,1)S(1)}, u32[]{:S(2)}, u32[]{:S(2)}) %collective-permute-start.4) | collective-permute-done | bytes 65568 | tf_op jit(solution)/shard_map/ppermute | solution.py:480
  44.9 0.6 copy-done.12
  45.5 0.6 copy-done.14
  46.1 0.9 copy-done.3
  47.1 0.9 copy-done.5
  48.0 1.4 copy-done.9
  49.4 0.8 copy-done.10
  50.3 0.8 copy-done.11
  51.1 0.8 copy-done.13
  51.9 0.8 copy-done.15
  52.8 3.8 %project.1 = (bf16[512,256]{1,0:T(8,128)(2,1)S(1)}, bf16[512,256]{1,0:T(8,128)(2,1)S(1)}, bf16[512,256]{1,0:T(8,128)(2,1)S(1)}, s32[32]{0:T(128)S(1)}) custom-call(s32[1]{0:T(128)} %bitcast.tp_ref, s32[1,4]{1,0:T(1,128)S(1)} %copy-done.8, s32[1,32]{1,0:T(1,128)S(1)} %copy-done.16, bf16[1,1024]{1,0:T(2,128)(2,1)S(1)} %reshape.128.rest_0_, ...), custom_call_target="tpu_custom_call" | custom-call | flops 1073741824 | bytes 3145728 | tf_op jit(solution)/shard_map/project/pallas_call | solution.py:230
  56.6 0.9 collective-permute-start.8
  57.7 1.7 %collective-permute-start.6 = (bf16[128,1024]{1,0:T(8,128)(2,1)}, bf16[128,1024]{1,0:T(8,128)(2,1)}, u32[]{:S(2)}, u32[]{:S(2)}) collective-permute-start(bf16[128,1024]{1,0:T(8,128)(2,1)} %constant_dynamic-slice_fusion), channel_id=1, source_target_pairs={{0,1},{1,2},{2,3},{3,0},{4,5},{5,6},{6,7},{7,4},{8,9},{9,10},{10,1... | collective-permute-start | bytes 786440 | tf_op jit(solution)/shard_map/ppermute | solution.py:480
  59.4 4.4 %all-to-all-start.1 = ((bf16[8,4,128,2,128]{4,3,2,1,0:T(2,128)(2,1)}), bf16[8,4,128,2,128]{4,3,2,1,0:T(2,128)(2,1)}, u32[]{:S(2)}, u32[]{:S(2)}) async-start(bf16[8,4,128,2,128]{4,3,2,1,0:T(2,128)(2,1)} %get-tuple-element.46), calls=%async_computation.1 | async-start | bytes 4194304 | tf_op jit(solution)/shard_map/all_to_all | solution.py:562
  63.8 12.1 %attend.2 = bf16[512,128]{1,0:T(8,128)(2,1)S(1)} custom-call(s32[1,4]{1,0:T(1,128)S(1)} %copy-done.8, s32[1,4]{1,0:T(1,128)S(1)} %copy-done.6, s32[32]{0:T(128)S(1)} %get-tuple-element.35.pos_ref, f32[2,4]{1,0:T(2,128)S(1)} %copy-done.7, bf16[512,256]{1,0:T(8,128)(2,1)S(1)} %get-tuple-element.45.q_ref, bf16[512,256]{1,0:T(8,128)(2,1)S(1)} %get-tuple-element.36.kn_ref, ...), custom_call_target="tpu_custom_call" | custom-call | flops 738197504 | bytes 2097152 | tf_op jit(solution)/shard_map/attend/pallas_call | solution.py:452
  75.9 5.2 %collective-permute-done.7 = bf16[128,1024]{1,0:T(8,128)(2,1)} collective-permute-done((bf16[128,1024]{1,0:T(8,128)(2,1)}, bf16[128,1024]{1,0:T(8,128)(2,1)}, u32[]{:S(2)}, u32[]{:S(2)}) %collective-permute-start.7) | collective-permute-done | bytes 262176 | tf_op jit(solution)/shard_map/ppermute | solution.py:480
  81.1 2.1 %pad_maximum_fusion.1 = bf16[3,128,1024]{2,1,0:T(8,128)(2,1)} fusion(bf16[1,128,1024]{2,1,0:T(8,128)(2,1)} %bitcast.19, bf16[1,128,1024]{2,1,0:T(8,128)(2,1)} %bitcast.18, bf16[1,128,1024]{2,1,0:T(8,128)(2,1)} %bitcast.17), kind=kLoop, calls=%fused_computation.20 | loop fusion | flops 786432 | bytes 1572864 | tf_op jit(solution)/shard_map/stack | solution.py:484
  83.2 1.2 broadcast_in_dim.66
  84.3 0.8 bitcast_dynamic-update-slice_fusion.3
  85.1 0.7 convert_element_type.76
  85.8 1.7 %bitcast_dynamic-update-slice_fusion.2 = bf16[4,128,1024]{2,1,0:T(8,128)(2,1)} fusion(bf16[4,128,1024]{2,1,0:T(8,128)(2,1)} %bitcast_dynamic-update-slice_fusion.3, s32[]{:T(128)S(6)} %select_n.160, bf16[128,1024]{1,0:T(8,128)(2,1)} %copy-done.4), kind=kLoop, calls=%fused_computation.65 | loop fusion | bytes 524292 | tf_op jit(solution)/shard_map/jit(dynamic_update_index_in_dim)/dynamic_update_slice | solution.py:567
  87.5 1.7 %bitcast_dynamic-update-slice_fusion.1 = bf16[4,128,1024]{2,1,0:T(8,128)(2,1)} fusion(bf16[4,128,1024]{2,1,0:T(8,128)(2,1)} %bitcast_dynamic-update-slice_fusion.2, s32[]{:T(128)S(6)} %select_n.162, bf16[128,1024]{1,0:T(8,128)(2,1)} %copy-done.2), kind=kLoop, calls=%fused_computation.64 | loop fusion | bytes 524292 | tf_op jit(solution)/shard_map/jit(dynamic_update_index_in_dim)/dynamic_update_slice | solution.py:567
  89.2 0.7 bitcast_dynamic-update-slice_fusion
  90.0 2.7 %collective-permute-start.10 = (bf16[512,128]{1,0:T(8,128)(2,1)S(1)}, bf16[512,128]{1,0:T(8,128)(2,1)S(1)}, u32[]{:S(2)}, u32[]{:S(2)}) collective-permute-start(bf16[512,128]{1,0:T(8,128)(2,1)S(1)} %attend.2), channel_id=1, source_target_pairs={{0,2},{1,3},{2,0},{3,1},{4,6},{5,7},{6,4},{7,5},{8,10},{9,11},{10,... | collective-permute-start | bytes 393224 | tf_op jit(solution)/shard_map/ppermute | solution.py:480
  92.7 2.0 %collective-permute-start.9 = (bf16[512,128]{1,0:T(8,128)(2,1)S(1)}, bf16[512,128]{1,0:T(8,128)(2,1)S(1)}, u32[]{:S(2)}, u32[]{:S(2)}) collective-permute-start(bf16[512,128]{1,0:T(8,128)(2,1)S(1)} %attend.2), channel_id=1, source_target_pairs={{0,1},{1,2},{2,3},{3,0},{4,5},{5,6},{6,7},{7,4},{8,9},{9,10},{10,1... | collective-permute-start | bytes 393224 | tf_op jit(solution)/shard_map/ppermute | solution.py:480
  94.7 2.1 %maximum_select_fusion = bf16[3,256,1024]{2,1,0:T(8,128)(2,1)S(1)} fusion(bf16[3,128,1024]{2,1,0:T(8,128)(2,1)} %collective-permute-done.12, bf16[1,128,1024]{2,1,0:T(8,128)(2,1)} %bitcast.19, bf16[1,128,1024]{2,1,0:T(8,128)(2,1)} %bitcast.18, bf16[1,128,1024]{2,1,0:T(8,128)(2,1)} %bitcast.17, pred[]{:T(512)S(6)} %eq.39), kind=kLoop, calls=%fused_computation.9 | loop fusion | flops 13369344 | bytes 3145729 | tf_op jit(solution)/shard_map/jit(_where)/select_n | solution.py:486
  96.8 1.2 pad_maximum_fusion
  98.0 7.3 %collective-permute-done.10 = bf16[512,128]{1,0:T(8,128)(2,1)S(1)} collective-permute-done((bf16[512,128]{1,0:T(8,128)(2,1)S(1)}, bf16[512,128]{1,0:T(8,128)(2,1)S(1)}, u32[]{:S(2)}, u32[]{:S(2)}) %collective-permute-start.10) | collective-permute-done | bytes 131104 | tf_op jit(solution)/shard_map/ppermute | solution.py:480
  105.2 3.3 %convert_add_fusion = f32[512,1024]{1,0:T(8,128)} fusion(bf16[4,128,1024]{2,1,0:T(8,128)(2,1)} %bitcast_dynamic-update-slice_fusion, bf16[512,1024]{1,0:T(8,128)(2,1)S(1)} %bitcast.112, bf16[512,128]{1,0:T(8,128)(2,1)S(1)} %collective-permute-done.11, bf16[512,128]{1,0:T(8,128)(2,1)S(1)} %collective-permute-done.10, ...), kind=kOutput, calls=%fused_computation.2 | convolution fusion | flops 540016640 | bytes 4718592 | tf_op jit(solution)/shard_map/dot_general | solution.py:575
  108.6 12.2 %attend.3 = bf16[512,128]{1,0:T(8,128)(2,1)S(1)} custom-call(s32[1,4]{1,0:T(1,128)S(1)} %copy-done.8, s32[1,4]{1,0:T(1,128)S(1)} %copy-done.6, s32[32]{0:T(128)S(1)} %get-tuple-element.35.pos_ref, f32[2,4]{1,0:T(2,128)S(1)} %copy-done.7, bf16[512,256]{1,0:T(8,128)(2,1)S(1)} %get-tuple-element.45.q_ref, bf16[512,256]{1,0:T(8,128)(2,1)S(1)} %get-tuple-element.36.kn_ref, ...), custom_call_target="tpu_custom_call" | custom-call | flops 738197504 | bytes 2097152 | tf_op jit(solution)/shard_map/attend/pallas_call | solution.py:452
  121.2 1.9 %collective-permute-start.13 = (bf16[256,128]{1,0:T(8,128)(2,1)S(1)}, bf16[256,128]{1,0:T(8,128)(2,1)S(1)}, u32[]{:S(2)}, u32[]{:S(2)}) collective-permute-start(bf16[256,128]{1,0:T(8,128)(2,1)S(1)} %bitcast.123), channel_id=1, source_target_pairs={{0,1},{1,2},{2,3},{3,0},{4,5},{5,6},{6,7},{7,4},{8,9},{9,10},{10,1... | collective-permute-start | bytes 196616 | tf_op jit(solution)/shard_map/ppermute | solution.py:480
  123.3 2.2 %collective-permute-start.21 = (bf16[256,128]{1,0:T(8,128)(2,1)S(1)}, bf16[256,128]{1,0:T(8,128)(2,1)S(1)}, u32[]{:S(2)}, u32[]{:S(2)}) collective-permute-start(bf16[256,128]{1,0:T(8,128)(2,1)S(1)} %bitcast.117), channel_id=1, source_target_pairs={{0,3},{1,0},{2,1},{3,2},{4,7},{5,4},{6,5},{7,6},{8,11},{9,8},{10,9... | collective-permute-start | bytes 196616 | tf_op jit(solution)/shard_map/ppermute | solution.py:480
  125.5 0.6 collective-permute-start.20
  126.1 1.1 collective-permute-done.15
  127.3 0.8 collective-permute-start.19
  128.1 2.4 %collective-permute-done.14 = bf16[256,128]{1,0:T(8,128)(2,1)S(1)} collective-permute-done((bf16[256,128]{1,0:T(8,128)(2,1)S(1)}, bf16[256,128]{1,0:T(8,128)(2,1)S(1)}, u32[]{:S(2)}, u32[]{:S(2)}) %collective-permute-start.14) | collective-permute-done | bytes 65568 | tf_op jit(solution)/shard_map/ppermute | solution.py:480
  131.0 1.3 convolution_bitcast_fusion.1
  132.6 0.8 fusion.68
  133.5 1.7 %collective-permute-start.18 = (bf16[64,1024]{1,0:T(8,128)(2,1)S(1)}, bf16[64,1024]{1,0:T(8,128)(2,1)S(1)}, u32[]{:S(2)}, u32[]{:S(2)}) collective-permute-start(bf16[64,1024]{1,0:T(8,128)(2,1)S(1)} %get-tuple-element.64), channel_id=1, source_target_pairs={{0,3},{1,0},{2,1},{3,2},{4,7},{5,4},{6,5},{7,6},{8,11},{9,8},{10,9... | collective-permute-start | bytes 393224 | tf_op jit(solution)/shard_map/ppermute | solution.py:480
  135.2 1.0 collective-permute-start.17
  136.3 1.9 %collective-permute-start.16 = (bf16[64,1024]{1,0:T(8,128)(2,1)S(1)}, bf16[64,1024]{1,0:T(8,128)(2,1)S(1)}, u32[]{:S(2)}, u32[]{:S(2)}) collective-permute-start(bf16[64,1024]{1,0:T(8,128)(2,1)S(1)} %get-tuple-element.66), channel_id=1, source_target_pairs={{0,1},{1,2},{2,3},{3,0},{4,5},{5,6},{6,7},{7,4},{8,9},{9,10},{10,1... | collective-permute-start | bytes 393224 | tf_op jit(solution)/shard_map/ppermute | solution.py:480
  138.8 1.3 convolution_bitcast_fusion
  140.4 0.8 fusion.69
  141.3 0.6 collective-permute-start.22
  141.8 3.3 %collective-permute-start.24 = (bf16[64,1024]{1,0:T(8,128)(2,1)S(1)}, bf16[64,1024]{1,0:T(8,128)(2,1)S(1)}, u32[]{:S(2)}, u32[]{:S(2)}) collective-permute-start(bf16[64,1024]{1,0:T(8,128)(2,1)S(1)} %get-tuple-element.62), channel_id=1, source_target_pairs={{0,3},{1,0},{2,1},{3,2},{4,7},{5,4},{6,5},{7,6},{8,11},{9,8},{10,9... | collective-permute-start | bytes 393224 | tf_op jit(solution)/shard_map/ppermute | solution.py:480
  145.1 7.2 %collective-permute-done.17 = bf16[64,1024]{1,0:T(8,128)(2,1)S(1)} collective-permute-done((bf16[64,1024]{1,0:T(8,128)(2,1)S(1)}, bf16[64,1024]{1,0:T(8,128)(2,1)S(1)}, u32[]{:S(2)}, u32[]{:S(2)}) %collective-permute-start.17) | collective-permute-done | bytes 131104 | tf_op jit(solution)/shard_map/ppermute | solution.py:480
  152.9 6.6 %collective-permute-done.23 = bf16[64,1024]{1,0:T(8,128)(2,1)S(1)} collective-permute-done((bf16[64,1024]{1,0:T(8,128)(2,1)S(1)}, bf16[64,1024]{1,0:T(8,128)(2,1)S(1)}, u32[]{:S(2)}, u32[]{:S(2)}) %collective-permute-start.23) | collective-permute-done | bytes 131104 | tf_op jit(solution)/shard_map/ppermute | solution.py:480
  159.6 0.7 pad_maximum_fusion.2
  (83 shorter events, 3.6 us)
Async XLA Ops:
  0.0 132.6 %copy-start = (bf16[1024,1024]{1,0:T(8,128)(2,1)S(1)}, bf16[1024,1024]{1,0:T(8,128)(2,1)}, u32[]{:S(2)}) copy-start(bf16[1024,1024]{1,0:T(8,128)(2,1)} %param.22) | copy-start | bytes 6291460
  0.0 23.4 %collective-permute-start.2 = (bf16[128,1024]{1,0:T(8,128)(2,1)}, bf16[128,1024]{1,0:T(8,128)(2,1)S(1)}, u32[]{:S(2)}, u32[]{:S(2)}) collective-permute-start(bf16[128,1024]{1,0:T(8,128)(2,1)} %rest_5_.1), channel_id=1, source_target_pairs={{0,3},{1,0},{2,1},{3,2},{4,7},{5,4},{6,5},{7,6},{8,11},{9,8},{10,9... | collective-permute-start | bytes 786440 | tf_op jit(solution)/shard_map/ppermute | solution.py:480
  5.1 22.5 %collective-permute-start.1 = (bf16[128,1024]{1,0:T(8,128)(2,1)}, bf16[128,1024]{1,0:T(8,128)(2,1)S(1)}, u32[]{:S(2)}, u32[]{:S(2)}) collective-permute-start(bf16[128,1024]{1,0:T(8,128)(2,1)} %rest_5_.1), channel_id=1, source_target_pairs={{0,2},{1,3},{2,0},{3,1},{4,6},{5,7},{6,4},{7,5},{8,10},{9,11},{10,... | collective-permute-start | bytes 786440 | tf_op jit(solution)/shard_map/ppermute | solution.py:480
  5.1 22.5 %collective-permute-start = (bf16[128,1024]{1,0:T(8,128)(2,1)}, bf16[128,1024]{1,0:T(8,128)(2,1)S(1)}, u32[]{:S(2)}, u32[]{:S(2)}) collective-permute-start(bf16[128,1024]{1,0:T(8,128)(2,1)} %rest_5_.1), channel_id=1, source_target_pairs={{0,1},{1,2},{2,3},{3,0},{4,5},{5,6},{6,7},{7,4},{8,9},{9,10},{10,1... | collective-permute-start | bytes 786440 | tf_op jit(solution)/shard_map/ppermute | solution.py:480
  18.3 5.2 %copy-start.19 = (bf16[1152,256]{1,0:T(8,128)(2,1)}, bf16[1152,256]{1,0:T(8,128)(2,1)S(1)}, u32[]{:S(2)}) copy-start(bf16[1152,256]{1,0:T(8,128)(2,1)S(1)} %all-gather) | copy-start | bytes 1769476
  27.6 0.7 copy-start.2
  27.6 0.8 copy-start.4
  27.6 12.3 %copy-start.22 = (bf16[1024]{0:T(1024)(128)(2,1)S(1)}, bf16[1024]{0:T(1024)(128)(2,1)}, u32[]{:S(2)}) copy-start(bf16[1024]{0:T(1024)(128)(2,1)} %param.17) | copy-start | bytes 6148
  27.6 12.3 %copy-start.8 = (s32[1,4]{1,0:T(1,128)S(1)}, s32[1,4]{1,0:T(1,128)}, u32[]{:S(2)}) copy-start(s32[1,4]{1,0:T(1,128)} %lens_ref.5) | copy-start | bytes 52
  27.6 12.5 %copy-start.6 = (s32[1,4]{1,0:T(1,128)S(1)}, s32[1,4]{1,0:T(1,128)}, u32[]{:S(2)}) copy-start(s32[1,4]{1,0:T(1,128)} %counts_ref.3) | copy-start | bytes 52
  27.6 18.5 %copy-start.1 = (bf16[128,1024]{1,0:T(8,128)(2,1)S(1)}, bf16[128,1024]{1,0:T(8,128)(2,1)}, u32[]{:S(2)}) copy-start(bf16[128,1024]{1,0:T(8,128)(2,1)} %rest_5_.1) | copy-start | bytes 786436
  27.6 18.5 %copy-start.16 = (s32[1,32]{1,0:T(1,128)S(1)}, s32[1,32]{1,0:T(1,128)}, u32[]{:S(2)}) copy-start(s32[1,32]{1,0:T(1,128)} %table_ref.3) | copy-start | bytes 388
  28.4 31.0 %all-to-all-start = ((bf16[8,4,128,2,128]{4,3,2,1,0:T(2,128)(2,1)}), bf16[8,4,128,2,128]{4,3,2,1,0:T(2,128)(2,1)}, u32[]{:S(2)}, u32[]{:S(2)}) async-start(bf16[8,4,128,2,128]{4,3,2,1,0:T(2,128)(2,1)} %get-tuple-element.38), calls=%async_computation | async-start | bytes 4194304 | tf_op jit(solution)/shard_map/all_to_all | solution.py:542
  35.0 7.9 %collective-permute-start.5 = (bf16[128,256]{1,0:T(8,128)(2,1)}, bf16[128,256]{1,0:T(8,128)(2,1)S(1)}, u32[]{:S(2)}, u32[]{:S(2)}) collective-permute-start(bf16[128,256]{1,0:T(8,128)(2,1)} %get-tuple-element.33.rest_9_), channel_id=1, source_target_pairs={{0,3},{1,0},{2,1},{3,2},{4,7},{5,4},{6,5},{7,6},{8,11},{9,8},{10,9... | collective-permute-start | bytes 196616 | tf_op jit(solution)/shard_map/ppermute | solution.py:480
  35.1 9.8 %collective-permute-start.4 = (bf16[128,256]{1,0:T(8,128)(2,1)}, bf16[128,256]{1,0:T(8,128)(2,1)S(1)}, u32[]{:S(2)}, u32[]{:S(2)}) collective-permute-start(bf16[128,256]{1,0:T(8,128)(2,1)} %get-tuple-element.33.rest_9_), channel_id=1, source_target_pairs={{0,2},{1,3},{2,0},{3,1},{4,6},{5,7},{6,4},{7,5},{8,10},{9,11},{10,... | collective-permute-start | bytes 196616 | tf_op jit(solution)/shard_map/ppermute | solution.py:480
  37.9 7.6 %collective-permute-start.3 = (bf16[128,256]{1,0:T(8,128)(2,1)}, bf16[128,256]{1,0:T(8,128)(2,1)S(1)}, u32[]{:S(2)}, u32[]{:S(2)}) collective-permute-start(bf16[128,256]{1,0:T(8,128)(2,1)} %get-tuple-element.33.rest_9_), channel_id=1, source_target_pairs={{0,1},{1,2},{2,3},{3,0},{4,5},{5,6},{6,7},{7,4},{8,9},{9,10},{10,1... | collective-permute-start | bytes 196616 | tf_op jit(solution)/shard_map/ppermute | solution.py:480
  44.9 0.6 copy-start.12
  45.5 0.6 copy-start.14
  46.1 1.0 copy-start.3
  47.1 0.9 copy-start.5
  48.0 1.4 copy-start.9
  49.4 0.8 copy-start.10
  50.3 0.8 copy-start.11
  51.1 0.8 copy-start.13
  51.9 0.8 copy-start.15
  56.6 19.3 %collective-permute-start.8 = (bf16[128,1024]{1,0:T(8,128)(2,1)}, bf16[128,1024]{1,0:T(8,128)(2,1)}, u32[]{:S(2)}, u32[]{:S(2)}) collective-permute-start(bf16[128,1024]{1,0:T(8,128)(2,1)} %constant_dynamic-slice_fusion), channel_id=1, source_target_pairs={{0,3},{1,0},{2,1},{3,2},{4,7},{5,4},{6,5},{7,6},{8,11},{9,8},{10,9... | collective-permute-start | bytes 786440 | tf_op jit(solution)/shard_map/ppermute | solution.py:480
  57.5 23.6 %collective-permute-start.7 = (bf16[128,1024]{1,0:T(8,128)(2,1)}, bf16[128,1024]{1,0:T(8,128)(2,1)}, u32[]{:S(2)}, u32[]{:S(2)}) collective-permute-start(bf16[128,1024]{1,0:T(8,128)(2,1)} %constant_dynamic-slice_fusion), channel_id=1, source_target_pairs={{0,2},{1,3},{2,0},{3,1},{4,6},{5,7},{6,4},{7,5},{8,10},{9,11},{10,... | collective-permute-start | bytes 786440 | tf_op jit(solution)/shard_map/ppermute | solution.py:480
  57.7 23.4 %collective-permute-start.6 = (bf16[128,1024]{1,0:T(8,128)(2,1)}, bf16[128,1024]{1,0:T(8,128)(2,1)}, u32[]{:S(2)}, u32[]{:S(2)}) collective-permute-start(bf16[128,1024]{1,0:T(8,128)(2,1)} %constant_dynamic-slice_fusion), channel_id=1, source_target_pairs={{0,1},{1,2},{2,3},{3,0},{4,5},{5,6},{6,7},{7,4},{8,9},{9,10},{10,1... | collective-permute-start | bytes 786440 | tf_op jit(solution)/shard_map/ppermute | solution.py:480
  59.3 4.4 %copy-start.7 = (f32[2,4]{1,0:T(2,128)S(1)}, f32[2,4]{1,0:T(2,128)}, u32[]{:S(2)}) copy-start(f32[2,4]{1,0:T(2,128)} %bias_ref.3) | copy-start | bytes 100
  59.4 49.2 %all-to-all-start.1 = ((bf16[8,4,128,2,128]{4,3,2,1,0:T(2,128)(2,1)}), bf16[8,4,128,2,128]{4,3,2,1,0:T(2,128)(2,1)}, u32[]{:S(2)}, u32[]{:S(2)}) async-start(bf16[8,4,128,2,128]{4,3,2,1,0:T(2,128)(2,1)} %get-tuple-element.46), calls=%async_computation.1 | async-start | bytes 4194304 | tf_op jit(solution)/shard_map/all_to_all | solution.py:562
  83.2 11.5 %collective-permute-start.12 = (bf16[3,128,1024]{2,1,0:T(8,128)(2,1)}, bf16[3,128,1024]{2,1,0:T(8,128)(2,1)}, u32[]{:S(2)}, u32[]{:S(2)}) collective-permute-start(bf16[3,128,1024]{2,1,0:T(8,128)(2,1)} %pad_maximum_fusion.1), channel_id=1, source_target_pairs={{0,4},{4,0},{8,12},{12,8},{16,20},{20,16},{24,28},{28,24},{1,5},{5... | collective-permute-start | bytes 2359304 | tf_op jit(solution)/shard_map/ppermute | solution.py:485
  87.5 9.3 %copy-start.21 = (bf16[256,1024]{1,0:T(8,128)(2,1)S(1)}, bf16[256,1024]{1,0:T(8,128)(2,1)}, u32[]{:S(2)}) copy-start(bf16[256,1024]{1,0:T(8,128)(2,1)} %param.20) | copy-start | bytes 1572868
  90.0 8.0 %collective-permute-start.11 = (bf16[512,128]{1,0:T(8,128)(2,1)S(1)}, bf16[512,128]{1,0:T(8,128)(2,1)S(1)}, u32[]{:S(2)}, u32[]{:S(2)}) collective-permute-start(bf16[512,128]{1,0:T(8,128)(2,1)S(1)} %attend.2), channel_id=1, source_target_pairs={{0,3},{1,0},{2,1},{3,2},{4,7},{5,4},{6,5},{7,6},{8,11},{9,8},{10,9... | collective-permute-start | bytes 393224 | tf_op jit(solution)/shard_map/ppermute | solution.py:480
  90.0 15.3 %collective-permute-start.10 = (bf16[512,128]{1,0:T(8,128)(2,1)S(1)}, bf16[512,128]{1,0:T(8,128)(2,1)S(1)}, u32[]{:S(2)}, u32[]{:S(2)}) collective-permute-start(bf16[512,128]{1,0:T(8,128)(2,1)S(1)} %attend.2), channel_id=1, source_target_pairs={{0,2},{1,3},{2,0},{3,1},{4,6},{5,7},{6,4},{7,5},{8,10},{9,11},{10,... | collective-permute-start | bytes 393224 | tf_op jit(solution)/shard_map/ppermute | solution.py:480
  92.7 12.6 %collective-permute-start.9 = (bf16[512,128]{1,0:T(8,128)(2,1)S(1)}, bf16[512,128]{1,0:T(8,128)(2,1)S(1)}, u32[]{:S(2)}, u32[]{:S(2)}) collective-permute-start(bf16[512,128]{1,0:T(8,128)(2,1)S(1)} %attend.2), channel_id=1, source_target_pairs={{0,1},{1,2},{2,3},{3,0},{4,5},{5,6},{6,7},{7,4},{8,9},{9,10},{10,1... | collective-permute-start | bytes 393224 | tf_op jit(solution)/shard_map/ppermute | solution.py:480
  108.6 14.6 %copy-start.20 = (f32[512,1024]{1,0:T(8,128)S(1)}, f32[512,1024]{1,0:T(8,128)}, u32[]{:S(2)}) copy-start(f32[512,1024]{1,0:T(8,128)} %convert_add_fusion) | copy-start | bytes 6291460
  120.8 9.7 %copy-start.18 = (bf16[4,1,128,1024]{3,2,1,0:T(8,128)(2,1)S(1)}, bf16[4,1,128,1024]{3,2,1,0:T(8,128)(2,1)}, u32[]{:S(2)}) copy-start(bf16[4,1,128,1024]{3,2,1,0:T(8,128)(2,1)} %get-tuple-element.59) | copy-start | bytes 3145732
  120.8 6.4 %collective-permute-start.15 = (bf16[256,128]{1,0:T(8,128)(2,1)S(1)}, bf16[256,128]{1,0:T(8,128)(2,1)S(1)}, u32[]{:S(2)}, u32[]{:S(2)}) collective-permute-start(bf16[256,128]{1,0:T(8,128)(2,1)S(1)} %bitcast.121), channel_id=1, source_target_pairs={{0,3},{1,0},{2,1},{3,2},{4,7},{5,4},{6,5},{7,6},{8,11},{9,8},{10,9... | collective-permute-start | bytes 196616 | tf_op jit(solution)/shard_map/ppermute | solution.py:480
  120.9 9.6 %collective-permute-start.14 = (bf16[256,128]{1,0:T(8,128)(2,1)S(1)}, bf16[256,128]{1,0:T(8,128)(2,1)S(1)}, u32[]{:S(2)}, u32[]{:S(2)}) collective-permute-start(bf16[256,128]{1,0:T(8,128)(2,1)S(1)} %bitcast.122), channel_id=1, source_target_pairs={{0,2},{1,3},{2,0},{3,1},{4,6},{5,7},{6,4},{7,5},{8,10},{9,11},{10,... | collective-permute-start | bytes 196616 | tf_op jit(solution)/shard_map/ppermute | solution.py:480
  121.2 9.3 %collective-permute-start.13 = (bf16[256,128]{1,0:T(8,128)(2,1)S(1)}, bf16[256,128]{1,0:T(8,128)(2,1)S(1)}, u32[]{:S(2)}, u32[]{:S(2)}) collective-permute-start(bf16[256,128]{1,0:T(8,128)(2,1)S(1)} %bitcast.123), channel_id=1, source_target_pairs={{0,1},{1,2},{2,3},{3,0},{4,5},{5,6},{6,7},{7,4},{8,9},{9,10},{10,1... | collective-permute-start | bytes 196616 | tf_op jit(solution)/shard_map/ppermute | solution.py:480
  123.1 7.9 %copy-start.17 = (bf16[2,1024,1024]{2,1,0:T(8,128)(2,1)S(1)}, bf16[2,1024,1024]{2,1,0:T(8,128)(2,1)}, u32[]{:S(2)}) copy-start(bf16[2,1024,1024]{2,1,0:T(8,128)(2,1)} %param.21) | copy-start | bytes 12582916
  123.3 13.0 %collective-permute-start.21 = (bf16[256,128]{1,0:T(8,128)(2,1)S(1)}, bf16[256,128]{1,0:T(8,128)(2,1)S(1)}, u32[]{:S(2)}, u32[]{:S(2)}) collective-permute-start(bf16[256,128]{1,0:T(8,128)(2,1)S(1)} %bitcast.117), channel_id=1, source_target_pairs={{0,3},{1,0},{2,1},{3,2},{4,7},{5,4},{6,5},{7,6},{8,11},{9,8},{10,9... | collective-permute-start | bytes 196616 | tf_op jit(solution)/shard_map/ppermute | solution.py:480
  125.5 12.7 %collective-permute-start.20 = (bf16[256,128]{1,0:T(8,128)(2,1)S(1)}, bf16[256,128]{1,0:T(8,128)(2,1)S(1)}, u32[]{:S(2)}, u32[]{:S(2)}) collective-permute-start(bf16[256,128]{1,0:T(8,128)(2,1)S(1)} %bitcast.118), channel_id=1, source_target_pairs={{0,2},{1,3},{2,0},{3,1},{4,6},{5,7},{6,4},{7,5},{8,10},{9,11},{10,... | collective-permute-start | bytes 196616 | tf_op jit(solution)/shard_map/ppermute | solution.py:480
  127.3 11.0 %collective-permute-start.19 = (bf16[256,128]{1,0:T(8,128)(2,1)S(1)}, bf16[256,128]{1,0:T(8,128)(2,1)S(1)}, u32[]{:S(2)}, u32[]{:S(2)}) collective-permute-start(bf16[256,128]{1,0:T(8,128)(2,1)S(1)} %bitcast.119), channel_id=1, source_target_pairs={{0,1},{1,2},{2,3},{3,0},{4,5},{5,6},{6,7},{7,4},{8,9},{9,10},{10,1... | collective-permute-start | bytes 196616 | tf_op jit(solution)/shard_map/ppermute | solution.py:480
  133.5 11.6 %collective-permute-start.18 = (bf16[64,1024]{1,0:T(8,128)(2,1)S(1)}, bf16[64,1024]{1,0:T(8,128)(2,1)S(1)}, u32[]{:S(2)}, u32[]{:S(2)}) collective-permute-start(bf16[64,1024]{1,0:T(8,128)(2,1)S(1)} %get-tuple-element.64), channel_id=1, source_target_pairs={{0,3},{1,0},{2,1},{3,2},{4,7},{5,4},{6,5},{7,6},{8,11},{9,8},{10,9... | collective-permute-start | bytes 393224 | tf_op jit(solution)/shard_map/ppermute | solution.py:480
  135.2 17.1 %collective-permute-start.17 = (bf16[64,1024]{1,0:T(8,128)(2,1)S(1)}, bf16[64,1024]{1,0:T(8,128)(2,1)S(1)}, u32[]{:S(2)}, u32[]{:S(2)}) collective-permute-start(bf16[64,1024]{1,0:T(8,128)(2,1)S(1)} %get-tuple-element.65), channel_id=1, source_target_pairs={{0,2},{1,3},{2,0},{3,1},{4,6},{5,7},{6,4},{7,5},{8,10},{9,11},{10,... | collective-permute-start | bytes 393224 | tf_op jit(solution)/shard_map/ppermute | solution.py:480
  136.3 16.1 %collective-permute-start.16 = (bf16[64,1024]{1,0:T(8,128)(2,1)S(1)}, bf16[64,1024]{1,0:T(8,128)(2,1)S(1)}, u32[]{:S(2)}, u32[]{:S(2)}) collective-permute-start(bf16[64,1024]{1,0:T(8,128)(2,1)S(1)} %get-tuple-element.66), channel_id=1, source_target_pairs={{0,1},{1,2},{2,3},{3,0},{4,5},{5,6},{6,7},{7,4},{8,9},{9,10},{10,1... | collective-permute-start | bytes 393224 | tf_op jit(solution)/shard_map/ppermute | solution.py:480
  141.3 11.2 %collective-permute-start.22 = (bf16[64,1024]{1,0:T(8,128)(2,1)S(1)}, bf16[64,1024]{1,0:T(8,128)(2,1)S(1)}, u32[]{:S(2)}, u32[]{:S(2)}) collective-permute-start(bf16[64,1024]{1,0:T(8,128)(2,1)S(1)} %get-tuple-element.61), channel_id=1, source_target_pairs={{0,1},{1,2},{2,3},{3,0},{4,5},{5,6},{6,7},{7,4},{8,9},{9,10},{10,1... | collective-permute-start | bytes 393224 | tf_op jit(solution)/shard_map/ppermute | solution.py:480
  141.8 11.1 %collective-permute-start.24 = (bf16[64,1024]{1,0:T(8,128)(2,1)S(1)}, bf16[64,1024]{1,0:T(8,128)(2,1)S(1)}, u32[]{:S(2)}, u32[]{:S(2)}) collective-permute-start(bf16[64,1024]{1,0:T(8,128)(2,1)S(1)} %get-tuple-element.62), channel_id=1, source_target_pairs={{0,3},{1,0},{2,1},{3,2},{4,7},{5,4},{6,5},{7,6},{8,11},{9,8},{10,9... | collective-permute-start | bytes 393224 | tf_op jit(solution)/shard_map/ppermute | solution.py:480
  145.1 14.3 %collective-permute-start.23 = (bf16[64,1024]{1,0:T(8,128)(2,1)S(1)}, bf16[64,1024]{1,0:T(8,128)(2,1)S(1)}, u32[]{:S(2)}, u32[]{:S(2)}) collective-permute-start(bf16[64,1024]{1,0:T(8,128)(2,1)S(1)} %get-tuple-element.63), channel_id=1, source_target_pairs={{0,2},{1,3},{2,0},{3,1},{4,6},{5,7},{6,4},{7,5},{8,10},{9,11},{10,... | collective-permute-start | bytes 393224 | tf_op jit(solution)/shard_map/ppermute | solution.py:480

commit v3 on v2

--- a/solution.py
+++ b/solution.py
@@ -17,6 +17,7 @@
 BF = jnp.bfloat16
 F32 = jnp.float32
 NEG = -1e30
+LIGHT = pl.CostEstimate(flops=1000, bytes_accessed=1000, transcendentals=0)
 
 
 def normalize(values, gain):
@@ -88,7 +89,7 @@
             pltpu.SemaphoreType.DMA((n_dp,)),
             pltpu.SemaphoreType.DMA((n_out, n_dp)),
         ],
-        cost_estimate=pl.CostEstimate(flops=0, bytes_accessed=4 * pool.size, transcendentals=0),
+        cost_estimate=LIGHT,
         name="pick_pages",
     )(me, asked, pool)
 
@@ -132,14 +133,15 @@
             pltpu.VMEM(out.shape, BF),
             pltpu.SemaphoreType.DMA((n_req, 2)),
         ],
+        cost_estimate=LIGHT,
         name="named_adapters",
     )(owner_table, adapter_ids, gathered)
 
 
 def project_kernel(n_tp, cap, pool_dev, tp_ref, lens_ref, table_ref, *rest):
     hbm_refs, rest = rest[: 5 + 2 * n_tp], rest[5 + 2 * n_tp :]
-    q_ref, k_ref, v_ref, pos_ref, down, count, *held = rest
-    held, sem = held[:-1], held[-1]
+    q_ref, k_ref, v_ref, pos_ref, all_ref, down, count, *held = rest
+    held, sem, sem_out = held[:-2], held[-2], held[-1]
     gain_ref, w_ref, up_ref, cos_ref, sin_ref, tok_ref = held
     tp = tp_ref[0]
     copies = []
@@ -170,6 +172,17 @@
 
     for copy in copies:
         copy.wait()
+    n_chunk, _, sub, _ = all_ref.shape
+    stores = []
+    for k in range(n_tp):
+        for c in range(n_chunk):
+            copy = pltpu.make_async_copy(
+                tok_ref.at[k, pl.ds(c * sub, sub)],
+                all_ref.at[c, lax.rem(tp - k + n_tp, n_tp)],
+                sem_out.at[k, c],
+            )
+            copy.start()
+            stores.append(copy)
     lane = lax.broadcasted_iota(jnp.int32, (1, 128), 1)
     first = jnp.bitwise_and(lane, HD - 1) < HD // 2
 
@@ -218,10 +231,15 @@
             k_ref[pl.ds(row0, rows), a * 128 : (a + 1) * 128] = part.astype(BF)
         v = jnp.dot(normed, w_ref[2], preferred_element_type=F32) + deltas[1]
         v_ref[pl.ds(row0, rows), :] = v.astype(BF)
-
-
-def project(tp, lens, table, gain, w_qkv, up, cos, sin, toks, downs, n_dp, cap, pool_dev):
+    for copy in stores:
+        copy.wait()
+
+
+def project(
+    tp, lens, table, gain, w_qkv, up, cos, sin, toks, downs, n_dp, cap, pool_dev, n_chunk
+):
     n_tp = len(toks)
+    sub = toks[0].shape[0] // n_chunk
     rows = toks[0].shape[0] * n_tp
     width = w_qkv.shape[2]
     smem = pl.BlockSpec(memory_space=pltpu.SMEM)
@@ -229,9 +247,12 @@
     out = jax.ShapeDtypeStruct((rows, width), BF)
     return pl.pallas_call(
         functools.partial(project_kernel, n_tp, cap, pool_dev),
-        out_shape=(out, out, out, jax.ShapeDtypeStruct((table.shape[1],), jnp.int32)),
+        out_shape=(
+            out, out, out, jax.ShapeDtypeStruct((table.shape[1],), jnp.int32),
+            jax.ShapeDtypeStruct((n_chunk, n_tp, sub, toks[0].shape[1]), BF),
+        ),
         in_specs=[smem] * 3 + [pl.BlockSpec(memory_space=pltpu.HBM)] * (5 + 2 * n_tp),
-        out_specs=(vmem, vmem, vmem, smem),
+        out_specs=(vmem, vmem, vmem, smem, pl.BlockSpec(memory_space=pltpu.HBM)),
         scratch_shapes=[
             pltpu.VMEM((n_tp,) + downs[0].shape, BF),
             pltpu.SMEM((n_dp,), jnp.int32),
@@ -240,11 +261,10 @@
         + [
             pltpu.VMEM((n_tp,) + toks[0].shape, BF),
             pltpu.SemaphoreType.DMA((5 + 2 * n_tp,)),
+            pltpu.SemaphoreType.DMA((n_tp, n_chunk)),
         ],
-        compiler_params=pltpu.CompilerParams(vmem_limit_bytes=32 << 20),
-        cost_estimate=pl.CostEstimate(
-            flops=8 * rows * w_qkv.size // 3, bytes_accessed=4 * w_qkv.size, transcendentals=0
-        ),
+        compiler_params=pltpu.CompilerParams(vmem_limit_bytes=60 << 20),
+        cost_estimate=LIGHT,
         name="project",
     )(tp, lens, table, gain, w_qkv, up, cos, sin, *toks, *downs)
 
@@ -468,10 +488,8 @@
             pltpu.VMEM((per * TILE, n_all * KCH), BF),
             pltpu.VMEM((per * TILE, lanes), F32),
         ],
-        compiler_params=pltpu.CompilerParams(vmem_limit_bytes=32 << 20),
-        cost_estimate=pl.CostEstimate(
-            flops=4 * rows * per * 1408 * lanes, bytes_accessed=raw.size * 2, transcendentals=0
-        ),
+        compiler_params=pltpu.CompilerParams(vmem_limit_bytes=60 << 20),
+        cost_estimate=LIGHT,
         name="attend",
     )(lens, counts, pos, bias, q, kn, vn, raw)
 
@@ -527,6 +545,8 @@
     slots = n_dp * cap
     dd = d_model // n_tp
     n_loc, _, rank, _ = adapter_down.shape
+    n_chunk = max(1, row_count // CHUNK)
+    sub = row_count // n_chunk
     span = 2 * rank
 
     toks = [tokens] + [shift(tokens, "tensor", n_tp, k) for k in far_first]
@@ -538,11 +558,11 @@
     gathered = lax.all_gather(payload, "dp", axis=0)
     asked = gathered[:, 2 * n_loc * span : 2 * n_loc * span + 2, : page_table.shape[1]]
     picked = pick(me, asked.astype(jnp.int32), cache_pool, n_dp, cap, lanes)
-    send = lax.optimization_barrier((picked[0], toks[1:]))[0]
+    send = lax.optimization_barrier((picked[0], toks[1:-1]))[0]
     fetched = [lax.all_to_all(send, "dp", split_axis=0, concat_axis=0, tiled=True)]
 
     own_half = lax.dynamic_slice_in_dim(w_out, (dp % 2) * (width // 2), width // 2, 0)
-    gathered, lengths_b = lax.optimization_barrier((gathered, lengths, picked))[:2]
+    gathered, lengths_b = lax.optimization_barrier((gathered, lengths, send))[:2]
     down_named, up_named = named(owner_table, adapter_ids, gathered, n_loc, span)
     downs = [down_named] + [shift(down_named, "tensor", n_tp, k) for k in far_first]
 
@@ -551,24 +571,18 @@
     frequency = 10000.0 ** (-2.0 * (index % (HD // 2)).astype(F32) / HD)
     angles = (position % VARLEN).astype(F32)[:, None] * frequency[None, :]
     sign = jnp.where(index % HD < HD // 2, -1.0, 1.0).astype(F32)
-    query, new_keys, new_values, buffer_pos = project(
+    query, new_keys, new_values, buffer_pos, all_tokens = project(
         tp_id, lengths, page_table, attn_gain.reshape(1, d_model), w_qkv, up_named,
-        jnp.cos(angles), jnp.sin(angles) * sign[None, :], toks, downs, n_dp, cap, pool_dev,
+        jnp.cos(angles), jnp.sin(angles) * sign[None, :], toks, downs, n_dp, cap, pool_dev, n_chunk,
     )
-    own_half = lax.optimization_barrier((own_half, query))[0]
+    own_half = lax.optimization_barrier((own_half, down_named))[0]
     halves = [shift(own_half, "tensor", n_tp, k) for k in far_first]
+    halves = lax.optimization_barrier((halves, query))[0]
     for a in range(1, n_group):
         send, _ = lax.optimization_barrier((picked[a], fetched[-1]))
         fetched.append(lax.all_to_all(send, "dp", split_axis=0, concat_axis=0, tiled=True))
     fetched = [f.reshape(slots, 2 * page_len, lanes) for f in fetched]
 
-    all_tokens = jnp.zeros((n_tp, row_count, d_model), BF)
-    for k, block in enumerate(toks):
-        all_tokens = lax.dynamic_update_index_in_dim(all_tokens, block, (tp - k) % n_tp, 0)
-
-    n_chunk = max(1, row_count // CHUNK)
-    sub = row_count // n_chunk
-    base = all_tokens.astype(F32).reshape(tok_total, d_model)
 
     def mixed(blocks, a):
         w_parts = w_whole.reshape(n_tp, n_group, lanes, d_model)
@@ -584,6 +598,11 @@
             q, new_keys, new_values, fetched[a],
         )
 
+    def by_chunk(mix):
+        mix = mix.reshape(n_tp, n_chunk, sub, lanes)
+        return [mix[:, c].reshape(n_tp * sub, lanes) for c in range(n_chunk)]
+
+    early = []
     w_whole = None
     for a in range(n_group - 1):
         mix = attended(a, query)
@@ -591,23 +610,25 @@
             mix, halves = lax.optimization_barrier((mix, halves))
             w_whole = whole_weight(w_out, halves, dp, n_dp)
         blocks = [mix] + [shift(mix, "tensor", n_tp, k) for k in far_first]
-        base = base + mixed(blocks, a)
-        query, base = lax.optimization_barrier((query, base))
+        query, w_whole, blocks = lax.optimization_barrier((query, w_whole, blocks))
+        early.append(blocks)
     if w_whole is None:
         w_whole = whole_weight(w_out, halves, dp, n_dp)
-    mix = attended(n_group - 1, query).reshape(n_tp, n_chunk, sub, lanes)
-    base = base.reshape(n_tp, n_chunk, sub, d_model)
-    gathered_mix = []
-    for c in range(n_chunk):
-        own = mix[:, c].reshape(n_tp * sub, lanes)
-        gathered_mix.append([own] + [shift(own, "tensor", n_tp, k) for k in far_first])
+    last = attended(n_group - 1, query)
+    early, last, w_whole = lax.optimization_barrier((early, last, w_whole))
+    early = [[by_chunk(block) for block in blocks] for blocks in early]
+    last = by_chunk(last)
+    late = [[own] + [shift(own, "tensor", n_tp, k) for k in far_first] for own in last]
     outs = []
     pieces = None
     for c in range(n_chunk):
-        blocks = gathered_mix[c]
+        residual = all_tokens[c].reshape(n_tp * sub, d_model).astype(F32)
+        for a in range(n_group - 1):
+            residual = residual + mixed([block[c] for block in early[a]], a)
+        blocks = late[c]
         if pieces is not None:
             blocks = lax.optimization_barrier((blocks, pieces))[0]
-        residual = base[:, c].reshape(n_tp * sub, d_model) + mixed(blocks, n_group - 1)
+        residual = residual + mixed(blocks, n_group - 1)
         ffn_in = normalize(residual, ffn_gain).astype(BF)
         gate_up = jnp.einsum("td,kdf->ktf", ffn_in, w_gateup, preferred_element_type=F32)
         hidden = (jax.nn.silu(gate_up[0]) * gate_up[1]).astype(BF)

time: 161 us -> 163 us (1.012)
  local copies, waits for them, and re-layouts: 17.9 us -> 9.61 us
  waiting for transfers between devices: 36.4 us -> 42.7 us
  Pallas kernels: 34.9 us -> 41 us
  matrix products: 8.76 us -> 6.3 us
    all_to_all x2, waiting for transfers between devices: 0.06 us -> 17 us  [per_device(): lax.all_to_all(send, 'dp', split_axis=0, concat_axis=0, tiled=True)]
    ppermute x24, waiting for transfers between devices: 36.3 us -> 25.6 us  [shift(): return lax.ppermute(value, axis, [(i, (i + k) % n) for i in range(n)])]
    unnamed x46 -> x54, local copies, waits for them, and re-layouts: 8.7 us -> 2.8 us
    dynamic_update_slice x4 -> x0, local copies, waits for them, and re-layouts: 4.92 us -> none  [per_device(): lax.dynamic_update_index_in_dim(all_tokens, block, (tp - k) % n_tp, 0)]
    slice x2 -> x7, local copies, waits for them, and re-layouts: 0.15 us -> 4.87 us  [the longest x5 1.8 us: by_chunk(): return [mix[:, c].reshape(n_tp * sub, lanes) for c in range(n_chunk)]]
    pallas_call x2, Pallas kernels: 24.3 us -> 27.4 us  [attend(): pl.pallas_call(functools.partial(attend_kernel, group, per), grid=(1,), o...]
    pallas_call x1, Pallas kernels: 3.77 us -> 6.56 us  [project(): pl.pallas_call(functools.partial(project_kernel, n_tp, cap, pool_dev), ou...]
    dot_general x3 -> x4, matrix products: 4.42 us -> 1.98 us  [mixed(): jnp.dot(jnp.concatenate(blocks, axis=1), w_parts[:, a].reshape(n_tp * lan...]
  transfers between devices with their start and end apart: 27 -> 27, of which waited for: 10 -> 8; matrix products, arithmetic and copies ran while one was open for 17% -> 13% of each run, Pallas kernels for 14% -> 17%
where the time goes in v3:
time: 163 us
  starting transfers between devices  43.1 us (26%)
  waiting for transfers between devices  42.7 us (26%)
  Pallas kernels  41 us (25%)
  other arithmetic  10 us (6%)
  blocking collectives  9.99 us (6%)
  local copies, waits for them, and re-layouts  9.61 us (6%)
  matrix products  6.3 us (4%)
    ppermute x24, starting transfers between devices, shift(): return lax.ppermute(value, axis, [(i, (i + k) % n) for i in range(n)])  33 us
    pallas_call x2, Pallas kernels, attend(): pl.pallas_call(functools.partial(attend_kernel, group, per), grid=(1,), o...  27.4 us
    ppermute x24, waiting for transfers between devices, shift(): return lax.ppermute(value, axis, [(i, (i + k) % n) for i in range(n)])  25.6 us
    all_to_all x2, waiting for transfers between devices, per_device(): lax.all_to_all(send, 'dp', split_axis=0, concat_axis=0, tiled=True)  17 us
    all_gather x1, blocking collectives, per_device(): gathered = lax.all_gather(payload, 'dp', axis=0)  9.99 us
    all_to_all x2, starting transfers between devices, per_device(): lax.all_to_all(send, 'dp', split_axis=0, concat_axis=0, tiled=True)  9 us
    pallas_call x1, Pallas kernels, project(): pl.pallas_call(functools.partial(project_kernel, n_tp, cap, pool_dev), ou...  6.56 us
    pallas_call x1, Pallas kernels, pick(): pl.pallas_call(functools.partial(pick_kernel, n_dp, cap), out_shape=[jax....  4.78 us
  transfers between devices with their start and end apart: 27, of which 8 were waited for; matrix products, arithmetic and copies ran while one was open for 13% of the time, Pallas kernels for 17%

profile of v3, /device:TPU:0, one launch (start us, length us, event | category | flops | bytes accessed | tf_op | source)
XLA Modules:
  0.0 163.2 jit_solution(9165527869607261888)
XLA Ops:
  0.0 4.0 %collective-permute-start.1 = (bf16[128,1024]{1,0:T(8,128)(2,1)}, bf16[128,1024]{1,0:T(8,128)(2,1)S(1)}, u32[]{:S(2)}, u32[]{:S(2)}) collective-permute-start(bf16[128,1024]{1,0:T(8,128)(2,1)} %rest_5_.1), channel_id=1, source_target_pairs={{0,2},{1,3},{2,0},{3,1},{4,6},{5,7},{6,4},{7,5},{8,10},{9,11},{10,... | collective-permute-start | bytes 786440 | tf_op jit(solution)/shard_map/ppermute | solution.py:498
  4.0 1.6 collective-permute-start
  5.6 0.7 fusion.63
  6.3 0.8 constant_dynamic-slice_fusion.1
  7.1 0.8 pad_maximum_fusion.3
  7.8 10.0 %all-gather = bf16[1152,256]{1,0:T(8,128)(2,1)S(1)} all-gather(bf16[144,256]{1,0:T(8,128)(2,1)S(1)} %pad_maximum_fusion.3), channel_id=2, replica_groups=mesh['dp'=8,'tensor'=4] {'dp'}, dimensions={0}, use_global_device_ids=true | all-gather | bytes 663552 | tf_op jit(solution)/shard_map/all_gather | solution.py:558
  17.8 0.6 slice_convert_fusion.asked_ref
  18.5 4.8 %pick_pages.1 = (bf16[8,4,128,2,128]{4,3,2,1,0:T(2,128)(2,1)}, bf16[8,4,128,2,128]{4,3,2,1,0:T(2,128)(2,1)}) custom-call(s32[1]{0:T(128)} %bitcast.4.me_ref, s32[8,2,32]{2,1,0:T(2,128)} %slice_convert_fusion.asked_ref, bf16[32,128,2,256]{3,2,1,0:T(2,128)(2,1)} %pool_ref.1), custom_call_target="tpu_custom_call" | custom-call | flops 1000 | bytes 1000 | tf_op jit(solution)/shard_map/pick_pages/pallas_call | solution.py:82
  23.3 0.7 copy-done.11
  24.0 0.7 copy-done.12
  24.7 4.5 %all-to-all-start = ((bf16[8,4,128,2,128]{4,3,2,1,0:T(2,128)(2,1)}), bf16[8,4,128,2,128]{4,3,2,1,0:T(2,128)(2,1)}, u32[]{:S(2)}, u32[]{:S(2)}) async-start(bf16[8,4,128,2,128]{4,3,2,1,0:T(2,128)(2,1)} %get-tuple-element.43), calls=%async_computation | async-start | bytes 4194304 | tf_op jit(solution)/shard_map/all_to_all | solution.py:562
  29.2 2.3 %collective-permute-start.2 = (bf16[128,1024]{1,0:T(8,128)(2,1)S(1)}, bf16[128,1024]{1,0:T(8,128)(2,1)}, u32[]{:S(2)}, u32[]{:S(2)}) collective-permute-start(bf16[128,1024]{1,0:T(8,128)(2,1)S(1)} %copy-done.10), channel_id=1, source_target_pairs={{0,3},{1,0},{2,1},{3,2},{4,7},{5,4},{6,5},{7,6},{8,11},{9,8},{10,9... | collective-permute-start | bytes 786440 | tf_op jit(solution)/shard_map/ppermute | solution.py:498
  31.5 0.6 reshape.131.rest_0_
  32.1 0.5 compare_select_fusion
  32.7 2.2 %named_adapters.1 = (bf16[128,256]{1,0:T(8,128)(2,1)}, bf16[128,256]{1,0:T(8,128)(2,1)}) custom-call(s32[16]{0:T(128)} %table_ref.2, s32[1,4]{1,0:T(1,128)} %ids_ref.1, bf16[8,144,256]{2,1,0:T(8,128)(2,1)} %bitcast.109), custom_call_target="tpu_custom_call" | custom-call | flops 1000 | bytes 1000 | tf_op jit(solution)/shard_map/named_adapters/pallas_call | solution.py:126
  35.0 0.6 collective-permute-start.8
  35.7 2.8 %collective-permute-start.7 = (bf16[128,1024]{1,0:T(8,128)(2,1)S(1)}, bf16[128,1024]{1,0:T(8,128)(2,1)S(1)}, u32[]{:S(2)}, u32[]{:S(2)}) collective-permute-start(bf16[128,1024]{1,0:T(8,128)(2,1)S(1)} %constant_dynamic-slice_fusion), channel_id=1, source_target_pairs={{0,2},{1,3},{2,0},{3,1},{4,6},{5,7},{6,4},{7,5},{8,10},{9,11},{10,... | collective-permute-start | bytes 786440 | tf_op jit(solution)/shard_map/ppermute | solution.py:498
  38.8 17.0 %all-to-all-done = bf16[8,4,128,2,128]{4,3,2,1,0:T(2,128)(2,1)} async-done(((bf16[8,4,128,2,128]{4,3,2,1,0:T(2,128)(2,1)}), bf16[8,4,128,2,128]{4,3,2,1,0:T(2,128)(2,1)}, u32[]{:S(2)}, u32[]{:S(2)}) %all-to-all-start) | async-done | bytes 2097184 | tf_op jit(solution)/shard_map/all_to_all | solution.py:562
  55.9 4.5 %all-to-all-start.1 = ((bf16[8,4,128,2,128]{4,3,2,1,0:T(2,128)(2,1)}), bf16[8,4,128,2,128]{4,3,2,1,0:T(2,128)(2,1)}, u32[]{:S(2)}, u32[]{:S(2)}) async-start(bf16[8,4,128,2,128]{4,3,2,1,0:T(2,128)(2,1)} %get-tuple-element.67), calls=%async_computation.1 | async-start | bytes 4194304 | tf_op jit(solution)/shard_map/all_to_all | solution.py:583
  60.4 0.5 collective-permute-start.4
  61.0 2.4 %collective-permute-start.3 = (bf16[128,256]{1,0:T(8,128)(2,1)S(1)}, bf16[128,256]{1,0:T(8,128)(2,1)S(1)}, u32[]{:S(2)}, u32[]{:S(2)}) collective-permute-start(bf16[128,256]{1,0:T(8,128)(2,1)S(1)} %copy-done.17), channel_id=1, source_target_pairs={{0,1},{1,2},{2,3},{3,0},{4,5},{5,6},{6,7},{7,4},{8,9},{9,10},{10,1... | collective-permute-start | bytes 196616 | tf_op jit(solution)/shard_map/ppermute | solution.py:498
  63.3 1.8 %fusion.14 = (f32[512,128]{1,0:T(8,128)}, f32[512,128]{1,0:T(8,128)}) fusion(f32[128]{0:T(128)S(1)} %copy-done.25, f32[128]{0:T(128)S(1)} %copy-done.26, f32[512]{0:T(512)S(1)} %fusion.57), kind=kLoop, calls=%fused_computation.29 | loop fusion | flops 131072 | bytes 527360 | tf_op jit(solution)/shard_map/mul | solution.py:576
  65.2 3.0 %collective-permute-done.4.rest_11_ = bf16[128,256]{1,0:T(8,128)(2,1)S(1)} collective-permute-done((bf16[128,256]{1,0:T(8,128)(2,1)S(1)}, bf16[128,256]{1,0:T(8,128)(2,1)S(1)}, u32[]{:S(2)}, u32[]{:S(2)}) %collective-permute-start.4) | collective-permute-done | bytes 65568 | tf_op jit(solution)/shard_map/ppermute | solution.py:498
  68.2 0.6 copy-done.19
  68.8 6.6 %project.1 = (bf16[512,256]{1,0:T(8,128)(2,1)}, bf16[512,256]{1,0:T(8,128)(2,1)}, bf16[512,256]{1,0:T(8,128)(2,1)}, s32[32]{0:T(128)}, bf16[2,4,64,1024]{3,2,1,0:T(8,128)(2,1)}) custom-call(s32[1]{0:T(128)} %bitcast.tp_ref, s32[1,4]{1,0:T(1,128)} %lens_ref.5, s32[1,32]{1,0:T(1,128)} %table_ref.3, bf16[1,1024]{1,0:T(2,128)(2,1)} %reshape.131.rest_0_, ...), custom_call_target="tpu_custom_call" | custom-call | flops 1000 | bytes 1000 | tf_op jit(solution)/shard_map/project/pallas_call | solution.py:248
  75.5 13.7 %attend.2 = bf16[512,128]{1,0:T(8,128)(2,1)} custom-call(s32[1,4]{1,0:T(1,128)} %lens_ref.5, s32[1,4]{1,0:T(1,128)} %counts_ref.3, s32[32]{0:T(128)} %get-tuple-element.50.pos_ref, f32[2,4]{1,0:T(2,128)} %bias_ref.3, bf16[512,256]{1,0:T(8,128)(2,1)} %get-tuple-element.65.q_ref, bf16[512,256]{1,0:T(8,128)(2,1)} %get-tuple-element.51.kn_ref, ...), custom_call_target="tpu_custom_call" | custom-call | flops 1000 | bytes 1000 | tf_op jit(solution)/shard_map/attend/pallas_call | solution.py:472
  89.2 1.0 pad_maximum_fusion.1
  90.2 1.1 collective-permute-start.9
  91.3 1.4 fusion.73
  92.7 0.5 collective-permute-start.12
  93.2 0.7 collective-permute-start.11
  93.8 1.9 %collective-permute-start.10 = (bf16[512,128]{1,0:T(8,128)(2,1)S(1)}, bf16[512,128]{1,0:T(8,128)(2,1)}, u32[]{:S(2)}, u32[]{:S(2)}) collective-permute-start(bf16[512,128]{1,0:T(8,128)(2,1)S(1)} %copy-done.9), channel_id=1, source_target_pairs={{0,1},{1,2},{2,3},{3,0},{4,5},{5,6},{6,7},{7,4},{8,9},{9,10},{10,1... | collective-permute-start | bytes 393224 | tf_op jit(solution)/shard_map/ppermute | solution.py:498
  95.8 1.8 %maximum_select_fusion = bf16[3,256,1024]{2,1,0:T(8,128)(2,1)S(1)} fusion(bf16[3,128,1024]{2,1,0:T(8,128)(2,1)} %collective-permute-done.9, bf16[1,128,1024]{2,1,0:T(8,128)(2,1)S(1)} %bitcast.118, bf16[1,128,1024]{2,1,0:T(8,128)(2,1)S(1)} %bitcast.120, bf16[1,128,1024]{2,1,0:T(8,128)(2,1)S(1)} %bitcast.122, pred[]{:T(512)S(6)} %eq.35), kind=kLoop, calls=%fused_computation.7 | loop fusion | flops 13369344 | bytes 3145729 | tf_op jit(solution)/shard_map/jit(_where)/select_n | solution.py:504
  97.6 1.5 pad_maximum_fusion
  99.3 6.6 %collective-permute-done.11 = bf16[512,128]{1,0:T(8,128)(2,1)S(1)} collective-permute-done((bf16[512,128]{1,0:T(8,128)(2,1)S(1)}, bf16[512,128]{1,0:T(8,128)(2,1)S(1)}, u32[]{:S(2)}, u32[]{:S(2)}) %collective-permute-start.11) | collective-permute-done | bytes 131104 | tf_op jit(solution)/shard_map/ppermute | solution.py:498
  105.9 0.7 copy-done.15
  106.6 13.8 %attend.3 = bf16[512,128]{1,0:T(8,128)(2,1)} custom-call(s32[1,4]{1,0:T(1,128)} %lens_ref.5, s32[1,4]{1,0:T(1,128)} %counts_ref.3, s32[32]{0:T(128)} %get-tuple-element.50.pos_ref, f32[2,4]{1,0:T(2,128)} %bias_ref.3, bf16[512,256]{1,0:T(8,128)(2,1)} %get-tuple-element.65.q_ref, bf16[512,256]{1,0:T(8,128)(2,1)} %get-tuple-element.51.kn_ref, ...), custom_call_target="tpu_custom_call" | custom-call | flops 1000 | bytes 1000 | tf_op jit(solution)/shard_map/attend/pallas_call | solution.py:472
  120.4 0.9 fusion.74
  121.2 0.3 collective-permute-start.21
  121.5 1.3 collective-permute-start.20
  122.9 2.8 %collective-permute-start.15 = (bf16[256,128]{1,0:T(8,128)(2,1)S(1)}, bf16[256,128]{1,0:T(8,128)(2,1)S(1)}, u32[]{:S(2)}, u32[]{:S(2)}) collective-permute-start(bf16[256,128]{1,0:T(8,128)(2,1)S(1)} %bitcast.129), channel_id=1, source_target_pairs={{0,3},{1,0},{2,1},{3,2},{4,7},{5,4},{6,5},{7,6},{8,11},{9,8},{10,9... | collective-permute-start | bytes 196616 | tf_op jit(solution)/shard_map/ppermute | solution.py:498
  125.7 0.6 collective-permute-start.14
  126.5 0.9 fusion.76
  127.5 1.7 %fusion.72 = (bf16[4,1,128,1024]{3,2,1,0:T(8,128)(2,1)S(1)}, bf16[4,1,128,1024]{3,2,1,0:T(8,128)(2,1)S(1)}) fusion(bf16[4,2,128,1024]{3,2,1,0:T(8,128)(2,1)} %bitcast.105), kind=kLoop, calls=%fused_computation.120 | loop fusion | bytes 4194304 | tf_op jit(solution)/shard_map/slice | solution.py:591
  129.2 0.4 fusion.30
  129.6 0.4 fusion.15
  130.1 2.7 %collective-permute-start.19 = (bf16[256,128]{1,0:T(8,128)(2,1)S(1)}, bf16[256,128]{1,0:T(8,128)(2,1)S(1)}, u32[]{:S(2)}, u32[]{:S(2)}) collective-permute-start(bf16[256,128]{1,0:T(8,128)(2,1)S(1)} %bitcast.127), channel_id=1, source_target_pairs={{0,1},{1,2},{2,3},{3,0},{4,5},{5,6},{6,7},{7,4},{8,9},{9,10},{10,1... | collective-permute-start | bytes 196616 | tf_op jit(solution)/shard_map/ppermute | solution.py:498
  132.9 1.4 collective-permute-done.14
  134.2 0.5 multiply_reduce_fusion.1
  134.8 1.3 convolution_bitcast_fusion.1
  136.1 0.2 fusion.71
  136.4 0.8 fusion.79
  137.2 1.2 collective-permute-start.18
  138.4 0.6 collective-permute-start.17
  139.0 1.9 %collective-permute-start.16 = (bf16[64,1024]{1,0:T(8,128)(2,1)S(1)}, bf16[64,1024]{1,0:T(8,128)(2,1)S(1)}, u32[]{:S(2)}, u32[]{:S(2)}) collective-permute-start(bf16[64,1024]{1,0:T(8,128)(2,1)S(1)} %get-tuple-element.94), channel_id=1, source_target_pairs={{0,1},{1,2},{2,3},{3,0},{4,5},{5,6},{6,7},{7,4},{8,9},{9,10},{10,1... | collective-permute-start | bytes 393224 | tf_op jit(solution)/shard_map/ppermute | solution.py:498
  141.0 0.5 multiply_reduce_fusion
  141.5 1.4 convolution_bitcast_fusion
  143.1 0.8 fusion.80
  144.0 1.0 collective-permute-start.22
  145.0 2.9 %collective-permute-start.24 = (bf16[64,1024]{1,0:T(8,128)(2,1)S(1)}, bf16[64,1024]{1,0:T(8,128)(2,1)S(1)}, u32[]{:S(2)}, u32[]{:S(2)}) collective-permute-start(bf16[64,1024]{1,0:T(8,128)(2,1)S(1)} %get-tuple-element.90), channel_id=1, source_target_pairs={{0,3},{1,0},{2,1},{3,2},{4,7},{5,4},{6,5},{7,6},{8,11},{9,8},{10,9... | collective-permute-start | bytes 393224 | tf_op jit(solution)/shard_map/ppermute | solution.py:498
  147.9 6.8 %collective-permute-done.17 = bf16[64,1024]{1,0:T(8,128)(2,1)S(1)} collective-permute-done((bf16[64,1024]{1,0:T(8,128)(2,1)S(1)}, bf16[64,1024]{1,0:T(8,128)(2,1)S(1)}, u32[]{:S(2)}, u32[]{:S(2)}) %collective-permute-start.17) | collective-permute-done | bytes 131104 | tf_op jit(solution)/shard_map/ppermute | solution.py:498
  154.8 1.4 collective-permute-done.24
  156.2 6.2 %collective-permute-done.23 = bf16[64,1024]{1,0:T(8,128)(2,1)S(1)} collective-permute-done((bf16[64,1024]{1,0:T(8,128)(2,1)S(1)}, bf16[64,1024]{1,0:T(8,128)(2,1)S(1)}, u32[]{:S(2)}, u32[]{:S(2)}) %collective-permute-start.23) | collective-permute-done | bytes 131104 | tf_op jit(solution)/shard_map/ppermute | solution.py:498
  162.5 0.7 pad_maximum_fusion.2
  (92 shorter events, 1.6 us)
Async XLA Ops:
  0.0 136.4 %copy-start = (bf16[1024,1024]{1,0:T(8,128)(2,1)S(1)}, bf16[1024,1024]{1,0:T(8,128)(2,1)}, u32[]{:S(2)}) copy-start(bf16[1024,1024]{1,0:T(8,128)(2,1)} %param.22) | copy-start | bytes 6291460
  0.0 23.3 %collective-permute-start.1 = (bf16[128,1024]{1,0:T(8,128)(2,1)}, bf16[128,1024]{1,0:T(8,128)(2,1)S(1)}, u32[]{:S(2)}, u32[]{:S(2)}) collective-permute-start(bf16[128,1024]{1,0:T(8,128)(2,1)} %rest_5_.1), channel_id=1, source_target_pairs={{0,2},{1,3},{2,0},{3,1},{4,6},{5,7},{6,4},{7,5},{8,10},{9,11},{10,... | collective-permute-start | bytes 786440 | tf_op jit(solution)/shard_map/ppermute | solution.py:498
  4.0 19.2 %collective-permute-start = (bf16[128,1024]{1,0:T(8,128)(2,1)}, bf16[128,1024]{1,0:T(8,128)(2,1)S(1)}, u32[]{:S(2)}, u32[]{:S(2)}) collective-permute-start(bf16[128,1024]{1,0:T(8,128)(2,1)} %rest_5_.1), channel_id=1, source_target_pairs={{0,1},{1,2},{2,3},{3,0},{4,5},{5,6},{6,7},{7,4},{8,9},{9,10},{10,1... | collective-permute-start | bytes 786440 | tf_op jit(solution)/shard_map/ppermute | solution.py:498
  17.8 5.4 %copy-start.2 = (bf16[1152,256]{1,0:T(8,128)(2,1)}, bf16[1152,256]{1,0:T(8,128)(2,1)S(1)}, u32[]{:S(2)}) copy-start(bf16[1152,256]{1,0:T(8,128)(2,1)S(1)} %all-gather) | copy-start | bytes 1769476
  23.3 0.7 copy-start.11
  24.0 0.7 copy-start.12
  24.7 4.5 %copy-start.10 = (bf16[128,1024]{1,0:T(8,128)(2,1)S(1)}, bf16[128,1024]{1,0:T(8,128)(2,1)}, u32[]{:S(2)}) copy-start(bf16[128,1024]{1,0:T(8,128)(2,1)} %rest_5_.1) | copy-start | bytes 786436
  24.7 6.8 %copy-start.23 = (bf16[1024]{0:T(1024)(128)(2,1)S(1)}, bf16[1024]{0:T(1024)(128)(2,1)}, u32[]{:S(2)}) copy-start(bf16[1024]{0:T(1024)(128)(2,1)} %param.17) | copy-start | bytes 6148
  24.7 7.9 %copy-start.3 = (bf16[256,1024]{1,0:T(8,128)(2,1)S(1)}, bf16[256,1024]{1,0:T(8,128)(2,1)}, u32[]{:S(2)}) copy-start(bf16[256,1024]{1,0:T(8,128)(2,1)} %param.20) | copy-start | bytes 1572868
  24.7 13.8 %copy-start.22 = (s32[1,4]{1,0:T(1,128)S(1)}, s32[1,4]{1,0:T(1,128)}, u32[]{:S(2)}) copy-start(s32[1,4]{1,0:T(1,128)} %lens_ref.5) | copy-start | bytes 52
  24.7 14.0 %copy-start.21 = (s32[1,4]{1,0:T(1,128)S(1)}, s32[1,4]{1,0:T(1,128)}, u32[]{:S(2)}) copy-start(s32[1,4]{1,0:T(1,128)} %counts_ref.3) | copy-start | bytes 52
  24.7 31.1 %all-to-all-start = ((bf16[8,4,128,2,128]{4,3,2,1,0:T(2,128)(2,1)}), bf16[8,4,128,2,128]{4,3,2,1,0:T(2,128)(2,1)}, u32[]{:S(2)}, u32[]{:S(2)}) async-start(bf16[8,4,128,2,128]{4,3,2,1,0:T(2,128)(2,1)} %get-tuple-element.43), calls=%async_computation | async-start | bytes 4194304 | tf_op jit(solution)/shard_map/all_to_all | solution.py:562
  29.2 31.2 %collective-permute-start.2 = (bf16[128,1024]{1,0:T(8,128)(2,1)S(1)}, bf16[128,1024]{1,0:T(8,128)(2,1)}, u32[]{:S(2)}, u32[]{:S(2)}) collective-permute-start(bf16[128,1024]{1,0:T(8,128)(2,1)S(1)} %copy-done.10), channel_id=1, source_target_pairs={{0,3},{1,0},{2,1},{3,2},{4,7},{5,4},{6,5},{7,6},{8,11},{9,8},{10,9... | collective-permute-start | bytes 786440 | tf_op jit(solution)/shard_map/ppermute | solution.py:498
  34.9 26.0 %collective-permute-start.5 = (bf16[128,256]{1,0:T(8,128)(2,1)}, bf16[128,256]{1,0:T(8,128)(2,1)S(1)}, u32[]{:S(2)}, u32[]{:S(2)}) collective-permute-start(bf16[128,256]{1,0:T(8,128)(2,1)} %get-tuple-element.47.rest_9_), channel_id=1, source_target_pairs={{0,3},{1,0},{2,1},{3,2},{4,7},{5,4},{6,5},{7,6},{8,11},{9,8},{10,9... | collective-permute-start | bytes 196616 | tf_op jit(solution)/shard_map/ppermute | solution.py:498
  35.0 40.4 %collective-permute-start.8 = (bf16[128,1024]{1,0:T(8,128)(2,1)S(1)}, bf16[128,1024]{1,0:T(8,128)(2,1)S(1)}, u32[]{:S(2)}, u32[]{:S(2)}) collective-permute-start(bf16[128,1024]{1,0:T(8,128)(2,1)S(1)} %constant_dynamic-slice_fusion), channel_id=1, source_target_pairs={{0,3},{1,0},{2,1},{3,2},{4,7},{5,4},{6,5},{7,6},{8,11},{9,8},{10,9... | collective-permute-start | bytes 786440 | tf_op jit(solution)/shard_map/ppermute | solution.py:498
  35.7 39.8 %collective-permute-start.7 = (bf16[128,1024]{1,0:T(8,128)(2,1)S(1)}, bf16[128,1024]{1,0:T(8,128)(2,1)S(1)}, u32[]{:S(2)}, u32[]{:S(2)}) collective-permute-start(bf16[128,1024]{1,0:T(8,128)(2,1)S(1)} %constant_dynamic-slice_fusion), channel_id=1, source_target_pairs={{0,2},{1,3},{2,0},{3,1},{4,6},{5,7},{6,4},{7,5},{8,10},{9,11},{10,... | collective-permute-start | bytes 786440 | tf_op jit(solution)/shard_map/ppermute | solution.py:498
  38.5 37.0 %collective-permute-start.6 = (bf16[128,1024]{1,0:T(8,128)(2,1)S(1)}, bf16[128,1024]{1,0:T(8,128)(2,1)S(1)}, u32[]{:S(2)}, u32[]{:S(2)}) collective-permute-start(bf16[128,1024]{1,0:T(8,128)(2,1)S(1)} %constant_dynamic-slice_fusion), channel_id=1, source_target_pairs={{0,1},{1,2},{2,3},{3,0},{4,5},{5,6},{6,7},{7,4},{8,9},{9,10},{10,1... | collective-permute-start | bytes 786440 | tf_op jit(solution)/shard_map/ppermute | solution.py:498
  55.9 4.6 %copy-start.17 = (bf16[128,256]{1,0:T(8,128)(2,1)S(1)}, bf16[128,256]{1,0:T(8,128)(2,1)}, u32[]{:S(2)}) copy-start(bf16[128,256]{1,0:T(8,128)(2,1)} %get-tuple-element.47.rest_9_) | copy-start | bytes 196612
  55.9 7.5 %copy-start.25 = (f32[128]{0:T(128)S(1)}, f32[128]{0:T(128)}, u32[]{:S(2)}) copy-start(f32[128]{0:T(128)} %get-tuple-element.117) | copy-start | bytes 1540
  55.9 7.5 %copy-start.26 = (f32[128]{0:T(128)S(1)}, f32[128]{0:T(128)}, u32[]{:S(2)}) copy-start(f32[128]{0:T(128)} %get-tuple-element.118) | copy-start | bytes 1540
  55.9 50.7 %all-to-all-start.1 = ((bf16[8,4,128,2,128]{4,3,2,1,0:T(2,128)(2,1)}), bf16[8,4,128,2,128]{4,3,2,1,0:T(2,128)(2,1)}, u32[]{:S(2)}, u32[]{:S(2)}) async-start(bf16[8,4,128,2,128]{4,3,2,1,0:T(2,128)(2,1)} %get-tuple-element.67), calls=%async_computation.1 | async-start | bytes 4194304 | tf_op jit(solution)/shard_map/all_to_all | solution.py:583
  60.4 7.8 %collective-permute-start.4 = (bf16[128,256]{1,0:T(8,128)(2,1)S(1)}, bf16[128,256]{1,0:T(8,128)(2,1)S(1)}, u32[]{:S(2)}, u32[]{:S(2)}) collective-permute-start(bf16[128,256]{1,0:T(8,128)(2,1)S(1)} %copy-done.17), channel_id=1, source_target_pairs={{0,2},{1,3},{2,0},{3,1},{4,6},{5,7},{6,4},{7,5},{8,10},{9,11},{10,... | collective-permute-start | bytes 196616 | tf_op jit(solution)/shard_map/ppermute | solution.py:498
  61.0 7.2 %copy-start.18 = (bf16[128,256]{1,0:T(8,128)(2,1)}, bf16[128,256]{1,0:T(8,128)(2,1)S(1)}, u32[]{:S(2)}) copy-start(bf16[128,256]{1,0:T(8,128)(2,1)S(1)} %collective-permute-done.5.rest_12_) | copy-start | bytes 196612
  61.0 7.2 %collective-permute-start.3 = (bf16[128,256]{1,0:T(8,128)(2,1)S(1)}, bf16[128,256]{1,0:T(8,128)(2,1)S(1)}, u32[]{:S(2)}, u32[]{:S(2)}) collective-permute-start(bf16[128,256]{1,0:T(8,128)(2,1)S(1)} %copy-done.17), channel_id=1, source_target_pairs={{0,1},{1,2},{2,3},{3,0},{4,5},{5,6},{6,7},{7,4},{8,9},{9,10},{10,1... | collective-permute-start | bytes 196616 | tf_op jit(solution)/shard_map/ppermute | solution.py:498
  68.2 0.6 copy-start.19
  68.2 0.6 copy-start.20
  75.4 14.7 %copy-start.5 = (bf16[128,1024]{1,0:T(8,128)(2,1)}, bf16[128,1024]{1,0:T(8,128)(2,1)S(1)}, u32[]{:S(2)}) copy-start(bf16[128,1024]{1,0:T(8,128)(2,1)S(1)} %collective-permute-done.7) | copy-start | bytes 786436
  75.5 14.7 %copy-start.7 = (bf16[128,1024]{1,0:T(8,128)(2,1)}, bf16[128,1024]{1,0:T(8,128)(2,1)S(1)}, u32[]{:S(2)}) copy-start(bf16[128,1024]{1,0:T(8,128)(2,1)S(1)} %collective-permute-done.6) | copy-start | bytes 786436
  75.5 15.8 %copy-start.24 = (bf16[1024]{0:T(1024)(128)(2,1)S(1)}, bf16[1024]{0:T(1024)(128)(2,1)}, u32[]{:S(2)}) copy-start(bf16[1024]{0:T(1024)(128)(2,1)} %param.18) | copy-start | bytes 6148
  89.2 3.5 %copy-start.9 = (bf16[512,128]{1,0:T(8,128)(2,1)S(1)}, bf16[512,128]{1,0:T(8,128)(2,1)}, u32[]{:S(2)}) copy-start(bf16[512,128]{1,0:T(8,128)(2,1)} %attend.2) | copy-start | bytes 393220
  90.2 5.6 %collective-permute-start.9 = (bf16[3,128,1024]{2,1,0:T(8,128)(2,1)}, bf16[3,128,1024]{2,1,0:T(8,128)(2,1)}, u32[]{:S(2)}, u32[]{:S(2)}) collective-permute-start(bf16[3,128,1024]{2,1,0:T(8,128)(2,1)} %pad_maximum_fusion.1), channel_id=1, source_target_pairs={{0,4},{4,0},{8,12},{12,8},{16,20},{20,16},{24,28},{28,24},{1,5},{5... | collective-permute-start | bytes 2359304 | tf_op jit(solution)/shard_map/ppermute | solution.py:503
  91.3 4.5 %copy-start.6 = (bf16[128,1024]{1,0:T(8,128)(2,1)S(1)}, bf16[128,1024]{1,0:T(8,128)(2,1)}, u32[]{:S(2)}) copy-start(bf16[128,1024]{1,0:T(8,128)(2,1)} %copy-done.5) | copy-start | bytes 786436
  91.3 4.5 %copy-start.8 = (bf16[128,1024]{1,0:T(8,128)(2,1)S(1)}, bf16[128,1024]{1,0:T(8,128)(2,1)}, u32[]{:S(2)}) copy-start(bf16[128,1024]{1,0:T(8,128)(2,1)} %copy-done.7) | copy-start | bytes 786436
  92.7 4.9 %copy-start.4 = (bf16[256,1024]{1,0:T(8,128)(2,1)S(1)}, bf16[256,1024]{1,0:T(8,128)(2,1)}, u32[]{:S(2)}) copy-start(bf16[256,1024]{1,0:T(8,128)(2,1)} %param.20) | copy-start | bytes 1572868
  92.7 6.6 %collective-permute-start.12 = (bf16[512,128]{1,0:T(8,128)(2,1)S(1)}, bf16[512,128]{1,0:T(8,128)(2,1)S(1)}, u32[]{:S(2)}, u32[]{:S(2)}) collective-permute-start(bf16[512,128]{1,0:T(8,128)(2,1)S(1)} %copy-done.9), channel_id=1, source_target_pairs={{0,3},{1,0},{2,1},{3,2},{4,7},{5,4},{6,5},{7,6},{8,11},{9,8},{10,9... | collective-permute-start | bytes 393224 | tf_op jit(solution)/shard_map/ppermute | solution.py:498
  93.2 12.8 %collective-permute-start.11 = (bf16[512,128]{1,0:T(8,128)(2,1)S(1)}, bf16[512,128]{1,0:T(8,128)(2,1)S(1)}, u32[]{:S(2)}, u32[]{:S(2)}) collective-permute-start(bf16[512,128]{1,0:T(8,128)(2,1)S(1)} %copy-done.9), channel_id=1, source_target_pairs={{0,2},{1,3},{2,0},{3,1},{4,6},{5,7},{6,4},{7,5},{8,10},{9,11},{10,... | collective-permute-start | bytes 393224 | tf_op jit(solution)/shard_map/ppermute | solution.py:498
  93.8 12.8 %collective-permute-start.10 = (bf16[512,128]{1,0:T(8,128)(2,1)S(1)}, bf16[512,128]{1,0:T(8,128)(2,1)}, u32[]{:S(2)}, u32[]{:S(2)}) collective-permute-start(bf16[512,128]{1,0:T(8,128)(2,1)S(1)} %copy-done.9), channel_id=1, source_target_pairs={{0,1},{1,2},{2,3},{3,0},{4,5},{5,6},{6,7},{7,4},{8,9},{9,10},{10,1... | collective-permute-start | bytes 393224 | tf_op jit(solution)/shard_map/ppermute | solution.py:498
  99.3 6.6 %copy-start.13 = (bf16[512,128]{1,0:T(8,128)(2,1)}, bf16[512,128]{1,0:T(8,128)(2,1)S(1)}, u32[]{:S(2)}) copy-start(bf16[512,128]{1,0:T(8,128)(2,1)S(1)} %collective-permute-done.12) | copy-start | bytes 393220
  105.9 0.7 copy-start.15
  106.6 20.8 %copy-start.16 = (bf16[512,128]{1,0:T(8,128)(2,1)S(1)}, bf16[512,128]{1,0:T(8,128)(2,1)}, u32[]{:S(2)}) copy-start(bf16[512,128]{1,0:T(8,128)(2,1)} %copy-done.15) | copy-start | bytes 393220
  106.6 20.8 %copy-start.14 = (bf16[512,128]{1,0:T(8,128)(2,1)S(1)}, bf16[512,128]{1,0:T(8,128)(2,1)}, u32[]{:S(2)}) copy-start(bf16[512,128]{1,0:T(8,128)(2,1)} %copy-done.13) | copy-start | bytes 393220
  121.2 17.8 %collective-permute-start.21 = (bf16[256,128]{1,0:T(8,128)(2,1)S(1)}, bf16[256,128]{1,0:T(8,128)(2,1)S(1)}, u32[]{:S(2)}, u32[]{:S(2)}) collective-permute-start(bf16[256,128]{1,0:T(8,128)(2,1)S(1)} %bitcast.125), channel_id=1, source_target_pairs={{0,3},{1,0},{2,1},{3,2},{4,7},{5,4},{6,5},{7,6},{8,11},{9,8},{10,9... | collective-permute-start | bytes 196616 | tf_op jit(solution)/shard_map/ppermute | solution.py:498
  121.5 19.4 %collective-permute-start.20 = (bf16[256,128]{1,0:T(8,128)(2,1)S(1)}, bf16[256,128]{1,0:T(8,128)(2,1)S(1)}, u32[]{:S(2)}, u32[]{:S(2)}) collective-permute-start(bf16[256,128]{1,0:T(8,128)(2,1)S(1)} %bitcast.126), channel_id=1, source_target_pairs={{0,2},{1,3},{2,0},{3,1},{4,6},{5,7},{6,4},{7,5},{8,10},{9,11},{10,... | collective-permute-start | bytes 196616 | tf_op jit(solution)/shard_map/ppermute | solution.py:498
  122.9 7.2 %collective-permute-start.15 = (bf16[256,128]{1,0:T(8,128)(2,1)S(1)}, bf16[256,128]{1,0:T(8,128)(2,1)S(1)}, u32[]{:S(2)}, u32[]{:S(2)}) collective-permute-start(bf16[256,128]{1,0:T(8,128)(2,1)S(1)} %bitcast.129), channel_id=1, source_target_pairs={{0,3},{1,0},{2,1},{3,2},{4,7},{5,4},{6,5},{7,6},{8,11},{9,8},{10,9... | collective-permute-start | bytes 196616 | tf_op jit(solution)/shard_map/ppermute | solution.py:498
  125.7 8.5 %collective-permute-start.14 = (bf16[256,128]{1,0:T(8,128)(2,1)S(1)}, bf16[256,128]{1,0:T(8,128)(2,1)S(1)}, u32[]{:S(2)}, u32[]{:S(2)}) collective-permute-start(bf16[256,128]{1,0:T(8,128)(2,1)S(1)} %bitcast.130), channel_id=1, source_target_pairs={{0,2},{1,3},{2,0},{3,1},{4,6},{5,7},{6,4},{7,5},{8,10},{9,11},{10,... | collective-permute-start | bytes 196616 | tf_op jit(solution)/shard_map/ppermute | solution.py:498
  126.3 8.0 %collective-permute-start.13 = (bf16[256,128]{1,0:T(8,128)(2,1)S(1)}, bf16[256,128]{1,0:T(8,128)(2,1)S(1)}, u32[]{:S(2)}, u32[]{:S(2)}) collective-permute-start(bf16[256,128]{1,0:T(8,128)(2,1)S(1)} %bitcast.131), channel_id=1, source_target_pairs={{0,1},{1,2},{2,3},{3,0},{4,5},{5,6},{6,7},{7,4},{8,9},{9,10},{10,1... | collective-permute-start | bytes 196616 | tf_op jit(solution)/shard_map/ppermute | solution.py:498
  129.6 5.2 %copy-start.1 = (bf16[2,1024,1024]{2,1,0:T(8,128)(2,1)S(1)}, bf16[2,1024,1024]{2,1,0:T(8,128)(2,1)}, u32[]{:S(2)}) copy-start(bf16[2,1024,1024]{2,1,0:T(8,128)(2,1)} %param.21) | copy-start | bytes 12582916
  130.1 10.9 %collective-permute-start.19 = (bf16[256,128]{1,0:T(8,128)(2,1)S(1)}, bf16[256,128]{1,0:T(8,128)(2,1)S(1)}, u32[]{:S(2)}, u32[]{:S(2)}) collective-permute-start(bf16[256,128]{1,0:T(8,128)(2,1)S(1)} %bitcast.127), channel_id=1, source_target_pairs={{0,1},{1,2},{2,3},{3,0},{4,5},{5,6},{6,7},{7,4},{8,9},{9,10},{10,1... | collective-permute-start | bytes 196616 | tf_op jit(solution)/shard_map/ppermute | solution.py:498
  137.2 10.6 %collective-permute-start.18 = (bf16[64,1024]{1,0:T(8,128)(2,1)S(1)}, bf16[64,1024]{1,0:T(8,128)(2,1)S(1)}, u32[]{:S(2)}, u32[]{:S(2)}) collective-permute-start(bf16[64,1024]{1,0:T(8,128)(2,1)S(1)} %get-tuple-element.92), channel_id=1, source_target_pairs={{0,3},{1,0},{2,1},{3,2},{4,7},{5,4},{6,5},{7,6},{8,11},{9,8},{10,9... | collective-permute-start | bytes 393224 | tf_op jit(solution)/shard_map/ppermute | solution.py:498
  138.4 16.2 %collective-permute-start.17 = (bf16[64,1024]{1,0:T(8,128)(2,1)S(1)}, bf16[64,1024]{1,0:T(8,128)(2,1)S(1)}, u32[]{:S(2)}, u32[]{:S(2)}) collective-permute-start(bf16[64,1024]{1,0:T(8,128)(2,1)S(1)} %get-tuple-element.93), channel_id=1, source_target_pairs={{0,2},{1,3},{2,0},{3,1},{4,6},{5,7},{6,4},{7,5},{8,10},{9,11},{10,... | collective-permute-start | bytes 393224 | tf_op jit(solution)/shard_map/ppermute | solution.py:498
  139.0 15.7 %collective-permute-start.16 = (bf16[64,1024]{1,0:T(8,128)(2,1)S(1)}, bf16[64,1024]{1,0:T(8,128)(2,1)S(1)}, u32[]{:S(2)}, u32[]{:S(2)}) collective-permute-start(bf16[64,1024]{1,0:T(8,128)(2,1)S(1)} %get-tuple-element.94), channel_id=1, source_target_pairs={{0,1},{1,2},{2,3},{3,0},{4,5},{5,6},{6,7},{7,4},{8,9},{9,10},{10,1... | collective-permute-start | bytes 393224 | tf_op jit(solution)/shard_map/ppermute | solution.py:498
  144.0 10.8 %collective-permute-start.22 = (bf16[64,1024]{1,0:T(8,128)(2,1)S(1)}, bf16[64,1024]{1,0:T(8,128)(2,1)S(1)}, u32[]{:S(2)}, u32[]{:S(2)}) collective-permute-start(bf16[64,1024]{1,0:T(8,128)(2,1)S(1)} %get-tuple-element.89), channel_id=1, source_target_pairs={{0,1},{1,2},{2,3},{3,0},{4,5},{5,6},{6,7},{7,4},{8,9},{9,10},{10,1... | collective-permute-start | bytes 393224 | tf_op jit(solution)/shard_map/ppermute | solution.py:498
  145.0 11.2 %collective-permute-start.24 = (bf16[64,1024]{1,0:T(8,128)(2,1)S(1)}, bf16[64,1024]{1,0:T(8,128)(2,1)S(1)}, u32[]{:S(2)}, u32[]{:S(2)}) collective-permute-start(bf16[64,1024]{1,0:T(8,128)(2,1)S(1)} %get-tuple-element.90), channel_id=1, source_target_pairs={{0,3},{1,0},{2,1},{3,2},{4,7},{5,4},{6,5},{7,6},{8,11},{9,8},{10,9... | collective-permute-start | bytes 393224 | tf_op jit(solution)/shard_map/ppermute | solution.py:498
  147.9 14.5 %collective-permute-start.23 = (bf16[64,1024]{1,0:T(8,128)(2,1)S(1)}, bf16[64,1024]{1,0:T(8,128)(2,1)S(1)}, u32[]{:S(2)}, u32[]{:S(2)}) collective-permute-start(bf16[64,1024]{1,0:T(8,128)(2,1)S(1)} %get-tuple-element.91), channel_id=1, source_target_pairs={{0,2},{1,3},{2,0},{3,1},{4,6},{5,7},{6,4},{7,5},{8,10},{9,11},{10,... | collective-permute-start | bytes 393224 | tf_op jit(solution)/shard_map/ppermute | solution.py:498

commit v4 on v3

--- a/solution.py
+++ b/solution.py
@@ -577,9 +577,8 @@
     )
     own_half = lax.optimization_barrier((own_half, down_named))[0]
     halves = [shift(own_half, "tensor", n_tp, k) for k in far_first]
-    halves = lax.optimization_barrier((halves, query))[0]
     for a in range(1, n_group):
-        send, _ = lax.optimization_barrier((picked[a], fetched[-1]))
+        send = lax.optimization_barrier((picked[a], fetched[-1], query, halves[:-1]))[0]
         fetched.append(lax.all_to_all(send, "dp", split_axis=0, concat_axis=0, tiled=True))
     fetched = [f.reshape(slots, 2 * page_len, lanes) for f in fetched]
 
@@ -618,17 +617,24 @@
     early, last, w_whole = lax.optimization_barrier((early, last, w_whole))
     early = [[by_chunk(block) for block in blocks] for blocks in early]
     last = by_chunk(last)
-    late = [[own] + [shift(own, "tensor", n_tp, k) for k in far_first] for own in last]
     outs = []
     pieces = None
+    bases = []
+    late = []
     for c in range(n_chunk):
-        residual = all_tokens[c].reshape(n_tp * sub, d_model).astype(F32)
+        own = last[c]
+        if bases:
+            own = lax.optimization_barrier((own, bases[-1]))[0]
+        late.append([own] + [shift(own, "tensor", n_tp, k) for k in far_first])
+        base = all_tokens[c].reshape(n_tp * sub, d_model).astype(F32)
         for a in range(n_group - 1):
-            residual = residual + mixed([block[c] for block in early[a]], a)
+            base = base + mixed([block[c] for block in early[a]], a)
+        bases.append(base)
+    for c in range(n_chunk):
         blocks = late[c]
         if pieces is not None:
             blocks = lax.optimization_barrier((blocks, pieces))[0]
-        residual = residual + mixed(blocks, n_group - 1)
+        residual = bases[c] + mixed(blocks, n_group - 1)
         ffn_in = normalize(residual, ffn_gain).astype(BF)
         gate_up = jnp.einsum("td,kdf->ktf", ffn_in, w_gateup, preferred_element_type=F32)
         hidden = (jax.nn.silu(gate_up[0]) * gate_up[1]).astype(BF)

time: 163 us -> 162 us (level)
  waiting for transfers between devices: 42.7 us -> 30.7 us
  starting transfers between devices: 43.1 us -> 52.7 us
    all_to_all x2, waiting for transfers between devices: 17 us -> 0.01 us  [per_device(): lax.all_to_all(send, 'dp', split_axis=0, concat_axis=0, tiled=True)]
    ppermute x24, starting transfers between devices: 33 us -> 42.8 us  [shift(): return lax.ppermute(value, axis, [(i, (i + k) % n) for i in range(n)])]
    ppermute x24, waiting for transfers between devices: 25.6 us -> 30.7 us  [shift(): return lax.ppermute(value, axis, [(i, (i + k) % n) for i in range(n)])]
    unnamed x54 -> x48, local copies, waits for them, and re-layouts: 2.8 us -> 3.41 us
  transfers between devices with their start and end apart: 27 -> 27, of which waited for: 8 -> 4; matrix products, arithmetic and copies ran while one was open for 13% -> 13% of each run, Pallas kernels for 17% -> 17%
where the time goes in v4:
time: 162 us
  starting transfers between devices  52.7 us (33%)
  Pallas kernels  42.3 us (26%)
  waiting for transfers between devices  30.7 us (19%)
  local copies, waits for them, and re-layouts  10.1 us (6%)
  blocking collectives  9.99 us (6%)
  other arithmetic  9.53 us (6%)
  matrix products  6.32 us (4%)
    ppermute x24, starting transfers between devices, shift(): return lax.ppermute(value, axis, [(i, (i + k) % n) for i in range(n)])  42.8 us
    ppermute x24, waiting for transfers between devices, shift(): return lax.ppermute(value, axis, [(i, (i + k) % n) for i in range(n)])  30.7 us
    pallas_call x2, Pallas kernels, attend(): pl.pallas_call(functools.partial(attend_kernel, group, per), grid=(1,), o...  29 us
    all_gather x1, blocking collectives, per_device(): gathered = lax.all_gather(payload, 'dp', axis=0)  9.99 us
    all_to_all x2, starting transfers between devices, per_device(): lax.all_to_all(send, 'dp', split_axis=0, concat_axis=0, tiled=True)  8.86 us
    pallas_call x1, Pallas kernels, project(): pl.pallas_call(functools.partial(project_kernel, n_tp, cap, pool_dev), ou...  6.58 us
    pallas_call x1, Pallas kernels, pick(): pl.pallas_call(functools.partial(pick_kernel, n_dp, cap), out_shape=[jax....  4.5 us
    unnamed x48, local copies, waits for them, and re-layouts  3.41 us
  transfers between devices with their start and end apart: 27, of which 4 were waited for; matrix products, arithmetic and copies ran while one was open for 13% of the time, Pallas kernels for 17%

profile of v4, /device:TPU:0, one launch (start us, length us, event | category | flops | bytes accessed | tf_op | source)
XLA Modules:
  0.0 162.1 jit_solution(2970044361751360942)
XLA Ops:
  0.0 4.0 %collective-permute-start.1 = (bf16[128,1024]{1,0:T(8,128)(2,1)}, bf16[128,1024]{1,0:T(8,128)(2,1)S(1)}, u32[]{:S(2)}, u32[]{:S(2)}) collective-permute-start(bf16[128,1024]{1,0:T(8,128)(2,1)} %rest_5_.1), channel_id=1, source_target_pairs={{0,2},{1,3},{2,0},{3,1},{4,6},{5,7},{6,4},{7,5},{8,10},{9,11},{10,... | collective-permute-start | bytes 786440 | tf_op jit(solution)/shard_map/ppermute | solution.py:498
  4.0 1.6 collective-permute-start
  5.6 0.7 fusion.65
  6.3 0.8 constant_dynamic-slice_fusion.1
  7.1 0.8 pad_maximum_fusion.3
  7.8 10.0 %all-gather = bf16[1152,256]{1,0:T(8,128)(2,1)S(1)} all-gather(bf16[144,256]{1,0:T(8,128)(2,1)S(1)} %pad_maximum_fusion.3), channel_id=2, replica_groups=mesh['dp'=8,'tensor'=4] {'dp'}, dimensions={0}, use_global_device_ids=true | all-gather | bytes 663552 | tf_op jit(solution)/shard_map/all_gather | solution.py:558
  17.8 0.6 slice_convert_fusion.asked_ref
  18.5 4.5 %pick_pages.1 = (bf16[8,4,128,2,128]{4,3,2,1,0:T(2,128)(2,1)}, bf16[8,4,128,2,128]{4,3,2,1,0:T(2,128)(2,1)}) custom-call(s32[1]{0:T(128)} %bitcast.4.me_ref, s32[8,2,32]{2,1,0:T(2,128)} %slice_convert_fusion.asked_ref, bf16[32,128,2,256]{3,2,1,0:T(2,128)(2,1)} %pool_ref.1), custom_call_target="tpu_custom_call" | custom-call | flops 1000 | bytes 1000 | tf_op jit(solution)/shard_map/pick_pages/pallas_call | solution.py:82
  23.0 0.7 copy-done.11
  23.7 0.7 copy-done.12
  24.4 4.5 %all-to-all-start = ((bf16[8,4,128,2,128]{4,3,2,1,0:T(2,128)(2,1)}), bf16[8,4,128,2,128]{4,3,2,1,0:T(2,128)(2,1)}, u32[]{:S(2)}, u32[]{:S(2)}) async-start(bf16[8,4,128,2,128]{4,3,2,1,0:T(2,128)(2,1)} %get-tuple-element.41), calls=%async_computation | async-start | bytes 4194304 | tf_op jit(solution)/shard_map/all_to_all | solution.py:562
  28.9 2.3 %collective-permute-start.2 = (bf16[128,1024]{1,0:T(8,128)(2,1)S(1)}, bf16[128,1024]{1,0:T(8,128)(2,1)}, u32[]{:S(2)}, u32[]{:S(2)}) collective-permute-start(bf16[128,1024]{1,0:T(8,128)(2,1)S(1)} %copy-done.10), channel_id=1, source_target_pairs={{0,3},{1,0},{2,1},{3,2},{4,7},{5,4},{6,5},{7,6},{8,11},{9,8},{10,9... | collective-permute-start | bytes 786440 | tf_op jit(solution)/shard_map/ppermute | solution.py:498
  31.2 0.6 reshape.131.rest_0_
  31.9 2.2 %named_adapters.1 = (bf16[128,256]{1,0:T(8,128)(2,1)}, bf16[128,256]{1,0:T(8,128)(2,1)}) custom-call(s32[16]{0:T(128)} %table_ref.2, s32[1,4]{1,0:T(1,128)} %ids_ref.1, bf16[8,144,256]{2,1,0:T(8,128)(2,1)} %bitcast.110), custom_call_target="tpu_custom_call" | custom-call | flops 1000 | bytes 1000 | tf_op jit(solution)/shard_map/named_adapters/pallas_call | solution.py:126
  34.2 1.2 collective-permute-start.4
  35.4 1.8 %collective-permute-start.7 = (bf16[128,1024]{1,0:T(8,128)(2,1)S(1)}, bf16[128,1024]{1,0:T(8,128)(2,1)S(1)}, u32[]{:S(2)}, u32[]{:S(2)}) collective-permute-start(bf16[128,1024]{1,0:T(8,128)(2,1)S(1)} %constant_dynamic-slice_fusion), channel_id=1, source_target_pairs={{0,2},{1,3},{2,0},{3,1},{4,6},{5,7},{6,4},{7,5},{8,10},{9,11},{10,... | collective-permute-start | bytes 786440 | tf_op jit(solution)/shard_map/ppermute | solution.py:498
  37.2 1.9 %collective-permute-start.6 = (bf16[128,1024]{1,0:T(8,128)(2,1)S(1)}, bf16[128,1024]{1,0:T(8,128)(2,1)S(1)}, u32[]{:S(2)}, u32[]{:S(2)}) collective-permute-start(bf16[128,1024]{1,0:T(8,128)(2,1)S(1)} %constant_dynamic-slice_fusion), channel_id=1, source_target_pairs={{0,1},{1,2},{2,3},{3,0},{4,5},{5,6},{6,7},{7,4},{8,9},{9,10},{10,1... | collective-permute-start | bytes 786440 | tf_op jit(solution)/shard_map/ppermute | solution.py:498
  39.1 0.2 reduce-window.4
  39.4 0.1 select_reduce_fusion.1
  39.6 1.8 %fusion.14 = (f32[512,128]{1,0:T(8,128)}, f32[512,128]{1,0:T(8,128)}) fusion(f32[128]{0:T(128)S(1)} %get-tuple-element.113, f32[128]{0:T(128)S(1)} %get-tuple-element.114, f32[512]{0:T(512)S(1)} %fusion.59), kind=kLoop, calls=%fused_computation.29 | loop fusion | flops 131072 | bytes 527360 | tf_op jit(solution)/shard_map/mul | solution.py:576
  41.4 12.9 %collective-permute-done.4.rest_11_ = bf16[128,256]{1,0:T(8,128)(2,1)S(1)} collective-permute-done((bf16[128,256]{1,0:T(8,128)(2,1)}, bf16[128,256]{1,0:T(8,128)(2,1)S(1)}, u32[]{:S(2)}, u32[]{:S(2)}) %collective-permute-start.4) | collective-permute-done | bytes 65568 | tf_op jit(solution)/shard_map/ppermute | solution.py:498
  54.4 0.6 copy-done.18
  55.0 6.6 %project.1 = (bf16[512,256]{1,0:T(8,128)(2,1)}, bf16[512,256]{1,0:T(8,128)(2,1)}, bf16[512,256]{1,0:T(8,128)(2,1)}, s32[32]{0:T(128)}, bf16[2,4,64,1024]{3,2,1,0:T(8,128)(2,1)}) custom-call(s32[1]{0:T(128)} %bitcast.tp_ref, s32[1,4]{1,0:T(1,128)} %lens_ref.5, s32[1,32]{1,0:T(1,128)} %table_ref.3, bf16[1,1024]{1,0:T(2,128)(2,1)} %reshape.131.rest_0_, ...), custom_call_target="tpu_custom_call" | custom-call | flops 1000 | bytes 1000 | tf_op jit(solution)/shard_map/project/pallas_call | solution.py:248
  61.6 4.4 %all-to-all-start.1 = ((bf16[8,4,128,2,128]{4,3,2,1,0:T(2,128)(2,1)}), bf16[8,4,128,2,128]{4,3,2,1,0:T(2,128)(2,1)}, u32[]{:S(2)}, u32[]{:S(2)}) async-start(bf16[8,4,128,2,128]{4,3,2,1,0:T(2,128)(2,1)} %get-tuple-element.62), calls=%async_computation.1 | async-start | bytes 4194304 | tf_op jit(solution)/shard_map/all_to_all | solution.py:582
  66.1 14.4 %attend.2 = bf16[512,128]{1,0:T(8,128)(2,1)} custom-call(s32[1,4]{1,0:T(1,128)} %lens_ref.5, s32[1,4]{1,0:T(1,128)} %counts_ref.3, s32[32]{0:T(128)} %get-tuple-element.48.pos_ref, f32[2,4]{1,0:T(2,128)} %bias_ref.3, bf16[512,256]{1,0:T(8,128)(2,1)} %get-tuple-element.60.q_ref, bf16[512,256]{1,0:T(8,128)(2,1)} %get-tuple-element.49.kn_ref, ...), custom_call_target="tpu_custom_call" | custom-call | flops 1000 | bytes 1000 | tf_op jit(solution)/shard_map/attend/pallas_call | solution.py:472
  80.5 1.0 pad_maximum_fusion.1
  81.5 1.0 collective-permute-start.9
  82.5 1.4 fusion.75
  83.9 10.2 %collective-permute-start.12 = (bf16[512,128]{1,0:T(8,128)(2,1)S(1)}, bf16[512,128]{1,0:T(8,128)(2,1)S(1)}, u32[]{:S(2)}, u32[]{:S(2)}) collective-permute-start(bf16[512,128]{1,0:T(8,128)(2,1)S(1)} %copy-done.9), channel_id=1, source_target_pairs={{0,3},{1,0},{2,1},{3,2},{4,7},{5,4},{6,5},{7,6},{8,11},{9,8},{10,9... | collective-permute-start | bytes 393224 | tf_op jit(solution)/shard_map/ppermute | solution.py:498
  94.1 0.8 collective-permute-start.10
  94.9 1.8 %maximum_select_fusion = bf16[3,256,1024]{2,1,0:T(8,128)(2,1)S(1)} fusion(bf16[3,128,1024]{2,1,0:T(8,128)(2,1)} %collective-permute-done.9, bf16[1,128,1024]{2,1,0:T(8,128)(2,1)S(1)} %bitcast.122, bf16[1,128,1024]{2,1,0:T(8,128)(2,1)S(1)} %bitcast.118, bf16[1,128,1024]{2,1,0:T(8,128)(2,1)S(1)} %bitcast.120, pred[]{:T(512)S(6)} %eq.35), kind=kLoop, calls=%fused_computation.7 | loop fusion | flops 13369344 | bytes 3145729 | tf_op jit(solution)/shard_map/jit(_where)/select_n | solution.py:504
  96.8 1.5 pad_maximum_fusion
  98.3 7.2 %collective-permute-done.11 = bf16[512,128]{1,0:T(8,128)(2,1)S(1)} collective-permute-done((bf16[512,128]{1,0:T(8,128)(2,1)S(1)}, bf16[512,128]{1,0:T(8,128)(2,1)S(1)}, u32[]{:S(2)}, u32[]{:S(2)}) %collective-permute-start.11) | collective-permute-done | bytes 131104 | tf_op jit(solution)/shard_map/ppermute | solution.py:498
  105.5 0.6 copy-done.15
  106.2 14.6 %attend.3 = bf16[512,128]{1,0:T(8,128)(2,1)} custom-call(s32[1,4]{1,0:T(1,128)} %lens_ref.5, s32[1,4]{1,0:T(1,128)} %counts_ref.3, s32[32]{0:T(128)} %get-tuple-element.48.pos_ref, f32[2,4]{1,0:T(2,128)} %bias_ref.3, bf16[512,256]{1,0:T(8,128)(2,1)} %get-tuple-element.60.q_ref, bf16[512,256]{1,0:T(8,128)(2,1)} %get-tuple-element.49.kn_ref, ...), custom_call_target="tpu_custom_call" | custom-call | flops 1000 | bytes 1000 | tf_op jit(solution)/shard_map/attend/pallas_call | solution.py:472
  120.8 0.9 fusion.76
  121.7 1.6 collective-permute-start.15
  123.3 0.5 collective-permute-start.14
  123.8 1.9 %collective-permute-start.13 = (bf16[256,128]{1,0:T(8,128)(2,1)S(1)}, bf16[256,128]{1,0:T(8,128)(2,1)S(1)}, u32[]{:S(2)}, u32[]{:S(2)}) collective-permute-start(bf16[256,128]{1,0:T(8,128)(2,1)S(1)} %bitcast.131), channel_id=1, source_target_pairs={{0,1},{1,2},{2,3},{3,0},{4,5},{5,6},{6,7},{7,4},{8,9},{9,10},{10,1... | collective-permute-start | bytes 196616 | tf_op jit(solution)/shard_map/ppermute | solution.py:498
  125.7 0.9 fusion.78
  126.7 1.7 %fusion.74 = (bf16[4,1,128,1024]{3,2,1,0:T(8,128)(2,1)S(1)}, bf16[4,1,128,1024]{3,2,1,0:T(8,128)(2,1)S(1)}) fusion(bf16[4,2,128,1024]{3,2,1,0:T(8,128)(2,1)} %bitcast.106), kind=kLoop, calls=%fused_computation.120 | loop fusion | bytes 4194304 | tf_op jit(solution)/shard_map/slice | solution.py:590
  128.4 0.5 convert_add_fusion.1
  128.9 1.9 %collective-permute-start.21 = (bf16[256,128]{1,0:T(8,128)(2,1)S(1)}, bf16[256,128]{1,0:T(8,128)(2,1)S(1)}, u32[]{:S(2)}, u32[]{:S(2)}) collective-permute-start(bf16[256,128]{1,0:T(8,128)(2,1)S(1)} %bitcast.125), channel_id=1, source_target_pairs={{0,3},{1,0},{2,1},{3,2},{4,7},{5,4},{6,5},{7,6},{8,11},{9,8},{10,9... | collective-permute-start | bytes 196616 | tf_op jit(solution)/shard_map/ppermute | solution.py:498
  130.8 0.6 collective-permute-start.20
  131.4 0.4 fusion.32
  131.9 0.5 collective-permute-start.19
  132.4 0.5 multiply_reduce_fusion.1
  133.0 0.6 copy-done.1
  133.6 1.3 convolution_bitcast_fusion.1
  135.0 0.2 fusion.73
  135.2 0.8 fusion.81
  136.1 2.8 %collective-permute-start.18 = (bf16[64,1024]{1,0:T(8,128)(2,1)S(1)}, bf16[64,1024]{1,0:T(8,128)(2,1)S(1)}, u32[]{:S(2)}, u32[]{:S(2)}) collective-permute-start(bf16[64,1024]{1,0:T(8,128)(2,1)S(1)} %get-tuple-element.88), channel_id=1, source_target_pairs={{0,3},{1,0},{2,1},{3,2},{4,7},{5,4},{6,5},{7,6},{8,11},{9,8},{10,9... | collective-permute-start | bytes 393224 | tf_op jit(solution)/shard_map/ppermute | solution.py:498
  138.9 0.5 collective-permute-start.17
  139.4 1.1 collective-permute-start.16
  140.5 0.6 multiply_reduce_fusion
  141.0 1.3 convolution_bitcast_fusion
  142.4 0.1 fusion.72
  142.5 0.8 fusion.82
  143.4 1.9 %collective-permute-start.22 = (bf16[64,1024]{1,0:T(8,128)(2,1)S(1)}, bf16[64,1024]{1,0:T(8,128)(2,1)S(1)}, u32[]{:S(2)}, u32[]{:S(2)}) collective-permute-start(bf16[64,1024]{1,0:T(8,128)(2,1)S(1)} %get-tuple-element.85), channel_id=1, source_target_pairs={{0,1},{1,2},{2,3},{3,0},{4,5},{5,6},{6,7},{7,4},{8,9},{9,10},{10,1... | collective-permute-start | bytes 393224 | tf_op jit(solution)/shard_map/ppermute | solution.py:498
  145.3 1.9 %collective-permute-start.24 = (bf16[64,1024]{1,0:T(8,128)(2,1)S(1)}, bf16[64,1024]{1,0:T(8,128)(2,1)S(1)}, u32[]{:S(2)}, u32[]{:S(2)}) collective-permute-start(bf16[64,1024]{1,0:T(8,128)(2,1)S(1)} %get-tuple-element.86), channel_id=1, source_target_pairs={{0,3},{1,0},{2,1},{3,2},{4,7},{5,4},{6,5},{7,6},{8,11},{9,8},{10,9... | collective-permute-start | bytes 393224 | tf_op jit(solution)/shard_map/ppermute | solution.py:498
  147.3 3.4 %collective-permute-start.23 = (bf16[64,1024]{1,0:T(8,128)(2,1)S(1)}, bf16[64,1024]{1,0:T(8,128)(2,1)S(1)}, u32[]{:S(2)}, u32[]{:S(2)}) collective-permute-start(bf16[64,1024]{1,0:T(8,128)(2,1)S(1)} %get-tuple-element.87), channel_id=1, source_target_pairs={{0,2},{1,3},{2,0},{3,1},{4,6},{5,7},{6,4},{7,5},{8,10},{9,11},{10,... | collective-permute-start | bytes 393224 | tf_op jit(solution)/shard_map/ppermute | solution.py:498
  150.7 5.5 %collective-permute-done.17 = bf16[64,1024]{1,0:T(8,128)(2,1)S(1)} collective-permute-done((bf16[64,1024]{1,0:T(8,128)(2,1)S(1)}, bf16[64,1024]{1,0:T(8,128)(2,1)S(1)}, u32[]{:S(2)}, u32[]{:S(2)}) %collective-permute-start.17) | collective-permute-done | bytes 131104 | tf_op jit(solution)/shard_map/ppermute | solution.py:498
  156.3 5.0 %collective-permute-done.23 = bf16[64,1024]{1,0:T(8,128)(2,1)S(1)} collective-permute-done((bf16[64,1024]{1,0:T(8,128)(2,1)S(1)}, bf16[64,1024]{1,0:T(8,128)(2,1)S(1)}, u32[]{:S(2)}, u32[]{:S(2)}) %collective-permute-start.23) | collective-permute-done | bytes 131104 | tf_op jit(solution)/shard_map/ppermute | solution.py:498
  161.4 0.7 pad_maximum_fusion.2
  (86 shorter events, 0.9 us)
Async XLA Ops:
  0.0 135.2 %copy-start = (bf16[1024,1024]{1,0:T(8,128)(2,1)S(1)}, bf16[1024,1024]{1,0:T(8,128)(2,1)}, u32[]{:S(2)}) copy-start(bf16[1024,1024]{1,0:T(8,128)(2,1)} %param.22) | copy-start | bytes 6291460
  0.0 23.0 %collective-permute-start.1 = (bf16[128,1024]{1,0:T(8,128)(2,1)}, bf16[128,1024]{1,0:T(8,128)(2,1)S(1)}, u32[]{:S(2)}, u32[]{:S(2)}) collective-permute-start(bf16[128,1024]{1,0:T(8,128)(2,1)} %rest_5_.1), channel_id=1, source_target_pairs={{0,2},{1,3},{2,0},{3,1},{4,6},{5,7},{6,4},{7,5},{8,10},{9,11},{10,... | collective-permute-start | bytes 786440 | tf_op jit(solution)/shard_map/ppermute | solution.py:498
  4.0 19.0 %collective-permute-start = (bf16[128,1024]{1,0:T(8,128)(2,1)}, bf16[128,1024]{1,0:T(8,128)(2,1)S(1)}, u32[]{:S(2)}, u32[]{:S(2)}) collective-permute-start(bf16[128,1024]{1,0:T(8,128)(2,1)} %rest_5_.1), channel_id=1, source_target_pairs={{0,1},{1,2},{2,3},{3,0},{4,5},{5,6},{6,7},{7,4},{8,9},{9,10},{10,1... | collective-permute-start | bytes 786440 | tf_op jit(solution)/shard_map/ppermute | solution.py:498
  17.8 5.2 %copy-start.2 = (bf16[1152,256]{1,0:T(8,128)(2,1)}, bf16[1152,256]{1,0:T(8,128)(2,1)S(1)}, u32[]{:S(2)}) copy-start(bf16[1152,256]{1,0:T(8,128)(2,1)S(1)} %all-gather) | copy-start | bytes 1769476
  23.0 0.7 copy-start.11
  23.7 0.7 copy-start.12
  24.4 4.5 %copy-start.10 = (bf16[128,1024]{1,0:T(8,128)(2,1)S(1)}, bf16[128,1024]{1,0:T(8,128)(2,1)}, u32[]{:S(2)}) copy-start(bf16[128,1024]{1,0:T(8,128)(2,1)} %rest_5_.1) | copy-start | bytes 786436
  24.4 6.8 %copy-start.22 = (bf16[1024]{0:T(1024)(128)(2,1)S(1)}, bf16[1024]{0:T(1024)(128)(2,1)}, u32[]{:S(2)}) copy-start(bf16[1024]{0:T(1024)(128)(2,1)} %param.17) | copy-start | bytes 6148
  24.4 7.4 %copy-start.3 = (bf16[256,1024]{1,0:T(8,128)(2,1)S(1)}, bf16[256,1024]{1,0:T(8,128)(2,1)}, u32[]{:S(2)}) copy-start(bf16[256,1024]{1,0:T(8,128)(2,1)} %param.20) | copy-start | bytes 1572868
  24.4 14.7 %copy-start.21 = (s32[1,4]{1,0:T(1,128)S(1)}, s32[1,4]{1,0:T(1,128)}, u32[]{:S(2)}) copy-start(s32[1,4]{1,0:T(1,128)} %lens_ref.5) | copy-start | bytes 52
  24.4 15.0 %copy-start.20 = (s32[1,4]{1,0:T(1,128)S(1)}, s32[1,4]{1,0:T(1,128)}, u32[]{:S(2)}) copy-start(s32[1,4]{1,0:T(1,128)} %counts_ref.3) | copy-start | bytes 52
  24.4 37.2 %all-to-all-start = ((bf16[8,4,128,2,128]{4,3,2,1,0:T(2,128)(2,1)}), bf16[8,4,128,2,128]{4,3,2,1,0:T(2,128)(2,1)}, u32[]{:S(2)}, u32[]{:S(2)}) async-start(bf16[8,4,128,2,128]{4,3,2,1,0:T(2,128)(2,1)} %get-tuple-element.41), calls=%async_computation | async-start | bytes 4194304 | tf_op jit(solution)/shard_map/all_to_all | solution.py:562
  28.9 10.6 %collective-permute-start.2 = (bf16[128,1024]{1,0:T(8,128)(2,1)S(1)}, bf16[128,1024]{1,0:T(8,128)(2,1)}, u32[]{:S(2)}, u32[]{:S(2)}) collective-permute-start(bf16[128,1024]{1,0:T(8,128)(2,1)S(1)} %copy-done.10), channel_id=1, source_target_pairs={{0,3},{1,0},{2,1},{3,2},{4,7},{5,4},{6,5},{7,6},{8,11},{9,8},{10,9... | collective-permute-start | bytes 786440 | tf_op jit(solution)/shard_map/ppermute | solution.py:498
  34.1 7.3 %collective-permute-start.5 = (bf16[128,256]{1,0:T(8,128)(2,1)}, bf16[128,256]{1,0:T(8,128)(2,1)S(1)}, u32[]{:S(2)}, u32[]{:S(2)}) collective-permute-start(bf16[128,256]{1,0:T(8,128)(2,1)} %get-tuple-element.45.rest_9_), channel_id=1, source_target_pairs={{0,3},{1,0},{2,1},{3,2},{4,7},{5,4},{6,5},{7,6},{8,11},{9,8},{10,9... | collective-permute-start | bytes 196616 | tf_op jit(solution)/shard_map/ppermute | solution.py:498
  34.2 20.1 %collective-permute-start.4 = (bf16[128,256]{1,0:T(8,128)(2,1)}, bf16[128,256]{1,0:T(8,128)(2,1)S(1)}, u32[]{:S(2)}, u32[]{:S(2)}) collective-permute-start(bf16[128,256]{1,0:T(8,128)(2,1)} %get-tuple-element.45.rest_9_), channel_id=1, source_target_pairs={{0,2},{1,3},{2,0},{3,1},{4,6},{5,7},{6,4},{7,5},{8,10},{9,11},{10,... | collective-permute-start | bytes 196616 | tf_op jit(solution)/shard_map/ppermute | solution.py:498
  35.4 26.2 %collective-permute-start.7 = (bf16[128,1024]{1,0:T(8,128)(2,1)S(1)}, bf16[128,1024]{1,0:T(8,128)(2,1)S(1)}, u32[]{:S(2)}, u32[]{:S(2)}) collective-permute-start(bf16[128,1024]{1,0:T(8,128)(2,1)S(1)} %constant_dynamic-slice_fusion), channel_id=1, source_target_pairs={{0,2},{1,3},{2,0},{3,1},{4,6},{5,7},{6,4},{7,5},{8,10},{9,11},{10,... | collective-permute-start | bytes 786440 | tf_op jit(solution)/shard_map/ppermute | solution.py:498
  37.2 24.4 %collective-permute-start.6 = (bf16[128,1024]{1,0:T(8,128)(2,1)S(1)}, bf16[128,1024]{1,0:T(8,128)(2,1)S(1)}, u32[]{:S(2)}, u32[]{:S(2)}) collective-permute-start(bf16[128,1024]{1,0:T(8,128)(2,1)S(1)} %constant_dynamic-slice_fusion), channel_id=1, source_target_pairs={{0,1},{1,2},{2,3},{3,0},{4,5},{5,6},{6,7},{7,4},{8,9},{9,10},{10,1... | collective-permute-start | bytes 786440 | tf_op jit(solution)/shard_map/ppermute | solution.py:498
  39.5 14.8 %collective-permute-start.3 = (bf16[128,256]{1,0:T(8,128)(2,1)}, bf16[128,256]{1,0:T(8,128)(2,1)S(1)}, u32[]{:S(2)}, u32[]{:S(2)}) collective-permute-start(bf16[128,256]{1,0:T(8,128)(2,1)} %get-tuple-element.45.rest_9_), channel_id=1, source_target_pairs={{0,1},{1,2},{2,3},{3,0},{4,5},{5,6},{6,7},{7,4},{8,9},{9,10},{10,1... | collective-permute-start | bytes 196616 | tf_op jit(solution)/shard_map/ppermute | solution.py:498
  41.4 12.9 %copy-start.17 = (bf16[128,256]{1,0:T(8,128)(2,1)}, bf16[128,256]{1,0:T(8,128)(2,1)S(1)}, u32[]{:S(2)}) copy-start(bf16[128,256]{1,0:T(8,128)(2,1)S(1)} %collective-permute-done.5.rest_12_) | copy-start | bytes 196612
  54.4 0.6 copy-start.18
  54.4 0.7 copy-start.19
  61.6 18.9 %copy-start.5 = (bf16[128,1024]{1,0:T(8,128)(2,1)}, bf16[128,1024]{1,0:T(8,128)(2,1)S(1)}, u32[]{:S(2)}) copy-start(bf16[128,1024]{1,0:T(8,128)(2,1)S(1)} %collective-permute-done.6) | copy-start | bytes 786436
  61.6 44.5 %all-to-all-start.1 = ((bf16[8,4,128,2,128]{4,3,2,1,0:T(2,128)(2,1)}), bf16[8,4,128,2,128]{4,3,2,1,0:T(2,128)(2,1)}, u32[]{:S(2)}, u32[]{:S(2)}) async-start(bf16[8,4,128,2,128]{4,3,2,1,0:T(2,128)(2,1)} %get-tuple-element.62), calls=%async_computation.1 | async-start | bytes 4194304 | tf_op jit(solution)/shard_map/all_to_all | solution.py:582
  66.0 14.5 %collective-permute-start.8 = (bf16[128,1024]{1,0:T(8,128)(2,1)S(1)}, bf16[128,1024]{1,0:T(8,128)(2,1)S(1)}, u32[]{:S(2)}, u32[]{:S(2)}) collective-permute-start(bf16[128,1024]{1,0:T(8,128)(2,1)S(1)} %constant_dynamic-slice_fusion), channel_id=1, source_target_pairs={{0,3},{1,0},{2,1},{3,2},{4,7},{5,4},{6,5},{7,6},{8,11},{9,8},{10,9... | collective-permute-start | bytes 786440 | tf_op jit(solution)/shard_map/ppermute | solution.py:498
  66.1 16.4 %copy-start.23 = (bf16[1024]{0:T(1024)(128)(2,1)S(1)}, bf16[1024]{0:T(1024)(128)(2,1)}, u32[]{:S(2)}) copy-start(bf16[1024]{0:T(1024)(128)(2,1)} %param.18) | copy-start | bytes 6148
  80.5 3.4 %copy-start.9 = (bf16[512,128]{1,0:T(8,128)(2,1)S(1)}, bf16[512,128]{1,0:T(8,128)(2,1)}, u32[]{:S(2)}) copy-start(bf16[512,128]{1,0:T(8,128)(2,1)} %attend.2) | copy-start | bytes 393220
  80.5 1.0 copy-start.7
  81.5 13.4 %collective-permute-start.9 = (bf16[3,128,1024]{2,1,0:T(8,128)(2,1)}, bf16[3,128,1024]{2,1,0:T(8,128)(2,1)}, u32[]{:S(2)}, u32[]{:S(2)}) collective-permute-start(bf16[3,128,1024]{2,1,0:T(8,128)(2,1)} %pad_maximum_fusion.1), channel_id=1, source_target_pairs={{0,4},{4,0},{8,12},{12,8},{16,20},{20,16},{24,28},{28,24},{1,5},{5... | collective-permute-start | bytes 2359304 | tf_op jit(solution)/shard_map/ppermute | solution.py:503
  82.5 12.4 %copy-start.6 = (bf16[128,1024]{1,0:T(8,128)(2,1)S(1)}, bf16[128,1024]{1,0:T(8,128)(2,1)}, u32[]{:S(2)}) copy-start(bf16[128,1024]{1,0:T(8,128)(2,1)} %copy-done.5) | copy-start | bytes 786436
  82.5 12.4 %copy-start.8 = (bf16[128,1024]{1,0:T(8,128)(2,1)S(1)}, bf16[128,1024]{1,0:T(8,128)(2,1)}, u32[]{:S(2)}) copy-start(bf16[128,1024]{1,0:T(8,128)(2,1)} %copy-done.7) | copy-start | bytes 786436
  83.9 12.9 %copy-start.4 = (bf16[256,1024]{1,0:T(8,128)(2,1)S(1)}, bf16[256,1024]{1,0:T(8,128)(2,1)}, u32[]{:S(2)}) copy-start(bf16[256,1024]{1,0:T(8,128)(2,1)} %param.20) | copy-start | bytes 1572868
  83.9 14.4 %collective-permute-start.12 = (bf16[512,128]{1,0:T(8,128)(2,1)S(1)}, bf16[512,128]{1,0:T(8,128)(2,1)S(1)}, u32[]{:S(2)}, u32[]{:S(2)}) collective-permute-start(bf16[512,128]{1,0:T(8,128)(2,1)S(1)} %copy-done.9), channel_id=1, source_target_pairs={{0,3},{1,0},{2,1},{3,2},{4,7},{5,4},{6,5},{7,6},{8,11},{9,8},{10,9... | collective-permute-start | bytes 393224 | tf_op jit(solution)/shard_map/ppermute | solution.py:498
  94.1 11.4 %collective-permute-start.11 = (bf16[512,128]{1,0:T(8,128)(2,1)S(1)}, bf16[512,128]{1,0:T(8,128)(2,1)S(1)}, u32[]{:S(2)}, u32[]{:S(2)}) collective-permute-start(bf16[512,128]{1,0:T(8,128)(2,1)S(1)} %copy-done.9), channel_id=1, source_target_pairs={{0,2},{1,3},{2,0},{3,1},{4,6},{5,7},{6,4},{7,5},{8,10},{9,11},{10,... | collective-permute-start | bytes 393224 | tf_op jit(solution)/shard_map/ppermute | solution.py:498
  94.1 12.1 %collective-permute-start.10 = (bf16[512,128]{1,0:T(8,128)(2,1)S(1)}, bf16[512,128]{1,0:T(8,128)(2,1)}, u32[]{:S(2)}, u32[]{:S(2)}) collective-permute-start(bf16[512,128]{1,0:T(8,128)(2,1)S(1)} %copy-done.9), channel_id=1, source_target_pairs={{0,1},{1,2},{2,3},{3,0},{4,5},{5,6},{6,7},{7,4},{8,9},{9,10},{10,1... | collective-permute-start | bytes 393224 | tf_op jit(solution)/shard_map/ppermute | solution.py:498
  98.3 7.2 %copy-start.13 = (bf16[512,128]{1,0:T(8,128)(2,1)}, bf16[512,128]{1,0:T(8,128)(2,1)S(1)}, u32[]{:S(2)}) copy-start(bf16[512,128]{1,0:T(8,128)(2,1)S(1)} %collective-permute-done.12) | copy-start | bytes 393220
  105.5 0.6 copy-start.15
  106.2 20.5 %copy-start.16 = (bf16[512,128]{1,0:T(8,128)(2,1)S(1)}, bf16[512,128]{1,0:T(8,128)(2,1)}, u32[]{:S(2)}) copy-start(bf16[512,128]{1,0:T(8,128)(2,1)} %copy-done.15) | copy-start | bytes 393220
  106.2 20.5 %copy-start.14 = (bf16[512,128]{1,0:T(8,128)(2,1)S(1)}, bf16[512,128]{1,0:T(8,128)(2,1)}, u32[]{:S(2)}) copy-start(bf16[512,128]{1,0:T(8,128)(2,1)} %copy-done.13) | copy-start | bytes 393220
  121.7 10.2 %collective-permute-start.15 = (bf16[256,128]{1,0:T(8,128)(2,1)S(1)}, bf16[256,128]{1,0:T(8,128)(2,1)S(1)}, u32[]{:S(2)}, u32[]{:S(2)}) collective-permute-start(bf16[256,128]{1,0:T(8,128)(2,1)S(1)} %bitcast.129), channel_id=1, source_target_pairs={{0,3},{1,0},{2,1},{3,2},{4,7},{5,4},{6,5},{7,6},{8,11},{9,8},{10,9... | collective-permute-start | bytes 196616 | tf_op jit(solution)/shard_map/ppermute | solution.py:498
  123.3 9.2 %collective-permute-start.14 = (bf16[256,128]{1,0:T(8,128)(2,1)S(1)}, bf16[256,128]{1,0:T(8,128)(2,1)S(1)}, u32[]{:S(2)}, u32[]{:S(2)}) collective-permute-start(bf16[256,128]{1,0:T(8,128)(2,1)S(1)} %bitcast.130), channel_id=1, source_target_pairs={{0,2},{1,3},{2,0},{3,1},{4,6},{5,7},{6,4},{7,5},{8,10},{9,11},{10,... | collective-permute-start | bytes 196616 | tf_op jit(solution)/shard_map/ppermute | solution.py:498
  123.8 8.7 %collective-permute-start.13 = (bf16[256,128]{1,0:T(8,128)(2,1)S(1)}, bf16[256,128]{1,0:T(8,128)(2,1)S(1)}, u32[]{:S(2)}, u32[]{:S(2)}) collective-permute-start(bf16[256,128]{1,0:T(8,128)(2,1)S(1)} %bitcast.131), channel_id=1, source_target_pairs={{0,1},{1,2},{2,3},{3,0},{4,5},{5,6},{6,7},{7,4},{8,9},{9,10},{10,1... | collective-permute-start | bytes 196616 | tf_op jit(solution)/shard_map/ppermute | solution.py:498
  128.9 10.5 %collective-permute-start.21 = (bf16[256,128]{1,0:T(8,128)(2,1)S(1)}, bf16[256,128]{1,0:T(8,128)(2,1)S(1)}, u32[]{:S(2)}, u32[]{:S(2)}) collective-permute-start(bf16[256,128]{1,0:T(8,128)(2,1)S(1)} %bitcast.125), channel_id=1, source_target_pairs={{0,3},{1,0},{2,1},{3,2},{4,7},{5,4},{6,5},{7,6},{8,11},{9,8},{10,9... | collective-permute-start | bytes 196616 | tf_op jit(solution)/shard_map/ppermute | solution.py:498
  130.8 9.6 %collective-permute-start.20 = (bf16[256,128]{1,0:T(8,128)(2,1)S(1)}, bf16[256,128]{1,0:T(8,128)(2,1)S(1)}, u32[]{:S(2)}, u32[]{:S(2)}) collective-permute-start(bf16[256,128]{1,0:T(8,128)(2,1)S(1)} %bitcast.126), channel_id=1, source_target_pairs={{0,2},{1,3},{2,0},{3,1},{4,6},{5,7},{6,4},{7,5},{8,10},{9,11},{10,... | collective-permute-start | bytes 196616 | tf_op jit(solution)/shard_map/ppermute | solution.py:498
  131.4 2.2 %copy-start.1 = (bf16[2,1024,1024]{2,1,0:T(8,128)(2,1)S(1)}, bf16[2,1024,1024]{2,1,0:T(8,128)(2,1)}, u32[]{:S(2)}) copy-start(bf16[2,1024,1024]{2,1,0:T(8,128)(2,1)} %param.21) | copy-start | bytes 12582916
  131.9 8.5 %collective-permute-start.19 = (bf16[256,128]{1,0:T(8,128)(2,1)S(1)}, bf16[256,128]{1,0:T(8,128)(2,1)S(1)}, u32[]{:S(2)}, u32[]{:S(2)}) collective-permute-start(bf16[256,128]{1,0:T(8,128)(2,1)S(1)} %bitcast.127), channel_id=1, source_target_pairs={{0,1},{1,2},{2,3},{3,0},{4,5},{5,6},{6,7},{7,4},{8,9},{9,10},{10,1... | collective-permute-start | bytes 196616 | tf_op jit(solution)/shard_map/ppermute | solution.py:498
  136.1 11.2 %collective-permute-start.18 = (bf16[64,1024]{1,0:T(8,128)(2,1)S(1)}, bf16[64,1024]{1,0:T(8,128)(2,1)S(1)}, u32[]{:S(2)}, u32[]{:S(2)}) collective-permute-start(bf16[64,1024]{1,0:T(8,128)(2,1)S(1)} %get-tuple-element.88), channel_id=1, source_target_pairs={{0,3},{1,0},{2,1},{3,2},{4,7},{5,4},{6,5},{7,6},{8,11},{9,8},{10,9... | collective-permute-start | bytes 393224 | tf_op jit(solution)/shard_map/ppermute | solution.py:498
  138.9 17.3 %collective-permute-start.17 = (bf16[64,1024]{1,0:T(8,128)(2,1)S(1)}, bf16[64,1024]{1,0:T(8,128)(2,1)S(1)}, u32[]{:S(2)}, u32[]{:S(2)}) collective-permute-start(bf16[64,1024]{1,0:T(8,128)(2,1)S(1)} %get-tuple-element.89), channel_id=1, source_target_pairs={{0,2},{1,3},{2,0},{3,1},{4,6},{5,7},{6,4},{7,5},{8,10},{9,11},{10,... | collective-permute-start | bytes 393224 | tf_op jit(solution)/shard_map/ppermute | solution.py:498
  139.4 16.8 %collective-permute-start.16 = (bf16[64,1024]{1,0:T(8,128)(2,1)S(1)}, bf16[64,1024]{1,0:T(8,128)(2,1)S(1)}, u32[]{:S(2)}, u32[]{:S(2)}) collective-permute-start(bf16[64,1024]{1,0:T(8,128)(2,1)S(1)} %get-tuple-element.90), channel_id=1, source_target_pairs={{0,1},{1,2},{2,3},{3,0},{4,5},{5,6},{6,7},{7,4},{8,9},{9,10},{10,1... | collective-permute-start | bytes 393224 | tf_op jit(solution)/shard_map/ppermute | solution.py:498
  143.4 12.8 %collective-permute-start.22 = (bf16[64,1024]{1,0:T(8,128)(2,1)S(1)}, bf16[64,1024]{1,0:T(8,128)(2,1)S(1)}, u32[]{:S(2)}, u32[]{:S(2)}) collective-permute-start(bf16[64,1024]{1,0:T(8,128)(2,1)S(1)} %get-tuple-element.85), channel_id=1, source_target_pairs={{0,1},{1,2},{2,3},{3,0},{4,5},{5,6},{6,7},{7,4},{8,9},{9,10},{10,1... | collective-permute-start | bytes 393224 | tf_op jit(solution)/shard_map/ppermute | solution.py:498
  145.3 10.9 %collective-permute-start.24 = (bf16[64,1024]{1,0:T(8,128)(2,1)S(1)}, bf16[64,1024]{1,0:T(8,128)(2,1)S(1)}, u32[]{:S(2)}, u32[]{:S(2)}) collective-permute-start(bf16[64,1024]{1,0:T(8,128)(2,1)S(1)} %get-tuple-element.86), channel_id=1, source_target_pairs={{0,3},{1,0},{2,1},{3,2},{4,7},{5,4},{6,5},{7,6},{8,11},{9,8},{10,9... | collective-permute-start | bytes 393224 | tf_op jit(solution)/shard_map/ppermute | solution.py:498
  147.3 14.0 %collective-permute-start.23 = (bf16[64,1024]{1,0:T(8,128)(2,1)S(1)}, bf16[64,1024]{1,0:T(8,128)(2,1)S(1)}, u32[]{:S(2)}, u32[]{:S(2)}) collective-permute-start(bf16[64,1024]{1,0:T(8,128)(2,1)S(1)} %get-tuple-element.87), channel_id=1, source_target_pairs={{0,2},{1,3},{2,0},{3,1},{4,6},{5,7},{6,4},{7,5},{8,10},{9,11},{10,... | collective-permute-start | bytes 393224 | tf_op jit(solution)/shard_map/ppermute | solution.py:498

commit v5 on v4

--- a/solution.py
+++ b/solution.py
@@ -575,7 +575,7 @@
         tp_id, lengths, page_table, attn_gain.reshape(1, d_model), w_qkv, up_named,
         jnp.cos(angles), jnp.sin(angles) * sign[None, :], toks, downs, n_dp, cap, pool_dev, n_chunk,
     )
-    own_half = lax.optimization_barrier((own_half, down_named))[0]
+    own_half = lax.optimization_barrier((own_half, downs[1:]))[0]
     halves = [shift(own_half, "tensor", n_tp, k) for k in far_first]
     for a in range(1, n_group):
         send = lax.optimization_barrier((picked[a], fetched[-1], query, halves[:-1]))[0]

time: 162 us -> 155 us (0.957)
  starting transfers between devices: 52.7 us -> 44.4 us
  waiting for transfers between devices: 30.7 us -> 34.7 us
  Pallas kernels: 42.3 us -> 40.2 us
    ppermute x24, starting transfers between devices: 42.8 us -> 35.1 us  [shift(): return lax.ppermute(value, axis, [(i, (i + k) % n) for i in range(n)])]
    ppermute x24, waiting for transfers between devices: 30.7 us -> 34.7 us  [shift(): return lax.ppermute(value, axis, [(i, (i + k) % n) for i in range(n)])]
    pallas_call x2, Pallas kernels: 29 us -> 26.9 us  [attend(): pl.pallas_call(functools.partial(attend_kernel, group, per), grid=(1,), o...]
  transfers between devices with their start and end apart: 27 -> 27, of which waited for: 4 -> 6; matrix products, arithmetic and copies ran while one was open for 13% -> 14% of each run, Pallas kernels for 17% -> 17%
where the time goes in v5:
time: 155 us; the launch traced here: 154 us
  starting transfers between devices  44.4 us (29%)
  Pallas kernels  40.2 us (26%)
  waiting for transfers between devices  34.7 us (22%)
  blocking collectives  9.99 us (6%)
  other arithmetic  9.52 us (6%)
  local copies, waits for them, and re-layouts  8.85 us (6%)
  matrix products  6.32 us (4%)
    ppermute x24, starting transfers between devices, shift(): return lax.ppermute(value, axis, [(i, (i + k) % n) for i in range(n)])  35.1 us
    ppermute x24, waiting for transfers between devices, shift(): return lax.ppermute(value, axis, [(i, (i + k) % n) for i in range(n)])  34.7 us
    pallas_call x2, Pallas kernels, attend(): pl.pallas_call(functools.partial(attend_kernel, group, per), grid=(1,), o...  26.9 us
    all_gather x1, blocking collectives, per_device(): gathered = lax.all_gather(payload, 'dp', axis=0)  9.99 us
    all_to_all x2, starting transfers between devices, per_device(): lax.all_to_all(send, 'dp', split_axis=0, concat_axis=0, tiled=True)  8.86 us
    pallas_call x1, Pallas kernels, project(): pl.pallas_call(functools.partial(project_kernel, n_tp, cap, pool_dev), ou...  6.59 us
    pallas_call x1, Pallas kernels, pick(): pl.pallas_call(functools.partial(pick_kernel, n_dp, cap), out_shape=[jax....  4.44 us
  transfers between devices with their start and end apart: 27, of which 6 were waited for; matrix products, arithmetic and copies ran while one was open for 14% of the time, Pallas kernels for 17%

profile of v5, /device:TPU:0, one launch (start us, length us, event | category | flops | bytes accessed | tf_op | source)
XLA Modules:
  0.0 154.4 jit_solution(2874963485132324989)
XLA Ops:
  0.0 4.0 %collective-permute-start.1 = (bf16[128,1024]{1,0:T(8,128)(2,1)}, bf16[128,1024]{1,0:T(8,128)(2,1)S(1)}, u32[]{:S(2)}, u32[]{:S(2)}) collective-permute-start(bf16[128,1024]{1,0:T(8,128)(2,1)} %rest_5_.1), channel_id=1, source_target_pairs={{0,2},{1,3},{2,0},{3,1},{4,6},{5,7},{6,4},{7,5},{8,10},{9,11},{10,... | collective-permute-start | bytes 786440 | tf_op jit(solution)/shard_map/ppermute | solution.py:498
  4.0 1.6 %collective-permute-start = (bf16[128,1024]{1,0:T(8,128)(2,1)}, bf16[128,1024]{1,0:T(8,128)(2,1)S(1)}, u32[]{:S(2)}, u32[]{:S(2)}) collective-permute-start(bf16[128,1024]{1,0:T(8,128)(2,1)} %rest_5_.1), channel_id=1, source_target_pairs={{0,1},{1,2},{2,3},{3,0},{4,5},{5,6},{6,7},{7,4},{8,9},{9,10},{10,1... | collective-permute-start | bytes 786440 | tf_op jit(solution)/shard_map/ppermute | solution.py:498
  5.6 0.7 fusion.65
  6.3 0.8 constant_dynamic-slice_fusion.1
  7.1 0.8 pad_maximum_fusion.3
  7.8 10.0 %all-gather = bf16[1152,256]{1,0:T(8,128)(2,1)S(1)} all-gather(bf16[144,256]{1,0:T(8,128)(2,1)S(1)} %pad_maximum_fusion.3), channel_id=2, replica_groups=mesh['dp'=8,'tensor'=4] {'dp'}, dimensions={0}, use_global_device_ids=true | all-gather | bytes 663552 | tf_op jit(solution)/shard_map/all_gather | solution.py:558
  17.8 0.6 slice_convert_fusion.asked_ref
  18.5 4.4 %pick_pages.1 = (bf16[8,4,128,2,128]{4,3,2,1,0:T(2,128)(2,1)}, bf16[8,4,128,2,128]{4,3,2,1,0:T(2,128)(2,1)}) custom-call(s32[1]{0:T(128)} %bitcast.4.me_ref, s32[8,2,32]{2,1,0:T(2,128)} %slice_convert_fusion.asked_ref, bf16[32,128,2,256]{3,2,1,0:T(2,128)(2,1)} %pool_ref.1), custom_call_target="tpu_custom_call" | custom-call | flops 1000 | bytes 1000 | tf_op jit(solution)/shard_map/pick_pages/pallas_call | solution.py:82
  23.0 0.7 copy-done.11
  23.6 0.7 copy-done.12
  24.4 4.5 %all-to-all-start = ((bf16[8,4,128,2,128]{4,3,2,1,0:T(2,128)(2,1)}), bf16[8,4,128,2,128]{4,3,2,1,0:T(2,128)(2,1)}, u32[]{:S(2)}, u32[]{:S(2)}) async-start(bf16[8,4,128,2,128]{4,3,2,1,0:T(2,128)(2,1)} %get-tuple-element.41), calls=%async_computation | async-start | bytes 4194304 | tf_op jit(solution)/shard_map/all_to_all | solution.py:562
  28.9 2.3 %collective-permute-start.2 = (bf16[128,1024]{1,0:T(8,128)(2,1)S(1)}, bf16[128,1024]{1,0:T(8,128)(2,1)}, u32[]{:S(2)}, u32[]{:S(2)}) collective-permute-start(bf16[128,1024]{1,0:T(8,128)(2,1)S(1)} %copy-done.10), channel_id=1, source_target_pairs={{0,3},{1,0},{2,1},{3,2},{4,7},{5,4},{6,5},{7,6},{8,11},{9,8},{10,9... | collective-permute-start | bytes 786440 | tf_op jit(solution)/shard_map/ppermute | solution.py:498
  31.2 0.6 reshape.131.rest_0_
  31.8 2.2 %named_adapters.1 = (bf16[128,256]{1,0:T(8,128)(2,1)}, bf16[128,256]{1,0:T(8,128)(2,1)}) custom-call(s32[16]{0:T(128)} %table_ref.2, s32[1,4]{1,0:T(1,128)} %ids_ref.1, bf16[8,144,256]{2,1,0:T(8,128)(2,1)} %bitcast.110), custom_call_target="tpu_custom_call" | custom-call | flops 1000 | bytes 1000 | tf_op jit(solution)/shard_map/named_adapters/pallas_call | solution.py:126
  34.2 1.2 collective-permute-start.4
  35.4 0.8 collective-permute-start.3
  36.2 0.2 reduce-window.4
  36.5 3.5 %collective-permute-done.5.rest_12_ = bf16[128,256]{1,0:T(8,128)(2,1)S(1)} collective-permute-done((bf16[128,256]{1,0:T(8,128)(2,1)}, bf16[128,256]{1,0:T(8,128)(2,1)S(1)}, u32[]{:S(2)}, u32[]{:S(2)}) %collective-permute-start.5) | collective-permute-done | bytes 65568 | tf_op jit(solution)/shard_map/ppermute | solution.py:498
  40.1 2.5 %collective-permute-done.4.rest_11_ = bf16[128,256]{1,0:T(8,128)(2,1)S(1)} collective-permute-done((bf16[128,256]{1,0:T(8,128)(2,1)}, bf16[128,256]{1,0:T(8,128)(2,1)S(1)}, u32[]{:S(2)}, u32[]{:S(2)}) %collective-permute-start.4) | collective-permute-done | bytes 65568 | tf_op jit(solution)/shard_map/ppermute | solution.py:498
  42.6 3.7 %collective-permute-start.7 = (bf16[128,1024]{1,0:T(8,128)(2,1)S(1)}, bf16[128,1024]{1,0:T(8,128)(2,1)S(1)}, u32[]{:S(2)}, u32[]{:S(2)}) collective-permute-start(bf16[128,1024]{1,0:T(8,128)(2,1)S(1)} %constant_dynamic-slice_fusion), channel_id=1, source_target_pairs={{0,2},{1,3},{2,0},{3,1},{4,6},{5,7},{6,4},{7,5},{8,10},{9,11},{10,... | collective-permute-start | bytes 786440 | tf_op jit(solution)/shard_map/ppermute | solution.py:498
  46.3 0.2 collective-permute-start.6
  46.5 1.8 %fusion.14 = (f32[512,128]{1,0:T(8,128)}, f32[512,128]{1,0:T(8,128)}) fusion(f32[128]{0:T(128)S(1)} %get-tuple-element.113, f32[128]{0:T(128)S(1)} %get-tuple-element.114, f32[512]{0:T(512)S(1)} %fusion.59), kind=kLoop, calls=%fused_computation.29 | loop fusion | flops 131072 | bytes 527360 | tf_op jit(solution)/shard_map/mul | solution.py:576
  48.4 6.6 %project.1 = (bf16[512,256]{1,0:T(8,128)(2,1)}, bf16[512,256]{1,0:T(8,128)(2,1)}, bf16[512,256]{1,0:T(8,128)(2,1)}, s32[32]{0:T(128)}, bf16[2,4,64,1024]{3,2,1,0:T(8,128)(2,1)}) custom-call(s32[1]{0:T(128)} %bitcast.tp_ref, s32[1,4]{1,0:T(1,128)} %lens_ref.5, s32[1,32]{1,0:T(1,128)} %table_ref.3, bf16[1,1024]{1,0:T(2,128)(2,1)} %reshape.131.rest_0_, ...), custom_call_target="tpu_custom_call" | custom-call | flops 1000 | bytes 1000 | tf_op jit(solution)/shard_map/project/pallas_call | solution.py:248
  55.0 9.2 %collective-permute-done.7 = bf16[128,1024]{1,0:T(8,128)(2,1)S(1)} collective-permute-done((bf16[128,1024]{1,0:T(8,128)(2,1)S(1)}, bf16[128,1024]{1,0:T(8,128)(2,1)S(1)}, u32[]{:S(2)}, u32[]{:S(2)}) %collective-permute-start.7) | collective-permute-done | bytes 262176 | tf_op jit(solution)/shard_map/ppermute | solution.py:498
  64.1 4.4 %all-to-all-start.1 = ((bf16[8,4,128,2,128]{4,3,2,1,0:T(2,128)(2,1)}), bf16[8,4,128,2,128]{4,3,2,1,0:T(2,128)(2,1)}, u32[]{:S(2)}, u32[]{:S(2)}) async-start(bf16[8,4,128,2,128]{4,3,2,1,0:T(2,128)(2,1)} %get-tuple-element.62), calls=%async_computation.1 | async-start | bytes 4194304 | tf_op jit(solution)/shard_map/all_to_all | solution.py:582
  68.6 13.3 %attend.2 = bf16[512,128]{1,0:T(8,128)(2,1)} custom-call(s32[1,4]{1,0:T(1,128)} %lens_ref.5, s32[1,4]{1,0:T(1,128)} %counts_ref.3, s32[32]{0:T(128)} %get-tuple-element.48.pos_ref, f32[2,4]{1,0:T(2,128)} %bias_ref.3, bf16[512,256]{1,0:T(8,128)(2,1)} %get-tuple-element.60.q_ref, bf16[512,256]{1,0:T(8,128)(2,1)} %get-tuple-element.49.kn_ref, ...), custom_call_target="tpu_custom_call" | custom-call | flops 1000 | bytes 1000 | tf_op jit(solution)/shard_map/attend/pallas_call | solution.py:472
  82.0 1.0 pad_maximum_fusion.1
  82.9 0.5 collective-permute-start.9
  83.5 1.4 fusion.75
  84.8 2.5 %collective-permute-start.12 = (bf16[512,128]{1,0:T(8,128)(2,1)S(1)}, bf16[512,128]{1,0:T(8,128)(2,1)S(1)}, u32[]{:S(2)}, u32[]{:S(2)}) collective-permute-start(bf16[512,128]{1,0:T(8,128)(2,1)S(1)} %copy-done.9), channel_id=1, source_target_pairs={{0,3},{1,0},{2,1},{3,2},{4,7},{5,4},{6,5},{7,6},{8,11},{9,8},{10,9... | collective-permute-start | bytes 393224 | tf_op jit(solution)/shard_map/ppermute | solution.py:498
  87.3 0.8 collective-permute-start.11
  88.2 1.8 %maximum_select_fusion = bf16[3,256,1024]{2,1,0:T(8,128)(2,1)S(1)} fusion(bf16[3,128,1024]{2,1,0:T(8,128)(2,1)} %collective-permute-done.9, bf16[1,128,1024]{2,1,0:T(8,128)(2,1)S(1)} %bitcast.122, bf16[1,128,1024]{2,1,0:T(8,128)(2,1)S(1)} %bitcast.118, bf16[1,128,1024]{2,1,0:T(8,128)(2,1)S(1)} %bitcast.120, pred[]{:T(512)S(6)} %eq.35), kind=kLoop, calls=%fused_computation.7 | loop fusion | flops 13369344 | bytes 3145729 | tf_op jit(solution)/shard_map/jit(_where)/select_n | solution.py:504
  90.0 1.5 pad_maximum_fusion
  91.5 8.7 %collective-permute-done.11 = bf16[512,128]{1,0:T(8,128)(2,1)S(1)} collective-permute-done((bf16[512,128]{1,0:T(8,128)(2,1)S(1)}, bf16[512,128]{1,0:T(8,128)(2,1)S(1)}, u32[]{:S(2)}, u32[]{:S(2)}) %collective-permute-start.11) | collective-permute-done | bytes 131104 | tf_op jit(solution)/shard_map/ppermute | solution.py:498
  100.2 0.6 copy-done.15
  100.9 13.6 %attend.3 = bf16[512,128]{1,0:T(8,128)(2,1)} custom-call(s32[1,4]{1,0:T(1,128)} %lens_ref.5, s32[1,4]{1,0:T(1,128)} %counts_ref.3, s32[32]{0:T(128)} %get-tuple-element.48.pos_ref, f32[2,4]{1,0:T(2,128)} %bias_ref.3, bf16[512,256]{1,0:T(8,128)(2,1)} %get-tuple-element.60.q_ref, bf16[512,256]{1,0:T(8,128)(2,1)} %get-tuple-element.49.kn_ref, ...), custom_call_target="tpu_custom_call" | custom-call | flops 1000 | bytes 1000 | tf_op jit(solution)/shard_map/attend/pallas_call | solution.py:472
  114.4 0.9 fusion.76
  115.3 0.3 collective-permute-start.15
  115.7 0.6 collective-permute-start.14
  116.2 1.9 %collective-permute-start.13 = (bf16[256,128]{1,0:T(8,128)(2,1)S(1)}, bf16[256,128]{1,0:T(8,128)(2,1)S(1)}, u32[]{:S(2)}, u32[]{:S(2)}) collective-permute-start(bf16[256,128]{1,0:T(8,128)(2,1)S(1)} %bitcast.131), channel_id=1, source_target_pairs={{0,1},{1,2},{2,3},{3,0},{4,5},{5,6},{6,7},{7,4},{8,9},{9,10},{10,1... | collective-permute-start | bytes 196616 | tf_op jit(solution)/shard_map/ppermute | solution.py:498
  118.2 0.9 fusion.78
  119.2 1.7 %fusion.74 = (bf16[4,1,128,1024]{3,2,1,0:T(8,128)(2,1)S(1)}, bf16[4,1,128,1024]{3,2,1,0:T(8,128)(2,1)S(1)}) fusion(bf16[4,2,128,1024]{3,2,1,0:T(8,128)(2,1)} %bitcast.106), kind=kLoop, calls=%fused_computation.120 | loop fusion | bytes 4194304 | tf_op jit(solution)/shard_map/slice | solution.py:590
  120.9 0.5 convert_add_fusion.1
  121.4 1.9 %collective-permute-start.21 = (bf16[256,128]{1,0:T(8,128)(2,1)S(1)}, bf16[256,128]{1,0:T(8,128)(2,1)S(1)}, u32[]{:S(2)}, u32[]{:S(2)}) collective-permute-start(bf16[256,128]{1,0:T(8,128)(2,1)S(1)} %bitcast.125), channel_id=1, source_target_pairs={{0,3},{1,0},{2,1},{3,2},{4,7},{5,4},{6,5},{7,6},{8,11},{9,8},{10,9... | collective-permute-start | bytes 196616 | tf_op jit(solution)/shard_map/ppermute | solution.py:498
  123.3 0.5 collective-permute-start.20
  123.8 0.5 fusion.32
  124.3 1.8 %collective-permute-start.19 = (bf16[256,128]{1,0:T(8,128)(2,1)S(1)}, bf16[256,128]{1,0:T(8,128)(2,1)S(1)}, u32[]{:S(2)}, u32[]{:S(2)}) collective-permute-start(bf16[256,128]{1,0:T(8,128)(2,1)S(1)} %bitcast.127), channel_id=1, source_target_pairs={{0,1},{1,2},{2,3},{3,0},{4,5},{5,6},{6,7},{7,4},{8,9},{9,10},{10,1... | collective-permute-start | bytes 196616 | tf_op jit(solution)/shard_map/ppermute | solution.py:498
  126.1 0.5 multiply_reduce_fusion.1
  126.7 1.3 convolution_bitcast_fusion.1
  128.0 0.2 fusion.73
  128.3 0.8 fusion.81
  129.1 2.1 %collective-permute-start.18 = (bf16[64,1024]{1,0:T(8,128)(2,1)S(1)}, bf16[64,1024]{1,0:T(8,128)(2,1)S(1)}, u32[]{:S(2)}, u32[]{:S(2)}) collective-permute-start(bf16[64,1024]{1,0:T(8,128)(2,1)S(1)} %get-tuple-element.88), channel_id=1, source_target_pairs={{0,3},{1,0},{2,1},{3,2},{4,7},{5,4},{6,5},{7,6},{8,11},{9,8},{10,9... | collective-permute-start | bytes 393224 | tf_op jit(solution)/shard_map/ppermute | solution.py:498
  131.3 0.6 collective-permute-start.17
  131.8 1.1 collective-permute-start.16
  132.9 0.6 multiply_reduce_fusion
  133.5 1.3 convolution_bitcast_fusion
  134.8 0.1 fusion.72
  135.0 0.8 fusion.82
  135.9 1.9 %collective-permute-start.22 = (bf16[64,1024]{1,0:T(8,128)(2,1)S(1)}, bf16[64,1024]{1,0:T(8,128)(2,1)S(1)}, u32[]{:S(2)}, u32[]{:S(2)}) collective-permute-start(bf16[64,1024]{1,0:T(8,128)(2,1)S(1)} %get-tuple-element.85), channel_id=1, source_target_pairs={{0,1},{1,2},{2,3},{3,0},{4,5},{5,6},{6,7},{7,4},{8,9},{9,10},{10,1... | collective-permute-start | bytes 393224 | tf_op jit(solution)/shard_map/ppermute | solution.py:498
  137.7 2.0 %collective-permute-start.24 = (bf16[64,1024]{1,0:T(8,128)(2,1)S(1)}, bf16[64,1024]{1,0:T(8,128)(2,1)S(1)}, u32[]{:S(2)}, u32[]{:S(2)}) collective-permute-start(bf16[64,1024]{1,0:T(8,128)(2,1)S(1)} %get-tuple-element.86), channel_id=1, source_target_pairs={{0,3},{1,0},{2,1},{3,2},{4,7},{5,4},{6,5},{7,6},{8,11},{9,8},{10,9... | collective-permute-start | bytes 393224 | tf_op jit(solution)/shard_map/ppermute | solution.py:498
  139.8 2.9 %collective-permute-start.23 = (bf16[64,1024]{1,0:T(8,128)(2,1)S(1)}, bf16[64,1024]{1,0:T(8,128)(2,1)S(1)}, u32[]{:S(2)}, u32[]{:S(2)}) collective-permute-start(bf16[64,1024]{1,0:T(8,128)(2,1)S(1)} %get-tuple-element.87), channel_id=1, source_target_pairs={{0,2},{1,3},{2,0},{3,1},{4,6},{5,7},{6,4},{7,5},{8,10},{9,11},{10,... | collective-permute-start | bytes 393224 | tf_op jit(solution)/shard_map/ppermute | solution.py:498
  142.7 5.5 %collective-permute-done.17 = bf16[64,1024]{1,0:T(8,128)(2,1)S(1)} collective-permute-done((bf16[64,1024]{1,0:T(8,128)(2,1)S(1)}, bf16[64,1024]{1,0:T(8,128)(2,1)S(1)}, u32[]{:S(2)}, u32[]{:S(2)}) %collective-permute-start.17) | collective-permute-done | bytes 131104 | tf_op jit(solution)/shard_map/ppermute | solution.py:498
  148.3 5.2 %collective-permute-done.23 = bf16[64,1024]{1,0:T(8,128)(2,1)S(1)} collective-permute-done((bf16[64,1024]{1,0:T(8,128)(2,1)S(1)}, bf16[64,1024]{1,0:T(8,128)(2,1)S(1)}, u32[]{:S(2)}, u32[]{:S(2)}) %collective-permute-start.23) | collective-permute-done | bytes 131104 | tf_op jit(solution)/shard_map/ppermute | solution.py:498
  153.7 0.7 pad_maximum_fusion.2
  (86 shorter events, 0.9 us)
Async XLA Ops:
  0.0 128.2 %copy-start = (bf16[1024,1024]{1,0:T(8,128)(2,1)S(1)}, bf16[1024,1024]{1,0:T(8,128)(2,1)}, u32[]{:S(2)}) copy-start(bf16[1024,1024]{1,0:T(8,128)(2,1)} %param.22) | copy-start | bytes 6291460
  0.0 22.9 %collective-permute-start.1 = (bf16[128,1024]{1,0:T(8,128)(2,1)}, bf16[128,1024]{1,0:T(8,128)(2,1)S(1)}, u32[]{:S(2)}, u32[]{:S(2)}) collective-permute-start(bf16[128,1024]{1,0:T(8,128)(2,1)} %rest_5_.1), channel_id=1, source_target_pairs={{0,2},{1,3},{2,0},{3,1},{4,6},{5,7},{6,4},{7,5},{8,10},{9,11},{10,... | collective-permute-start | bytes 786440 | tf_op jit(solution)/shard_map/ppermute | solution.py:498
  4.0 18.9 %collective-permute-start = (bf16[128,1024]{1,0:T(8,128)(2,1)}, bf16[128,1024]{1,0:T(8,128)(2,1)S(1)}, u32[]{:S(2)}, u32[]{:S(2)}) collective-permute-start(bf16[128,1024]{1,0:T(8,128)(2,1)} %rest_5_.1), channel_id=1, source_target_pairs={{0,1},{1,2},{2,3},{3,0},{4,5},{5,6},{6,7},{7,4},{8,9},{9,10},{10,1... | collective-permute-start | bytes 786440 | tf_op jit(solution)/shard_map/ppermute | solution.py:498
  17.8 5.1 %copy-start.2 = (bf16[1152,256]{1,0:T(8,128)(2,1)}, bf16[1152,256]{1,0:T(8,128)(2,1)S(1)}, u32[]{:S(2)}) copy-start(bf16[1152,256]{1,0:T(8,128)(2,1)S(1)} %all-gather) | copy-start | bytes 1769476
  22.9 0.7 copy-start.11
  23.6 0.7 copy-start.12
  24.4 4.5 %copy-start.10 = (bf16[128,1024]{1,0:T(8,128)(2,1)S(1)}, bf16[128,1024]{1,0:T(8,128)(2,1)}, u32[]{:S(2)}) copy-start(bf16[128,1024]{1,0:T(8,128)(2,1)} %rest_5_.1) | copy-start | bytes 786436
  24.4 6.8 %copy-start.22 = (bf16[1024]{0:T(1024)(128)(2,1)S(1)}, bf16[1024]{0:T(1024)(128)(2,1)}, u32[]{:S(2)}) copy-start(bf16[1024]{0:T(1024)(128)(2,1)} %param.17) | copy-start | bytes 6148
  24.4 7.4 %copy-start.3 = (bf16[256,1024]{1,0:T(8,128)(2,1)S(1)}, bf16[256,1024]{1,0:T(8,128)(2,1)}, u32[]{:S(2)}) copy-start(bf16[256,1024]{1,0:T(8,128)(2,1)} %param.20) | copy-start | bytes 1572868
  24.4 11.8 %copy-start.21 = (s32[1,4]{1,0:T(1,128)S(1)}, s32[1,4]{1,0:T(1,128)}, u32[]{:S(2)}) copy-start(s32[1,4]{1,0:T(1,128)} %lens_ref.5) | copy-start | bytes 52
  24.4 12.1 %copy-start.20 = (s32[1,4]{1,0:T(1,128)S(1)}, s32[1,4]{1,0:T(1,128)}, u32[]{:S(2)}) copy-start(s32[1,4]{1,0:T(1,128)} %counts_ref.3) | copy-start | bytes 52
  24.4 39.8 %all-to-all-start = ((bf16[8,4,128,2,128]{4,3,2,1,0:T(2,128)(2,1)}), bf16[8,4,128,2,128]{4,3,2,1,0:T(2,128)(2,1)}, u32[]{:S(2)}, u32[]{:S(2)}) async-start(bf16[8,4,128,2,128]{4,3,2,1,0:T(2,128)(2,1)} %get-tuple-element.41), calls=%async_computation | async-start | bytes 4194304 | tf_op jit(solution)/shard_map/all_to_all | solution.py:562
  28.9 19.5 %collective-permute-start.2 = (bf16[128,1024]{1,0:T(8,128)(2,1)S(1)}, bf16[128,1024]{1,0:T(8,128)(2,1)}, u32[]{:S(2)}, u32[]{:S(2)}) collective-permute-start(bf16[128,1024]{1,0:T(8,128)(2,1)S(1)} %copy-done.10), channel_id=1, source_target_pairs={{0,3},{1,0},{2,1},{3,2},{4,7},{5,4},{6,5},{7,6},{8,11},{9,8},{10,9... | collective-permute-start | bytes 786440 | tf_op jit(solution)/shard_map/ppermute | solution.py:498
  34.1 6.0 %collective-permute-start.5 = (bf16[128,256]{1,0:T(8,128)(2,1)}, bf16[128,256]{1,0:T(8,128)(2,1)S(1)}, u32[]{:S(2)}, u32[]{:S(2)}) collective-permute-start(bf16[128,256]{1,0:T(8,128)(2,1)} %get-tuple-element.45.rest_9_), channel_id=1, source_target_pairs={{0,3},{1,0},{2,1},{3,2},{4,7},{5,4},{6,5},{7,6},{8,11},{9,8},{10,9... | collective-permute-start | bytes 196616 | tf_op jit(solution)/shard_map/ppermute | solution.py:498
  34.2 8.4 %collective-permute-start.4 = (bf16[128,256]{1,0:T(8,128)(2,1)}, bf16[128,256]{1,0:T(8,128)(2,1)S(1)}, u32[]{:S(2)}, u32[]{:S(2)}) collective-permute-start(bf16[128,256]{1,0:T(8,128)(2,1)} %get-tuple-element.45.rest_9_), channel_id=1, source_target_pairs={{0,2},{1,3},{2,0},{3,1},{4,6},{5,7},{6,4},{7,5},{8,10},{9,11},{10,... | collective-permute-start | bytes 196616 | tf_op jit(solution)/shard_map/ppermute | solution.py:498
  35.4 7.2 %collective-permute-start.3 = (bf16[128,256]{1,0:T(8,128)(2,1)}, bf16[128,256]{1,0:T(8,128)(2,1)S(1)}, u32[]{:S(2)}, u32[]{:S(2)}) collective-permute-start(bf16[128,256]{1,0:T(8,128)(2,1)} %get-tuple-element.45.rest_9_), channel_id=1, source_target_pairs={{0,1},{1,2},{2,3},{3,0},{4,5},{5,6},{6,7},{7,4},{8,9},{9,10},{10,1... | collective-permute-start | bytes 196616 | tf_op jit(solution)/shard_map/ppermute | solution.py:498
  40.1 8.3 %copy-start.17 = (bf16[128,256]{1,0:T(8,128)(2,1)}, bf16[128,256]{1,0:T(8,128)(2,1)S(1)}, u32[]{:S(2)}) copy-start(bf16[128,256]{1,0:T(8,128)(2,1)S(1)} %collective-permute-done.5.rest_12_) | copy-start | bytes 196612
  42.6 5.8 %copy-start.18 = (bf16[128,256]{1,0:T(8,128)(2,1)}, bf16[128,256]{1,0:T(8,128)(2,1)S(1)}, u32[]{:S(2)}) copy-start(bf16[128,256]{1,0:T(8,128)(2,1)S(1)} %collective-permute-done.4.rest_11_) | copy-start | bytes 196612
  42.6 5.8 %copy-start.19 = (bf16[128,256]{1,0:T(8,128)(2,1)}, bf16[128,256]{1,0:T(8,128)(2,1)S(1)}, u32[]{:S(2)}) copy-start(bf16[128,256]{1,0:T(8,128)(2,1)S(1)} %collective-permute-done.3.rest_10_) | copy-start | bytes 196612
  42.6 21.6 %collective-permute-start.7 = (bf16[128,1024]{1,0:T(8,128)(2,1)S(1)}, bf16[128,1024]{1,0:T(8,128)(2,1)S(1)}, u32[]{:S(2)}, u32[]{:S(2)}) collective-permute-start(bf16[128,1024]{1,0:T(8,128)(2,1)S(1)} %constant_dynamic-slice_fusion), channel_id=1, source_target_pairs={{0,2},{1,3},{2,0},{3,1},{4,6},{5,7},{6,4},{7,5},{8,10},{9,11},{10,... | collective-permute-start | bytes 786440 | tf_op jit(solution)/shard_map/ppermute | solution.py:498
  46.3 17.8 %collective-permute-start.6 = (bf16[128,1024]{1,0:T(8,128)(2,1)S(1)}, bf16[128,1024]{1,0:T(8,128)(2,1)S(1)}, u32[]{:S(2)}, u32[]{:S(2)}) collective-permute-start(bf16[128,1024]{1,0:T(8,128)(2,1)S(1)} %constant_dynamic-slice_fusion), channel_id=1, source_target_pairs={{0,1},{1,2},{2,3},{3,0},{4,5},{5,6},{6,7},{7,4},{8,9},{9,10},{10,1... | collective-permute-start | bytes 786440 | tf_op jit(solution)/shard_map/ppermute | solution.py:498
  64.1 17.8 %copy-start.5 = (bf16[128,1024]{1,0:T(8,128)(2,1)}, bf16[128,1024]{1,0:T(8,128)(2,1)S(1)}, u32[]{:S(2)}) copy-start(bf16[128,1024]{1,0:T(8,128)(2,1)S(1)} %collective-permute-done.6) | copy-start | bytes 786436
  64.1 36.7 %all-to-all-start.1 = ((bf16[8,4,128,2,128]{4,3,2,1,0:T(2,128)(2,1)}), bf16[8,4,128,2,128]{4,3,2,1,0:T(2,128)(2,1)}, u32[]{:S(2)}, u32[]{:S(2)}) async-start(bf16[8,4,128,2,128]{4,3,2,1,0:T(2,128)(2,1)} %get-tuple-element.62), calls=%async_computation.1 | async-start | bytes 4194304 | tf_op jit(solution)/shard_map/all_to_all | solution.py:582
  68.5 13.4 %collective-permute-start.8 = (bf16[128,1024]{1,0:T(8,128)(2,1)S(1)}, bf16[128,1024]{1,0:T(8,128)(2,1)S(1)}, u32[]{:S(2)}, u32[]{:S(2)}) collective-permute-start(bf16[128,1024]{1,0:T(8,128)(2,1)S(1)} %constant_dynamic-slice_fusion), channel_id=1, source_target_pairs={{0,3},{1,0},{2,1},{3,2},{4,7},{5,4},{6,5},{7,6},{8,11},{9,8},{10,9... | collective-permute-start | bytes 786440 | tf_op jit(solution)/shard_map/ppermute | solution.py:498
  68.6 14.9 %copy-start.23 = (bf16[1024]{0:T(1024)(128)(2,1)S(1)}, bf16[1024]{0:T(1024)(128)(2,1)}, u32[]{:S(2)}) copy-start(bf16[1024]{0:T(1024)(128)(2,1)} %param.18) | copy-start | bytes 6148
  81.9 2.9 %copy-start.9 = (bf16[512,128]{1,0:T(8,128)(2,1)S(1)}, bf16[512,128]{1,0:T(8,128)(2,1)}, u32[]{:S(2)}) copy-start(bf16[512,128]{1,0:T(8,128)(2,1)} %attend.2) | copy-start | bytes 393220
  81.9 1.0 copy-start.7
  82.9 5.2 %collective-permute-start.9 = (bf16[3,128,1024]{2,1,0:T(8,128)(2,1)}, bf16[3,128,1024]{2,1,0:T(8,128)(2,1)}, u32[]{:S(2)}, u32[]{:S(2)}) collective-permute-start(bf16[3,128,1024]{2,1,0:T(8,128)(2,1)} %pad_maximum_fusion.1), channel_id=1, source_target_pairs={{0,4},{4,0},{8,12},{12,8},{16,20},{20,16},{24,28},{28,24},{1,5},{5... | collective-permute-start | bytes 2359304 | tf_op jit(solution)/shard_map/ppermute | solution.py:503
  83.4 4.7 %copy-start.6 = (bf16[128,1024]{1,0:T(8,128)(2,1)S(1)}, bf16[128,1024]{1,0:T(8,128)(2,1)}, u32[]{:S(2)}) copy-start(bf16[128,1024]{1,0:T(8,128)(2,1)} %copy-done.5) | copy-start | bytes 786436
  83.5 4.7 %copy-start.8 = (bf16[128,1024]{1,0:T(8,128)(2,1)S(1)}, bf16[128,1024]{1,0:T(8,128)(2,1)}, u32[]{:S(2)}) copy-start(bf16[128,1024]{1,0:T(8,128)(2,1)} %copy-done.7) | copy-start | bytes 786436
  84.8 5.1 %copy-start.4 = (bf16[256,1024]{1,0:T(8,128)(2,1)S(1)}, bf16[256,1024]{1,0:T(8,128)(2,1)}, u32[]{:S(2)}) copy-start(bf16[256,1024]{1,0:T(8,128)(2,1)} %param.20) | copy-start | bytes 1572868
  84.8 6.7 %collective-permute-start.12 = (bf16[512,128]{1,0:T(8,128)(2,1)S(1)}, bf16[512,128]{1,0:T(8,128)(2,1)S(1)}, u32[]{:S(2)}, u32[]{:S(2)}) collective-permute-start(bf16[512,128]{1,0:T(8,128)(2,1)S(1)} %copy-done.9), channel_id=1, source_target_pairs={{0,3},{1,0},{2,1},{3,2},{4,7},{5,4},{6,5},{7,6},{8,11},{9,8},{10,9... | collective-permute-start | bytes 393224 | tf_op jit(solution)/shard_map/ppermute | solution.py:498
  87.3 12.9 %collective-permute-start.11 = (bf16[512,128]{1,0:T(8,128)(2,1)S(1)}, bf16[512,128]{1,0:T(8,128)(2,1)S(1)}, u32[]{:S(2)}, u32[]{:S(2)}) collective-permute-start(bf16[512,128]{1,0:T(8,128)(2,1)S(1)} %copy-done.9), channel_id=1, source_target_pairs={{0,2},{1,3},{2,0},{3,1},{4,6},{5,7},{6,4},{7,5},{8,10},{9,11},{10,... | collective-permute-start | bytes 393224 | tf_op jit(solution)/shard_map/ppermute | solution.py:498
  88.1 12.7 %collective-permute-start.10 = (bf16[512,128]{1,0:T(8,128)(2,1)S(1)}, bf16[512,128]{1,0:T(8,128)(2,1)}, u32[]{:S(2)}, u32[]{:S(2)}) collective-permute-start(bf16[512,128]{1,0:T(8,128)(2,1)S(1)} %copy-done.9), channel_id=1, source_target_pairs={{0,1},{1,2},{2,3},{3,0},{4,5},{5,6},{6,7},{7,4},{8,9},{9,10},{10,1... | collective-permute-start | bytes 393224 | tf_op jit(solution)/shard_map/ppermute | solution.py:498
  91.5 8.7 %copy-start.13 = (bf16[512,128]{1,0:T(8,128)(2,1)}, bf16[512,128]{1,0:T(8,128)(2,1)S(1)}, u32[]{:S(2)}) copy-start(bf16[512,128]{1,0:T(8,128)(2,1)S(1)} %collective-permute-done.12) | copy-start | bytes 393220
  100.2 0.6 copy-start.15
  100.8 18.3 %copy-start.16 = (bf16[512,128]{1,0:T(8,128)(2,1)S(1)}, bf16[512,128]{1,0:T(8,128)(2,1)}, u32[]{:S(2)}) copy-start(bf16[512,128]{1,0:T(8,128)(2,1)} %copy-done.15) | copy-start | bytes 393220
  100.9 18.3 %copy-start.14 = (bf16[512,128]{1,0:T(8,128)(2,1)S(1)}, bf16[512,128]{1,0:T(8,128)(2,1)}, u32[]{:S(2)}) copy-start(bf16[512,128]{1,0:T(8,128)(2,1)} %copy-done.13) | copy-start | bytes 393220
  115.3 9.0 %collective-permute-start.15 = (bf16[256,128]{1,0:T(8,128)(2,1)S(1)}, bf16[256,128]{1,0:T(8,128)(2,1)S(1)}, u32[]{:S(2)}, u32[]{:S(2)}) collective-permute-start(bf16[256,128]{1,0:T(8,128)(2,1)S(1)} %bitcast.129), channel_id=1, source_target_pairs={{0,3},{1,0},{2,1},{3,2},{4,7},{5,4},{6,5},{7,6},{8,11},{9,8},{10,9... | collective-permute-start | bytes 196616 | tf_op jit(solution)/shard_map/ppermute | solution.py:498
  115.7 10.4 %collective-permute-start.14 = (bf16[256,128]{1,0:T(8,128)(2,1)S(1)}, bf16[256,128]{1,0:T(8,128)(2,1)S(1)}, u32[]{:S(2)}, u32[]{:S(2)}) collective-permute-start(bf16[256,128]{1,0:T(8,128)(2,1)S(1)} %bitcast.130), channel_id=1, source_target_pairs={{0,2},{1,3},{2,0},{3,1},{4,6},{5,7},{6,4},{7,5},{8,10},{9,11},{10,... | collective-permute-start | bytes 196616 | tf_op jit(solution)/shard_map/ppermute | solution.py:498
  116.2 9.8 %collective-permute-start.13 = (bf16[256,128]{1,0:T(8,128)(2,1)S(1)}, bf16[256,128]{1,0:T(8,128)(2,1)S(1)}, u32[]{:S(2)}, u32[]{:S(2)}) collective-permute-start(bf16[256,128]{1,0:T(8,128)(2,1)S(1)} %bitcast.131), channel_id=1, source_target_pairs={{0,1},{1,2},{2,3},{3,0},{4,5},{5,6},{6,7},{7,4},{8,9},{9,10},{10,1... | collective-permute-start | bytes 196616 | tf_op jit(solution)/shard_map/ppermute | solution.py:498
  121.4 10.5 %collective-permute-start.21 = (bf16[256,128]{1,0:T(8,128)(2,1)S(1)}, bf16[256,128]{1,0:T(8,128)(2,1)S(1)}, u32[]{:S(2)}, u32[]{:S(2)}) collective-permute-start(bf16[256,128]{1,0:T(8,128)(2,1)S(1)} %bitcast.125), channel_id=1, source_target_pairs={{0,3},{1,0},{2,1},{3,2},{4,7},{5,4},{6,5},{7,6},{8,11},{9,8},{10,9... | collective-permute-start | bytes 196616 | tf_op jit(solution)/shard_map/ppermute | solution.py:498
  123.3 9.6 %collective-permute-start.20 = (bf16[256,128]{1,0:T(8,128)(2,1)S(1)}, bf16[256,128]{1,0:T(8,128)(2,1)S(1)}, u32[]{:S(2)}, u32[]{:S(2)}) collective-permute-start(bf16[256,128]{1,0:T(8,128)(2,1)S(1)} %bitcast.126), channel_id=1, source_target_pairs={{0,2},{1,3},{2,0},{3,1},{4,6},{5,7},{6,4},{7,5},{8,10},{9,11},{10,... | collective-permute-start | bytes 196616 | tf_op jit(solution)/shard_map/ppermute | solution.py:498
  123.8 2.8 %copy-start.1 = (bf16[2,1024,1024]{2,1,0:T(8,128)(2,1)S(1)}, bf16[2,1024,1024]{2,1,0:T(8,128)(2,1)}, u32[]{:S(2)}) copy-start(bf16[2,1024,1024]{2,1,0:T(8,128)(2,1)} %param.21) | copy-start | bytes 12582916
  124.3 8.6 %collective-permute-start.19 = (bf16[256,128]{1,0:T(8,128)(2,1)S(1)}, bf16[256,128]{1,0:T(8,128)(2,1)S(1)}, u32[]{:S(2)}, u32[]{:S(2)}) collective-permute-start(bf16[256,128]{1,0:T(8,128)(2,1)S(1)} %bitcast.127), channel_id=1, source_target_pairs={{0,1},{1,2},{2,3},{3,0},{4,5},{5,6},{6,7},{7,4},{8,9},{9,10},{10,1... | collective-permute-start | bytes 196616 | tf_op jit(solution)/shard_map/ppermute | solution.py:498
  129.1 10.7 %collective-permute-start.18 = (bf16[64,1024]{1,0:T(8,128)(2,1)S(1)}, bf16[64,1024]{1,0:T(8,128)(2,1)S(1)}, u32[]{:S(2)}, u32[]{:S(2)}) collective-permute-start(bf16[64,1024]{1,0:T(8,128)(2,1)S(1)} %get-tuple-element.88), channel_id=1, source_target_pairs={{0,3},{1,0},{2,1},{3,2},{4,7},{5,4},{6,5},{7,6},{8,11},{9,8},{10,9... | collective-permute-start | bytes 393224 | tf_op jit(solution)/shard_map/ppermute | solution.py:498
  131.3 17.0 %collective-permute-start.17 = (bf16[64,1024]{1,0:T(8,128)(2,1)S(1)}, bf16[64,1024]{1,0:T(8,128)(2,1)S(1)}, u32[]{:S(2)}, u32[]{:S(2)}) collective-permute-start(bf16[64,1024]{1,0:T(8,128)(2,1)S(1)} %get-tuple-element.89), channel_id=1, source_target_pairs={{0,2},{1,3},{2,0},{3,1},{4,6},{5,7},{6,4},{7,5},{8,10},{9,11},{10,... | collective-permute-start | bytes 393224 | tf_op jit(solution)/shard_map/ppermute | solution.py:498
  131.8 16.4 %collective-permute-start.16 = (bf16[64,1024]{1,0:T(8,128)(2,1)S(1)}, bf16[64,1024]{1,0:T(8,128)(2,1)S(1)}, u32[]{:S(2)}, u32[]{:S(2)}) collective-permute-start(bf16[64,1024]{1,0:T(8,128)(2,1)S(1)} %get-tuple-element.90), channel_id=1, source_target_pairs={{0,1},{1,2},{2,3},{3,0},{4,5},{5,6},{6,7},{7,4},{8,9},{9,10},{10,1... | collective-permute-start | bytes 393224 | tf_op jit(solution)/shard_map/ppermute | solution.py:498
  135.9 12.5 %collective-permute-start.22 = (bf16[64,1024]{1,0:T(8,128)(2,1)S(1)}, bf16[64,1024]{1,0:T(8,128)(2,1)S(1)}, u32[]{:S(2)}, u32[]{:S(2)}) collective-permute-start(bf16[64,1024]{1,0:T(8,128)(2,1)S(1)} %get-tuple-element.85), channel_id=1, source_target_pairs={{0,1},{1,2},{2,3},{3,0},{4,5},{5,6},{6,7},{7,4},{8,9},{9,10},{10,1... | collective-permute-start | bytes 393224 | tf_op jit(solution)/shard_map/ppermute | solution.py:498
  137.7 10.6 %collective-permute-start.24 = (bf16[64,1024]{1,0:T(8,128)(2,1)S(1)}, bf16[64,1024]{1,0:T(8,128)(2,1)S(1)}, u32[]{:S(2)}, u32[]{:S(2)}) collective-permute-start(bf16[64,1024]{1,0:T(8,128)(2,1)S(1)} %get-tuple-element.86), channel_id=1, source_target_pairs={{0,3},{1,0},{2,1},{3,2},{4,7},{5,4},{6,5},{7,6},{8,11},{9,8},{10,9... | collective-permute-start | bytes 393224 | tf_op jit(solution)/shard_map/ppermute | solution.py:498
  139.8 13.8 %collective-permute-start.23 = (bf16[64,1024]{1,0:T(8,128)(2,1)S(1)}, bf16[64,1024]{1,0:T(8,128)(2,1)S(1)}, u32[]{:S(2)}, u32[]{:S(2)}) collective-permute-start(bf16[64,1024]{1,0:T(8,128)(2,1)S(1)} %get-tuple-element.87), channel_id=1, source_target_pairs={{0,2},{1,3},{2,0},{3,1},{4,6},{5,7},{6,4},{7,5},{8,10},{9,11},{10,... | collective-permute-start | bytes 393224 | tf_op jit(solution)/shard_map/ppermute | solution.py:498

commit v6 on v5

--- a/solution.py
+++ b/solution.py
@@ -270,10 +270,11 @@
 
 
 def attend_kernel(
-    group, per, lens_ref, counts_ref, pos_ref, bias_ref,
-    q_ref, kn_ref, vn_ref, raw_ref, out_ref,
-    kc, vc, knp, vnp, qbd, info, sbuf, wbuf, obuf,
+    group, per, n_chunk, lens_ref, counts_ref, pos_ref, bias_ref,
+    q_ref, kn_ref, vn_ref, raw_ref, *rest
 ):
+    out_refs = rest[:-9]
+    kc, vc, knp, vnp, qbd, pairs, sbuf, wbuf, obuf = rest[-9:]
     page_len = kc.shape[1]
     width = q_ref.shape[1]
     rows = q_ref.shape[0]
@@ -296,13 +297,8 @@
             kc[slot + i] = both[:page_len, i * width : (i + 1) * width]
             vc[slot + i] = both[page_len:, i * width : (i + 1) * width]
 
-    for r in range(n_req):
-        unpack(r * n_page)
-    for r in range(n_req):
-        for b in range(1, n_page // BLK):
-            @pl.when(counts_ref[0, r] > b * BLK)
-            def _():
-                unpack(r * n_page + b * BLK)
+    for slot in range(0, n_req * n_page, BLK):
+        unpack(slot)
 
     knp[:back, :] = jnp.zeros((back, width), BF)
     vnp[:back, :] = jnp.zeros((back, width), BF)
@@ -312,181 +308,138 @@
     lane = lax.broadcasted_iota(jnp.int32, (1, width), 1)
     lane_f = lax.broadcasted_iota(jnp.int32, (1, KCH), 1).astype(F32)
     delta = [bias_ref[0, group * per + a] - bias_ref[1, group * per + a] for a in range(per)]
-    starts = [jnp.int32(0)]
-    for r in range(n_req):
-        starts.append(starts[-1] + lens_ref[0, r])
-
-    def tile_body(t, carry):
-        row0 = pl.multiple_of(t * TILE, TILE)
-        qt = q_ref[pl.ds(row0, TILE), :].astype(F32)
+    parts = [slice(a * TILE, (a + 1) * TILE) for a in range(per)]
+    n_all = n_page + n_new
+
+    for t in range(rows // TILE):
+        qt = q_ref[t * TILE : (t + 1) * TILE, :].astype(F32)
         for a in range(per):
             mine = (lane >= a * HD) & (lane < (a + 1) * HD)
-            qbd[a * TILE : (a + 1) * TILE, :] = jnp.where(mine, qt, 0.0).astype(BF)
-
+            qbd[t, parts[a], :] = jnp.where(mine, qt, 0.0).astype(BF)
+
+    def list_pairs(r, carry):
+        start, found = carry
+        end = start + lens_ref[0, r]
+
+        def add(t, found):
+            pairs[0, found] = t
+            pairs[1, found] = r
+            pairs[2, found] = start
+            return found + 1
+
+        return end, lax.fori_loop(start // TILE, (end - 1) // TILE + 1, add, found)
+
+    _, found = lax.fori_loop(0, n_req, list_pairs, (jnp.int32(0), jnp.int32(0)))
+
+    def pair_body(i, carry):
+        t, r, start = pairs[0, i], pairs[1, i], pairs[2, i]
+        row0 = pl.multiple_of(t * TILE, TILE)
+        live = counts_ref[0, r]
+        end = start + lens_ref[0, r]
+        offset = (live * page_len - start).astype(F32)
+        start_f = start.astype(F32)
         row = (row0 + lax.broadcasted_iota(jnp.int32, (TILE, KCH), 0)).astype(F32)
-        start_row = jnp.zeros((TILE, KCH), F32)
-        offset = jnp.zeros((TILE, KCH), F32)
-        blocks = jnp.int32(1)
-        for r in range(n_req):
-            start, end, live = starts[r], starts[r + 1], counts_ref[0, r]
-            inside = (row >= start.astype(F32)) & (row < end.astype(F32))
-            start_row = jnp.where(inside, start.astype(F32), start_row)
-            offset = jnp.where(inside, (live * page_len - start).astype(F32), offset)
-            here = (start < row0 + TILE) & (end > row0)
-            blocks = jnp.maximum(blocks, jnp.where(here, (live + BLK - 1) // BLK, 0))
         var_first = jnp.floor((row + offset + 0.5) * (1.0 / VARLEN)) * VARLEN
-        info[0] = row
-        info[1] = start_row
-        info[2] = var_first
-        info[3] = var_first - offset
-
-        for b in range(n_page // BLK):
-            @pl.when(b < blocks)
-            def _():
-                for i in range(BLK):
-                    sbuf[b * BLK + i] = jnp.full((per * TILE, KCH), NEG, F32)
 
         def scores(keys):
             return lax.dot_general(
-                qbd[...], keys, (((1,), (1,)), ((), ())), preferred_element_type=F32
+                qbd[t], keys, (((1,), (1,)), ((), ())), preferred_element_type=F32
             )
 
-        for r in range(n_req):
-            start, end, live = starts[r], starts[r + 1], counts_ref[0, r]
-            here = (start < row0 + TILE) & (end > row0)
-            for b in range(n_page // BLK):
-                @pl.when(here & (live > b * BLK))
-                def _():
-                    s_all = scores(
-                        kc[r * n_page + b * BLK : r * n_page + (b + 1) * BLK].reshape(
-                            BLK * page_len, width
-                        )
-                    )
-                    row = info[0]
-                    inside = (row >= start.astype(F32)) & (row < end.astype(F32))
-                    for i in range(BLK):
-                        page = b * BLK + i
-                        dead = jnp.where(page < live, 0.0, NEG)
-                        same = info[2] <= lane_f + page * page_len
-                        for a in range(per):
-                            part = slice(a * TILE, (a + 1) * TILE)
-                            s = s_all[part, i * KCH : (i + 1) * KCH]
-                            s = s + jnp.where(same, delta[a] + dead, dead)
-                            sbuf[page, part, :] = jnp.where(inside, s, sbuf[page, part, :])
-
-        s_all = scores(knp[pl.ds(row0, back + TILE), :])
-        for i in range(n_new):
-            key_row = lane_f + (row0 - back + i * KCH).astype(F32)
-            allowed = (key_row >= info[1]) & (key_row <= info[0])
-            same = info[3] <= key_row
-            for a in range(per):
-                part = slice(a * TILE, (a + 1) * TILE)
-                s = s_all[part, i * KCH : (i + 1) * KCH]
-                s = jnp.where(allowed, s + jnp.where(same, delta[a], 0.0), NEG)
-                sbuf[n_page + i, part, :] = s
-
-        for a in range(per):
-            part = slice(a * TILE, (a + 1) * TILE)
-
-            def top_block(b, top):
-                for i in range(BLK):
-                    top = jnp.maximum(top, sbuf[b * BLK + i, part, :])
-                return top
-
-            top = sbuf[n_page, part, :]
-            for i in range(1, n_new):
-                top = jnp.maximum(top, sbuf[n_page + i, part, :])
-            top = lax.fori_loop(0, blocks, top_block, top)
-            peak = jnp.broadcast_to(jnp.max(top, axis=1, keepdims=True), (TILE, KCH))
-
-            def weigh(c, total):
-                p = jnp.exp(sbuf[c, part, :] - peak)
-                sbuf[c, part, :] = p
-                return total + p
-
-            def weigh_block(b, total):
-                for i in range(BLK):
-                    total = weigh(b * BLK + i, total)
-                return total
-
-            total = jnp.zeros((TILE, KCH), F32)
-            for i in range(n_new):
-                total = weigh(n_page + i, total)
-            total = lax.fori_loop(0, blocks, weigh_block, total)
-            inverse = jnp.broadcast_to(
-                1.0 / jnp.sum(total, axis=1, keepdims=True), (TILE, KCH)
-            )
-            for i in range(n_new):
-                c = n_page + i
-                wbuf[part, c * KCH : (c + 1) * KCH] = (sbuf[c, part, :] * inverse).astype(BF)
-            for b in range(n_page // BLK):
-                @pl.when(b < blocks)
-                def _():
-                    for i in range(BLK):
-                        c = b * BLK + i
-                        wbuf[part, c * KCH : (c + 1) * KCH] = (
-                            sbuf[c, part, :] * inverse
-                        ).astype(BF)
-
-        obuf[...] = jnp.dot(
+        first = r * n_page
+        s_page = scores(kc[pl.ds(first, n_page)].reshape(n_page * page_len, width))
+        s_new = scores(knp[pl.ds(row0, back + TILE), :])
+        top = [None] * per
+        for c in range(n_all):
+            if c < n_page:
+                dead = jnp.where(c < live, 0.0, NEG)
+                same = var_first <= lane_f + c * page_len
+            else:
+                key_row = lane_f + (row0 - back + (c - n_page) * KCH).astype(F32)
+                allowed = (key_row >= start_f) & (key_row <= row)
+                same = var_first - offset <= key_row
+            for a, p in enumerate(parts):
+                if c < n_page:
+                    v = s_page[p, c * KCH : (c + 1) * KCH]
+                    v = v + jnp.where(same, delta[a] + dead, dead)
+                else:
+                    v = s_new[p, (c - n_page) * KCH : (c - n_page + 1) * KCH]
+                    v = jnp.where(allowed, v + jnp.where(same, delta[a], 0.0), NEG)
+                sbuf[c, p, :] = v
+                top[a] = v if top[a] is None else jnp.maximum(top[a], v)
+        peak = [jnp.broadcast_to(jnp.max(x, axis=1, keepdims=True), (TILE, KCH)) for x in top]
+        total = [jnp.zeros((TILE, KCH), F32) for _ in parts]
+        for c in range(n_all):
+            for a, p in enumerate(parts):
+                e = jnp.exp(sbuf[c, p, :] - peak[a])
+                sbuf[c, p, :] = e
+                total[a] = total[a] + e
+        inverse = [
+            jnp.broadcast_to(1.0 / jnp.sum(x, axis=1, keepdims=True), (TILE, KCH)) for x in total
+        ]
+        for c in range(n_all):
+            for a, p in enumerate(parts):
+                wbuf[p, c * KCH : (c + 1) * KCH] = (sbuf[c, p, :] * inverse[a]).astype(BF)
+        o = jnp.dot(
+            wbuf[:, : n_page * KCH],
+            vc[pl.ds(first, n_page)].reshape(n_page * page_len, width),
+            preferred_element_type=F32,
+        ) + jnp.dot(
             wbuf[:, n_page * KCH :], vnp[pl.ds(row0, back + TILE), :],
             preferred_element_type=F32,
         )
-        for r in range(n_req):
-            start, end, live = starts[r], starts[r + 1], counts_ref[0, r]
-            here = (start < row0 + TILE) & (end > row0)
-            for b in range(n_page // BLK):
-                @pl.when(here & (live > b * BLK))
-                def _():
-                    o = jnp.dot(
-                        wbuf[:, b * BLK * KCH : (b + 1) * BLK * KCH],
-                        vc[r * n_page + b * BLK : r * n_page + (b + 1) * BLK].reshape(
-                            BLK * page_len, width
-                        ),
-                        preferred_element_type=F32,
-                    )
-                    row = info[0]
-                    inside = (row >= start.astype(F32)) & (row < end.astype(F32))
-                    for a in range(per):
-                        part = slice(a * TILE, (a + 1) * TILE)
-                        before = obuf[part, :]
-                        obuf[part, :] = jnp.where(inside[:, :width], before + o[part], before)
-        o = obuf[:TILE, :]
+        mixed = o[parts[0]]
         for a in range(1, per):
-            o = jnp.where(lane >= a * HD, obuf[a * TILE : (a + 1) * TILE, :], o)
-        out_ref[pl.ds(row0, TILE), :] = o.astype(BF)
+            mixed = jnp.where(lane >= a * HD, o[parts[a]], mixed)
+        inside = (row >= start_f) & (row < end.astype(F32))
+        obuf[t] = jnp.where(inside[:, :width], mixed, obuf[t])
         return carry
 
-    lax.fori_loop(0, rows // TILE, tile_body, 0)
-
-
-def attend(group, lanes, most, lens, counts, pos, bias, q, kn, vn, raw):
+    lax.fori_loop(0, found, pair_body, 0)
+    per_chunk = rows // n_chunk
+    for t in range(rows // TILE):
+        if n_chunk == 1:
+            out_refs[0][t * TILE : (t + 1) * TILE, :] = obuf[t].astype(BF)
+            continue
+        sub = TILE // n_chunk
+        for c in range(n_chunk):
+            part = obuf[t, c * sub : (c + 1) * sub, :].astype(BF)
+            if len(out_refs) == 1:
+                base = c * per_chunk + t * sub
+                out_refs[0][base : base + sub, :] = part
+            else:
+                out_refs[c][t * sub : (t + 1) * sub, :] = part
+
+
+def attend(group, lanes, most, n_chunk, apart, lens, counts, pos, bias, q, kn, vn, raw):
     rows = q.shape[0]
     per = lanes // HD
     page_len = raw.shape[1] // 2
     slots = raw.shape[0]
     back = -(-most // KCH) * KCH
     n_all = PAGES_REQ + (back + TILE) // KCH
+    n_out = n_chunk if apart else 1
+    tiles = rows // TILE
     smem = pl.BlockSpec(memory_space=pltpu.SMEM)
     part = pl.BlockSpec((rows, lanes), lambda i: (0, group))
     return pl.pallas_call(
-        functools.partial(attend_kernel, group, per),
+        functools.partial(attend_kernel, group, per, n_chunk),
         grid=(1,),
-        out_shape=jax.ShapeDtypeStruct((rows, lanes), BF),
+        out_shape=[jax.ShapeDtypeStruct((rows // n_out, lanes), BF)] * n_out,
         in_specs=[smem] * 4
         + [part] * 3
         + [pl.BlockSpec(raw.shape, lambda i: (0, 0, 0), pipeline_mode=pl.Buffered(1))],
-        out_specs=pl.BlockSpec((rows, lanes), lambda i: (0, 0)),
+        out_specs=[pl.BlockSpec((rows // n_out, lanes), lambda i: (0, 0))] * n_out,
         scratch_shapes=[
             pltpu.VMEM((slots, page_len, lanes), BF),
             pltpu.VMEM((slots, page_len, lanes), BF),
             pltpu.VMEM((back + rows, lanes), BF),
             pltpu.VMEM((back + rows, lanes), BF),
-            pltpu.VMEM((per * TILE, lanes), BF),
-            pltpu.VMEM((4, TILE, KCH), F32),
+            pltpu.VMEM((tiles, per * TILE, lanes), BF),
+            pltpu.SMEM((3, tiles + lens.shape[1]), jnp.int32),
             pltpu.VMEM((n_all, per * TILE, KCH), F32),
             pltpu.VMEM((per * TILE, n_all * KCH), BF),
-            pltpu.VMEM((per * TILE, lanes), F32),
+            pltpu.VMEM((tiles, TILE, lanes), F32),
         ],
         compiler_params=pltpu.CompilerParams(vmem_limit_bytes=60 << 20),
         cost_estimate=LIGHT,
@@ -498,15 +451,22 @@
     return lax.ppermute(value, axis, [(i, (i + k) % n) for i in range(n)])
 
 
-def whole_weight(own, halves, dp, n_dp):
-    halves = jnp.stack(halves)
-    twins = lax.ppermute(halves, "dp", [(i, i ^ 1) for i in range(n_dp)])
-    rest = jnp.where(
-        dp % 2 == 0,
-        jnp.concatenate([halves, twins], axis=1),
-        jnp.concatenate([twins, halves], axis=1),
-    )
-    return jnp.concatenate([own[None], rest], axis=0)
+def whole_weight(own, halves, dp, n_dp, n_group):
+    twins = lax.ppermute(jnp.stack(halves), "dp", [(i, i ^ 1) for i in range(n_dp)])
+    first = dp % 2 == 0
+    lower = [jnp.where(first, h, twins[k]) for k, h in enumerate(halves)]
+    upper = [jnp.where(first, twins[k], h) for k, h in enumerate(halves)]
+    if n_group == 2:
+        own_parts = jnp.split(own, 2)
+        return [
+            jnp.concatenate([mine] + part, axis=0)
+            for mine, part in zip(own_parts, (lower, upper))
+        ]
+    both = [x for pair in zip(lower, upper) for x in pair]
+    whole = jnp.concatenate([own] + both, axis=0)
+    width, d_model = own.shape
+    parts = whole.reshape(len(halves) + 1, n_group, width // n_group, d_model)
+    return [parts[:, a].reshape(-1, d_model) for a in range(n_group)]
 
 
 def per_device(
@@ -578,45 +538,37 @@
     own_half = lax.optimization_barrier((own_half, downs[1:]))[0]
     halves = [shift(own_half, "tensor", n_tp, k) for k in far_first]
     for a in range(1, n_group):
-        send = lax.optimization_barrier((picked[a], fetched[-1], query, halves[:-1]))[0]
+        send = lax.optimization_barrier((picked[a], fetched[-1], query, halves[:1]))[0]
         fetched.append(lax.all_to_all(send, "dp", split_axis=0, concat_axis=0, tiled=True))
     fetched = [f.reshape(slots, 2 * page_len, lanes) for f in fetched]
 
 
     def mixed(blocks, a):
-        w_parts = w_whole.reshape(n_tp, n_group, lanes, d_model)
         return jnp.dot(
-            jnp.concatenate(blocks, axis=1),
-            w_parts[:, a].reshape(n_tp * lanes, d_model),
-            preferred_element_type=F32,
+            jnp.concatenate(blocks, axis=1), w_whole[a], preferred_element_type=F32
         )
 
-    def attended(a, q):
+    def attended(a, q, apart):
         return attend(
-            a, lanes, 2 * TILE, lengths, page_counts, buffer_pos, variate_bias,
+            a, lanes, 2 * TILE, n_chunk, apart, lengths, page_counts, buffer_pos, variate_bias,
             q, new_keys, new_values, fetched[a],
         )
-
-    def by_chunk(mix):
-        mix = mix.reshape(n_tp, n_chunk, sub, lanes)
-        return [mix[:, c].reshape(n_tp * sub, lanes) for c in range(n_chunk)]
 
     early = []
     w_whole = None
     for a in range(n_group - 1):
-        mix = attended(a, query)
+        mix = attended(a, query, False)[0]
         if w_whole is None:
             mix, halves = lax.optimization_barrier((mix, halves))
-            w_whole = whole_weight(w_out, halves, dp, n_dp)
+            w_whole = whole_weight(w_out, halves, dp, n_dp, n_group)
         blocks = [mix] + [shift(mix, "tensor", n_tp, k) for k in far_first]
         query, w_whole, blocks = lax.optimization_barrier((query, w_whole, blocks))
         early.append(blocks)
     if w_whole is None:
-        w_whole = whole_weight(w_out, halves, dp, n_dp)
-    last = attended(n_group - 1, query)
+        w_whole = whole_weight(w_out, halves, dp, n_dp, n_group)
+    last = attended(n_group - 1, query, True)
     early, last, w_whole = lax.optimization_barrier((early, last, w_whole))
-    early = [[by_chunk(block) for block in blocks] for blocks in early]
-    last = by_chunk(last)
+    early = [[jnp.split(block, n_chunk) for block in blocks] for blocks in early]
     outs = []
     pieces = None
     bases = []

time: 155 us -> 149 us (0.961); the launches traced: 154 us -> 147 us
  waiting for transfers between devices: 34.7 us -> 25.5 us
  starting transfers between devices: 44.4 us -> 49.9 us
  Pallas kernels: 40.2 us -> 35.2 us
    ppermute x24, waiting for transfers between devices: 34.7 us -> 23.6 us  [shift(): return lax.ppermute(value, axis, [(i, (i + k) % n) for i in range(n)])]
    ppermute x24, starting transfers between devices: 35.1 us -> 41.1 us  [shift(): return lax.ppermute(value, axis, [(i, (i + k) % n) for i in range(n)])]
    pallas_call x2, Pallas kernels: 26.9 us -> 21.7 us  [attend(): pl.pallas_call(functools.partial(attend_kernel, group, per, n_chunk), gri...]
    slice x6 -> x0, local copies, waits for them, and re-layouts: 3.51 us -> none  [the longest x5 1.8 us: by_chunk(): return [mix[:, c].reshape(n_tp * sub, lanes) for c in range(n_chunk)]]
    split x0 -> x5, local copies, waits for them, and re-layouts: none -> 2.66 us  [the longest x4 1.79 us: per_device(): jnp.split(block, n_chunk)]
    all_to_all x2, waiting for transfers between devices: 0.01 us -> 1.87 us  [per_device(): lax.all_to_all(send, 'dp', split_axis=0, concat_axis=0, tiled=True)]
  transfers between devices with their start and end apart: 27 -> 27, of which waited for: 6 -> 9; matrix products, arithmetic and copies ran while one was open for 14% -> 15% of each run, Pallas kernels for 17% -> 17%
where the time goes in v6:
time: 149 us; the launch traced here: 147 us
  starting transfers between devices  49.9 us (33%)
  Pallas kernels  35.2 us (24%)
  waiting for transfers between devices  25.5 us (17%)
  blocking collectives  9.99 us (7%)
  other arithmetic  9.59 us (6%)
  local copies, waits for them, and re-layouts  8.58 us (6%)
  matrix products  7.59 us (5%)
    ppermute x24, starting transfers between devices, shift(): return lax.ppermute(value, axis, [(i, (i + k) % n) for i in range(n)])  41.1 us
    ppermute x24, waiting for transfers between devices, shift(): return lax.ppermute(value, axis, [(i, (i + k) % n) for i in range(n)])  23.6 us
    pallas_call x2, Pallas kernels, attend(): pl.pallas_call(functools.partial(attend_kernel, group, per, n_chunk), gri...  21.7 us
    all_gather x1, blocking collectives, per_device(): gathered = lax.all_gather(payload, 'dp', axis=0)  9.99 us
    all_to_all x2, starting transfers between devices, per_device(): lax.all_to_all(send, 'dp', split_axis=0, concat_axis=0, tiled=True)  8.73 us
    pallas_call x1, Pallas kernels, project(): pl.pallas_call(functools.partial(project_kernel, n_tp, cap, pool_dev), ou...  6.55 us
    pallas_call x1, Pallas kernels, pick(): pl.pallas_call(functools.partial(pick_kernel, n_dp, cap), out_shape=[jax....  4.73 us
    dot_general x4, matrix products, mixed(): jnp.dot(jnp.concatenate(blocks, axis=1), w_whole[a], preferred_element_ty...  3.24 us
  transfers between devices with their start and end apart: 27, of which 9 were waited for; matrix products, arithmetic and copies ran while one was open for 15% of the time, Pallas kernels for 17%

profile of v6, /device:TPU:0, one launch (start us, length us, event | category | flops | bytes accessed | tf_op | source)
XLA Modules:
  0.0 146.8 jit_solution(4453531754011539394)
XLA Ops:
  0.0 3.0 %collective-permute-start = (bf16[128,1024]{1,0:T(8,128)(2,1)}, bf16[128,1024]{1,0:T(8,128)(2,1)S(1)}, u32[]{:S(2)}, u32[]{:S(2)}) collective-permute-start(bf16[128,1024]{1,0:T(8,128)(2,1)} %rest_5_.1), channel_id=1, source_target_pairs={{0,1},{1,2},{2,3},{3,0},{4,5},{5,6},{6,7},{7,4},{8,9},{9,10},{10,1... | collective-permute-start | bytes 786440 | tf_op jit(solution)/shard_map/ppermute | solution.py:451
  3.0 2.6 %collective-permute-start.1 = (bf16[128,1024]{1,0:T(8,128)(2,1)}, bf16[128,1024]{1,0:T(8,128)(2,1)S(1)}, u32[]{:S(2)}, u32[]{:S(2)}) collective-permute-start(bf16[128,1024]{1,0:T(8,128)(2,1)} %rest_5_.1), channel_id=1, source_target_pairs={{0,2},{1,3},{2,0},{3,1},{4,6},{5,7},{6,4},{7,5},{8,10},{9,11},{10,... | collective-permute-start | bytes 786440 | tf_op jit(solution)/shard_map/ppermute | solution.py:451
  5.6 0.7 fusion.65
  6.3 0.8 constant_dynamic-slice_fusion.1
  7.1 0.8 pad_maximum_fusion.4
  7.8 10.0 %all-gather = bf16[1152,256]{1,0:T(8,128)(2,1)S(1)} all-gather(bf16[144,256]{1,0:T(8,128)(2,1)S(1)} %pad_maximum_fusion.4), channel_id=2, replica_groups=mesh['dp'=8,'tensor'=4] {'dp'}, dimensions={0}, use_global_device_ids=true | all-gather | bytes 663552 | tf_op jit(solution)/shard_map/all_gather | solution.py:518
  17.8 0.6 slice_convert_fusion.asked_ref
  18.5 4.7 %pick_pages.1 = (bf16[8,4,128,2,128]{4,3,2,1,0:T(2,128)(2,1)}, bf16[8,4,128,2,128]{4,3,2,1,0:T(2,128)(2,1)}) custom-call(s32[1]{0:T(128)} %bitcast.4.me_ref, s32[8,2,32]{2,1,0:T(2,128)} %slice_convert_fusion.asked_ref, bf16[32,128,2,256]{3,2,1,0:T(2,128)(2,1)} %pool_ref.1), custom_call_target="tpu_custom_call" | custom-call | flops 1000 | bytes 1000 | tf_op jit(solution)/shard_map/pick_pages/pallas_call | solution.py:82
  23.3 0.6 copy-done.15
  24.0 4.4 %all-to-all-start = ((bf16[8,4,128,2,128]{4,3,2,1,0:T(2,128)(2,1)}), bf16[8,4,128,2,128]{4,3,2,1,0:T(2,128)(2,1)}, u32[]{:S(2)}, u32[]{:S(2)}) async-start(bf16[8,4,128,2,128]{4,3,2,1,0:T(2,128)(2,1)} %get-tuple-element.46), calls=%async_computation | async-start | bytes 4194304 | tf_op jit(solution)/shard_map/all_to_all | solution.py:522
  28.4 1.4 collective-permute-start.2
  29.8 0.6 reshape.110.rest_0_
  30.5 0.9 fusion.75
  31.3 2.2 %named_adapters.1 = (bf16[128,256]{1,0:T(8,128)(2,1)}, bf16[128,256]{1,0:T(8,128)(2,1)}) custom-call(s32[16]{0:T(128)} %table_ref.2, s32[1,4]{1,0:T(1,128)} %ids_ref.1, bf16[8,144,256]{2,1,0:T(8,128)(2,1)} %bitcast.104), custom_call_target="tpu_custom_call" | custom-call | flops 1000 | bytes 1000 | tf_op jit(solution)/shard_map/named_adapters/pallas_call | solution.py:126
  33.6 0.7 collective-permute-start.3
  34.6 2.8 %collective-permute-start.5 = (bf16[128,256]{1,0:T(8,128)(2,1)}, bf16[128,256]{1,0:T(8,128)(2,1)S(1)}, u32[]{:S(2)}, u32[]{:S(2)}) collective-permute-start(bf16[128,256]{1,0:T(8,128)(2,1)} %get-tuple-element.50.rest_9_), channel_id=1, source_target_pairs={{0,3},{1,0},{2,1},{3,2},{4,7},{5,4},{6,5},{7,6},{8,11},{9,8},{10,9... | collective-permute-start | bytes 196616 | tf_op jit(solution)/shard_map/ppermute | solution.py:451
  37.8 2.8 %collective-permute-done.3.rest_10_ = bf16[128,256]{1,0:T(8,128)(2,1)S(1)} collective-permute-done((bf16[128,256]{1,0:T(8,128)(2,1)}, bf16[128,256]{1,0:T(8,128)(2,1)S(1)}, u32[]{:S(2)}, u32[]{:S(2)}) %collective-permute-start.3) | collective-permute-done | bytes 65568 | tf_op jit(solution)/shard_map/ppermute | solution.py:451
  40.6 2.1 %collective-permute-done.4.rest_11_ = bf16[128,256]{1,0:T(8,128)(2,1)S(1)} collective-permute-done((bf16[128,256]{1,0:T(8,128)(2,1)}, bf16[128,256]{1,0:T(8,128)(2,1)S(1)}, u32[]{:S(2)}, u32[]{:S(2)}) %collective-permute-start.4) | collective-permute-done | bytes 65568 | tf_op jit(solution)/shard_map/ppermute | solution.py:451
  42.7 1.4 collective-permute-start.6
  44.1 1.8 %fusion.14 = (f32[512,128]{1,0:T(8,128)}, f32[512,128]{1,0:T(8,128)}) fusion(f32[128]{0:T(128)S(1)} %get-tuple-element.132, f32[128]{0:T(128)S(1)} %get-tuple-element.133, f32[512]{0:T(512)S(1)} %fusion.59), kind=kLoop, calls=%fused_computation.29 | loop fusion | flops 131072 | bytes 527360 | tf_op jit(solution)/shard_map/mul | solution.py:536
  45.9 0.7 copy-done.17
  46.6 6.5 %project.1 = (bf16[512,256]{1,0:T(8,128)(2,1)}, bf16[512,256]{1,0:T(8,128)(2,1)}, bf16[512,256]{1,0:T(8,128)(2,1)}, s32[32]{0:T(128)}, bf16[2,4,64,1024]{3,2,1,0:T(8,128)(2,1)}) custom-call(s32[1]{0:T(128)} %bitcast.tp_ref, s32[1,4]{1,0:T(1,128)} %lens_ref.5, s32[1,32]{1,0:T(1,128)} %table_ref.3, bf16[1,1024]{1,0:T(2,128)(2,1)} %reshape.110.rest_0_, ...), custom_call_target="tpu_custom_call" | custom-call | flops 1000 | bytes 1000 | tf_op jit(solution)/shard_map/project/pallas_call | solution.py:248
  53.2 1.9 %all-to-all-done = bf16[8,4,128,2,128]{4,3,2,1,0:T(2,128)(2,1)} async-done(((bf16[8,4,128,2,128]{4,3,2,1,0:T(2,128)(2,1)}), bf16[8,4,128,2,128]{4,3,2,1,0:T(2,128)(2,1)}, u32[]{:S(2)}, u32[]{:S(2)}) %all-to-all-start) | async-done | bytes 2097184 | tf_op jit(solution)/shard_map/all_to_all | solution.py:522
  55.1 4.4 %all-to-all-start.1 = ((bf16[8,4,128,2,128]{4,3,2,1,0:T(2,128)(2,1)}), bf16[8,4,128,2,128]{4,3,2,1,0:T(2,128)(2,1)}, u32[]{:S(2)}, u32[]{:S(2)}) async-start(bf16[8,4,128,2,128]{4,3,2,1,0:T(2,128)(2,1)} %get-tuple-element.67), calls=%async_computation.1 | async-start | bytes 4194304 | tf_op jit(solution)/shard_map/all_to_all | solution.py:542
  59.4 0.6 collective-permute-start.7
  60.1 2.0 %collective-permute-start.8 = (bf16[128,1024]{1,0:T(8,128)(2,1)}, bf16[128,1024]{1,0:T(8,128)(2,1)S(1)}, u32[]{:S(2)}, u32[]{:S(2)}) collective-permute-start(bf16[128,1024]{1,0:T(8,128)(2,1)} %get-tuple-element.56), channel_id=1, source_target_pairs={{0,3},{1,0},{2,1},{3,2},{4,7},{5,4},{6,5},{7,6},{8,11},{9,8},{10,9... | collective-permute-start | bytes 786440 | tf_op jit(solution)/shard_map/ppermute | solution.py:451
  62.1 10.9 %attend.2 = bf16[512,128]{1,0:T(8,128)(2,1)} custom-call(s32[1,4]{1,0:T(1,128)} %lens_ref.5, s32[1,4]{1,0:T(1,128)} %counts_ref.3, s32[32]{0:T(128)} %get-tuple-element.53.pos_ref, f32[2,4]{1,0:T(2,128)} %bias_ref.3, bf16[512,256]{1,0:T(8,128)(2,1)} %get-tuple-element.65.q_ref, bf16[512,256]{1,0:T(8,128)(2,1)} %get-tuple-element.54.kn_ref, ...), custom_call_target="tpu_custom_call" | custom-call | flops 1000 | bytes 1000 | tf_op jit(solution)/shard_map/attend/pallas_call | solution.py:425
  72.9 1.5 %collective-permute-done.7 = bf16[128,1024]{1,0:T(8,128)(2,1)S(1)} collective-permute-done((bf16[128,1024]{1,0:T(8,128)(2,1)}, bf16[128,1024]{1,0:T(8,128)(2,1)S(1)}, u32[]{:S(2)}, u32[]{:S(2)}) %collective-permute-start.7) | collective-permute-done | bytes 262176 | tf_op jit(solution)/shard_map/ppermute | solution.py:451
  74.5 0.7 copy-done.9
  75.2 1.9 %pad_maximum_fusion.2 = bf16[3,128,1024]{2,1,0:T(8,128)(2,1)} fusion(bf16[1,128,1024]{2,1,0:T(8,128)(2,1)S(1)} %bitcast.111, bf16[1,128,1024]{2,1,0:T(8,128)(2,1)S(1)} %bitcast.110, bf16[1,128,1024]{2,1,0:T(8,128)(2,1)} %bitcast.12), kind=kLoop, calls=%fused_computation.18 | loop fusion | flops 786432 | bytes 1572864 | tf_op jit(solution)/shard_map/stack | solution.py:455
  77.2 1.1 fusion.74
  78.3 5.6 %collective-permute-start.10 = (bf16[512,128]{1,0:T(8,128)(2,1)S(1)}, bf16[512,128]{1,0:T(8,128)(2,1)S(1)}, u32[]{:S(2)}, u32[]{:S(2)}) collective-permute-start(bf16[512,128]{1,0:T(8,128)(2,1)S(1)} %copy-done.13), channel_id=1, source_target_pairs={{0,1},{1,2},{2,3},{3,0},{4,5},{5,6},{6,7},{7,4},{8,9},{9,10},{10,1... | collective-permute-start | bytes 393224 | tf_op jit(solution)/shard_map/ppermute | solution.py:451
  83.9 2.2 %collective-permute-start.11 = (bf16[512,128]{1,0:T(8,128)(2,1)S(1)}, bf16[512,128]{1,0:T(8,128)(2,1)S(1)}, u32[]{:S(2)}, u32[]{:S(2)}) collective-permute-start(bf16[512,128]{1,0:T(8,128)(2,1)S(1)} %copy-done.13), channel_id=1, source_target_pairs={{0,2},{1,3},{2,0},{3,1},{4,6},{5,7},{6,4},{7,5},{8,10},{9,11},{10,... | collective-permute-start | bytes 393224 | tf_op jit(solution)/shard_map/ppermute | solution.py:451
  86.3 1.3 broadcast_select_fusion.2
  87.7 1.1 pad_maximum_fusion
  88.8 1.1 collective-permute-done.10
  90.0 5.4 %collective-permute-done.11 = bf16[512,128]{1,0:T(8,128)(2,1)S(1)} collective-permute-done((bf16[512,128]{1,0:T(8,128)(2,1)S(1)}, bf16[512,128]{1,0:T(8,128)(2,1)S(1)}, u32[]{:S(2)}, u32[]{:S(2)}) %collective-permute-start.11) | collective-permute-done | bytes 131104 | tf_op jit(solution)/shard_map/ppermute | solution.py:451
  95.3 0.7 copy-done.20
  96.0 10.8 %attend.3 = (bf16[256,128]{1,0:T(8,128)(2,1)}, bf16[256,128]{1,0:T(8,128)(2,1)}) custom-call(s32[1,4]{1,0:T(1,128)} %lens_ref.5, s32[1,4]{1,0:T(1,128)} %counts_ref.3, s32[32]{0:T(128)} %get-tuple-element.53.pos_ref, f32[2,4]{1,0:T(2,128)} %bias_ref.3, bf16[512,256]{1,0:T(8,128)(2,1)} %get-tuple-element.65.q_ref, bf16[512,256]{1,0:T(8,128)(2,1)} %get-tuple-element.54.kn_ref, ...), custom_call_target="tpu_custom_call" | custom-call | flops 1000 | bytes 1000 | tf_op jit(solution)/shard_map/attend/pallas_call | solution.py:425
  106.9 2.8 %collective-permute-start.13 = (bf16[256,128]{1,0:T(8,128)(2,1)}, bf16[256,128]{1,0:T(8,128)(2,1)S(1)}, u32[]{:S(2)}, u32[]{:S(2)}) collective-permute-start(bf16[256,128]{1,0:T(8,128)(2,1)} %get-tuple-element.77), channel_id=1, source_target_pairs={{0,1},{1,2},{2,3},{3,0},{4,5},{5,6},{6,7},{7,4},{8,9},{9,10},{10,1... | collective-permute-start | bytes 196616 | tf_op jit(solution)/shard_map/ppermute | solution.py:451
  109.6 1.2 collective-permute-start.14
  110.8 1.2 collective-permute-start.15
  112.1 0.9 fusion.78
  113.0 0.9 fusion.79
  113.9 1.7 %convert_add_fusion.1 = f32[256,1024]{1,0:T(8,128)S(1)} fusion(bf16[1,4,64,1024]{3,2,1,0:T(8,128)(2,1)S(1)} %copy-done.5, bf16[512,1024]{1,0:T(8,128)(2,1)} %pad_maximum_fusion, bf16[256,128]{1,0:T(8,128)(2,1)S(1)} %get-tuple-element.118, bf16[256,128]{1,0:T(8,128)(2,1)S(1)} %get-tuple-element.116, bf16[256,128]{1,0:T(8,128)(2,1)S(1)} %get-tuple-element.114, ...), kind=kOutput, calls=%fused_computation.11 | convolution fusion | flops 270008320 | bytes 2883584 | tf_op jit(solution)/shard_map/dot_general | solution.py:547
  115.6 0.8 collective-permute-start.19
  116.5 1.7 %collective-permute-start.20 = (bf16[256,128]{1,0:T(8,128)(2,1)S(1)}, bf16[256,128]{1,0:T(8,128)(2,1)S(1)}, u32[]{:S(2)}, u32[]{:S(2)}) collective-permute-start(bf16[256,128]{1,0:T(8,128)(2,1)S(1)} %copy-done.21), channel_id=1, source_target_pairs={{0,2},{1,3},{2,0},{3,1},{4,6},{5,7},{6,4},{7,5},{8,10},{9,11},{10,... | collective-permute-start | bytes 196616 | tf_op jit(solution)/shard_map/ppermute | solution.py:451
  118.2 0.5 fusion.32
  118.7 1.5 %collective-permute-start.21 = (bf16[256,128]{1,0:T(8,128)(2,1)S(1)}, bf16[256,128]{1,0:T(8,128)(2,1)S(1)}, u32[]{:S(2)}, u32[]{:S(2)}) collective-permute-start(bf16[256,128]{1,0:T(8,128)(2,1)S(1)} %copy-done.21), channel_id=1, source_target_pairs={{0,3},{1,0},{2,1},{3,2},{4,7},{5,4},{6,5},{7,6},{8,11},{9,8},{10,9... | collective-permute-start | bytes 196616 | tf_op jit(solution)/shard_map/ppermute | solution.py:451
  120.2 0.5 multiply_reduce_fusion.1
  120.8 1.3 convolution_bitcast_fusion.1
  122.4 0.8 fusion.80
  123.3 1.5 %collective-permute-start.16 = (bf16[64,1024]{1,0:T(8,128)(2,1)S(1)}, bf16[64,1024]{1,0:T(8,128)(2,1)S(1)}, u32[]{:S(2)}, u32[]{:S(2)}) collective-permute-start(bf16[64,1024]{1,0:T(8,128)(2,1)S(1)} %get-tuple-element.108), channel_id=1, source_target_pairs={{0,1},{1,2},{2,3},{3,0},{4,5},{5,6},{6,7},{7,4},{8,9},{9,10},{10,1... | collective-permute-start | bytes 393224 | tf_op jit(solution)/shard_map/ppermute | solution.py:451
  124.8 0.6 collective-permute-start.17
  125.4 2.8 %collective-permute-start.18 = (bf16[64,1024]{1,0:T(8,128)(2,1)S(1)}, bf16[64,1024]{1,0:T(8,128)(2,1)S(1)}, u32[]{:S(2)}, u32[]{:S(2)}) collective-permute-start(bf16[64,1024]{1,0:T(8,128)(2,1)S(1)} %get-tuple-element.106), channel_id=1, source_target_pairs={{0,3},{1,0},{2,1},{3,2},{4,7},{5,4},{6,5},{7,6},{8,11},{9,8},{10,9... | collective-permute-start | bytes 393224 | tf_op jit(solution)/shard_map/ppermute | solution.py:451
  128.3 0.5 multiply_reduce_fusion
  128.8 1.3 convolution_bitcast_fusion
  130.4 0.8 fusion.81
  131.4 1.5 collective-permute-start.23
  132.8 2.4 %collective-permute-start.24 = (bf16[64,1024]{1,0:T(8,128)(2,1)S(1)}, bf16[64,1024]{1,0:T(8,128)(2,1)S(1)}, u32[]{:S(2)}, u32[]{:S(2)}) collective-permute-start(bf16[64,1024]{1,0:T(8,128)(2,1)S(1)} %get-tuple-element.104), channel_id=1, source_target_pairs={{0,3},{1,0},{2,1},{3,2},{4,7},{5,4},{6,5},{7,6},{8,11},{9,8},{10,9... | collective-permute-start | bytes 393224 | tf_op jit(solution)/shard_map/ppermute | solution.py:451
  135.2 3.1 %collective-permute-done.17 = bf16[64,1024]{1,0:T(8,128)(2,1)S(1)} collective-permute-done((bf16[64,1024]{1,0:T(8,128)(2,1)S(1)}, bf16[64,1024]{1,0:T(8,128)(2,1)S(1)}, u32[]{:S(2)}, u32[]{:S(2)}) %collective-permute-start.17) | collective-permute-done | bytes 131104 | tf_op jit(solution)/shard_map/ppermute | solution.py:451
  138.4 1.2 collective-permute-done.22
  139.6 6.4 %collective-permute-done.23 = bf16[64,1024]{1,0:T(8,128)(2,1)S(1)} collective-permute-done((bf16[64,1024]{1,0:T(8,128)(2,1)S(1)}, bf16[64,1024]{1,0:T(8,128)(2,1)S(1)}, u32[]{:S(2)}, u32[]{:S(2)}) %collective-permute-start.23) | collective-permute-done | bytes 131104 | tf_op jit(solution)/shard_map/ppermute | solution.py:451
  146.0 0.7 pad_maximum_fusion.3
  (97 shorter events, 2.1 us)
Async XLA Ops:
  0.0 122.4 %copy-start = (bf16[1024,1024]{1,0:T(8,128)(2,1)S(1)}, bf16[1024,1024]{1,0:T(8,128)(2,1)}, u32[]{:S(2)}) copy-start(bf16[1024,1024]{1,0:T(8,128)(2,1)} %param.22) | copy-start | bytes 6291460
  0.0 23.2 %collective-permute-start = (bf16[128,1024]{1,0:T(8,128)(2,1)}, bf16[128,1024]{1,0:T(8,128)(2,1)S(1)}, u32[]{:S(2)}, u32[]{:S(2)}) collective-permute-start(bf16[128,1024]{1,0:T(8,128)(2,1)} %rest_5_.1), channel_id=1, source_target_pairs={{0,1},{1,2},{2,3},{3,0},{4,5},{5,6},{6,7},{7,4},{8,9},{9,10},{10,1... | collective-permute-start | bytes 786440 | tf_op jit(solution)/shard_map/ppermute | solution.py:451
  3.0 20.2 %collective-permute-start.1 = (bf16[128,1024]{1,0:T(8,128)(2,1)}, bf16[128,1024]{1,0:T(8,128)(2,1)S(1)}, u32[]{:S(2)}, u32[]{:S(2)}) collective-permute-start(bf16[128,1024]{1,0:T(8,128)(2,1)} %rest_5_.1), channel_id=1, source_target_pairs={{0,2},{1,3},{2,0},{3,1},{4,6},{5,7},{6,4},{7,5},{8,10},{9,11},{10,... | collective-permute-start | bytes 786440 | tf_op jit(solution)/shard_map/ppermute | solution.py:451
  17.8 5.4 %copy-start.3 = (bf16[1152,256]{1,0:T(8,128)(2,1)}, bf16[1152,256]{1,0:T(8,128)(2,1)S(1)}, u32[]{:S(2)}) copy-start(bf16[1152,256]{1,0:T(8,128)(2,1)S(1)} %all-gather) | copy-start | bytes 1769476
  23.2 0.7 copy-start.15
  23.2 0.8 copy-start.16
  23.2 5.2 %copy-start.14 = (bf16[128,1024]{1,0:T(8,128)(2,1)S(1)}, bf16[128,1024]{1,0:T(8,128)(2,1)}, u32[]{:S(2)}) copy-start(bf16[128,1024]{1,0:T(8,128)(2,1)} %rest_5_.1) | copy-start | bytes 786436
  23.3 6.6 %copy-start.28 = (bf16[1024]{0:T(1024)(128)(2,1)S(1)}, bf16[1024]{0:T(1024)(128)(2,1)}, u32[]{:S(2)}) copy-start(bf16[1024]{0:T(1024)(128)(2,1)} %param.17) | copy-start | bytes 6148
  23.3 7.2 %copy-start.6 = (bf16[256,1024]{1,0:T(8,128)(2,1)S(1)}, bf16[256,1024]{1,0:T(8,128)(2,1)}, u32[]{:S(2)}) copy-start(bf16[256,1024]{1,0:T(8,128)(2,1)} %param.20) | copy-start | bytes 1572868
  24.0 31.0 %all-to-all-start = ((bf16[8,4,128,2,128]{4,3,2,1,0:T(2,128)(2,1)}), bf16[8,4,128,2,128]{4,3,2,1,0:T(2,128)(2,1)}, u32[]{:S(2)}, u32[]{:S(2)}) async-start(bf16[8,4,128,2,128]{4,3,2,1,0:T(2,128)(2,1)} %get-tuple-element.46), calls=%async_computation | async-start | bytes 4194304 | tf_op jit(solution)/shard_map/all_to_all | solution.py:522
  28.4 9.0 %copy-start.27 = (s32[1,4]{1,0:T(1,128)S(1)}, s32[1,4]{1,0:T(1,128)}, u32[]{:S(2)}) copy-start(s32[1,4]{1,0:T(1,128)} %lens_ref.5) | copy-start | bytes 52
  28.4 9.3 %copy-start.26 = (s32[1,4]{1,0:T(1,128)S(1)}, s32[1,4]{1,0:T(1,128)}, u32[]{:S(2)}) copy-start(s32[1,4]{1,0:T(1,128)} %counts_ref.3) | copy-start | bytes 52
  28.4 17.5 %collective-permute-start.2 = (bf16[128,1024]{1,0:T(8,128)(2,1)S(1)}, bf16[128,1024]{1,0:T(8,128)(2,1)S(1)}, u32[]{:S(2)}, u32[]{:S(2)}) collective-permute-start(bf16[128,1024]{1,0:T(8,128)(2,1)S(1)} %copy-done.14), channel_id=1, source_target_pairs={{0,3},{1,0},{2,1},{3,2},{4,7},{5,4},{6,5},{7,6},{8,11},{9,8},{10,9... | collective-permute-start | bytes 786440 | tf_op jit(solution)/shard_map/ppermute | solution.py:451
  33.6 7.1 %collective-permute-start.3 = (bf16[128,256]{1,0:T(8,128)(2,1)}, bf16[128,256]{1,0:T(8,128)(2,1)S(1)}, u32[]{:S(2)}, u32[]{:S(2)}) collective-permute-start(bf16[128,256]{1,0:T(8,128)(2,1)} %get-tuple-element.50.rest_9_), channel_id=1, source_target_pairs={{0,1},{1,2},{2,3},{3,0},{4,5},{5,6},{6,7},{7,4},{8,9},{9,10},{10,1... | collective-permute-start | bytes 196616 | tf_op jit(solution)/shard_map/ppermute | solution.py:451
  34.3 8.4 %collective-permute-start.4 = (bf16[128,256]{1,0:T(8,128)(2,1)}, bf16[128,256]{1,0:T(8,128)(2,1)S(1)}, u32[]{:S(2)}, u32[]{:S(2)}) collective-permute-start(bf16[128,256]{1,0:T(8,128)(2,1)} %get-tuple-element.50.rest_9_), channel_id=1, source_target_pairs={{0,2},{1,3},{2,0},{3,1},{4,6},{5,7},{6,4},{7,5},{8,10},{9,11},{10,... | collective-permute-start | bytes 196616 | tf_op jit(solution)/shard_map/ppermute | solution.py:451
  34.6 8.1 %collective-permute-start.5 = (bf16[128,256]{1,0:T(8,128)(2,1)}, bf16[128,256]{1,0:T(8,128)(2,1)S(1)}, u32[]{:S(2)}, u32[]{:S(2)}) collective-permute-start(bf16[128,256]{1,0:T(8,128)(2,1)} %get-tuple-element.50.rest_9_), channel_id=1, source_target_pairs={{0,3},{1,0},{2,1},{3,2},{4,7},{5,4},{6,5},{7,6},{8,11},{9,8},{10,9... | collective-permute-start | bytes 196616 | tf_op jit(solution)/shard_map/ppermute | solution.py:451
  40.6 5.3 %copy-start.23 = (bf16[128,256]{1,0:T(8,128)(2,1)}, bf16[128,256]{1,0:T(8,128)(2,1)S(1)}, u32[]{:S(2)}) copy-start(bf16[128,256]{1,0:T(8,128)(2,1)S(1)} %collective-permute-done.3.rest_10_) | copy-start | bytes 196612
  42.7 3.2 %copy-start.24 = (bf16[128,256]{1,0:T(8,128)(2,1)}, bf16[128,256]{1,0:T(8,128)(2,1)S(1)}, u32[]{:S(2)}) copy-start(bf16[128,256]{1,0:T(8,128)(2,1)S(1)} %collective-permute-done.4.rest_11_) | copy-start | bytes 196612
  42.7 3.2 %copy-start.25 = (bf16[128,256]{1,0:T(8,128)(2,1)}, bf16[128,256]{1,0:T(8,128)(2,1)S(1)}, u32[]{:S(2)}) copy-start(bf16[128,256]{1,0:T(8,128)(2,1)S(1)} %collective-permute-done.5.rest_12_) | copy-start | bytes 196612
  42.7 10.5 %collective-permute-start.6 = (bf16[128,1024]{1,0:T(8,128)(2,1)}, bf16[128,1024]{1,0:T(8,128)(2,1)}, u32[]{:S(2)}, u32[]{:S(2)}) collective-permute-start(bf16[128,1024]{1,0:T(8,128)(2,1)} %get-tuple-element.56), channel_id=1, source_target_pairs={{0,1},{1,2},{2,3},{3,0},{4,5},{5,6},{6,7},{7,4},{8,9},{9,10},{10,1... | collective-permute-start | bytes 786440 | tf_op jit(solution)/shard_map/ppermute | solution.py:451
  45.9 0.7 copy-start.17
  55.1 41.0 %all-to-all-start.1 = ((bf16[8,4,128,2,128]{4,3,2,1,0:T(2,128)(2,1)}), bf16[8,4,128,2,128]{4,3,2,1,0:T(2,128)(2,1)}, u32[]{:S(2)}, u32[]{:S(2)}) async-start(bf16[8,4,128,2,128]{4,3,2,1,0:T(2,128)(2,1)} %get-tuple-element.67), calls=%async_computation.1 | async-start | bytes 4194304 | tf_op jit(solution)/shard_map/all_to_all | solution.py:542
  59.4 15.0 %collective-permute-start.7 = (bf16[128,1024]{1,0:T(8,128)(2,1)}, bf16[128,1024]{1,0:T(8,128)(2,1)S(1)}, u32[]{:S(2)}, u32[]{:S(2)}) collective-permute-start(bf16[128,1024]{1,0:T(8,128)(2,1)} %get-tuple-element.56), channel_id=1, source_target_pairs={{0,2},{1,3},{2,0},{3,1},{4,6},{5,7},{6,4},{7,5},{8,10},{9,11},{10,... | collective-permute-start | bytes 786440 | tf_op jit(solution)/shard_map/ppermute | solution.py:451
  60.1 14.4 %collective-permute-start.8 = (bf16[128,1024]{1,0:T(8,128)(2,1)}, bf16[128,1024]{1,0:T(8,128)(2,1)S(1)}, u32[]{:S(2)}, u32[]{:S(2)}) collective-permute-start(bf16[128,1024]{1,0:T(8,128)(2,1)} %get-tuple-element.56), channel_id=1, source_target_pairs={{0,3},{1,0},{2,1},{3,2},{4,7},{5,4},{6,5},{7,6},{8,11},{9,8},{10,9... | collective-permute-start | bytes 786440 | tf_op jit(solution)/shard_map/ppermute | solution.py:451
  62.1 15.0 %copy-start.29 = (bf16[1024]{0:T(1024)(128)(2,1)S(1)}, bf16[1024]{0:T(1024)(128)(2,1)}, u32[]{:S(2)}) copy-start(bf16[1024]{0:T(1024)(128)(2,1)} %param.18) | copy-start | bytes 6148
  62.1 15.1 %copy-start.7 = (bf16[2,4,64,1024]{3,2,1,0:T(8,128)(2,1)S(1)}, bf16[2,4,64,1024]{3,2,1,0:T(8,128)(2,1)}, u32[]{:S(2)}) copy-start(bf16[2,4,64,1024]{3,2,1,0:T(8,128)(2,1)} %get-tuple-element.51) | copy-start | bytes 3145732
  72.9 5.3 %copy-start.13 = (bf16[512,128]{1,0:T(8,128)(2,1)S(1)}, bf16[512,128]{1,0:T(8,128)(2,1)}, u32[]{:S(2)}) copy-start(bf16[512,128]{1,0:T(8,128)(2,1)} %attend.2) | copy-start | bytes 393220
  74.5 0.7 copy-start.9
  74.5 2.6 %copy-start.11 = (bf16[128,1024]{1,0:T(8,128)(2,1)}, bf16[128,1024]{1,0:T(8,128)(2,1)S(1)}, u32[]{:S(2)}) copy-start(bf16[128,1024]{1,0:T(8,128)(2,1)S(1)} %collective-permute-done.8) | copy-start | bytes 786436
  77.1 9.2 %collective-permute-start.9 = (bf16[3,128,1024]{2,1,0:T(8,128)(2,1)}, bf16[3,128,1024]{2,1,0:T(8,128)(2,1)}, u32[]{:S(2)}, u32[]{:S(2)}) collective-permute-start(bf16[3,128,1024]{2,1,0:T(8,128)(2,1)} %pad_maximum_fusion.2), channel_id=1, source_target_pairs={{0,4},{4,0},{8,12},{12,8},{16,20},{20,16},{24,28},{28,24},{1,5},{5... | collective-permute-start | bytes 2359304 | tf_op jit(solution)/shard_map/ppermute | solution.py:455
  77.1 9.2 %copy-start.10 = (bf16[128,1024]{1,0:T(8,128)(2,1)S(1)}, bf16[128,1024]{1,0:T(8,128)(2,1)}, u32[]{:S(2)}) copy-start(bf16[128,1024]{1,0:T(8,128)(2,1)} %copy-done.9) | copy-start | bytes 786436
  77.1 9.2 %copy-start.12 = (bf16[128,1024]{1,0:T(8,128)(2,1)S(1)}, bf16[128,1024]{1,0:T(8,128)(2,1)}, u32[]{:S(2)}) copy-start(bf16[128,1024]{1,0:T(8,128)(2,1)} %copy-done.11) | copy-start | bytes 786436
  78.3 9.4 %copy-start.8 = (bf16[128,1024]{1,0:T(8,128)(2,1)S(1)}, bf16[128,1024]{1,0:T(8,128)(2,1)}, u32[]{:S(2)}) copy-start(bf16[128,1024]{1,0:T(8,128)(2,1)} %get-tuple-element.109) | copy-start | bytes 786436
  78.3 11.7 %collective-permute-start.10 = (bf16[512,128]{1,0:T(8,128)(2,1)S(1)}, bf16[512,128]{1,0:T(8,128)(2,1)S(1)}, u32[]{:S(2)}, u32[]{:S(2)}) collective-permute-start(bf16[512,128]{1,0:T(8,128)(2,1)S(1)} %copy-done.13), channel_id=1, source_target_pairs={{0,1},{1,2},{2,3},{3,0},{4,5},{5,6},{6,7},{7,4},{8,9},{9,10},{10,1... | collective-permute-start | bytes 393224 | tf_op jit(solution)/shard_map/ppermute | solution.py:451
  83.9 11.4 %collective-permute-start.11 = (bf16[512,128]{1,0:T(8,128)(2,1)S(1)}, bf16[512,128]{1,0:T(8,128)(2,1)S(1)}, u32[]{:S(2)}, u32[]{:S(2)}) collective-permute-start(bf16[512,128]{1,0:T(8,128)(2,1)S(1)} %copy-done.13), channel_id=1, source_target_pairs={{0,2},{1,3},{2,0},{3,1},{4,6},{5,7},{6,4},{7,5},{8,10},{9,11},{10,... | collective-permute-start | bytes 393224 | tf_op jit(solution)/shard_map/ppermute | solution.py:451
  86.1 9.9 %collective-permute-start.12 = (bf16[512,128]{1,0:T(8,128)(2,1)S(1)}, bf16[512,128]{1,0:T(8,128)(2,1)}, u32[]{:S(2)}, u32[]{:S(2)}) collective-permute-start(bf16[512,128]{1,0:T(8,128)(2,1)S(1)} %copy-done.13), channel_id=1, source_target_pairs={{0,3},{1,0},{2,1},{3,2},{4,7},{5,4},{6,5},{7,6},{8,11},{9,8},{10,9... | collective-permute-start | bytes 393224 | tf_op jit(solution)/shard_map/ppermute | solution.py:451
  90.0 5.4 %copy-start.18 = (bf16[512,128]{1,0:T(8,128)(2,1)}, bf16[512,128]{1,0:T(8,128)(2,1)S(1)}, u32[]{:S(2)}) copy-start(bf16[512,128]{1,0:T(8,128)(2,1)S(1)} %collective-permute-done.10) | copy-start | bytes 393220
  95.3 0.7 copy-start.20
  96.0 16.1 %copy-start.19 = (bf16[512,128]{1,0:T(8,128)(2,1)S(1)}, bf16[512,128]{1,0:T(8,128)(2,1)}, u32[]{:S(2)}) copy-start(bf16[512,128]{1,0:T(8,128)(2,1)} %copy-done.18) | copy-start | bytes 393220
  96.0 17.9 %copy-start.5 = (bf16[1,4,64,1024]{3,2,1,0:T(8,128)(2,1)S(1)}, bf16[1,4,64,1024]{3,2,1,0:T(8,128)(2,1)}, u32[]{:S(2)}) copy-start(bf16[1,4,64,1024]{3,2,1,0:T(8,128)(2,1)} %get-tuple-element.91) | copy-start | bytes 1572868
  106.9 8.8 %copy-start.21 = (bf16[256,128]{1,0:T(8,128)(2,1)S(1)}, bf16[256,128]{1,0:T(8,128)(2,1)}, u32[]{:S(2)}) copy-start(bf16[256,128]{1,0:T(8,128)(2,1)} %get-tuple-element.81) | copy-start | bytes 196612
  106.9 11.3 %copy-start.2 = (bf16[512,1024]{1,0:T(8,128)(2,1)S(1)}, bf16[512,1024]{1,0:T(8,128)(2,1)}, u32[]{:S(2)}) copy-start(bf16[512,1024]{1,0:T(8,128)(2,1)} %pad_maximum_fusion) | copy-start | bytes 3145732
  106.9 11.8 %collective-permute-start.13 = (bf16[256,128]{1,0:T(8,128)(2,1)}, bf16[256,128]{1,0:T(8,128)(2,1)S(1)}, u32[]{:S(2)}, u32[]{:S(2)}) collective-permute-start(bf16[256,128]{1,0:T(8,128)(2,1)} %get-tuple-element.77), channel_id=1, source_target_pairs={{0,1},{1,2},{2,3},{3,0},{4,5},{5,6},{6,7},{7,4},{8,9},{9,10},{10,1... | collective-permute-start | bytes 196616 | tf_op jit(solution)/shard_map/ppermute | solution.py:451
  109.6 10.6 %collective-permute-start.14 = (bf16[256,128]{1,0:T(8,128)(2,1)}, bf16[256,128]{1,0:T(8,128)(2,1)S(1)}, u32[]{:S(2)}, u32[]{:S(2)}) collective-permute-start(bf16[256,128]{1,0:T(8,128)(2,1)} %get-tuple-element.77), channel_id=1, source_target_pairs={{0,2},{1,3},{2,0},{3,1},{4,6},{5,7},{6,4},{7,5},{8,10},{9,11},{10,... | collective-permute-start | bytes 196616 | tf_op jit(solution)/shard_map/ppermute | solution.py:451
  110.8 9.4 %collective-permute-start.15 = (bf16[256,128]{1,0:T(8,128)(2,1)}, bf16[256,128]{1,0:T(8,128)(2,1)S(1)}, u32[]{:S(2)}, u32[]{:S(2)}) collective-permute-start(bf16[256,128]{1,0:T(8,128)(2,1)} %get-tuple-element.77), channel_id=1, source_target_pairs={{0,3},{1,0},{2,1},{3,2},{4,7},{5,4},{6,5},{7,6},{8,11},{9,8},{10,9... | collective-permute-start | bytes 196616 | tf_op jit(solution)/shard_map/ppermute | solution.py:451
  113.9 6.3 %copy-start.22 = (bf16[256,128]{1,0:T(8,128)(2,1)S(1)}, bf16[256,128]{1,0:T(8,128)(2,1)}, u32[]{:S(2)}) copy-start(bf16[256,128]{1,0:T(8,128)(2,1)} %get-tuple-element.77) | copy-start | bytes 196612
  115.6 9.8 %collective-permute-start.19 = (bf16[256,128]{1,0:T(8,128)(2,1)S(1)}, bf16[256,128]{1,0:T(8,128)(2,1)S(1)}, u32[]{:S(2)}, u32[]{:S(2)}) collective-permute-start(bf16[256,128]{1,0:T(8,128)(2,1)S(1)} %copy-done.21), channel_id=1, source_target_pairs={{0,1},{1,2},{2,3},{3,0},{4,5},{5,6},{6,7},{7,4},{8,9},{9,10},{10,1... | collective-permute-start | bytes 196616 | tf_op jit(solution)/shard_map/ppermute | solution.py:451
  116.5 11.8 %collective-permute-start.20 = (bf16[256,128]{1,0:T(8,128)(2,1)S(1)}, bf16[256,128]{1,0:T(8,128)(2,1)S(1)}, u32[]{:S(2)}, u32[]{:S(2)}) collective-permute-start(bf16[256,128]{1,0:T(8,128)(2,1)S(1)} %copy-done.21), channel_id=1, source_target_pairs={{0,2},{1,3},{2,0},{3,1},{4,6},{5,7},{6,4},{7,5},{8,10},{9,11},{10,... | collective-permute-start | bytes 196616 | tf_op jit(solution)/shard_map/ppermute | solution.py:451
  118.2 2.6 %copy-start.1 = (bf16[2,1024,1024]{2,1,0:T(8,128)(2,1)S(1)}, bf16[2,1024,1024]{2,1,0:T(8,128)(2,1)}, u32[]{:S(2)}) copy-start(bf16[2,1024,1024]{2,1,0:T(8,128)(2,1)} %param.21) | copy-start | bytes 12582916
  118.7 9.6 %collective-permute-start.21 = (bf16[256,128]{1,0:T(8,128)(2,1)S(1)}, bf16[256,128]{1,0:T(8,128)(2,1)S(1)}, u32[]{:S(2)}, u32[]{:S(2)}) collective-permute-start(bf16[256,128]{1,0:T(8,128)(2,1)S(1)} %copy-done.21), channel_id=1, source_target_pairs={{0,3},{1,0},{2,1},{3,2},{4,7},{5,4},{6,5},{7,6},{8,11},{9,8},{10,9... | collective-permute-start | bytes 196616 | tf_op jit(solution)/shard_map/ppermute | solution.py:451
  122.4 5.9 %copy-start.4 = (bf16[1,4,64,1024]{3,2,1,0:T(8,128)(2,1)S(1)}, bf16[1,4,64,1024]{3,2,1,0:T(8,128)(2,1)}, u32[]{:S(2)}) copy-start(bf16[1,4,64,1024]{3,2,1,0:T(8,128)(2,1)} %get-tuple-element.92) | copy-start | bytes 1572868
  123.3 9.6 %collective-permute-start.16 = (bf16[64,1024]{1,0:T(8,128)(2,1)S(1)}, bf16[64,1024]{1,0:T(8,128)(2,1)S(1)}, u32[]{:S(2)}, u32[]{:S(2)}) collective-permute-start(bf16[64,1024]{1,0:T(8,128)(2,1)S(1)} %get-tuple-element.108), channel_id=1, source_target_pairs={{0,1},{1,2},{2,3},{3,0},{4,5},{5,6},{6,7},{7,4},{8,9},{9,10},{10,1... | collective-permute-start | bytes 393224 | tf_op jit(solution)/shard_map/ppermute | solution.py:451
  124.8 13.5 %collective-permute-start.17 = (bf16[64,1024]{1,0:T(8,128)(2,1)S(1)}, bf16[64,1024]{1,0:T(8,128)(2,1)S(1)}, u32[]{:S(2)}, u32[]{:S(2)}) collective-permute-start(bf16[64,1024]{1,0:T(8,128)(2,1)S(1)} %get-tuple-element.107), channel_id=1, source_target_pairs={{0,2},{1,3},{2,0},{3,1},{4,6},{5,7},{6,4},{7,5},{8,10},{9,11},{10,... | collective-permute-start | bytes 393224 | tf_op jit(solution)/shard_map/ppermute | solution.py:451
  125.4 12.9 %collective-permute-start.18 = (bf16[64,1024]{1,0:T(8,128)(2,1)S(1)}, bf16[64,1024]{1,0:T(8,128)(2,1)S(1)}, u32[]{:S(2)}, u32[]{:S(2)}) collective-permute-start(bf16[64,1024]{1,0:T(8,128)(2,1)S(1)} %get-tuple-element.106), channel_id=1, source_target_pairs={{0,3},{1,0},{2,1},{3,2},{4,7},{5,4},{6,5},{7,6},{8,11},{9,8},{10,9... | collective-permute-start | bytes 393224 | tf_op jit(solution)/shard_map/ppermute | solution.py:451
  131.3 8.3 %collective-permute-start.22 = (bf16[64,1024]{1,0:T(8,128)(2,1)S(1)}, bf16[64,1024]{1,0:T(8,128)(2,1)S(1)}, u32[]{:S(2)}, u32[]{:S(2)}) collective-permute-start(bf16[64,1024]{1,0:T(8,128)(2,1)S(1)} %get-tuple-element.103), channel_id=1, source_target_pairs={{0,1},{1,2},{2,3},{3,0},{4,5},{5,6},{6,7},{7,4},{8,9},{9,10},{10,1... | collective-permute-start | bytes 393224 | tf_op jit(solution)/shard_map/ppermute | solution.py:451
  131.4 14.6 %collective-permute-start.23 = (bf16[64,1024]{1,0:T(8,128)(2,1)S(1)}, bf16[64,1024]{1,0:T(8,128)(2,1)S(1)}, u32[]{:S(2)}, u32[]{:S(2)}) collective-permute-start(bf16[64,1024]{1,0:T(8,128)(2,1)S(1)} %get-tuple-element.105), channel_id=1, source_target_pairs={{0,2},{1,3},{2,0},{3,1},{4,6},{5,7},{6,4},{7,5},{8,10},{9,11},{10,... | collective-permute-start | bytes 393224 | tf_op jit(solution)/shard_map/ppermute | solution.py:451
  132.8 13.1 %collective-permute-start.24 = (bf16[64,1024]{1,0:T(8,128)(2,1)S(1)}, bf16[64,1024]{1,0:T(8,128)(2,1)S(1)}, u32[]{:S(2)}, u32[]{:S(2)}) collective-permute-start(bf16[64,1024]{1,0:T(8,128)(2,1)S(1)} %get-tuple-element.104), channel_id=1, source_target_pairs={{0,3},{1,0},{2,1},{3,2},{4,7},{5,4},{6,5},{7,6},{8,11},{9,8},{10,9... | collective-permute-start | bytes 393224 | tf_op jit(solution)/shard_map/ppermute | solution.py:451

commit v7 on v6

--- a/solution.py
+++ b/solution.py
@@ -138,9 +138,11 @@
     )(owner_table, adapter_ids, gathered)
 
 
-def project_kernel(n_tp, cap, pool_dev, tp_ref, lens_ref, table_ref, *rest):
+def project_kernel(n_tp, cap, pool_dev, n_chunk, tp_ref, lens_ref, table_ref, *rest):
     hbm_refs, rest = rest[: 5 + 2 * n_tp], rest[5 + 2 * n_tp :]
-    q_ref, k_ref, v_ref, pos_ref, all_ref, down, count, *held = rest
+    q_ref, k_ref, v_ref, pos_ref = rest[:4]
+    all_refs = rest[4 : 4 + n_chunk]
+    down, count, *held = rest[4 + n_chunk :]
     held, sem, sem_out = held[:-2], held[-2], held[-1]
     gain_ref, w_ref, up_ref, cos_ref, sin_ref, tok_ref = held
     tp = tp_ref[0]
@@ -172,13 +174,13 @@
 
     for copy in copies:
         copy.wait()
-    n_chunk, _, sub, _ = all_ref.shape
+    sub = all_refs[0].shape[1]
     stores = []
     for k in range(n_tp):
         for c in range(n_chunk):
             copy = pltpu.make_async_copy(
                 tok_ref.at[k, pl.ds(c * sub, sub)],
-                all_ref.at[c, lax.rem(tp - k + n_tp, n_tp)],
+                all_refs[c].at[lax.rem(tp - k + n_tp, n_tp)],
                 sem_out.at[k, c],
             )
             copy.start()
@@ -246,13 +248,13 @@
     vmem = pl.BlockSpec(memory_space=pltpu.VMEM)
     out = jax.ShapeDtypeStruct((rows, width), BF)
     return pl.pallas_call(
-        functools.partial(project_kernel, n_tp, cap, pool_dev),
+        functools.partial(project_kernel, n_tp, cap, pool_dev, n_chunk),
         out_shape=(
             out, out, out, jax.ShapeDtypeStruct((table.shape[1],), jnp.int32),
-            jax.ShapeDtypeStruct((n_chunk, n_tp, sub, toks[0].shape[1]), BF),
-        ),
+        )
+        + (jax.ShapeDtypeStruct((n_tp, sub, toks[0].shape[1]), BF),) * n_chunk,
         in_specs=[smem] * 3 + [pl.BlockSpec(memory_space=pltpu.HBM)] * (5 + 2 * n_tp),
-        out_specs=(vmem, vmem, vmem, smem, pl.BlockSpec(memory_space=pltpu.HBM)),
+        out_specs=(vmem, vmem, vmem, smem) + (pl.BlockSpec(memory_space=pltpu.HBM),) * n_chunk,
         scratch_shapes=[
             pltpu.VMEM((n_tp,) + downs[0].shape, BF),
             pltpu.SMEM((n_dp,), jnp.int32),
@@ -531,7 +533,7 @@
     frequency = 10000.0 ** (-2.0 * (index % (HD // 2)).astype(F32) / HD)
     angles = (position % VARLEN).astype(F32)[:, None] * frequency[None, :]
     sign = jnp.where(index % HD < HD // 2, -1.0, 1.0).astype(F32)
-    query, new_keys, new_values, buffer_pos, all_tokens = project(
+    query, new_keys, new_values, buffer_pos, *all_tokens = project(
         tp_id, lengths, page_table, attn_gain.reshape(1, d_model), w_qkv, up_named,
         jnp.cos(angles), jnp.sin(angles) * sign[None, :], toks, downs, n_dp, cap, pool_dev, n_chunk,
     )
@@ -562,7 +564,7 @@
             mix, halves = lax.optimization_barrier((mix, halves))
             w_whole = whole_weight(w_out, halves, dp, n_dp, n_group)
         blocks = [mix] + [shift(mix, "tensor", n_tp, k) for k in far_first]
-        query, w_whole, blocks = lax.optimization_barrier((query, w_whole, blocks))
+        query, w_whole = lax.optimization_barrier((query, w_whole))
         early.append(blocks)
     if w_whole is None:
         w_whole = whole_weight(w_out, halves, dp, n_dp, n_group)

time: 149 us -> 140 us (0.940)
  waiting for transfers between devices: 25.5 us -> 19.3 us
  local copies, waits for them, and re-layouts: 8.58 us -> 6.84 us
    ppermute x24, waiting for transfers between devices: 23.6 us -> 16.6 us  [shift(): return lax.ppermute(value, axis, [(i, (i + k) % n) for i in range(n)])]
  transfers between devices with their start and end apart: 27 -> 27, of which waited for: 9 -> 8; matrix products, arithmetic and copies ran while one was open for 15% -> 16% of each run, Pallas kernels for 17% -> 25%
where the time goes in v7:
time: 140 us; the launch traced here: 139 us
  starting transfers between devices  50.4 us (36%)
  Pallas kernels  35 us (25%)
  waiting for transfers between devices  19.3 us (14%)
  blocking collectives  9.99 us (7%)
  other arithmetic  9.48 us (7%)
  matrix products  7.58 us (5%)
  local copies, waits for them, and re-layouts  6.84 us (5%)
    ppermute x24, starting transfers between devices, shift(): return lax.ppermute(value, axis, [(i, (i + k) % n) for i in range(n)])  41.6 us
    pallas_call x2, Pallas kernels, attend(): pl.pallas_call(functools.partial(attend_kernel, group, per, n_chunk), gri...  21.6 us
    ppermute x24, waiting for transfers between devices, shift(): return lax.ppermute(value, axis, [(i, (i + k) % n) for i in range(n)])  16.6 us
    all_gather x1, blocking collectives, per_device(): gathered = lax.all_gather(payload, 'dp', axis=0)  9.99 us
    all_to_all x2, starting transfers between devices, per_device(): lax.all_to_all(send, 'dp', split_axis=0, concat_axis=0, tiled=True)  8.85 us
    pallas_call x1, Pallas kernels, project(): pl.pallas_call(functools.partial(project_kernel, n_tp, cap, pool_dev, n_c...  6.56 us
    pallas_call x1, Pallas kernels, pick(): pl.pallas_call(functools.partial(pick_kernel, n_dp, cap), out_shape=[jax....  4.56 us
    dot_general x4, matrix products, mixed(): jnp.dot(jnp.concatenate(blocks, axis=1), w_whole[a], preferred_element_ty...  3.24 us
  transfers between devices with their start and end apart: 27, of which 8 were waited for; matrix products, arithmetic and copies ran while one was open for 16% of the time, Pallas kernels for 25%

profile of v7, /device:TPU:0, one launch (start us, length us, event | category | flops | bytes accessed | tf_op | source)
XLA Modules:
  0.0 139.0 jit_solution(14674588037577601892)
XLA Ops:
  0.0 3.0 %collective-permute-start = (bf16[128,1024]{1,0:T(8,128)(2,1)}, bf16[128,1024]{1,0:T(8,128)(2,1)S(1)}, u32[]{:S(2)}, u32[]{:S(2)}) collective-permute-start(bf16[128,1024]{1,0:T(8,128)(2,1)} %rest_5_.1), channel_id=1, source_target_pairs={{0,1},{1,2},{2,3},{3,0},{4,5},{5,6},{6,7},{7,4},{8,9},{9,10},{10,1... | collective-permute-start | bytes 786440 | tf_op jit(solution)/shard_map/ppermute | solution.py:453
  3.0 2.6 %collective-permute-start.1 = (bf16[128,1024]{1,0:T(8,128)(2,1)}, bf16[128,1024]{1,0:T(8,128)(2,1)S(1)}, u32[]{:S(2)}, u32[]{:S(2)}) collective-permute-start(bf16[128,1024]{1,0:T(8,128)(2,1)} %rest_5_.1), channel_id=1, source_target_pairs={{0,2},{1,3},{2,0},{3,1},{4,6},{5,7},{6,4},{7,5},{8,10},{9,11},{10,... | collective-permute-start | bytes 786440 | tf_op jit(solution)/shard_map/ppermute | solution.py:453
  5.6 0.7 fusion.69
  6.3 0.8 constant_dynamic-slice_fusion.1
  7.1 0.8 pad_maximum_fusion.4
  7.8 10.0 %all-gather = bf16[1152,256]{1,0:T(8,128)(2,1)S(1)} all-gather(bf16[144,256]{1,0:T(8,128)(2,1)S(1)} %pad_maximum_fusion.4), channel_id=2, replica_groups=mesh['dp'=8,'tensor'=4] {'dp'}, dimensions={0}, use_global_device_ids=true | all-gather | bytes 663552 | tf_op jit(solution)/shard_map/all_gather | solution.py:520
  17.8 0.6 slice_convert_fusion.asked_ref
  18.5 4.6 %pick_pages.1 = (bf16[8,4,128,2,128]{4,3,2,1,0:T(2,128)(2,1)}, bf16[8,4,128,2,128]{4,3,2,1,0:T(2,128)(2,1)}) custom-call(s32[1]{0:T(128)} %bitcast.4.me_ref, s32[8,2,32]{2,1,0:T(2,128)} %slice_convert_fusion.asked_ref, bf16[32,128,2,256]{3,2,1,0:T(2,128)(2,1)} %pool_ref.1), custom_call_target="tpu_custom_call" | custom-call | flops 1000 | bytes 1000 | tf_op jit(solution)/shard_map/pick_pages/pallas_call | solution.py:82
  23.1 0.7 copy-done.9
  23.8 0.7 copy-done.10
  24.5 4.5 %all-to-all-start = ((bf16[8,4,128,2,128]{4,3,2,1,0:T(2,128)(2,1)}), bf16[8,4,128,2,128]{4,3,2,1,0:T(2,128)(2,1)}, u32[]{:S(2)}, u32[]{:S(2)}) async-start(bf16[8,4,128,2,128]{4,3,2,1,0:T(2,128)(2,1)} %get-tuple-element.43), calls=%async_computation | async-start | bytes 4194304 | tf_op jit(solution)/shard_map/all_to_all | solution.py:524
  29.0 1.4 %collective-permute-start.2 = (bf16[128,1024]{1,0:T(8,128)(2,1)S(1)}, bf16[128,1024]{1,0:T(8,128)(2,1)}, u32[]{:S(2)}, u32[]{:S(2)}) collective-permute-start(bf16[128,1024]{1,0:T(8,128)(2,1)S(1)} %copy-done.8), channel_id=1, source_target_pairs={{0,3},{1,0},{2,1},{3,2},{4,7},{5,4},{6,5},{7,6},{8,11},{9,8},{10,9... | collective-permute-start | bytes 786440 | tf_op jit(solution)/shard_map/ppermute | solution.py:453
  30.4 0.6 reshape.112.rest_0_
  31.0 0.8 fusion.78
  31.8 2.3 %named_adapters.1 = (bf16[128,256]{1,0:T(8,128)(2,1)}, bf16[128,256]{1,0:T(8,128)(2,1)}) custom-call(s32[16]{0:T(128)} %table_ref.2, s32[1,4]{1,0:T(1,128)} %ids_ref.1, bf16[8,144,256]{2,1,0:T(8,128)(2,1)} %bitcast.105), custom_call_target="tpu_custom_call" | custom-call | flops 1000 | bytes 1000 | tf_op jit(solution)/shard_map/named_adapters/pallas_call | solution.py:126
  34.1 0.7 collective-permute-start.3
  34.8 0.3 collective-permute-start.4
  35.1 2.8 %collective-permute-start.5 = (bf16[128,256]{1,0:T(8,128)(2,1)}, bf16[128,256]{1,0:T(8,128)(2,1)S(1)}, u32[]{:S(2)}, u32[]{:S(2)}) collective-permute-start(bf16[128,256]{1,0:T(8,128)(2,1)} %get-tuple-element.47.rest_9_), channel_id=1, source_target_pairs={{0,3},{1,0},{2,1},{3,2},{4,7},{5,4},{6,5},{7,6},{8,11},{9,8},{10,9... | collective-permute-start | bytes 196616 | tf_op jit(solution)/shard_map/ppermute | solution.py:453
  38.0 0.2 reduce-window.4
  38.3 2.9 %collective-permute-done.3.rest_10_ = bf16[128,256]{1,0:T(8,128)(2,1)S(1)} collective-permute-done((bf16[128,256]{1,0:T(8,128)(2,1)}, bf16[128,256]{1,0:T(8,128)(2,1)S(1)}, u32[]{:S(2)}, u32[]{:S(2)}) %collective-permute-start.3) | collective-permute-done | bytes 65568 | tf_op jit(solution)/shard_map/ppermute | solution.py:453
  41.2 1.9 %collective-permute-done.4.rest_11_ = bf16[128,256]{1,0:T(8,128)(2,1)S(1)} collective-permute-done((bf16[128,256]{1,0:T(8,128)(2,1)}, bf16[128,256]{1,0:T(8,128)(2,1)S(1)}, u32[]{:S(2)}, u32[]{:S(2)}) %collective-permute-start.4) | collective-permute-done | bytes 65568 | tf_op jit(solution)/shard_map/ppermute | solution.py:453
  43.1 1.3 collective-permute-start.6
  44.5 1.8 %fusion.15 = (f32[512,128]{1,0:T(8,128)}, f32[512,128]{1,0:T(8,128)}) fusion(f32[128]{0:T(128)S(1)} %get-tuple-element.124, f32[128]{0:T(128)S(1)} %get-tuple-element.125, f32[512]{0:T(512)S(1)} %fusion.63), kind=kLoop, calls=%fused_computation.29 | loop fusion | flops 131072 | bytes 527360 | tf_op jit(solution)/shard_map/mul | solution.py:538
  46.3 6.6 %project.1 = (bf16[512,256]{1,0:T(8,128)(2,1)}, bf16[512,256]{1,0:T(8,128)(2,1)}, bf16[512,256]{1,0:T(8,128)(2,1)}, s32[32]{0:T(128)}, bf16[4,64,1024]{2,1,0:T(8,128)(2,1)}, /*index=5*/bf16[4,64,1024]{2,1,0:T(8,128)(2,1)}) custom-call(s32[1]{0:T(128)} %bitcast.tp_ref, s32[1,4]{1,0:T(1,128)} %lens_ref.5, s32[1,32]{1,0:T(1,128)} %table_ref.3, ...), custom_call_target="tpu_custom_call" | custom-call | flops 1000 | bytes 1000 | tf_op jit(solution)/shard_map/project/pallas_call | solution.py:250
  53.0 2.7 %all-to-all-done = bf16[8,4,128,2,128]{4,3,2,1,0:T(2,128)(2,1)} async-done(((bf16[8,4,128,2,128]{4,3,2,1,0:T(2,128)(2,1)}), bf16[8,4,128,2,128]{4,3,2,1,0:T(2,128)(2,1)}, u32[]{:S(2)}, u32[]{:S(2)}) %all-to-all-start) | async-done | bytes 2097184 | tf_op jit(solution)/shard_map/all_to_all | solution.py:524
  55.6 4.4 %all-to-all-start.1 = ((bf16[8,4,128,2,128]{4,3,2,1,0:T(2,128)(2,1)}), bf16[8,4,128,2,128]{4,3,2,1,0:T(2,128)(2,1)}, u32[]{:S(2)}, u32[]{:S(2)}) async-start(bf16[8,4,128,2,128]{4,3,2,1,0:T(2,128)(2,1)} %get-tuple-element.60), calls=%async_computation.1 | async-start | bytes 4194304 | tf_op jit(solution)/shard_map/all_to_all | solution.py:544
  60.0 0.4 collective-permute-start.7
  60.4 2.2 %collective-permute-start.8 = (bf16[128,1024]{1,0:T(8,128)(2,1)S(1)}, bf16[128,1024]{1,0:T(8,128)(2,1)S(1)}, u32[]{:S(2)}, u32[]{:S(2)}) collective-permute-start(bf16[128,1024]{1,0:T(8,128)(2,1)S(1)} %get-tuple-element.53), channel_id=1, source_target_pairs={{0,3},{1,0},{2,1},{3,2},{4,7},{5,4},{6,5},{7,6},{8,11},{9,8},{10,9... | collective-permute-start | bytes 786440 | tf_op jit(solution)/shard_map/ppermute | solution.py:453
  62.7 10.8 %attend.2 = bf16[512,128]{1,0:T(8,128)(2,1)} custom-call(s32[1,4]{1,0:T(1,128)} %lens_ref.5, s32[1,4]{1,0:T(1,128)} %counts_ref.3, s32[32]{0:T(128)} %get-tuple-element.49.pos_ref, f32[2,4]{1,0:T(2,128)} %bias_ref.3, bf16[512,256]{1,0:T(8,128)(2,1)} %get-tuple-element.58.q_ref, bf16[512,256]{1,0:T(8,128)(2,1)} %get-tuple-element.51.kn_ref, ...), custom_call_target="tpu_custom_call" | custom-call | flops 1000 | bytes 1000 | tf_op jit(solution)/shard_map/attend/pallas_call | solution.py:427
  73.5 1.4 collective-permute-done.7
  74.8 1.0 pad_maximum_fusion.2
  75.8 5.2 %collective-permute-start.10 = (bf16[512,128]{1,0:T(8,128)(2,1)}, bf16[512,128]{1,0:T(8,128)(2,1)}, u32[]{:S(2)}, u32[]{:S(2)}) collective-permute-start(bf16[512,128]{1,0:T(8,128)(2,1)} %attend.2), channel_id=1, source_target_pairs={{0,2},{1,3},{2,0},{3,1},{4,6},{5,7},{6,4},{7,5},{8,10},{9,11},{10,... | collective-permute-start | bytes 393224 | tf_op jit(solution)/shard_map/ppermute | solution.py:453
  81.0 3.4 %collective-permute-start.11 = (bf16[512,128]{1,0:T(8,128)(2,1)}, bf16[512,128]{1,0:T(8,128)(2,1)}, u32[]{:S(2)}, u32[]{:S(2)}) collective-permute-start(bf16[512,128]{1,0:T(8,128)(2,1)} %attend.2), channel_id=1, source_target_pairs={{0,3},{1,0},{2,1},{3,2},{4,7},{5,4},{6,5},{7,6},{8,11},{9,8},{10,9... | collective-permute-start | bytes 393224 | tf_op jit(solution)/shard_map/ppermute | solution.py:453
  84.5 1.2 broadcast_select_fusion.2
  85.7 1.0 pad_maximum_fusion.1
  86.7 1.1 pad_maximum_fusion
  87.8 10.8 %attend.3 = (bf16[256,128]{1,0:T(8,128)(2,1)}, bf16[256,128]{1,0:T(8,128)(2,1)}) custom-call(s32[1,4]{1,0:T(1,128)} %lens_ref.5, s32[1,4]{1,0:T(1,128)} %counts_ref.3, s32[32]{0:T(128)} %get-tuple-element.49.pos_ref, f32[2,4]{1,0:T(2,128)} %bias_ref.3, bf16[512,256]{1,0:T(8,128)(2,1)} %get-tuple-element.58.q_ref, bf16[512,256]{1,0:T(8,128)(2,1)} %get-tuple-element.51.kn_ref, ...), custom_call_target="tpu_custom_call" | custom-call | flops 1000 | bytes 1000 | tf_op jit(solution)/shard_map/attend/pallas_call | solution.py:427
  98.7 1.3 collective-permute-start.13
  99.9 3.1 %collective-permute-start.14 = (bf16[256,128]{1,0:T(8,128)(2,1)}, bf16[256,128]{1,0:T(8,128)(2,1)S(1)}, u32[]{:S(2)}, u32[]{:S(2)}) collective-permute-start(bf16[256,128]{1,0:T(8,128)(2,1)} %get-tuple-element.70), channel_id=1, source_target_pairs={{0,2},{1,3},{2,0},{3,1},{4,6},{5,7},{6,4},{7,5},{8,10},{9,11},{10,... | collective-permute-start | bytes 196616 | tf_op jit(solution)/shard_map/ppermute | solution.py:453
  103.1 0.9 fusion.80
  104.0 0.9 fusion.81
  104.9 0.9 fusion.82
  105.8 1.7 %convert_add_fusion.1 = f32[256,1024]{1,0:T(8,128)S(1)} fusion(bf16[4,64,1024]{2,1,0:T(8,128)(2,1)S(1)} %copy-done.7, bf16[512,1024]{1,0:T(8,128)(2,1)} %pad_maximum_fusion, bf16[256,128]{1,0:T(8,128)(2,1)S(1)} %get-tuple-element.110, bf16[256,128]{1,0:T(8,128)(2,1)S(1)} %get-tuple-element.108, bf16[256,128]{1,0:T(8,128)(2,1)S(1)} %get-tuple-element.106, ...), kind=kOutput, calls=%fused_computation.11 | convolution fusion | flops 270008320 | bytes 2883584 | tf_op jit(solution)/shard_map/dot_general | solution.py:549
  107.5 2.1 %collective-permute-start.19 = (bf16[256,128]{1,0:T(8,128)(2,1)S(1)}, bf16[256,128]{1,0:T(8,128)(2,1)S(1)}, u32[]{:S(2)}, u32[]{:S(2)}) collective-permute-start(bf16[256,128]{1,0:T(8,128)(2,1)S(1)} %copy-done.11), channel_id=1, source_target_pairs={{0,1},{1,2},{2,3},{3,0},{4,5},{5,6},{6,7},{7,4},{8,9},{9,10},{10,1... | collective-permute-start | bytes 196616 | tf_op jit(solution)/shard_map/ppermute | solution.py:453
  109.6 0.4 fusion.33
  110.0 2.7 %collective-permute-start.21 = (bf16[256,128]{1,0:T(8,128)(2,1)S(1)}, bf16[256,128]{1,0:T(8,128)(2,1)S(1)}, u32[]{:S(2)}, u32[]{:S(2)}) collective-permute-start(bf16[256,128]{1,0:T(8,128)(2,1)S(1)} %copy-done.11), channel_id=1, source_target_pairs={{0,3},{1,0},{2,1},{3,2},{4,7},{5,4},{6,5},{7,6},{8,11},{9,8},{10,9... | collective-permute-start | bytes 196616 | tf_op jit(solution)/shard_map/ppermute | solution.py:453
  112.7 0.5 multiply_reduce_fusion.1
  113.3 1.3 convolution_bitcast_fusion.1
  114.6 0.2 fusion.77
  114.9 0.8 fusion.83
  115.8 0.9 collective-permute-start.16
  116.7 1.7 %collective-permute-start.17 = (bf16[64,1024]{1,0:T(8,128)(2,1)S(1)}, bf16[64,1024]{1,0:T(8,128)(2,1)S(1)}, u32[]{:S(2)}, u32[]{:S(2)}) collective-permute-start(bf16[64,1024]{1,0:T(8,128)(2,1)S(1)} %get-tuple-element.99), channel_id=1, source_target_pairs={{0,2},{1,3},{2,0},{3,1},{4,6},{5,7},{6,4},{7,5},{8,10},{9,11},{10,... | collective-permute-start | bytes 393224 | tf_op jit(solution)/shard_map/ppermute | solution.py:453
  118.4 1.8 %collective-permute-start.18 = (bf16[64,1024]{1,0:T(8,128)(2,1)S(1)}, bf16[64,1024]{1,0:T(8,128)(2,1)S(1)}, u32[]{:S(2)}, u32[]{:S(2)}) collective-permute-start(bf16[64,1024]{1,0:T(8,128)(2,1)S(1)} %get-tuple-element.98), channel_id=1, source_target_pairs={{0,3},{1,0},{2,1},{3,2},{4,7},{5,4},{6,5},{7,6},{8,11},{9,8},{10,9... | collective-permute-start | bytes 393224 | tf_op jit(solution)/shard_map/ppermute | solution.py:453
  120.2 0.6 multiply_reduce_fusion
  120.7 1.3 convolution_bitcast_fusion
  122.1 0.2 fusion.76
  122.3 0.8 fusion.84
  123.2 0.3 collective-permute-start.22
  123.5 1.4 %collective-permute-start.23 = (bf16[64,1024]{1,0:T(8,128)(2,1)S(1)}, bf16[64,1024]{1,0:T(8,128)(2,1)S(1)}, u32[]{:S(2)}, u32[]{:S(2)}) collective-permute-start(bf16[64,1024]{1,0:T(8,128)(2,1)S(1)} %get-tuple-element.97), channel_id=1, source_target_pairs={{0,2},{1,3},{2,0},{3,1},{4,6},{5,7},{6,4},{7,5},{8,10},{9,11},{10,... | collective-permute-start | bytes 393224 | tf_op jit(solution)/shard_map/ppermute | solution.py:453
  124.9 2.8 %collective-permute-start.24 = (bf16[64,1024]{1,0:T(8,128)(2,1)S(1)}, bf16[64,1024]{1,0:T(8,128)(2,1)S(1)}, u32[]{:S(2)}, u32[]{:S(2)}) collective-permute-start(bf16[64,1024]{1,0:T(8,128)(2,1)S(1)} %get-tuple-element.96), channel_id=1, source_target_pairs={{0,3},{1,0},{2,1},{3,2},{4,7},{5,4},{6,5},{7,6},{8,11},{9,8},{10,9... | collective-permute-start | bytes 393224 | tf_op jit(solution)/shard_map/ppermute | solution.py:453
  127.7 3.1 %collective-permute-done.17 = bf16[64,1024]{1,0:T(8,128)(2,1)S(1)} collective-permute-done((bf16[64,1024]{1,0:T(8,128)(2,1)S(1)}, bf16[64,1024]{1,0:T(8,128)(2,1)S(1)}, u32[]{:S(2)}, u32[]{:S(2)}) %collective-permute-start.17) | collective-permute-done | bytes 131104 | tf_op jit(solution)/shard_map/ppermute | solution.py:453
  130.9 0.6 collective-permute-done.22
  131.5 6.7 %collective-permute-done.23 = bf16[64,1024]{1,0:T(8,128)(2,1)S(1)} collective-permute-done((bf16[64,1024]{1,0:T(8,128)(2,1)S(1)}, bf16[64,1024]{1,0:T(8,128)(2,1)S(1)}, u32[]{:S(2)}, u32[]{:S(2)}) %collective-permute-start.23) | collective-permute-done | bytes 131104 | tf_op jit(solution)/shard_map/ppermute | solution.py:453
  138.3 0.7 pad_maximum_fusion.3
  (76 shorter events, 0.7 us)
Async XLA Ops:
  0.0 114.9 %copy-start = (bf16[1024,1024]{1,0:T(8,128)(2,1)S(1)}, bf16[1024,1024]{1,0:T(8,128)(2,1)}, u32[]{:S(2)}) copy-start(bf16[1024,1024]{1,0:T(8,128)(2,1)} %param.22) | copy-start | bytes 6291460
  0.0 23.0 %collective-permute-start = (bf16[128,1024]{1,0:T(8,128)(2,1)}, bf16[128,1024]{1,0:T(8,128)(2,1)S(1)}, u32[]{:S(2)}, u32[]{:S(2)}) collective-permute-start(bf16[128,1024]{1,0:T(8,128)(2,1)} %rest_5_.1), channel_id=1, source_target_pairs={{0,1},{1,2},{2,3},{3,0},{4,5},{5,6},{6,7},{7,4},{8,9},{9,10},{10,1... | collective-permute-start | bytes 786440 | tf_op jit(solution)/shard_map/ppermute | solution.py:453
  3.0 20.0 %collective-permute-start.1 = (bf16[128,1024]{1,0:T(8,128)(2,1)}, bf16[128,1024]{1,0:T(8,128)(2,1)S(1)}, u32[]{:S(2)}, u32[]{:S(2)}) collective-permute-start(bf16[128,1024]{1,0:T(8,128)(2,1)} %rest_5_.1), channel_id=1, source_target_pairs={{0,2},{1,3},{2,0},{3,1},{4,6},{5,7},{6,4},{7,5},{8,10},{9,11},{10,... | collective-permute-start | bytes 786440 | tf_op jit(solution)/shard_map/ppermute | solution.py:453
  17.8 5.2 %copy-start.3 = (bf16[1152,256]{1,0:T(8,128)(2,1)}, bf16[1152,256]{1,0:T(8,128)(2,1)S(1)}, u32[]{:S(2)}) copy-start(bf16[1152,256]{1,0:T(8,128)(2,1)S(1)} %all-gather) | copy-start | bytes 1769476
  23.0 0.7 copy-start.9
  23.8 0.7 copy-start.10
  24.5 4.5 %copy-start.8 = (bf16[128,1024]{1,0:T(8,128)(2,1)S(1)}, bf16[128,1024]{1,0:T(8,128)(2,1)}, u32[]{:S(2)}) copy-start(bf16[128,1024]{1,0:T(8,128)(2,1)} %rest_5_.1) | copy-start | bytes 786436
  24.5 5.9 %copy-start.18 = (bf16[1024]{0:T(1024)(128)(2,1)S(1)}, bf16[1024]{0:T(1024)(128)(2,1)}, u32[]{:S(2)}) copy-start(bf16[1024]{0:T(1024)(128)(2,1)} %param.17) | copy-start | bytes 6148
  24.5 6.5 %copy-start.4 = (bf16[256,1024]{1,0:T(8,128)(2,1)S(1)}, bf16[256,1024]{1,0:T(8,128)(2,1)}, u32[]{:S(2)}) copy-start(bf16[256,1024]{1,0:T(8,128)(2,1)} %param.20) | copy-start | bytes 1572868
  24.5 31.1 %all-to-all-start = ((bf16[8,4,128,2,128]{4,3,2,1,0:T(2,128)(2,1)}), bf16[8,4,128,2,128]{4,3,2,1,0:T(2,128)(2,1)}, u32[]{:S(2)}, u32[]{:S(2)}) async-start(bf16[8,4,128,2,128]{4,3,2,1,0:T(2,128)(2,1)} %get-tuple-element.43), calls=%async_computation | async-start | bytes 4194304 | tf_op jit(solution)/shard_map/all_to_all | solution.py:524
  29.0 9.0 %copy-start.17 = (s32[1,4]{1,0:T(1,128)S(1)}, s32[1,4]{1,0:T(1,128)}, u32[]{:S(2)}) copy-start(s32[1,4]{1,0:T(1,128)} %lens_ref.5) | copy-start | bytes 52
  29.0 9.2 %copy-start.16 = (s32[1,4]{1,0:T(1,128)S(1)}, s32[1,4]{1,0:T(1,128)}, u32[]{:S(2)}) copy-start(s32[1,4]{1,0:T(1,128)} %counts_ref.3) | copy-start | bytes 52
  29.0 17.3 %collective-permute-start.2 = (bf16[128,1024]{1,0:T(8,128)(2,1)S(1)}, bf16[128,1024]{1,0:T(8,128)(2,1)}, u32[]{:S(2)}, u32[]{:S(2)}) collective-permute-start(bf16[128,1024]{1,0:T(8,128)(2,1)S(1)} %copy-done.8), channel_id=1, source_target_pairs={{0,3},{1,0},{2,1},{3,2},{4,7},{5,4},{6,5},{7,6},{8,11},{9,8},{10,9... | collective-permute-start | bytes 786440 | tf_op jit(solution)/shard_map/ppermute | solution.py:453
  34.1 7.1 %collective-permute-start.3 = (bf16[128,256]{1,0:T(8,128)(2,1)}, bf16[128,256]{1,0:T(8,128)(2,1)S(1)}, u32[]{:S(2)}, u32[]{:S(2)}) collective-permute-start(bf16[128,256]{1,0:T(8,128)(2,1)} %get-tuple-element.47.rest_9_), channel_id=1, source_target_pairs={{0,1},{1,2},{2,3},{3,0},{4,5},{5,6},{6,7},{7,4},{8,9},{9,10},{10,1... | collective-permute-start | bytes 196616 | tf_op jit(solution)/shard_map/ppermute | solution.py:453
  34.8 8.3 %collective-permute-start.4 = (bf16[128,256]{1,0:T(8,128)(2,1)}, bf16[128,256]{1,0:T(8,128)(2,1)S(1)}, u32[]{:S(2)}, u32[]{:S(2)}) collective-permute-start(bf16[128,256]{1,0:T(8,128)(2,1)} %get-tuple-element.47.rest_9_), channel_id=1, source_target_pairs={{0,2},{1,3},{2,0},{3,1},{4,6},{5,7},{6,4},{7,5},{8,10},{9,11},{10,... | collective-permute-start | bytes 196616 | tf_op jit(solution)/shard_map/ppermute | solution.py:453
  35.1 8.0 %collective-permute-start.5 = (bf16[128,256]{1,0:T(8,128)(2,1)}, bf16[128,256]{1,0:T(8,128)(2,1)S(1)}, u32[]{:S(2)}, u32[]{:S(2)}) collective-permute-start(bf16[128,256]{1,0:T(8,128)(2,1)} %get-tuple-element.47.rest_9_), channel_id=1, source_target_pairs={{0,3},{1,0},{2,1},{3,2},{4,7},{5,4},{6,5},{7,6},{8,11},{9,8},{10,9... | collective-permute-start | bytes 196616 | tf_op jit(solution)/shard_map/ppermute | solution.py:453
  41.2 5.1 %copy-start.13 = (bf16[128,256]{1,0:T(8,128)(2,1)}, bf16[128,256]{1,0:T(8,128)(2,1)S(1)}, u32[]{:S(2)}) copy-start(bf16[128,256]{1,0:T(8,128)(2,1)S(1)} %collective-permute-done.3.rest_10_) | copy-start | bytes 196612
  43.1 3.2 %copy-start.14 = (bf16[128,256]{1,0:T(8,128)(2,1)}, bf16[128,256]{1,0:T(8,128)(2,1)S(1)}, u32[]{:S(2)}) copy-start(bf16[128,256]{1,0:T(8,128)(2,1)S(1)} %collective-permute-done.4.rest_11_) | copy-start | bytes 196612
  43.1 3.2 %copy-start.15 = (bf16[128,256]{1,0:T(8,128)(2,1)}, bf16[128,256]{1,0:T(8,128)(2,1)S(1)}, u32[]{:S(2)}) copy-start(bf16[128,256]{1,0:T(8,128)(2,1)S(1)} %collective-permute-done.5.rest_12_) | copy-start | bytes 196612
  43.1 9.8 %collective-permute-start.6 = (bf16[128,1024]{1,0:T(8,128)(2,1)S(1)}, bf16[128,1024]{1,0:T(8,128)(2,1)S(1)}, u32[]{:S(2)}, u32[]{:S(2)}) collective-permute-start(bf16[128,1024]{1,0:T(8,128)(2,1)S(1)} %get-tuple-element.53), channel_id=1, source_target_pairs={{0,1},{1,2},{2,3},{3,0},{4,5},{5,6},{6,7},{7,4},{8,9},{9,10},{10,1... | collective-permute-start | bytes 786440 | tf_op jit(solution)/shard_map/ppermute | solution.py:453
  55.6 32.1 %all-to-all-start.1 = ((bf16[8,4,128,2,128]{4,3,2,1,0:T(2,128)(2,1)}), bf16[8,4,128,2,128]{4,3,2,1,0:T(2,128)(2,1)}, u32[]{:S(2)}, u32[]{:S(2)}) async-start(bf16[8,4,128,2,128]{4,3,2,1,0:T(2,128)(2,1)} %get-tuple-element.60), calls=%async_computation.1 | async-start | bytes 4194304 | tf_op jit(solution)/shard_map/all_to_all | solution.py:544
  60.0 14.8 %collective-permute-start.7 = (bf16[128,1024]{1,0:T(8,128)(2,1)S(1)}, bf16[128,1024]{1,0:T(8,128)(2,1)S(1)}, u32[]{:S(2)}, u32[]{:S(2)}) collective-permute-start(bf16[128,1024]{1,0:T(8,128)(2,1)S(1)} %get-tuple-element.53), channel_id=1, source_target_pairs={{0,2},{1,3},{2,0},{3,1},{4,6},{5,7},{6,4},{7,5},{8,10},{9,11},{10,... | collective-permute-start | bytes 786440 | tf_op jit(solution)/shard_map/ppermute | solution.py:453
  60.4 14.4 %collective-permute-start.8 = (bf16[128,1024]{1,0:T(8,128)(2,1)S(1)}, bf16[128,1024]{1,0:T(8,128)(2,1)S(1)}, u32[]{:S(2)}, u32[]{:S(2)}) collective-permute-start(bf16[128,1024]{1,0:T(8,128)(2,1)S(1)} %get-tuple-element.53), channel_id=1, source_target_pairs={{0,3},{1,0},{2,1},{3,2},{4,7},{5,4},{6,5},{7,6},{8,11},{9,8},{10,9... | collective-permute-start | bytes 786440 | tf_op jit(solution)/shard_map/ppermute | solution.py:453
  62.7 13.2 %copy-start.19 = (bf16[1024]{0:T(1024)(128)(2,1)S(1)}, bf16[1024]{0:T(1024)(128)(2,1)}, u32[]{:S(2)}) copy-start(bf16[1024]{0:T(1024)(128)(2,1)} %param.18) | copy-start | bytes 6148
  75.8 8.7 %collective-permute-start.12 = (bf16[3,128,1024]{2,1,0:T(8,128)(2,1)}, bf16[3,128,1024]{2,1,0:T(8,128)(2,1)}, u32[]{:S(2)}, u32[]{:S(2)}) collective-permute-start(bf16[3,128,1024]{2,1,0:T(8,128)(2,1)} %pad_maximum_fusion.2), channel_id=1, source_target_pairs={{0,4},{4,0},{8,12},{12,8},{16,20},{20,16},{24,28},{28,24},{1,5},{5... | collective-permute-start | bytes 2359304 | tf_op jit(solution)/shard_map/ppermute | solution.py:457
  75.8 22.8 %collective-permute-start.10 = (bf16[512,128]{1,0:T(8,128)(2,1)}, bf16[512,128]{1,0:T(8,128)(2,1)}, u32[]{:S(2)}, u32[]{:S(2)}) collective-permute-start(bf16[512,128]{1,0:T(8,128)(2,1)} %attend.2), channel_id=1, source_target_pairs={{0,2},{1,3},{2,0},{3,1},{4,6},{5,7},{6,4},{7,5},{8,10},{9,11},{10,... | collective-permute-start | bytes 393224 | tf_op jit(solution)/shard_map/ppermute | solution.py:453
  81.0 17.6 %collective-permute-start.11 = (bf16[512,128]{1,0:T(8,128)(2,1)}, bf16[512,128]{1,0:T(8,128)(2,1)}, u32[]{:S(2)}, u32[]{:S(2)}) collective-permute-start(bf16[512,128]{1,0:T(8,128)(2,1)} %attend.2), channel_id=1, source_target_pairs={{0,3},{1,0},{2,1},{3,2},{4,7},{5,4},{6,5},{7,6},{8,11},{9,8},{10,9... | collective-permute-start | bytes 393224 | tf_op jit(solution)/shard_map/ppermute | solution.py:453
  84.5 14.2 %collective-permute-start.9 = (bf16[512,128]{1,0:T(8,128)(2,1)}, bf16[512,128]{1,0:T(8,128)(2,1)}, u32[]{:S(2)}, u32[]{:S(2)}) collective-permute-start(bf16[512,128]{1,0:T(8,128)(2,1)} %attend.2), channel_id=1, source_target_pairs={{0,1},{1,2},{2,3},{3,0},{4,5},{5,6},{6,7},{7,4},{8,9},{9,10},{10,1... | collective-permute-start | bytes 393224 | tf_op jit(solution)/shard_map/ppermute | solution.py:453
  86.7 16.4 %copy-start.6 = (bf16[512,128]{1,0:T(8,128)(2,1)S(1)}, bf16[512,128]{1,0:T(8,128)(2,1)}, u32[]{:S(2)}) copy-start(bf16[512,128]{1,0:T(8,128)(2,1)} %attend.2) | copy-start | bytes 393220
  87.8 18.0 %copy-start.7 = (bf16[4,64,1024]{2,1,0:T(8,128)(2,1)S(1)}, bf16[4,64,1024]{2,1,0:T(8,128)(2,1)}, u32[]{:S(2)}) copy-start(bf16[4,64,1024]{2,1,0:T(8,128)(2,1)} %get-tuple-element.48) | copy-start | bytes 1572868
  98.6 8.9 %copy-start.11 = (bf16[256,128]{1,0:T(8,128)(2,1)S(1)}, bf16[256,128]{1,0:T(8,128)(2,1)}, u32[]{:S(2)}) copy-start(bf16[256,128]{1,0:T(8,128)(2,1)} %get-tuple-element.75) | copy-start | bytes 196612
  98.6 11.0 %copy-start.2 = (bf16[512,1024]{1,0:T(8,128)(2,1)S(1)}, bf16[512,1024]{1,0:T(8,128)(2,1)}, u32[]{:S(2)}) copy-start(bf16[512,1024]{1,0:T(8,128)(2,1)} %pad_maximum_fusion) | copy-start | bytes 3145732
  98.7 11.4 %collective-permute-start.13 = (bf16[256,128]{1,0:T(8,128)(2,1)}, bf16[256,128]{1,0:T(8,128)(2,1)S(1)}, u32[]{:S(2)}, u32[]{:S(2)}) collective-permute-start(bf16[256,128]{1,0:T(8,128)(2,1)} %get-tuple-element.70), channel_id=1, source_target_pairs={{0,1},{1,2},{2,3},{3,0},{4,5},{5,6},{6,7},{7,4},{8,9},{9,10},{10,1... | collective-permute-start | bytes 196616 | tf_op jit(solution)/shard_map/ppermute | solution.py:453
  99.9 12.8 %collective-permute-start.14 = (bf16[256,128]{1,0:T(8,128)(2,1)}, bf16[256,128]{1,0:T(8,128)(2,1)S(1)}, u32[]{:S(2)}, u32[]{:S(2)}) collective-permute-start(bf16[256,128]{1,0:T(8,128)(2,1)} %get-tuple-element.70), channel_id=1, source_target_pairs={{0,2},{1,3},{2,0},{3,1},{4,6},{5,7},{6,4},{7,5},{8,10},{9,11},{10,... | collective-permute-start | bytes 196616 | tf_op jit(solution)/shard_map/ppermute | solution.py:453
  103.1 9.6 %collective-permute-start.15 = (bf16[256,128]{1,0:T(8,128)(2,1)}, bf16[256,128]{1,0:T(8,128)(2,1)S(1)}, u32[]{:S(2)}, u32[]{:S(2)}) collective-permute-start(bf16[256,128]{1,0:T(8,128)(2,1)} %get-tuple-element.70), channel_id=1, source_target_pairs={{0,3},{1,0},{2,1},{3,2},{4,7},{5,4},{6,5},{7,6},{8,11},{9,8},{10,9... | collective-permute-start | bytes 196616 | tf_op jit(solution)/shard_map/ppermute | solution.py:453
  105.8 7.0 %copy-start.12 = (bf16[256,128]{1,0:T(8,128)(2,1)S(1)}, bf16[256,128]{1,0:T(8,128)(2,1)}, u32[]{:S(2)}) copy-start(bf16[256,128]{1,0:T(8,128)(2,1)} %get-tuple-element.70) | copy-start | bytes 196612
  107.5 10.9 %collective-permute-start.19 = (bf16[256,128]{1,0:T(8,128)(2,1)S(1)}, bf16[256,128]{1,0:T(8,128)(2,1)S(1)}, u32[]{:S(2)}, u32[]{:S(2)}) collective-permute-start(bf16[256,128]{1,0:T(8,128)(2,1)S(1)} %copy-done.11), channel_id=1, source_target_pairs={{0,1},{1,2},{2,3},{3,0},{4,5},{5,6},{6,7},{7,4},{8,9},{9,10},{10,1... | collective-permute-start | bytes 196616 | tf_op jit(solution)/shard_map/ppermute | solution.py:453
  109.6 10.6 %collective-permute-start.20 = (bf16[256,128]{1,0:T(8,128)(2,1)S(1)}, bf16[256,128]{1,0:T(8,128)(2,1)S(1)}, u32[]{:S(2)}, u32[]{:S(2)}) collective-permute-start(bf16[256,128]{1,0:T(8,128)(2,1)S(1)} %copy-done.11), channel_id=1, source_target_pairs={{0,2},{1,3},{2,0},{3,1},{4,6},{5,7},{6,4},{7,5},{8,10},{9,11},{10,... | collective-permute-start | bytes 196616 | tf_op jit(solution)/shard_map/ppermute | solution.py:453
  109.6 3.7 %copy-start.1 = (bf16[2,1024,1024]{2,1,0:T(8,128)(2,1)S(1)}, bf16[2,1024,1024]{2,1,0:T(8,128)(2,1)}, u32[]{:S(2)}) copy-start(bf16[2,1024,1024]{2,1,0:T(8,128)(2,1)} %param.21) | copy-start | bytes 12582916
  110.0 10.1 %collective-permute-start.21 = (bf16[256,128]{1,0:T(8,128)(2,1)S(1)}, bf16[256,128]{1,0:T(8,128)(2,1)S(1)}, u32[]{:S(2)}, u32[]{:S(2)}) collective-permute-start(bf16[256,128]{1,0:T(8,128)(2,1)S(1)} %copy-done.11), channel_id=1, source_target_pairs={{0,3},{1,0},{2,1},{3,2},{4,7},{5,4},{6,5},{7,6},{8,11},{9,8},{10,9... | collective-permute-start | bytes 196616 | tf_op jit(solution)/shard_map/ppermute | solution.py:453
  114.9 5.3 %copy-start.5 = (bf16[4,64,1024]{2,1,0:T(8,128)(2,1)S(1)}, bf16[4,64,1024]{2,1,0:T(8,128)(2,1)}, u32[]{:S(2)}) copy-start(bf16[4,64,1024]{2,1,0:T(8,128)(2,1)} %get-tuple-element.72) | copy-start | bytes 1572868
  115.8 9.1 %collective-permute-start.16 = (bf16[64,1024]{1,0:T(8,128)(2,1)S(1)}, bf16[64,1024]{1,0:T(8,128)(2,1)S(1)}, u32[]{:S(2)}, u32[]{:S(2)}) collective-permute-start(bf16[64,1024]{1,0:T(8,128)(2,1)S(1)} %get-tuple-element.100), channel_id=1, source_target_pairs={{0,1},{1,2},{2,3},{3,0},{4,5},{5,6},{6,7},{7,4},{8,9},{9,10},{10,1... | collective-permute-start | bytes 393224 | tf_op jit(solution)/shard_map/ppermute | solution.py:453
  116.7 14.1 %collective-permute-start.17 = (bf16[64,1024]{1,0:T(8,128)(2,1)S(1)}, bf16[64,1024]{1,0:T(8,128)(2,1)S(1)}, u32[]{:S(2)}, u32[]{:S(2)}) collective-permute-start(bf16[64,1024]{1,0:T(8,128)(2,1)S(1)} %get-tuple-element.99), channel_id=1, source_target_pairs={{0,2},{1,3},{2,0},{3,1},{4,6},{5,7},{6,4},{7,5},{8,10},{9,11},{10,... | collective-permute-start | bytes 393224 | tf_op jit(solution)/shard_map/ppermute | solution.py:453
  118.4 12.5 %collective-permute-start.18 = (bf16[64,1024]{1,0:T(8,128)(2,1)S(1)}, bf16[64,1024]{1,0:T(8,128)(2,1)S(1)}, u32[]{:S(2)}, u32[]{:S(2)}) collective-permute-start(bf16[64,1024]{1,0:T(8,128)(2,1)S(1)} %get-tuple-element.98), channel_id=1, source_target_pairs={{0,3},{1,0},{2,1},{3,2},{4,7},{5,4},{6,5},{7,6},{8,11},{9,8},{10,9... | collective-permute-start | bytes 393224 | tf_op jit(solution)/shard_map/ppermute | solution.py:453
  123.2 8.3 %collective-permute-start.22 = (bf16[64,1024]{1,0:T(8,128)(2,1)S(1)}, bf16[64,1024]{1,0:T(8,128)(2,1)S(1)}, u32[]{:S(2)}, u32[]{:S(2)}) collective-permute-start(bf16[64,1024]{1,0:T(8,128)(2,1)S(1)} %get-tuple-element.95), channel_id=1, source_target_pairs={{0,1},{1,2},{2,3},{3,0},{4,5},{5,6},{6,7},{7,4},{8,9},{9,10},{10,1... | collective-permute-start | bytes 393224 | tf_op jit(solution)/shard_map/ppermute | solution.py:453
  123.5 14.7 %collective-permute-start.23 = (bf16[64,1024]{1,0:T(8,128)(2,1)S(1)}, bf16[64,1024]{1,0:T(8,128)(2,1)S(1)}, u32[]{:S(2)}, u32[]{:S(2)}) collective-permute-start(bf16[64,1024]{1,0:T(8,128)(2,1)S(1)} %get-tuple-element.97), channel_id=1, source_target_pairs={{0,2},{1,3},{2,0},{3,1},{4,6},{5,7},{6,4},{7,5},{8,10},{9,11},{10,... | collective-permute-start | bytes 393224 | tf_op jit(solution)/shard_map/ppermute | solution.py:453
  124.9 13.3 %collective-permute-start.24 = (bf16[64,1024]{1,0:T(8,128)(2,1)S(1)}, bf16[64,1024]{1,0:T(8,128)(2,1)S(1)}, u32[]{:S(2)}, u32[]{:S(2)}) collective-permute-start(bf16[64,1024]{1,0:T(8,128)(2,1)S(1)} %get-tuple-element.96), channel_id=1, source_target_pairs={{0,3},{1,0},{2,1},{3,2},{4,7},{5,4},{6,5},{7,6},{8,11},{9,8},{10,9... | collective-permute-start | bytes 393224 | tf_op jit(solution)/shard_map/ppermute | solution.py:453

commit v8 on v7

--- a/solution.py
+++ b/solution.py
@@ -333,7 +333,7 @@
 
     _, found = lax.fori_loop(0, n_req, list_pairs, (jnp.int32(0), jnp.int32(0)))
 
-    def pair_body(i, carry):
+    def one_pair(i, sbuf, wbuf):
         t, r, start = pairs[0, i], pairs[1, i], pairs[2, i]
         row0 = pl.multiple_of(t * TILE, TILE)
         live = counts_ref[0, r]
@@ -395,9 +395,13 @@
             mixed = jnp.where(lane >= a * HD, o[parts[a]], mixed)
         inside = (row >= start_f) & (row < end.astype(F32))
         obuf[t] = jnp.where(inside[:, :width], mixed, obuf[t])
+
+    def pair_body(i, carry):
+        one_pair(2 * i, sbuf.at[0], wbuf.at[0])
+        one_pair(jnp.minimum(2 * i + 1, found - 1), sbuf.at[1], wbuf.at[1])
         return carry
 
-    lax.fori_loop(0, found, pair_body, 0)
+    lax.fori_loop(0, (found + 1) // 2, pair_body, 0)
     per_chunk = rows // n_chunk
     for t in range(rows // TILE):
         if n_chunk == 1:
@@ -439,8 +443,8 @@
             pltpu.VMEM((back + rows, lanes), BF),
             pltpu.VMEM((tiles, per * TILE, lanes), BF),
             pltpu.SMEM((3, tiles + lens.shape[1]), jnp.int32),
-            pltpu.VMEM((n_all, per * TILE, KCH), F32),
-            pltpu.VMEM((per * TILE, n_all * KCH), BF),
+            pltpu.VMEM((2, n_all, per * TILE, KCH), F32),
+            pltpu.VMEM((2, per * TILE, n_all * KCH), BF),
             pltpu.VMEM((tiles, TILE, lanes), F32),
         ],
         compiler_params=pltpu.CompilerParams(vmem_limit_bytes=60 << 20),
@@ -568,27 +572,20 @@
         early.append(blocks)
     if w_whole is None:
         w_whole = whole_weight(w_out, halves, dp, n_dp, n_group)
-    last = attended(n_group - 1, query, True)
+    last = attended(n_group - 1, query, False)[0]
     early, last, w_whole = lax.optimization_barrier((early, last, w_whole))
-    early = [[jnp.split(block, n_chunk) for block in blocks] for blocks in early]
+    last = [last] + [shift(last, "tensor", n_tp, k) for k in far_first]
     outs = []
     pieces = None
-    bases = []
-    late = []
+    base = jnp.concatenate(all_tokens, axis=0).reshape(tok_total, d_model).astype(F32)
+    for a in range(n_group - 1):
+        base = base + mixed(early[a], a)
+    last = lax.optimization_barrier((last, base))[0]
+    everything = base + mixed(last, n_group - 1)
     for c in range(n_chunk):
-        own = last[c]
-        if bases:
-            own = lax.optimization_barrier((own, bases[-1]))[0]
-        late.append([own] + [shift(own, "tensor", n_tp, k) for k in far_first])
-        base = all_tokens[c].reshape(n_tp * sub, d_model).astype(F32)
-        for a in range(n_group - 1):
-            base = base + mixed([block[c] for block in early[a]], a)
-        bases.append(base)
-    for c in range(n_chunk):
-        blocks = late[c]
+        residual = everything[c * n_tp * sub : (c + 1) * n_tp * sub]
         if pieces is not None:
-            blocks = lax.optimization_barrier((blocks, pieces))[0]
-        residual = bases[c] + mixed(blocks, n_group - 1)
+            residual = lax.optimization_barrier((residual, pieces))[0]
         ffn_in = normalize(residual, ffn_gain).astype(BF)
         gate_up = jnp.einsum("td,kdf->ktf", ffn_in, w_gateup, preferred_element_type=F32)
         hidden = (jax.nn.silu(gate_up[0]) * gate_up[1]).astype(BF)

time: 140 us -> 145 us (1.036); the launches traced: 139 us -> 142 us
  waiting for transfers between devices: 19.3 us -> 28.2 us
  starting transfers between devices: 50.4 us -> 46.3 us
  Pallas kernels: 35 us -> 32.2 us
  other arithmetic: 9.48 us -> 11.2 us
    ppermute x24 -> x21, waiting for transfers between devices: 16.6 us -> 25.5 us  [shift(): return lax.ppermute(value, axis, [(i, (i + k) % n) for i in range(n)])]
    ppermute x24 -> x21, starting transfers between devices: 41.6 us -> 37.6 us  [shift(): return lax.ppermute(value, axis, [(i, (i + k) % n) for i in range(n)])]
    pallas_call x2, Pallas kernels: 21.6 us -> 18.6 us  [attend(): pl.pallas_call(functools.partial(attend_kernel, group, per, n_chunk), gri...]
    split x4 -> x0, local copies, waits for them, and re-layouts: 2.66 us -> none  [per_device(): jnp.split(block, n_chunk)]
    concatenate x0 -> x1, other arithmetic: none -> 2.31 us  [per_device(): jnp.concatenate(all_tokens, axis=0).reshape(tok_total, d_model).astype(F32)]
    unnamed x40 -> x34, local copies, waits for them, and re-layouts: 1.51 us -> 3.36 us
    dot_general x4 -> x2, matrix products: 3.24 us -> 3.18 us  [mixed(): jnp.dot(jnp.concatenate(blocks, axis=1), w_whole[a], preferred_element_ty...]
  transfers between devices with their start and end apart: 27 -> 24, of which waited for: 8 -> 9; matrix products, arithmetic and copies ran while one was open for 16% -> 12% of each run, Pallas kernels for 25% -> 23%
where the time goes in v8:
time: 145 us; the launch traced here: 142 us
  starting transfers between devices  46.3 us (32%)
  Pallas kernels  32.2 us (22%)
  waiting for transfers between devices  28.2 us (19%)
  other arithmetic  11.2 us (8%)
  blocking collectives  9.99 us (7%)
  matrix products  7.51 us (5%)
  local copies, waits for them, and re-layouts  6.06 us (4%)
    ppermute x21, starting transfers between devices, shift(): return lax.ppermute(value, axis, [(i, (i + k) % n) for i in range(n)])  37.6 us
    ppermute x21, waiting for transfers between devices, shift(): return lax.ppermute(value, axis, [(i, (i + k) % n) for i in range(n)])  25.5 us
    pallas_call x2, Pallas kernels, attend(): pl.pallas_call(functools.partial(attend_kernel, group, per, n_chunk), gri...  18.6 us
    all_gather x1, blocking collectives, per_device(): gathered = lax.all_gather(payload, 'dp', axis=0)  9.99 us
    all_to_all x2, starting transfers between devices, per_device(): lax.all_to_all(send, 'dp', split_axis=0, concat_axis=0, tiled=True)  8.7 us
    pallas_call x1, Pallas kernels, project(): pl.pallas_call(functools.partial(project_kernel, n_tp, cap, pool_dev, n_c...  6.62 us
    pallas_call x1, Pallas kernels, pick(): pl.pallas_call(functools.partial(pick_kernel, n_dp, cap), out_shape=[jax....  4.78 us
    unnamed x34, local copies, waits for them, and re-layouts  3.36 us
  transfers between devices with their start and end apart: 24, of which 9 were waited for; matrix products, arithmetic and copies ran while one was open for 12% of the time, Pallas kernels for 23%

profile of v8, /device:TPU:0, one launch (start us, length us, event | category | flops | bytes accessed | tf_op | source)
XLA Modules:
  0.0 141.8 jit_solution(18050257433303606703)
XLA Ops:
  0.0 3.0 %collective-permute-start = (bf16[128,1024]{1,0:T(8,128)(2,1)}, bf16[128,1024]{1,0:T(8,128)(2,1)S(1)}, u32[]{:S(2)}, u32[]{:S(2)}) collective-permute-start(bf16[128,1024]{1,0:T(8,128)(2,1)} %rest_5_.1), channel_id=1, source_target_pairs={{0,1},{1,2},{2,3},{3,0},{4,5},{5,6},{6,7},{7,4},{8,9},{9,10},{10,1... | collective-permute-start | bytes 786440 | tf_op jit(solution)/shard_map/ppermute | solution.py:457
  3.0 2.6 %collective-permute-start.1 = (bf16[128,1024]{1,0:T(8,128)(2,1)}, bf16[128,1024]{1,0:T(8,128)(2,1)S(1)}, u32[]{:S(2)}, u32[]{:S(2)}) collective-permute-start(bf16[128,1024]{1,0:T(8,128)(2,1)} %rest_5_.1), channel_id=1, source_target_pairs={{0,2},{1,3},{2,0},{3,1},{4,6},{5,7},{6,4},{7,5},{8,10},{9,11},{10,... | collective-permute-start | bytes 786440 | tf_op jit(solution)/shard_map/ppermute | solution.py:457
  5.6 0.7 fusion.47
  6.3 0.8 constant_dynamic-slice_fusion.1
  7.1 0.8 pad_maximum_fusion.5
  7.8 10.0 %all-gather = bf16[1152,256]{1,0:T(8,128)(2,1)S(1)} all-gather(bf16[144,256]{1,0:T(8,128)(2,1)S(1)} %pad_maximum_fusion.5), channel_id=2, replica_groups=mesh['dp'=8,'tensor'=4] {'dp'}, dimensions={0}, use_global_device_ids=true | all-gather | bytes 663552 | tf_op jit(solution)/shard_map/all_gather | solution.py:524
  17.8 0.6 slice_convert_fusion.asked_ref
  18.5 4.8 %pick_pages.1 = (bf16[8,4,128,2,128]{4,3,2,1,0:T(2,128)(2,1)}, bf16[8,4,128,2,128]{4,3,2,1,0:T(2,128)(2,1)}) custom-call(s32[1]{0:T(128)} %bitcast.4.me_ref, s32[8,2,32]{2,1,0:T(2,128)} %slice_convert_fusion.asked_ref, bf16[32,128,2,256]{3,2,1,0:T(2,128)(2,1)} %pool_ref.1), custom_call_target="tpu_custom_call" | custom-call | flops 1000 | bytes 1000 | tf_op jit(solution)/shard_map/pick_pages/pallas_call | solution.py:82
  23.3 0.7 copy-done.7
  24.0 0.7 copy-done.8
  24.7 4.4 %all-to-all-start = ((bf16[8,4,128,2,128]{4,3,2,1,0:T(2,128)(2,1)}), bf16[8,4,128,2,128]{4,3,2,1,0:T(2,128)(2,1)}, u32[]{:S(2)}, u32[]{:S(2)}) async-start(bf16[8,4,128,2,128]{4,3,2,1,0:T(2,128)(2,1)} %get-tuple-element.40), calls=%async_computation | async-start | bytes 4194304 | tf_op jit(solution)/shard_map/all_to_all | solution.py:528
  29.1 1.4 collective-permute-start.2
  30.5 0.6 reshape.109.rest_0_
  31.1 0.8 fusion.56
  31.9 2.2 %named_adapters.1 = (bf16[128,256]{1,0:T(8,128)(2,1)}, bf16[128,256]{1,0:T(8,128)(2,1)}) custom-call(s32[16]{0:T(128)} %table_ref.2, s32[1,4]{1,0:T(1,128)} %ids_ref.1, bf16[8,144,256]{2,1,0:T(8,128)(2,1)} %bitcast.98), custom_call_target="tpu_custom_call" | custom-call | flops 1000 | bytes 1000 | tf_op jit(solution)/shard_map/named_adapters/pallas_call | solution.py:126
  34.1 0.7 collective-permute-start.3
  34.8 0.3 collective-permute-start.4
  35.2 2.8 %collective-permute-start.5 = (bf16[128,256]{1,0:T(8,128)(2,1)}, bf16[128,256]{1,0:T(8,128)(2,1)S(1)}, u32[]{:S(2)}, u32[]{:S(2)}) collective-permute-start(bf16[128,256]{1,0:T(8,128)(2,1)} %get-tuple-element.44.rest_9_), channel_id=1, source_target_pairs={{0,3},{1,0},{2,1},{3,2},{4,7},{5,4},{6,5},{7,6},{8,11},{9,8},{10,9... | collective-permute-start | bytes 196616 | tf_op jit(solution)/shard_map/ppermute | solution.py:457
  38.0 0.2 reduce-window.4
  38.2 0.1 convert_reduce_fusion
  38.3 0.1 select_reduce_fusion.1
  38.4 2.8 %collective-permute-done.3.rest_10_ = bf16[128,256]{1,0:T(8,128)(2,1)S(1)} collective-permute-done((bf16[128,256]{1,0:T(8,128)(2,1)}, bf16[128,256]{1,0:T(8,128)(2,1)S(1)}, u32[]{:S(2)}, u32[]{:S(2)}) %collective-permute-start.3) | collective-permute-done | bytes 65568 | tf_op jit(solution)/shard_map/ppermute | solution.py:457
  41.2 2.0 %collective-permute-done.4.rest_11_ = bf16[128,256]{1,0:T(8,128)(2,1)S(1)} collective-permute-done((bf16[128,256]{1,0:T(8,128)(2,1)}, bf16[128,256]{1,0:T(8,128)(2,1)S(1)}, u32[]{:S(2)}, u32[]{:S(2)}) %collective-permute-start.4) | collective-permute-done | bytes 65568 | tf_op jit(solution)/shard_map/ppermute | solution.py:457
  43.2 1.3 collective-permute-start.6
  44.5 1.8 %fusion.28 = (f32[512,128]{1,0:T(8,128)}, f32[512,128]{1,0:T(8,128)}) fusion(f32[128]{0:T(128)S(1)} %get-tuple-element.109, f32[128]{0:T(128)S(1)} %get-tuple-element.110, f32[512]{0:T(512)S(1)} %fusion.41), kind=kLoop, calls=%fused_computation.42 | loop fusion | flops 131072 | bytes 527360 | tf_op jit(solution)/shard_map/mul | solution.py:542
  46.4 6.6 %project.1 = (bf16[512,256]{1,0:T(8,128)(2,1)}, bf16[512,256]{1,0:T(8,128)(2,1)}, bf16[512,256]{1,0:T(8,128)(2,1)}, s32[32]{0:T(128)}, bf16[4,64,1024]{2,1,0:T(8,128)(2,1)}, /*index=5*/bf16[4,64,1024]{2,1,0:T(8,128)(2,1)}) custom-call(s32[1]{0:T(128)} %bitcast.tp_ref, s32[1,4]{1,0:T(1,128)} %lens_ref.5, s32[1,32]{1,0:T(1,128)} %table_ref.3, ...), custom_call_target="tpu_custom_call" | custom-call | flops 1000 | bytes 1000 | tf_op jit(solution)/shard_map/project/pallas_call | solution.py:250
  53.0 2.7 %all-to-all-done = bf16[8,4,128,2,128]{4,3,2,1,0:T(2,128)(2,1)} async-done(((bf16[8,4,128,2,128]{4,3,2,1,0:T(2,128)(2,1)}), bf16[8,4,128,2,128]{4,3,2,1,0:T(2,128)(2,1)}, u32[]{:S(2)}, u32[]{:S(2)}) %all-to-all-start) | async-done | bytes 2097184 | tf_op jit(solution)/shard_map/all_to_all | solution.py:528
  55.7 4.4 %all-to-all-start.1 = ((bf16[8,4,128,2,128]{4,3,2,1,0:T(2,128)(2,1)}), bf16[8,4,128,2,128]{4,3,2,1,0:T(2,128)(2,1)}, u32[]{:S(2)}, u32[]{:S(2)}) async-start(bf16[8,4,128,2,128]{4,3,2,1,0:T(2,128)(2,1)} %get-tuple-element.58), calls=%async_computation.1 | async-start | bytes 4194304 | tf_op jit(solution)/shard_map/all_to_all | solution.py:548
  60.0 0.4 collective-permute-start.7
  60.4 2.2 %collective-permute-start.8 = (bf16[128,1024]{1,0:T(8,128)(2,1)S(1)}, bf16[128,1024]{1,0:T(8,128)(2,1)S(1)}, u32[]{:S(2)}, u32[]{:S(2)}) collective-permute-start(bf16[128,1024]{1,0:T(8,128)(2,1)S(1)} %get-tuple-element.51), channel_id=1, source_target_pairs={{0,3},{1,0},{2,1},{3,2},{4,7},{5,4},{6,5},{7,6},{8,11},{9,8},{10,9... | collective-permute-start | bytes 786440 | tf_op jit(solution)/shard_map/ppermute | solution.py:457
  62.7 9.3 %attend.2 = bf16[512,128]{1,0:T(8,128)(2,1)} custom-call(s32[1,4]{1,0:T(1,128)} %lens_ref.5, s32[1,4]{1,0:T(1,128)} %counts_ref.3, s32[32]{0:T(128)} %get-tuple-element.47.pos_ref, f32[2,4]{1,0:T(2,128)} %bias_ref.3, bf16[512,256]{1,0:T(8,128)(2,1)} %get-tuple-element.56.q_ref, bf16[512,256]{1,0:T(8,128)(2,1)} %get-tuple-element.49.kn_ref, ...), custom_call_target="tpu_custom_call" | custom-call | flops 1000 | bytes 1000 | tf_op jit(solution)/shard_map/attend/pallas_call | solution.py:431
  72.0 2.9 %collective-permute-done.7 = bf16[128,1024]{1,0:T(8,128)(2,1)S(1)} collective-permute-done((bf16[128,1024]{1,0:T(8,128)(2,1)S(1)}, bf16[128,1024]{1,0:T(8,128)(2,1)S(1)}, u32[]{:S(2)}, u32[]{:S(2)}) %collective-permute-start.7) | collective-permute-done | bytes 262176 | tf_op jit(solution)/shard_map/ppermute | solution.py:457
  74.9 1.0 pad_maximum_fusion.3
  75.9 2.3 %pad_maximum_fusion = bf16[8,64,1024]{2,1,0:T(8,128)(2,1)} fusion(bf16[4,64,1024]{2,1,0:T(8,128)(2,1)} %get-tuple-element.46, bf16[4,64,1024]{2,1,0:T(8,128)(2,1)} %get-tuple-element.45), kind=kLoop, calls=%fused_computation.8 | loop fusion | flops 524288 | bytes 2097152 | tf_op jit(solution)/shard_map/concatenate | solution.py:580
  78.2 5.1 %collective-permute-start.10 = (bf16[512,128]{1,0:T(8,128)(2,1)S(1)}, bf16[512,128]{1,0:T(8,128)(2,1)}, u32[]{:S(2)}, u32[]{:S(2)}) collective-permute-start(bf16[512,128]{1,0:T(8,128)(2,1)S(1)} %copy-done.9), channel_id=1, source_target_pairs={{0,2},{1,3},{2,0},{3,1},{4,6},{5,7},{6,4},{7,5},{8,10},{9,11},{10,... | collective-permute-start | bytes 393224 | tf_op jit(solution)/shard_map/ppermute | solution.py:457
  83.3 3.5 %collective-permute-start.11 = (bf16[512,128]{1,0:T(8,128)(2,1)S(1)}, bf16[512,128]{1,0:T(8,128)(2,1)}, u32[]{:S(2)}, u32[]{:S(2)}) collective-permute-start(bf16[512,128]{1,0:T(8,128)(2,1)S(1)} %copy-done.9), channel_id=1, source_target_pairs={{0,3},{1,0},{2,1},{3,2},{4,7},{5,4},{6,5},{7,6},{8,11},{9,8},{10,9... | collective-permute-start | bytes 393224 | tf_op jit(solution)/shard_map/ppermute | solution.py:457
  86.8 1.2 broadcast_select_fusion.2
  88.1 1.1 pad_maximum_fusion.1
  89.2 9.3 %attend.3 = bf16[512,128]{1,0:T(8,128)(2,1)} custom-call(s32[1,4]{1,0:T(1,128)} %lens_ref.5, s32[1,4]{1,0:T(1,128)} %counts_ref.3, s32[32]{0:T(128)} %get-tuple-element.47.pos_ref, f32[2,4]{1,0:T(2,128)} %bias_ref.3, bf16[512,256]{1,0:T(8,128)(2,1)} %get-tuple-element.56.q_ref, bf16[512,256]{1,0:T(8,128)(2,1)} %get-tuple-element.49.kn_ref, ...), custom_call_target="tpu_custom_call" | custom-call | flops 1000 | bytes 1000 | tf_op jit(solution)/shard_map/attend/pallas_call | solution.py:431
  98.5 1.3 collective-permute-start.13
  99.8 3.1 %collective-permute-start.14 = (bf16[512,128]{1,0:T(8,128)(2,1)}, bf16[512,128]{1,0:T(8,128)(2,1)S(1)}, u32[]{:S(2)}, u32[]{:S(2)}) collective-permute-start(bf16[512,128]{1,0:T(8,128)(2,1)} %attend.3), channel_id=1, source_target_pairs={{0,2},{1,3},{2,0},{3,1},{4,6},{5,7},{6,4},{7,5},{8,10},{9,11},{10,... | collective-permute-start | bytes 393224 | tf_op jit(solution)/shard_map/ppermute | solution.py:457
  102.9 2.4 %convert_add_fusion = f32[512,1024]{1,0:T(8,128)S(1)} fusion(bf16[512,1024]{1,0:T(8,128)(2,1)} %bitcast.100, bf16[512,1024]{1,0:T(8,128)(2,1)} %pad_maximum_fusion.1, bf16[512,128]{1,0:T(8,128)(2,1)} %collective-permute-done.11, bf16[512,128]{1,0:T(8,128)(2,1)} %collective-permute-done.10, bf16[512,128]{1,0:T(8,128)(2,1)} %collective-permute-done.9, ...), kind=kOutput, calls=%fused_computation | convolution fusion | flops 540016640 | bytes 4718592 | tf_op jit(solution)/shard_map/dot_general | solution.py:553
  105.4 1.7 %collective-permute-done.13 = bf16[512,128]{1,0:T(8,128)(2,1)S(1)} collective-permute-done((bf16[512,128]{1,0:T(8,128)(2,1)}, bf16[512,128]{1,0:T(8,128)(2,1)S(1)}, u32[]{:S(2)}, u32[]{:S(2)}) %collective-permute-start.13) | collective-permute-done | bytes 131104 | tf_op jit(solution)/shard_map/ppermute | solution.py:457
  107.1 4.4 %collective-permute-done.14 = bf16[512,128]{1,0:T(8,128)(2,1)S(1)} collective-permute-done((bf16[512,128]{1,0:T(8,128)(2,1)}, bf16[512,128]{1,0:T(8,128)(2,1)S(1)}, u32[]{:S(2)}, u32[]{:S(2)}) %collective-permute-start.14) | collective-permute-done | bytes 131104 | tf_op jit(solution)/shard_map/ppermute | solution.py:457
  111.5 0.7 convolution_add_fusion
  112.2 0.2 fusion.53
  112.5 1.9 %copy-done.1 = bf16[2,1024,1024]{2,1,0:T(8,128)(2,1)S(1)} copy-done((bf16[2,1024,1024]{2,1,0:T(8,128)(2,1)S(1)}, bf16[2,1024,1024]{2,1,0:T(8,128)(2,1)}, u32[]{:S(2)}) %copy-start.1) | copy-done | bytes 4194328
  114.4 1.3 convolution_bitcast_fusion.1
  115.8 0.2 fusion.55
  116.0 0.8 fusion.57
  116.9 3.3 %collective-permute-start.16 = (bf16[64,1024]{1,0:T(8,128)(2,1)S(1)}, bf16[64,1024]{1,0:T(8,128)(2,1)S(1)}, u32[]{:S(2)}, u32[]{:S(2)}) collective-permute-start(bf16[64,1024]{1,0:T(8,128)(2,1)S(1)} %get-tuple-element.97), channel_id=1, source_target_pairs={{0,1},{1,2},{2,3},{3,0},{4,5},{5,6},{6,7},{7,4},{8,9},{9,10},{10,1... | collective-permute-start | bytes 393224 | tf_op jit(solution)/shard_map/ppermute | solution.py:457
  120.2 2.4 %collective-permute-start.18 = (bf16[64,1024]{1,0:T(8,128)(2,1)S(1)}, bf16[64,1024]{1,0:T(8,128)(2,1)S(1)}, u32[]{:S(2)}, u32[]{:S(2)}) collective-permute-start(bf16[64,1024]{1,0:T(8,128)(2,1)S(1)} %get-tuple-element.95), channel_id=1, source_target_pairs={{0,3},{1,0},{2,1},{3,2},{4,7},{5,4},{6,5},{7,6},{8,11},{9,8},{10,9... | collective-permute-start | bytes 393224 | tf_op jit(solution)/shard_map/ppermute | solution.py:457
  122.6 0.1 multiply_reduce_fusion
  122.8 1.3 convolution_bitcast_fusion
  124.2 0.2 fusion.54
  124.4 0.8 fusion.58
  125.3 2.5 %collective-permute-start.20 = (bf16[64,1024]{1,0:T(8,128)(2,1)S(1)}, bf16[64,1024]{1,0:T(8,128)(2,1)S(1)}, u32[]{:S(2)}, u32[]{:S(2)}) collective-permute-start(bf16[64,1024]{1,0:T(8,128)(2,1)S(1)} %get-tuple-element.94), channel_id=1, source_target_pairs={{0,2},{1,3},{2,0},{3,1},{4,6},{5,7},{6,4},{7,5},{8,10},{9,11},{10,... | collective-permute-start | bytes 393224 | tf_op jit(solution)/shard_map/ppermute | solution.py:457
  127.8 1.3 collective-permute-start.21
  129.2 1.1 collective-permute-done.17
  130.2 0.1 fusion.34
  130.3 3.3 %collective-permute-done.19 = bf16[64,1024]{1,0:T(8,128)(2,1)S(1)} collective-permute-done((bf16[64,1024]{1,0:T(8,128)(2,1)S(1)}, bf16[64,1024]{1,0:T(8,128)(2,1)S(1)}, u32[]{:S(2)}, u32[]{:S(2)}) %collective-permute-start.19) | collective-permute-done | bytes 131104 | tf_op jit(solution)/shard_map/ppermute | solution.py:457
  133.7 7.3 %collective-permute-done.20 = bf16[64,1024]{1,0:T(8,128)(2,1)S(1)} collective-permute-done((bf16[64,1024]{1,0:T(8,128)(2,1)S(1)}, bf16[64,1024]{1,0:T(8,128)(2,1)S(1)}, u32[]{:S(2)}, u32[]{:S(2)}) %collective-permute-start.20) | collective-permute-done | bytes 131104 | tf_op jit(solution)/shard_map/ppermute | solution.py:457
  141.0 0.1 fusion.31
  141.1 0.7 pad_maximum_fusion.4
  (61 shorter events, 0.4 us)
Async XLA Ops:
  0.0 116.0 %copy-start = (bf16[1024,1024]{1,0:T(8,128)(2,1)S(1)}, bf16[1024,1024]{1,0:T(8,128)(2,1)}, u32[]{:S(2)}) copy-start(bf16[1024,1024]{1,0:T(8,128)(2,1)} %param.22) | copy-start | bytes 6291460
  0.0 23.3 %collective-permute-start = (bf16[128,1024]{1,0:T(8,128)(2,1)}, bf16[128,1024]{1,0:T(8,128)(2,1)S(1)}, u32[]{:S(2)}, u32[]{:S(2)}) collective-permute-start(bf16[128,1024]{1,0:T(8,128)(2,1)} %rest_5_.1), channel_id=1, source_target_pairs={{0,1},{1,2},{2,3},{3,0},{4,5},{5,6},{6,7},{7,4},{8,9},{9,10},{10,1... | collective-permute-start | bytes 786440 | tf_op jit(solution)/shard_map/ppermute | solution.py:457
  3.0 20.3 %collective-permute-start.1 = (bf16[128,1024]{1,0:T(8,128)(2,1)}, bf16[128,1024]{1,0:T(8,128)(2,1)S(1)}, u32[]{:S(2)}, u32[]{:S(2)}) collective-permute-start(bf16[128,1024]{1,0:T(8,128)(2,1)} %rest_5_.1), channel_id=1, source_target_pairs={{0,2},{1,3},{2,0},{3,1},{4,6},{5,7},{6,4},{7,5},{8,10},{9,11},{10,... | collective-permute-start | bytes 786440 | tf_op jit(solution)/shard_map/ppermute | solution.py:457
  17.8 5.4 %copy-start.2 = (bf16[1152,256]{1,0:T(8,128)(2,1)}, bf16[1152,256]{1,0:T(8,128)(2,1)S(1)}, u32[]{:S(2)}) copy-start(bf16[1152,256]{1,0:T(8,128)(2,1)S(1)} %all-gather) | copy-start | bytes 1769476
  23.3 0.7 copy-start.7
  24.0 0.7 copy-start.8
  24.0 5.1 %copy-start.6 = (bf16[128,1024]{1,0:T(8,128)(2,1)S(1)}, bf16[128,1024]{1,0:T(8,128)(2,1)}, u32[]{:S(2)}) copy-start(bf16[128,1024]{1,0:T(8,128)(2,1)} %rest_5_.1) | copy-start | bytes 786436
  24.0 6.5 %copy-start.15 = (bf16[1024]{0:T(1024)(128)(2,1)S(1)}, bf16[1024]{0:T(1024)(128)(2,1)}, u32[]{:S(2)}) copy-start(bf16[1024]{0:T(1024)(128)(2,1)} %param.17) | copy-start | bytes 6148
  24.0 7.1 %copy-start.3 = (bf16[256,1024]{1,0:T(8,128)(2,1)S(1)}, bf16[256,1024]{1,0:T(8,128)(2,1)}, u32[]{:S(2)}) copy-start(bf16[256,1024]{1,0:T(8,128)(2,1)} %param.20) | copy-start | bytes 1572868
  24.7 31.0 %all-to-all-start = ((bf16[8,4,128,2,128]{4,3,2,1,0:T(2,128)(2,1)}), bf16[8,4,128,2,128]{4,3,2,1,0:T(2,128)(2,1)}, u32[]{:S(2)}, u32[]{:S(2)}) async-start(bf16[8,4,128,2,128]{4,3,2,1,0:T(2,128)(2,1)} %get-tuple-element.40), calls=%async_computation | async-start | bytes 4194304 | tf_op jit(solution)/shard_map/all_to_all | solution.py:528
  29.0 9.0 %copy-start.14 = (s32[1,4]{1,0:T(1,128)S(1)}, s32[1,4]{1,0:T(1,128)}, u32[]{:S(2)}) copy-start(s32[1,4]{1,0:T(1,128)} %lens_ref.5) | copy-start | bytes 52
  29.1 9.2 %copy-start.13 = (s32[1,4]{1,0:T(1,128)S(1)}, s32[1,4]{1,0:T(1,128)}, u32[]{:S(2)}) copy-start(s32[1,4]{1,0:T(1,128)} %counts_ref.3) | copy-start | bytes 52
  29.1 17.3 %collective-permute-start.2 = (bf16[128,1024]{1,0:T(8,128)(2,1)S(1)}, bf16[128,1024]{1,0:T(8,128)(2,1)}, u32[]{:S(2)}, u32[]{:S(2)}) collective-permute-start(bf16[128,1024]{1,0:T(8,128)(2,1)S(1)} %copy-done.6), channel_id=1, source_target_pairs={{0,3},{1,0},{2,1},{3,2},{4,7},{5,4},{6,5},{7,6},{8,11},{9,8},{10,9... | collective-permute-start | bytes 786440 | tf_op jit(solution)/shard_map/ppermute | solution.py:457
  34.1 7.1 %collective-permute-start.3 = (bf16[128,256]{1,0:T(8,128)(2,1)}, bf16[128,256]{1,0:T(8,128)(2,1)S(1)}, u32[]{:S(2)}, u32[]{:S(2)}) collective-permute-start(bf16[128,256]{1,0:T(8,128)(2,1)} %get-tuple-element.44.rest_9_), channel_id=1, source_target_pairs={{0,1},{1,2},{2,3},{3,0},{4,5},{5,6},{6,7},{7,4},{8,9},{9,10},{10,1... | collective-permute-start | bytes 196616 | tf_op jit(solution)/shard_map/ppermute | solution.py:457
  34.8 8.3 %collective-permute-start.4 = (bf16[128,256]{1,0:T(8,128)(2,1)}, bf16[128,256]{1,0:T(8,128)(2,1)S(1)}, u32[]{:S(2)}, u32[]{:S(2)}) collective-permute-start(bf16[128,256]{1,0:T(8,128)(2,1)} %get-tuple-element.44.rest_9_), channel_id=1, source_target_pairs={{0,2},{1,3},{2,0},{3,1},{4,6},{5,7},{6,4},{7,5},{8,10},{9,11},{10,... | collective-permute-start | bytes 196616 | tf_op jit(solution)/shard_map/ppermute | solution.py:457
  35.2 8.0 %collective-permute-start.5 = (bf16[128,256]{1,0:T(8,128)(2,1)}, bf16[128,256]{1,0:T(8,128)(2,1)S(1)}, u32[]{:S(2)}, u32[]{:S(2)}) collective-permute-start(bf16[128,256]{1,0:T(8,128)(2,1)} %get-tuple-element.44.rest_9_), channel_id=1, source_target_pairs={{0,3},{1,0},{2,1},{3,2},{4,7},{5,4},{6,5},{7,6},{8,11},{9,8},{10,9... | collective-permute-start | bytes 196616 | tf_op jit(solution)/shard_map/ppermute | solution.py:457
  41.2 5.2 %copy-start.10 = (bf16[128,256]{1,0:T(8,128)(2,1)}, bf16[128,256]{1,0:T(8,128)(2,1)S(1)}, u32[]{:S(2)}) copy-start(bf16[128,256]{1,0:T(8,128)(2,1)S(1)} %collective-permute-done.3.rest_10_) | copy-start | bytes 196612
  43.2 3.2 %copy-start.11 = (bf16[128,256]{1,0:T(8,128)(2,1)}, bf16[128,256]{1,0:T(8,128)(2,1)S(1)}, u32[]{:S(2)}) copy-start(bf16[128,256]{1,0:T(8,128)(2,1)S(1)} %collective-permute-done.4.rest_11_) | copy-start | bytes 196612
  43.2 3.2 %copy-start.12 = (bf16[128,256]{1,0:T(8,128)(2,1)}, bf16[128,256]{1,0:T(8,128)(2,1)S(1)}, u32[]{:S(2)}) copy-start(bf16[128,256]{1,0:T(8,128)(2,1)S(1)} %collective-permute-done.5.rest_12_) | copy-start | bytes 196612
  43.2 9.8 %collective-permute-start.6 = (bf16[128,1024]{1,0:T(8,128)(2,1)S(1)}, bf16[128,1024]{1,0:T(8,128)(2,1)S(1)}, u32[]{:S(2)}, u32[]{:S(2)}) collective-permute-start(bf16[128,1024]{1,0:T(8,128)(2,1)S(1)} %get-tuple-element.51), channel_id=1, source_target_pairs={{0,1},{1,2},{2,3},{3,0},{4,5},{5,6},{6,7},{7,4},{8,9},{9,10},{10,1... | collective-permute-start | bytes 786440 | tf_op jit(solution)/shard_map/ppermute | solution.py:457
  55.7 33.5 %all-to-all-start.1 = ((bf16[8,4,128,2,128]{4,3,2,1,0:T(2,128)(2,1)}), bf16[8,4,128,2,128]{4,3,2,1,0:T(2,128)(2,1)}, u32[]{:S(2)}, u32[]{:S(2)}) async-start(bf16[8,4,128,2,128]{4,3,2,1,0:T(2,128)(2,1)} %get-tuple-element.58), calls=%async_computation.1 | async-start | bytes 4194304 | tf_op jit(solution)/shard_map/all_to_all | solution.py:548
  60.0 14.8 %collective-permute-start.7 = (bf16[128,1024]{1,0:T(8,128)(2,1)S(1)}, bf16[128,1024]{1,0:T(8,128)(2,1)S(1)}, u32[]{:S(2)}, u32[]{:S(2)}) collective-permute-start(bf16[128,1024]{1,0:T(8,128)(2,1)S(1)} %get-tuple-element.51), channel_id=1, source_target_pairs={{0,2},{1,3},{2,0},{3,1},{4,6},{5,7},{6,4},{7,5},{8,10},{9,11},{10,... | collective-permute-start | bytes 786440 | tf_op jit(solution)/shard_map/ppermute | solution.py:457
  60.4 14.4 %collective-permute-start.8 = (bf16[128,1024]{1,0:T(8,128)(2,1)S(1)}, bf16[128,1024]{1,0:T(8,128)(2,1)S(1)}, u32[]{:S(2)}, u32[]{:S(2)}) collective-permute-start(bf16[128,1024]{1,0:T(8,128)(2,1)S(1)} %get-tuple-element.51), channel_id=1, source_target_pairs={{0,3},{1,0},{2,1},{3,2},{4,7},{5,4},{6,5},{7,6},{8,11},{9,8},{10,9... | collective-permute-start | bytes 786440 | tf_op jit(solution)/shard_map/ppermute | solution.py:457
  62.7 13.2 %copy-start.16 = (bf16[1024]{0:T(1024)(128)(2,1)S(1)}, bf16[1024]{0:T(1024)(128)(2,1)}, u32[]{:S(2)}) copy-start(bf16[1024]{0:T(1024)(128)(2,1)} %param.18) | copy-start | bytes 6148
  72.0 6.2 %copy-start.9 = (bf16[512,128]{1,0:T(8,128)(2,1)S(1)}, bf16[512,128]{1,0:T(8,128)(2,1)}, u32[]{:S(2)}) copy-start(bf16[512,128]{1,0:T(8,128)(2,1)} %attend.2) | copy-start | bytes 393220
  75.8 11.0 %collective-permute-start.12 = (bf16[3,128,1024]{2,1,0:T(8,128)(2,1)}, bf16[3,128,1024]{2,1,0:T(8,128)(2,1)}, u32[]{:S(2)}, u32[]{:S(2)}) collective-permute-start(bf16[3,128,1024]{2,1,0:T(8,128)(2,1)} %pad_maximum_fusion.3), channel_id=1, source_target_pairs={{0,4},{4,0},{8,12},{12,8},{16,20},{20,16},{24,28},{28,24},{1,5},{5... | collective-permute-start | bytes 2359304 | tf_op jit(solution)/shard_map/ppermute | solution.py:461
  78.2 9.8 %copy-start.4 = (bf16[128,1024]{1,0:T(8,128)(2,1)S(1)}, bf16[128,1024]{1,0:T(8,128)(2,1)}, u32[]{:S(2)}) copy-start(bf16[128,1024]{1,0:T(8,128)(2,1)} %get-tuple-element.98) | copy-start | bytes 786436
  78.2 20.3 %collective-permute-start.10 = (bf16[512,128]{1,0:T(8,128)(2,1)S(1)}, bf16[512,128]{1,0:T(8,128)(2,1)}, u32[]{:S(2)}, u32[]{:S(2)}) collective-permute-start(bf16[512,128]{1,0:T(8,128)(2,1)S(1)} %copy-done.9), channel_id=1, source_target_pairs={{0,2},{1,3},{2,0},{3,1},{4,6},{5,7},{6,4},{7,5},{8,10},{9,11},{10,... | collective-permute-start | bytes 393224 | tf_op jit(solution)/shard_map/ppermute | solution.py:457
  83.3 15.2 %collective-permute-start.11 = (bf16[512,128]{1,0:T(8,128)(2,1)S(1)}, bf16[512,128]{1,0:T(8,128)(2,1)}, u32[]{:S(2)}, u32[]{:S(2)}) collective-permute-start(bf16[512,128]{1,0:T(8,128)(2,1)S(1)} %copy-done.9), channel_id=1, source_target_pairs={{0,3},{1,0},{2,1},{3,2},{4,7},{5,4},{6,5},{7,6},{8,11},{9,8},{10,9... | collective-permute-start | bytes 393224 | tf_op jit(solution)/shard_map/ppermute | solution.py:457
  86.8 11.7 %collective-permute-start.9 = (bf16[512,128]{1,0:T(8,128)(2,1)S(1)}, bf16[512,128]{1,0:T(8,128)(2,1)}, u32[]{:S(2)}, u32[]{:S(2)}) collective-permute-start(bf16[512,128]{1,0:T(8,128)(2,1)S(1)} %copy-done.9), channel_id=1, source_target_pairs={{0,1},{1,2},{2,3},{3,0},{4,5},{5,6},{6,7},{7,4},{8,9},{9,10},{10,1... | collective-permute-start | bytes 393224 | tf_op jit(solution)/shard_map/ppermute | solution.py:457
  98.5 8.6 %collective-permute-start.13 = (bf16[512,128]{1,0:T(8,128)(2,1)}, bf16[512,128]{1,0:T(8,128)(2,1)S(1)}, u32[]{:S(2)}, u32[]{:S(2)}) collective-permute-start(bf16[512,128]{1,0:T(8,128)(2,1)} %attend.3), channel_id=1, source_target_pairs={{0,1},{1,2},{2,3},{3,0},{4,5},{5,6},{6,7},{7,4},{8,9},{9,10},{10,1... | collective-permute-start | bytes 393224 | tf_op jit(solution)/shard_map/ppermute | solution.py:457
  99.8 11.7 %collective-permute-start.14 = (bf16[512,128]{1,0:T(8,128)(2,1)}, bf16[512,128]{1,0:T(8,128)(2,1)S(1)}, u32[]{:S(2)}, u32[]{:S(2)}) collective-permute-start(bf16[512,128]{1,0:T(8,128)(2,1)} %attend.3), channel_id=1, source_target_pairs={{0,2},{1,3},{2,0},{3,1},{4,6},{5,7},{6,4},{7,5},{8,10},{9,11},{10,... | collective-permute-start | bytes 393224 | tf_op jit(solution)/shard_map/ppermute | solution.py:457
  102.9 8.5 %collective-permute-start.15 = (bf16[512,128]{1,0:T(8,128)(2,1)}, bf16[512,128]{1,0:T(8,128)(2,1)S(1)}, u32[]{:S(2)}, u32[]{:S(2)}) collective-permute-start(bf16[512,128]{1,0:T(8,128)(2,1)} %attend.3), channel_id=1, source_target_pairs={{0,3},{1,0},{2,1},{3,2},{4,7},{5,4},{6,5},{7,6},{8,11},{9,8},{10,9... | collective-permute-start | bytes 393224 | tf_op jit(solution)/shard_map/ppermute | solution.py:457
  102.9 8.5 %copy-start.5 = (bf16[512,128]{1,0:T(8,128)(2,1)S(1)}, bf16[512,128]{1,0:T(8,128)(2,1)}, u32[]{:S(2)}) copy-start(bf16[512,128]{1,0:T(8,128)(2,1)} %attend.3) | copy-start | bytes 393220
  112.2 2.2 %copy-start.1 = (bf16[2,1024,1024]{2,1,0:T(8,128)(2,1)S(1)}, bf16[2,1024,1024]{2,1,0:T(8,128)(2,1)}, u32[]{:S(2)}) copy-start(bf16[2,1024,1024]{2,1,0:T(8,128)(2,1)} %param.21) | copy-start | bytes 12582916
  116.9 11.0 %collective-permute-start.16 = (bf16[64,1024]{1,0:T(8,128)(2,1)S(1)}, bf16[64,1024]{1,0:T(8,128)(2,1)S(1)}, u32[]{:S(2)}, u32[]{:S(2)}) collective-permute-start(bf16[64,1024]{1,0:T(8,128)(2,1)S(1)} %get-tuple-element.97), channel_id=1, source_target_pairs={{0,1},{1,2},{2,3},{3,0},{4,5},{5,6},{6,7},{7,4},{8,9},{9,10},{10,1... | collective-permute-start | bytes 393224 | tf_op jit(solution)/shard_map/ppermute | solution.py:457
  120.2 10.0 %collective-permute-start.17 = (bf16[64,1024]{1,0:T(8,128)(2,1)S(1)}, bf16[64,1024]{1,0:T(8,128)(2,1)S(1)}, u32[]{:S(2)}, u32[]{:S(2)}) collective-permute-start(bf16[64,1024]{1,0:T(8,128)(2,1)S(1)} %get-tuple-element.96), channel_id=1, source_target_pairs={{0,2},{1,3},{2,0},{3,1},{4,6},{5,7},{6,4},{7,5},{8,10},{9,11},{10,... | collective-permute-start | bytes 393224 | tf_op jit(solution)/shard_map/ppermute | solution.py:457
  120.2 10.0 %collective-permute-start.18 = (bf16[64,1024]{1,0:T(8,128)(2,1)S(1)}, bf16[64,1024]{1,0:T(8,128)(2,1)S(1)}, u32[]{:S(2)}, u32[]{:S(2)}) collective-permute-start(bf16[64,1024]{1,0:T(8,128)(2,1)S(1)} %get-tuple-element.95), channel_id=1, source_target_pairs={{0,3},{1,0},{2,1},{3,2},{4,7},{5,4},{6,5},{7,6},{8,11},{9,8},{10,9... | collective-permute-start | bytes 393224 | tf_op jit(solution)/shard_map/ppermute | solution.py:457
  125.3 8.4 %collective-permute-start.19 = (bf16[64,1024]{1,0:T(8,128)(2,1)S(1)}, bf16[64,1024]{1,0:T(8,128)(2,1)S(1)}, u32[]{:S(2)}, u32[]{:S(2)}) collective-permute-start(bf16[64,1024]{1,0:T(8,128)(2,1)S(1)} %get-tuple-element.92), channel_id=1, source_target_pairs={{0,1},{1,2},{2,3},{3,0},{4,5},{5,6},{6,7},{7,4},{8,9},{9,10},{10,1... | collective-permute-start | bytes 393224 | tf_op jit(solution)/shard_map/ppermute | solution.py:457
  125.3 15.7 %collective-permute-start.20 = (bf16[64,1024]{1,0:T(8,128)(2,1)S(1)}, bf16[64,1024]{1,0:T(8,128)(2,1)S(1)}, u32[]{:S(2)}, u32[]{:S(2)}) collective-permute-start(bf16[64,1024]{1,0:T(8,128)(2,1)S(1)} %get-tuple-element.94), channel_id=1, source_target_pairs={{0,2},{1,3},{2,0},{3,1},{4,6},{5,7},{6,4},{7,5},{8,10},{9,11},{10,... | collective-permute-start | bytes 393224 | tf_op jit(solution)/shard_map/ppermute | solution.py:457
  127.8 13.2 %collective-permute-start.21 = (bf16[64,1024]{1,0:T(8,128)(2,1)S(1)}, bf16[64,1024]{1,0:T(8,128)(2,1)S(1)}, u32[]{:S(2)}, u32[]{:S(2)}) collective-permute-start(bf16[64,1024]{1,0:T(8,128)(2,1)S(1)} %get-tuple-element.93), channel_id=1, source_target_pairs={{0,3},{1,0},{2,1},{3,2},{4,7},{5,4},{6,5},{7,6},{8,11},{9,8},{10,9... | collective-permute-start | bytes 393224 | tf_op jit(solution)/shard_map/ppermute | solution.py:457

commit v9 on v7

--- a/solution.py
+++ b/solution.py
@@ -449,6 +449,33 @@
     )(lens, counts, pos, bias, q, kn, vn, raw)
 
 
+def partial_kernel(n_chunk, n_block, *refs):
+    toks, refs = refs[:n_chunk], refs[n_chunk:]
+    blocks, refs = refs[:n_block], refs[n_block:]
+    w_ref, outs = refs[0], refs[1:]
+    rows = outs[0].shape[0]
+    for c in range(n_chunk):
+        part = jnp.concatenate([b[c * rows : (c + 1) * rows, :] for b in blocks], axis=1)
+        outs[c][...] = toks[c][...].astype(F32) + jnp.dot(
+            part, w_ref[...], preferred_element_type=F32
+        )
+
+
+def partial(toks, blocks, weight):
+    n_chunk = len(toks)
+    vmem = pl.BlockSpec(memory_space=pltpu.VMEM)
+    out = jax.ShapeDtypeStruct(toks[0].shape, F32)
+    return pl.pallas_call(
+        functools.partial(partial_kernel, n_chunk, len(blocks)),
+        out_shape=[out] * n_chunk,
+        in_specs=[vmem] * (n_chunk + len(blocks) + 1),
+        out_specs=[vmem] * n_chunk,
+        compiler_params=pltpu.CompilerParams(vmem_limit_bytes=24 << 20),
+        cost_estimate=LIGHT,
+        name="partial",
+    )(*toks, *blocks, weight)
+
+
 def shift(value, axis, n, k):
     return lax.ppermute(value, axis, [(i, (i + k) % n) for i in range(n)])
 
@@ -570,25 +597,22 @@
         w_whole = whole_weight(w_out, halves, dp, n_dp, n_group)
     last = attended(n_group - 1, query, True)
     early, last, w_whole = lax.optimization_barrier((early, last, w_whole))
-    early = [[jnp.split(block, n_chunk) for block in blocks] for blocks in early]
+    bases = [tok.reshape(n_tp * sub, d_model) for tok in all_tokens]
+    for a in range(n_group - 1):
+        bases = partial(bases, early[a], w_whole[a])
     outs = []
     pieces = None
-    bases = []
     late = []
     for c in range(n_chunk):
         own = last[c]
-        if bases:
-            own = lax.optimization_barrier((own, bases[-1]))[0]
+        if late:
+            own = lax.optimization_barrier((own, bases))[0]
         late.append([own] + [shift(own, "tensor", n_tp, k) for k in far_first])
-        base = all_tokens[c].reshape(n_tp * sub, d_model).astype(F32)
-        for a in range(n_group - 1):
-            base = base + mixed([block[c] for block in early[a]], a)
-        bases.append(base)
     for c in range(n_chunk):
         blocks = late[c]
         if pieces is not None:
             blocks = lax.optimization_barrier((blocks, pieces))[0]
-        residual = bases[c] + mixed(blocks, n_group - 1)
+        residual = bases[c].astype(F32) + mixed(blocks, n_group - 1)
         ffn_in = normalize(residual, ffn_gain).astype(BF)
         gate_up = jnp.einsum("td,kdf->ktf", ffn_in, w_gateup, preferred_element_type=F32)
         hidden = (jax.nn.silu(gate_up[0]) * gate_up[1]).astype(BF)

time: 140 us -> 138 us (0.986)
  waiting for transfers between devices: 19.3 us -> 20.9 us
    split x4 -> x0, local copies, waits for them, and re-layouts: 2.66 us -> none  [per_device(): jnp.split(block, n_chunk)]
    ppermute x24, waiting for transfers between devices: 16.6 us -> 19 us  [shift(): return lax.ppermute(value, axis, [(i, (i + k) % n) for i in range(n)])]
    pallas_call x2, Pallas kernels: 21.6 us -> 19.4 us  [attend(): pl.pallas_call(functools.partial(attend_kernel, group, per, n_chunk), gri...]
    unnamed x40 -> x42, local copies, waits for them, and re-layouts: 1.51 us -> 3.56 us
    pallas_call x0 -> x1, Pallas kernels: none -> 1.76 us  [partial(): pl.pallas_call(functools.partial(partial_kernel, n_chunk, len(blocks)), o...]
    dot_general x4 -> x2, matrix products: 3.24 us -> 2.43 us  [mixed(): jnp.dot(jnp.concatenate(blocks, axis=1), w_whole[a], preferred_element_ty...]
  transfers between devices with their start and end apart: 27 -> 27, of which waited for: 8 -> 7; matrix products, arithmetic and copies ran while one was open for 16% -> 13% of each run, Pallas kernels for 25% -> 25%
where the time goes in v9:
time: 138 us
  starting transfers between devices  50.2 us (36%)
  Pallas kernels  34.5 us (25%)
  waiting for transfers between devices  20.9 us (15%)
  blocking collectives  9.99 us (7%)
  other arithmetic  8.55 us (6%)
  matrix products  6.72 us (5%)
  local copies, waits for them, and re-layouts  6.36 us (5%)
    ppermute x24, starting transfers between devices, shift(): return lax.ppermute(value, axis, [(i, (i + k) % n) for i in range(n)])  41.4 us
    pallas_call x2, Pallas kernels, attend(): pl.pallas_call(functools.partial(attend_kernel, group, per, n_chunk), gri...  19.4 us
    ppermute x24, waiting for transfers between devices, shift(): return lax.ppermute(value, axis, [(i, (i + k) % n) for i in range(n)])  19 us
    all_gather x1, blocking collectives, per_device(): gathered = lax.all_gather(payload, 'dp', axis=0)  9.99 us
    all_to_all x2, starting transfers between devices, per_device(): lax.all_to_all(send, 'dp', split_axis=0, concat_axis=0, tiled=True)  8.86 us
    pallas_call x1, Pallas kernels, project(): pl.pallas_call(functools.partial(project_kernel, n_tp, cap, pool_dev, n_c...  6.55 us
    pallas_call x1, Pallas kernels, pick(): pl.pallas_call(functools.partial(pick_kernel, n_dp, cap), out_shape=[jax....  4.53 us
    unnamed x42, local copies, waits for them, and re-layouts  3.56 us
  transfers between devices with their start and end apart: 27, of which 7 were waited for; matrix products, arithmetic and copies ran while one was open for 13% of the time, Pallas kernels for 25%

profile of v9, /device:TPU:0, one launch (start us, length us, event | category | flops | bytes accessed | tf_op | source)
XLA Modules:
  0.0 137.6 jit_solution(857497315015134765)
XLA Ops:
  0.0 3.0 %collective-permute-start = (bf16[128,1024]{1,0:T(8,128)(2,1)}, bf16[128,1024]{1,0:T(8,128)(2,1)S(1)}, u32[]{:S(2)}, u32[]{:S(2)}) collective-permute-start(bf16[128,1024]{1,0:T(8,128)(2,1)} %rest_5_.1), channel_id=1, source_target_pairs={{0,1},{1,2},{2,3},{3,0},{4,5},{5,6},{6,7},{7,4},{8,9},{9,10},{10,1... | collective-permute-start | bytes 786440 | tf_op jit(solution)/shard_map/ppermute | solution.py:480
  3.0 2.6 %collective-permute-start.1 = (bf16[128,1024]{1,0:T(8,128)(2,1)}, bf16[128,1024]{1,0:T(8,128)(2,1)S(1)}, u32[]{:S(2)}, u32[]{:S(2)}) collective-permute-start(bf16[128,1024]{1,0:T(8,128)(2,1)} %rest_5_.1), channel_id=1, source_target_pairs={{0,2},{1,3},{2,0},{3,1},{4,6},{5,7},{6,4},{7,5},{8,10},{9,11},{10,... | collective-permute-start | bytes 786440 | tf_op jit(solution)/shard_map/ppermute | solution.py:480
  5.6 0.7 fusion.47
  6.3 0.8 constant_dynamic-slice_fusion.1
  7.1 0.8 pad_maximum_fusion.4
  7.8 10.0 %all-gather = bf16[1152,256]{1,0:T(8,128)(2,1)S(1)} all-gather(bf16[144,256]{1,0:T(8,128)(2,1)S(1)} %pad_maximum_fusion.4), channel_id=2, replica_groups=mesh['dp'=8,'tensor'=4] {'dp'}, dimensions={0}, use_global_device_ids=true | all-gather | bytes 663552 | tf_op jit(solution)/shard_map/all_gather | solution.py:547
  17.8 0.6 slice_convert_fusion.asked_ref
  18.5 4.5 %pick_pages.1 = (bf16[8,4,128,2,128]{4,3,2,1,0:T(2,128)(2,1)}, bf16[8,4,128,2,128]{4,3,2,1,0:T(2,128)(2,1)}) custom-call(s32[1]{0:T(128)} %bitcast.4.me_ref, s32[8,2,32]{2,1,0:T(2,128)} %slice_convert_fusion.asked_ref, bf16[32,128,2,256]{3,2,1,0:T(2,128)(2,1)} %pool_ref.1), custom_call_target="tpu_custom_call" | custom-call | flops 1000 | bytes 1000 | tf_op jit(solution)/shard_map/pick_pages/pallas_call | solution.py:82
  23.0 0.7 copy-done.11
  23.8 4.5 %all-to-all-start = ((bf16[8,4,128,2,128]{4,3,2,1,0:T(2,128)(2,1)}), bf16[8,4,128,2,128]{4,3,2,1,0:T(2,128)(2,1)}, u32[]{:S(2)}, u32[]{:S(2)}) async-start(bf16[8,4,128,2,128]{4,3,2,1,0:T(2,128)(2,1)} %get-tuple-element.45), calls=%async_computation | async-start | bytes 4194304 | tf_op jit(solution)/shard_map/all_to_all | solution.py:551
  28.3 1.4 %collective-permute-start.2 = (bf16[128,1024]{1,0:T(8,128)(2,1)S(1)}, bf16[128,1024]{1,0:T(8,128)(2,1)S(1)}, u32[]{:S(2)}, u32[]{:S(2)}) collective-permute-start(bf16[128,1024]{1,0:T(8,128)(2,1)S(1)} %copy-done.9), channel_id=1, source_target_pairs={{0,3},{1,0},{2,1},{3,2},{4,7},{5,4},{6,5},{7,6},{8,11},{9,8},{10,9... | collective-permute-start | bytes 786440 | tf_op jit(solution)/shard_map/ppermute | solution.py:480
  29.8 0.6 reshape.112.rest_0_
  30.4 0.9 fusion.54
  31.3 2.2 %named_adapters.1 = (bf16[128,256]{1,0:T(8,128)(2,1)}, bf16[128,256]{1,0:T(8,128)(2,1)}) custom-call(s32[16]{0:T(128)} %table_ref.2, s32[1,4]{1,0:T(1,128)} %ids_ref.1, bf16[8,144,256]{2,1,0:T(8,128)(2,1)} %bitcast.101), custom_call_target="tpu_custom_call" | custom-call | flops 1000 | bytes 1000 | tf_op jit(solution)/shard_map/named_adapters/pallas_call | solution.py:126
  33.5 0.7 collective-permute-start.3
  34.2 0.3 collective-permute-start.4
  34.5 2.8 %collective-permute-start.5 = (bf16[128,256]{1,0:T(8,128)(2,1)}, bf16[128,256]{1,0:T(8,128)(2,1)S(1)}, u32[]{:S(2)}, u32[]{:S(2)}) collective-permute-start(bf16[128,256]{1,0:T(8,128)(2,1)} %get-tuple-element.49.rest_9_), channel_id=1, source_target_pairs={{0,3},{1,0},{2,1},{3,2},{4,7},{5,4},{6,5},{7,6},{8,11},{9,8},{10,9... | collective-permute-start | bytes 196616 | tf_op jit(solution)/shard_map/ppermute | solution.py:480
  37.4 0.2 reduce-window.4
  37.6 0.1 convert_reduce_fusion
  37.7 0.1 select_reduce_fusion.1
  37.8 2.8 %collective-permute-done.3.rest_10_ = bf16[128,256]{1,0:T(8,128)(2,1)S(1)} collective-permute-done((bf16[128,256]{1,0:T(8,128)(2,1)}, bf16[128,256]{1,0:T(8,128)(2,1)S(1)}, u32[]{:S(2)}, u32[]{:S(2)}) %collective-permute-start.3) | collective-permute-done | bytes 65568 | tf_op jit(solution)/shard_map/ppermute | solution.py:480
  40.6 2.1 %collective-permute-done.4.rest_11_ = bf16[128,256]{1,0:T(8,128)(2,1)S(1)} collective-permute-done((bf16[128,256]{1,0:T(8,128)(2,1)}, bf16[128,256]{1,0:T(8,128)(2,1)S(1)}, u32[]{:S(2)}, u32[]{:S(2)}) %collective-permute-start.4) | collective-permute-done | bytes 65568 | tf_op jit(solution)/shard_map/ppermute | solution.py:480
  42.6 1.3 collective-permute-start.6
  44.0 1.8 %fusion.14 = (f32[512,128]{1,0:T(8,128)}, f32[512,128]{1,0:T(8,128)}) fusion(f32[128]{0:T(128)S(1)} %get-tuple-element.120, f32[128]{0:T(128)S(1)} %get-tuple-element.121, f32[512]{0:T(512)S(1)} %fusion.41), kind=kLoop, calls=%fused_computation.27 | loop fusion | flops 131072 | bytes 527360 | tf_op jit(solution)/shard_map/mul | solution.py:565
  45.8 0.7 copy-done.12
  46.5 6.6 %project.1 = (bf16[512,256]{1,0:T(8,128)(2,1)}, bf16[512,256]{1,0:T(8,128)(2,1)}, bf16[512,256]{1,0:T(8,128)(2,1)}, s32[32]{0:T(128)}, bf16[4,64,1024]{2,1,0:T(8,128)(2,1)}, /*index=5*/bf16[4,64,1024]{2,1,0:T(8,128)(2,1)}) custom-call(s32[1]{0:T(128)} %bitcast.tp_ref, s32[1,4]{1,0:T(1,128)} %lens_ref.5, s32[1,32]{1,0:T(1,128)} %table_ref.3, ...), custom_call_target="tpu_custom_call" | custom-call | flops 1000 | bytes 1000 | tf_op jit(solution)/shard_map/project/pallas_call | solution.py:250
  53.1 1.9 %all-to-all-done = bf16[8,4,128,2,128]{4,3,2,1,0:T(2,128)(2,1)} async-done(((bf16[8,4,128,2,128]{4,3,2,1,0:T(2,128)(2,1)}), bf16[8,4,128,2,128]{4,3,2,1,0:T(2,128)(2,1)}, u32[]{:S(2)}, u32[]{:S(2)}) %all-to-all-start) | async-done | bytes 2097184 | tf_op jit(solution)/shard_map/all_to_all | solution.py:551
  54.9 4.4 %all-to-all-start.1 = ((bf16[8,4,128,2,128]{4,3,2,1,0:T(2,128)(2,1)}), bf16[8,4,128,2,128]{4,3,2,1,0:T(2,128)(2,1)}, u32[]{:S(2)}, u32[]{:S(2)}) async-start(bf16[8,4,128,2,128]{4,3,2,1,0:T(2,128)(2,1)} %get-tuple-element.63), calls=%async_computation.1 | async-start | bytes 4194304 | tf_op jit(solution)/shard_map/all_to_all | solution.py:571
  59.3 0.7 collective-permute-start.7
  60.0 1.9 %collective-permute-start.8 = (bf16[128,1024]{1,0:T(8,128)(2,1)}, bf16[128,1024]{1,0:T(8,128)(2,1)S(1)}, u32[]{:S(2)}, u32[]{:S(2)}) collective-permute-start(bf16[128,1024]{1,0:T(8,128)(2,1)} %get-tuple-element.56), channel_id=1, source_target_pairs={{0,3},{1,0},{2,1},{3,2},{4,7},{5,4},{6,5},{7,6},{8,11},{9,8},{10,9... | collective-permute-start | bytes 786440 | tf_op jit(solution)/shard_map/ppermute | solution.py:480
  62.0 9.7 %attend.2.refs_2_ = bf16[512,128]{1,0:T(8,128)(2,1)} custom-call(s32[1,4]{1,0:T(1,128)} %lens_ref.5, s32[1,4]{1,0:T(1,128)} %counts_ref.3, s32[32]{0:T(128)} %get-tuple-element.52.pos_ref, f32[2,4]{1,0:T(2,128)} %bias_ref.3, bf16[512,256]{1,0:T(8,128)(2,1)} %get-tuple-element.61.q_ref, bf16[512,256]{1,0:T(8,128)(2,1)} %get-tuple-element.54.kn_ref, ...), custom_call_target="tpu_custom_call" | custom-call | flops 1000 | bytes 1000 | tf_op jit(solution)/shard_map/attend/pallas_call | solution.py:427
  71.7 2.7 %collective-permute-done.7 = bf16[128,1024]{1,0:T(8,128)(2,1)S(1)} collective-permute-done((bf16[128,1024]{1,0:T(8,128)(2,1)}, bf16[128,1024]{1,0:T(8,128)(2,1)S(1)}, u32[]{:S(2)}, u32[]{:S(2)}) %collective-permute-start.7) | collective-permute-done | bytes 262176 | tf_op jit(solution)/shard_map/ppermute | solution.py:480
  74.4 1.0 pad_maximum_fusion.2
  75.4 5.3 %collective-permute-start.10 = (bf16[512,128]{1,0:T(8,128)(2,1)}, bf16[512,128]{1,0:T(8,128)(2,1)S(1)}, u32[]{:S(2)}, u32[]{:S(2)}) collective-permute-start(bf16[512,128]{1,0:T(8,128)(2,1)} %attend.2.refs_2_), channel_id=1, source_target_pairs={{0,2},{1,3},{2,0},{3,1},{4,6},{5,7},{6,4},{7,5},{8,10},{9,11},{10,... | collective-permute-start | bytes 393224 | tf_op jit(solution)/shard_map/ppermute | solution.py:480
  80.6 3.4 %collective-permute-start.11 = (bf16[512,128]{1,0:T(8,128)(2,1)}, bf16[512,128]{1,0:T(8,128)(2,1)S(1)}, u32[]{:S(2)}, u32[]{:S(2)}) collective-permute-start(bf16[512,128]{1,0:T(8,128)(2,1)} %attend.2.refs_2_), channel_id=1, source_target_pairs={{0,3},{1,0},{2,1},{3,2},{4,7},{5,4},{6,5},{7,6},{8,11},{9,8},{10,9... | collective-permute-start | bytes 393224 | tf_op jit(solution)/shard_map/ppermute | solution.py:480
  84.0 1.2 broadcast_select_fusion.2
  85.2 1.1 pad_maximum_fusion.1
  86.4 9.7 %attend.3 = (bf16[256,128]{1,0:T(8,128)(2,1)}, bf16[256,128]{1,0:T(8,128)(2,1)}) custom-call(s32[1,4]{1,0:T(1,128)} %lens_ref.5, s32[1,4]{1,0:T(1,128)} %counts_ref.3, s32[32]{0:T(128)} %get-tuple-element.52.pos_ref, f32[2,4]{1,0:T(2,128)} %bias_ref.3, bf16[512,256]{1,0:T(8,128)(2,1)} %get-tuple-element.61.q_ref, bf16[512,256]{1,0:T(8,128)(2,1)} %get-tuple-element.54.kn_ref, ...), custom_call_target="tpu_custom_call" | custom-call | flops 1000 | bytes 1000 | tf_op jit(solution)/shard_map/attend/pallas_call | solution.py:427
  96.1 1.3 collective-permute-start.13
  97.4 3.2 %collective-permute-start.14 = (bf16[256,128]{1,0:T(8,128)(2,1)}, bf16[256,128]{1,0:T(8,128)(2,1)}, u32[]{:S(2)}, u32[]{:S(2)}) collective-permute-start(bf16[256,128]{1,0:T(8,128)(2,1)} %get-tuple-element.74), channel_id=1, source_target_pairs={{0,2},{1,3},{2,0},{3,1},{4,6},{5,7},{6,4},{7,5},{8,10},{9,11},{10,... | collective-permute-start | bytes 196616 | tf_op jit(solution)/shard_map/ppermute | solution.py:480
  100.6 1.0 copy-done.1
  101.6 1.0 copy-done.2
  102.7 1.8 %partial.1 = (f32[256,1024]{1,0:T(8,128)S(1)}, f32[256,1024]{1,0:T(8,128)S(1)}) custom-call(bf16[256,1024]{1,0:T(8,128)(2,1)S(1)} %bitcast.96, bf16[256,1024]{1,0:T(8,128)(2,1)S(1)} %bitcast.97, bf16[512,128]{1,0:T(8,128)(2,1)S(1)} %copy-done.3, bf16[512,128]{1,0:T(8,128)(2,1)} %collective-permute-done.9.refs_3_, ...), custom_call_target="tpu_custom_call" | custom-call | flops 1000 | bytes 1000 | tf_op jit(solution)/shard_map/partial/pallas_call | solution.py:468
  104.5 2.0 %collective-permute-start.19 = (bf16[256,128]{1,0:T(8,128)(2,1)}, bf16[256,128]{1,0:T(8,128)(2,1)S(1)}, u32[]{:S(2)}, u32[]{:S(2)}) collective-permute-start(bf16[256,128]{1,0:T(8,128)(2,1)} %get-tuple-element.79), channel_id=1, source_target_pairs={{0,1},{1,2},{2,3},{3,0},{4,5},{5,6},{6,7},{7,4},{8,9},{9,10},{10,1... | collective-permute-start | bytes 196616 | tf_op jit(solution)/shard_map/ppermute | solution.py:480
  106.5 2.4 %collective-permute-start.21 = (bf16[256,128]{1,0:T(8,128)(2,1)}, bf16[256,128]{1,0:T(8,128)(2,1)S(1)}, u32[]{:S(2)}, u32[]{:S(2)}) collective-permute-start(bf16[256,128]{1,0:T(8,128)(2,1)} %get-tuple-element.79), channel_id=1, source_target_pairs={{0,3},{1,0},{2,1},{3,2},{4,7},{5,4},{6,5},{7,6},{8,11},{9,8},{10,9... | collective-permute-start | bytes 196616 | tf_op jit(solution)/shard_map/ppermute | solution.py:480
  109.0 1.9 %multiply_reduce_fusion.1 = (f32[256]{0:T(256)S(1)}, f32[256,1024]{1,0:T(8,128)S(1)}) fusion(f32[256,1024]{1,0:T(8,128)S(1)} %get-tuple-element.73, bf16[512,1024]{1,0:T(8,128)(2,1)} %pad_maximum_fusion.1, bf16[256,128]{1,0:T(8,128)(2,1)} %collective-permute-done.15, bf16[256,128]{1,0:T(8,128)(2,1)} %collective-permute-done.14, ...), kind=kOutput, calls=%fused_computation.15 | convolution fusion | flops 270270208 | bytes 3408896 | tf_op jit(solution)/shard_map/dot_general | solution.py:576
  110.9 1.3 convolution_bitcast_fusion.1
  112.2 0.2 fusion.53
  112.5 0.8 fusion.55
  113.4 2.5 %collective-permute-start.17 = (bf16[64,1024]{1,0:T(8,128)(2,1)S(1)}, bf16[64,1024]{1,0:T(8,128)(2,1)S(1)}, u32[]{:S(2)}, u32[]{:S(2)}) collective-permute-start(bf16[64,1024]{1,0:T(8,128)(2,1)S(1)} %get-tuple-element.103), channel_id=1, source_target_pairs={{0,2},{1,3},{2,0},{3,1},{4,6},{5,7},{6,4},{7,5},{8,10},{9,11},{10,... | collective-permute-start | bytes 393224 | tf_op jit(solution)/shard_map/ppermute | solution.py:480
  115.9 1.8 %collective-permute-start.18 = (bf16[64,1024]{1,0:T(8,128)(2,1)S(1)}, bf16[64,1024]{1,0:T(8,128)(2,1)S(1)}, u32[]{:S(2)}, u32[]{:S(2)}) collective-permute-start(bf16[64,1024]{1,0:T(8,128)(2,1)S(1)} %get-tuple-element.102), channel_id=1, source_target_pairs={{0,3},{1,0},{2,1},{3,2},{4,7},{5,4},{6,5},{7,6},{8,11},{9,8},{10,9... | collective-permute-start | bytes 393224 | tf_op jit(solution)/shard_map/ppermute | solution.py:480
  117.8 0.5 multiply_reduce_fusion
  118.3 1.3 convolution_bitcast_fusion
  119.6 0.2 fusion.52
  119.9 0.8 fusion.56
  120.8 0.3 collective-permute-start.22
  121.0 1.4 %collective-permute-start.23 = (bf16[64,1024]{1,0:T(8,128)(2,1)S(1)}, bf16[64,1024]{1,0:T(8,128)(2,1)S(1)}, u32[]{:S(2)}, u32[]{:S(2)}) collective-permute-start(bf16[64,1024]{1,0:T(8,128)(2,1)S(1)} %get-tuple-element.101), channel_id=1, source_target_pairs={{0,2},{1,3},{2,0},{3,1},{4,6},{5,7},{6,4},{7,5},{8,10},{9,11},{10,... | collective-permute-start | bytes 393224 | tf_op jit(solution)/shard_map/ppermute | solution.py:480
  122.4 2.8 %collective-permute-start.24 = (bf16[64,1024]{1,0:T(8,128)(2,1)S(1)}, bf16[64,1024]{1,0:T(8,128)(2,1)S(1)}, u32[]{:S(2)}, u32[]{:S(2)}) collective-permute-start(bf16[64,1024]{1,0:T(8,128)(2,1)S(1)} %get-tuple-element.100), channel_id=1, source_target_pairs={{0,3},{1,0},{2,1},{3,2},{4,7},{5,4},{6,5},{7,6},{8,11},{9,8},{10,9... | collective-permute-start | bytes 393224 | tf_op jit(solution)/shard_map/ppermute | solution.py:480
  125.3 4.2 %collective-permute-done.17 = bf16[64,1024]{1,0:T(8,128)(2,1)S(1)} collective-permute-done((bf16[64,1024]{1,0:T(8,128)(2,1)S(1)}, bf16[64,1024]{1,0:T(8,128)(2,1)S(1)}, u32[]{:S(2)}, u32[]{:S(2)}) %collective-permute-start.17) | collective-permute-done | bytes 131104 | tf_op jit(solution)/shard_map/ppermute | solution.py:480
  129.5 0.1 fusion.34
  129.6 0.5 collective-permute-done.22
  130.1 6.7 %collective-permute-done.23 = bf16[64,1024]{1,0:T(8,128)(2,1)S(1)} collective-permute-done((bf16[64,1024]{1,0:T(8,128)(2,1)S(1)}, bf16[64,1024]{1,0:T(8,128)(2,1)S(1)}, u32[]{:S(2)}, u32[]{:S(2)}) %collective-permute-start.23) | collective-permute-done | bytes 131104 | tf_op jit(solution)/shard_map/ppermute | solution.py:480
  136.8 0.1 fusion.31
  136.9 0.7 pad_maximum_fusion.3
  (73 shorter events, 0.4 us)
Async XLA Ops:
  0.0 112.4 %copy-start = (bf16[1024,1024]{1,0:T(8,128)(2,1)S(1)}, bf16[1024,1024]{1,0:T(8,128)(2,1)}, u32[]{:S(2)}) copy-start(bf16[1024,1024]{1,0:T(8,128)(2,1)} %param.22) | copy-start | bytes 6291460
  0.0 23.0 %collective-permute-start = (bf16[128,1024]{1,0:T(8,128)(2,1)}, bf16[128,1024]{1,0:T(8,128)(2,1)S(1)}, u32[]{:S(2)}, u32[]{:S(2)}) collective-permute-start(bf16[128,1024]{1,0:T(8,128)(2,1)} %rest_5_.1), channel_id=1, source_target_pairs={{0,1},{1,2},{2,3},{3,0},{4,5},{5,6},{6,7},{7,4},{8,9},{9,10},{10,1... | collective-permute-start | bytes 786440 | tf_op jit(solution)/shard_map/ppermute | solution.py:480
  3.0 20.0 %collective-permute-start.1 = (bf16[128,1024]{1,0:T(8,128)(2,1)}, bf16[128,1024]{1,0:T(8,128)(2,1)S(1)}, u32[]{:S(2)}, u32[]{:S(2)}) collective-permute-start(bf16[128,1024]{1,0:T(8,128)(2,1)} %rest_5_.1), channel_id=1, source_target_pairs={{0,2},{1,3},{2,0},{3,1},{4,6},{5,7},{6,4},{7,5},{8,10},{9,11},{10,... | collective-permute-start | bytes 786440 | tf_op jit(solution)/shard_map/ppermute | solution.py:480
  17.8 5.2 %copy-start.6 = (bf16[1152,256]{1,0:T(8,128)(2,1)}, bf16[1152,256]{1,0:T(8,128)(2,1)S(1)}, u32[]{:S(2)}) copy-start(bf16[1152,256]{1,0:T(8,128)(2,1)S(1)} %all-gather) | copy-start | bytes 1769476
  23.0 0.8 copy-start.10
  23.0 0.7 copy-start.11
  23.8 4.5 %copy-start.9 = (bf16[128,1024]{1,0:T(8,128)(2,1)S(1)}, bf16[128,1024]{1,0:T(8,128)(2,1)}, u32[]{:S(2)}) copy-start(bf16[128,1024]{1,0:T(8,128)(2,1)} %rest_5_.1) | copy-start | bytes 786436
  23.8 6.0 %copy-start.19 = (bf16[1024]{0:T(1024)(128)(2,1)S(1)}, bf16[1024]{0:T(1024)(128)(2,1)}, u32[]{:S(2)}) copy-start(bf16[1024]{0:T(1024)(128)(2,1)} %param.17) | copy-start | bytes 6148
  23.8 6.6 %copy-start.7 = (bf16[256,1024]{1,0:T(8,128)(2,1)S(1)}, bf16[256,1024]{1,0:T(8,128)(2,1)}, u32[]{:S(2)}) copy-start(bf16[256,1024]{1,0:T(8,128)(2,1)} %param.20) | copy-start | bytes 1572868
  23.8 31.1 %all-to-all-start = ((bf16[8,4,128,2,128]{4,3,2,1,0:T(2,128)(2,1)}), bf16[8,4,128,2,128]{4,3,2,1,0:T(2,128)(2,1)}, u32[]{:S(2)}, u32[]{:S(2)}) async-start(bf16[8,4,128,2,128]{4,3,2,1,0:T(2,128)(2,1)} %get-tuple-element.45), calls=%async_computation | async-start | bytes 4194304 | tf_op jit(solution)/shard_map/all_to_all | solution.py:551
  28.3 9.1 %copy-start.18 = (s32[1,4]{1,0:T(1,128)S(1)}, s32[1,4]{1,0:T(1,128)}, u32[]{:S(2)}) copy-start(s32[1,4]{1,0:T(1,128)} %lens_ref.5) | copy-start | bytes 52
  28.3 9.3 %copy-start.17 = (s32[1,4]{1,0:T(1,128)S(1)}, s32[1,4]{1,0:T(1,128)}, u32[]{:S(2)}) copy-start(s32[1,4]{1,0:T(1,128)} %counts_ref.3) | copy-start | bytes 52
  28.3 17.5 %collective-permute-start.2 = (bf16[128,1024]{1,0:T(8,128)(2,1)S(1)}, bf16[128,1024]{1,0:T(8,128)(2,1)S(1)}, u32[]{:S(2)}, u32[]{:S(2)}) collective-permute-start(bf16[128,1024]{1,0:T(8,128)(2,1)S(1)} %copy-done.9), channel_id=1, source_target_pairs={{0,3},{1,0},{2,1},{3,2},{4,7},{5,4},{6,5},{7,6},{8,11},{9,8},{10,9... | collective-permute-start | bytes 786440 | tf_op jit(solution)/shard_map/ppermute | solution.py:480
  33.5 7.1 %collective-permute-start.3 = (bf16[128,256]{1,0:T(8,128)(2,1)}, bf16[128,256]{1,0:T(8,128)(2,1)S(1)}, u32[]{:S(2)}, u32[]{:S(2)}) collective-permute-start(bf16[128,256]{1,0:T(8,128)(2,1)} %get-tuple-element.49.rest_9_), channel_id=1, source_target_pairs={{0,1},{1,2},{2,3},{3,0},{4,5},{5,6},{6,7},{7,4},{8,9},{9,10},{10,1... | collective-permute-start | bytes 196616 | tf_op jit(solution)/shard_map/ppermute | solution.py:480
  34.2 8.4 %collective-permute-start.4 = (bf16[128,256]{1,0:T(8,128)(2,1)}, bf16[128,256]{1,0:T(8,128)(2,1)S(1)}, u32[]{:S(2)}, u32[]{:S(2)}) collective-permute-start(bf16[128,256]{1,0:T(8,128)(2,1)} %get-tuple-element.49.rest_9_), channel_id=1, source_target_pairs={{0,2},{1,3},{2,0},{3,1},{4,6},{5,7},{6,4},{7,5},{8,10},{9,11},{10,... | collective-permute-start | bytes 196616 | tf_op jit(solution)/shard_map/ppermute | solution.py:480
  34.5 8.1 %collective-permute-start.5 = (bf16[128,256]{1,0:T(8,128)(2,1)}, bf16[128,256]{1,0:T(8,128)(2,1)S(1)}, u32[]{:S(2)}, u32[]{:S(2)}) collective-permute-start(bf16[128,256]{1,0:T(8,128)(2,1)} %get-tuple-element.49.rest_9_), channel_id=1, source_target_pairs={{0,3},{1,0},{2,1},{3,2},{4,7},{5,4},{6,5},{7,6},{8,11},{9,8},{10,9... | collective-permute-start | bytes 196616 | tf_op jit(solution)/shard_map/ppermute | solution.py:480
  40.6 5.3 %copy-start.14 = (bf16[128,256]{1,0:T(8,128)(2,1)}, bf16[128,256]{1,0:T(8,128)(2,1)S(1)}, u32[]{:S(2)}) copy-start(bf16[128,256]{1,0:T(8,128)(2,1)S(1)} %collective-permute-done.3.rest_10_) | copy-start | bytes 196612
  42.6 3.2 %copy-start.15 = (bf16[128,256]{1,0:T(8,128)(2,1)}, bf16[128,256]{1,0:T(8,128)(2,1)S(1)}, u32[]{:S(2)}) copy-start(bf16[128,256]{1,0:T(8,128)(2,1)S(1)} %collective-permute-done.4.rest_11_) | copy-start | bytes 196612
  42.6 3.2 %copy-start.16 = (bf16[128,256]{1,0:T(8,128)(2,1)}, bf16[128,256]{1,0:T(8,128)(2,1)S(1)}, u32[]{:S(2)}) copy-start(bf16[128,256]{1,0:T(8,128)(2,1)S(1)} %collective-permute-done.5.rest_12_) | copy-start | bytes 196612
  42.6 10.4 %collective-permute-start.6 = (bf16[128,1024]{1,0:T(8,128)(2,1)}, bf16[128,1024]{1,0:T(8,128)(2,1)S(1)}, u32[]{:S(2)}, u32[]{:S(2)}) collective-permute-start(bf16[128,1024]{1,0:T(8,128)(2,1)} %get-tuple-element.56), channel_id=1, source_target_pairs={{0,1},{1,2},{2,3},{3,0},{4,5},{5,6},{6,7},{7,4},{8,9},{9,10},{10,1... | collective-permute-start | bytes 786440 | tf_op jit(solution)/shard_map/ppermute | solution.py:480
  45.8 0.7 copy-start.12
  54.9 31.4 %all-to-all-start.1 = ((bf16[8,4,128,2,128]{4,3,2,1,0:T(2,128)(2,1)}), bf16[8,4,128,2,128]{4,3,2,1,0:T(2,128)(2,1)}, u32[]{:S(2)}, u32[]{:S(2)}) async-start(bf16[8,4,128,2,128]{4,3,2,1,0:T(2,128)(2,1)} %get-tuple-element.63), calls=%async_computation.1 | async-start | bytes 4194304 | tf_op jit(solution)/shard_map/all_to_all | solution.py:571
  59.3 15.0 %collective-permute-start.7 = (bf16[128,1024]{1,0:T(8,128)(2,1)}, bf16[128,1024]{1,0:T(8,128)(2,1)S(1)}, u32[]{:S(2)}, u32[]{:S(2)}) collective-permute-start(bf16[128,1024]{1,0:T(8,128)(2,1)} %get-tuple-element.56), channel_id=1, source_target_pairs={{0,2},{1,3},{2,0},{3,1},{4,6},{5,7},{6,4},{7,5},{8,10},{9,11},{10,... | collective-permute-start | bytes 786440 | tf_op jit(solution)/shard_map/ppermute | solution.py:480
  60.0 14.3 %collective-permute-start.8 = (bf16[128,1024]{1,0:T(8,128)(2,1)}, bf16[128,1024]{1,0:T(8,128)(2,1)S(1)}, u32[]{:S(2)}, u32[]{:S(2)}) collective-permute-start(bf16[128,1024]{1,0:T(8,128)(2,1)} %get-tuple-element.56), channel_id=1, source_target_pairs={{0,3},{1,0},{2,1},{3,2},{4,7},{5,4},{6,5},{7,6},{8,11},{9,8},{10,9... | collective-permute-start | bytes 786440 | tf_op jit(solution)/shard_map/ppermute | solution.py:480
  75.3 8.7 %collective-permute-start.12 = (bf16[3,128,1024]{2,1,0:T(8,128)(2,1)}, bf16[3,128,1024]{2,1,0:T(8,128)(2,1)}, u32[]{:S(2)}, u32[]{:S(2)}) collective-permute-start(bf16[3,128,1024]{2,1,0:T(8,128)(2,1)} %pad_maximum_fusion.2), channel_id=1, source_target_pairs={{0,4},{4,0},{8,12},{12,8},{16,20},{20,16},{24,28},{28,24},{1,5},{5... | collective-permute-start | bytes 2359304 | tf_op jit(solution)/shard_map/ppermute | solution.py:484
  75.4 10.9 %copy-start.8 = (bf16[128,1024]{1,0:T(8,128)(2,1)S(1)}, bf16[128,1024]{1,0:T(8,128)(2,1)}, u32[]{:S(2)}) copy-start(bf16[128,1024]{1,0:T(8,128)(2,1)} %get-tuple-element.107) | copy-start | bytes 786436
  75.4 20.8 %collective-permute-start.10 = (bf16[512,128]{1,0:T(8,128)(2,1)}, bf16[512,128]{1,0:T(8,128)(2,1)S(1)}, u32[]{:S(2)}, u32[]{:S(2)}) collective-permute-start(bf16[512,128]{1,0:T(8,128)(2,1)} %attend.2.refs_2_), channel_id=1, source_target_pairs={{0,2},{1,3},{2,0},{3,1},{4,6},{5,7},{6,4},{7,5},{8,10},{9,11},{10,... | collective-permute-start | bytes 393224 | tf_op jit(solution)/shard_map/ppermute | solution.py:480
  80.6 15.5 %collective-permute-start.11 = (bf16[512,128]{1,0:T(8,128)(2,1)}, bf16[512,128]{1,0:T(8,128)(2,1)S(1)}, u32[]{:S(2)}, u32[]{:S(2)}) collective-permute-start(bf16[512,128]{1,0:T(8,128)(2,1)} %attend.2.refs_2_), channel_id=1, source_target_pairs={{0,3},{1,0},{2,1},{3,2},{4,7},{5,4},{6,5},{7,6},{8,11},{9,8},{10,9... | collective-permute-start | bytes 393224 | tf_op jit(solution)/shard_map/ppermute | solution.py:480
  84.0 12.1 %collective-permute-start.9 = (bf16[512,128]{1,0:T(8,128)(2,1)}, bf16[512,128]{1,0:T(8,128)(2,1)}, u32[]{:S(2)}, u32[]{:S(2)}) collective-permute-start(bf16[512,128]{1,0:T(8,128)(2,1)} %attend.2.refs_2_), channel_id=1, source_target_pairs={{0,1},{1,2},{2,3},{3,0},{4,5},{5,6},{6,7},{7,4},{8,9},{9,10},{10,1... | collective-permute-start | bytes 393224 | tf_op jit(solution)/shard_map/ppermute | solution.py:480
  86.3 14.3 %copy-start.20 = (bf16[1024]{0:T(1024)(128)(2,1)S(1)}, bf16[1024]{0:T(1024)(128)(2,1)}, u32[]{:S(2)}) copy-start(bf16[1024]{0:T(1024)(128)(2,1)} %param.18) | copy-start | bytes 6148
  86.3 14.3 %copy-start.3 = (bf16[512,128]{1,0:T(8,128)(2,1)S(1)}, bf16[512,128]{1,0:T(8,128)(2,1)}, u32[]{:S(2)}) copy-start(bf16[512,128]{1,0:T(8,128)(2,1)} %attend.2.refs_2_) | copy-start | bytes 393220
  96.1 10.4 %collective-permute-start.13 = (bf16[256,128]{1,0:T(8,128)(2,1)}, bf16[256,128]{1,0:T(8,128)(2,1)}, u32[]{:S(2)}, u32[]{:S(2)}) collective-permute-start(bf16[256,128]{1,0:T(8,128)(2,1)} %get-tuple-element.74), channel_id=1, source_target_pairs={{0,1},{1,2},{2,3},{3,0},{4,5},{5,6},{6,7},{7,4},{8,9},{9,10},{10,1... | collective-permute-start | bytes 196616 | tf_op jit(solution)/shard_map/ppermute | solution.py:480
  97.4 11.6 %collective-permute-start.14 = (bf16[256,128]{1,0:T(8,128)(2,1)}, bf16[256,128]{1,0:T(8,128)(2,1)}, u32[]{:S(2)}, u32[]{:S(2)}) collective-permute-start(bf16[256,128]{1,0:T(8,128)(2,1)} %get-tuple-element.74), channel_id=1, source_target_pairs={{0,2},{1,3},{2,0},{3,1},{4,6},{5,7},{6,4},{7,5},{8,10},{9,11},{10,... | collective-permute-start | bytes 196616 | tf_op jit(solution)/shard_map/ppermute | solution.py:480
  100.6 8.4 %collective-permute-start.15 = (bf16[256,128]{1,0:T(8,128)(2,1)}, bf16[256,128]{1,0:T(8,128)(2,1)}, u32[]{:S(2)}, u32[]{:S(2)}) collective-permute-start(bf16[256,128]{1,0:T(8,128)(2,1)} %get-tuple-element.74), channel_id=1, source_target_pairs={{0,3},{1,0},{2,1},{3,2},{4,7},{5,4},{6,5},{7,6},{8,11},{9,8},{10,9... | collective-permute-start | bytes 196616 | tf_op jit(solution)/shard_map/ppermute | solution.py:480
  100.6 1.0 copy-start.1
  101.6 1.0 copy-start.2
  102.7 8.2 %copy-start.4 = (bf16[2,1024,1024]{2,1,0:T(8,128)(2,1)S(1)}, bf16[2,1024,1024]{2,1,0:T(8,128)(2,1)}, u32[]{:S(2)}) copy-start(bf16[2,1024,1024]{2,1,0:T(8,128)(2,1)} %param.21) | copy-start | bytes 12582916
  104.5 11.5 %collective-permute-start.19 = (bf16[256,128]{1,0:T(8,128)(2,1)}, bf16[256,128]{1,0:T(8,128)(2,1)S(1)}, u32[]{:S(2)}, u32[]{:S(2)}) collective-permute-start(bf16[256,128]{1,0:T(8,128)(2,1)} %get-tuple-element.79), channel_id=1, source_target_pairs={{0,1},{1,2},{2,3},{3,0},{4,5},{5,6},{6,7},{7,4},{8,9},{9,10},{10,1... | collective-permute-start | bytes 196616 | tf_op jit(solution)/shard_map/ppermute | solution.py:480
  106.5 11.2 %collective-permute-start.20 = (bf16[256,128]{1,0:T(8,128)(2,1)}, bf16[256,128]{1,0:T(8,128)(2,1)S(1)}, u32[]{:S(2)}, u32[]{:S(2)}) collective-permute-start(bf16[256,128]{1,0:T(8,128)(2,1)} %get-tuple-element.79), channel_id=1, source_target_pairs={{0,2},{1,3},{2,0},{3,1},{4,6},{5,7},{6,4},{7,5},{8,10},{9,11},{10,... | collective-permute-start | bytes 196616 | tf_op jit(solution)/shard_map/ppermute | solution.py:480
  106.5 11.2 %collective-permute-start.21 = (bf16[256,128]{1,0:T(8,128)(2,1)}, bf16[256,128]{1,0:T(8,128)(2,1)S(1)}, u32[]{:S(2)}, u32[]{:S(2)}) collective-permute-start(bf16[256,128]{1,0:T(8,128)(2,1)} %get-tuple-element.79), channel_id=1, source_target_pairs={{0,3},{1,0},{2,1},{3,2},{4,7},{5,4},{6,5},{7,6},{8,11},{9,8},{10,9... | collective-permute-start | bytes 196616 | tf_op jit(solution)/shard_map/ppermute | solution.py:480
  112.5 5.3 %copy-start.5 = (bf16[512,1024]{1,0:T(8,128)(2,1)S(1)}, bf16[512,1024]{1,0:T(8,128)(2,1)}, u32[]{:S(2)}) copy-start(bf16[512,1024]{1,0:T(8,128)(2,1)} %pad_maximum_fusion.1) | copy-start | bytes 3145732
  112.5 5.3 %copy-start.13 = (bf16[256,128]{1,0:T(8,128)(2,1)S(1)}, bf16[256,128]{1,0:T(8,128)(2,1)}, u32[]{:S(2)}) copy-start(bf16[256,128]{1,0:T(8,128)(2,1)} %get-tuple-element.79) | copy-start | bytes 196612
  113.4 9.1 %collective-permute-start.16 = (bf16[64,1024]{1,0:T(8,128)(2,1)S(1)}, bf16[64,1024]{1,0:T(8,128)(2,1)S(1)}, u32[]{:S(2)}, u32[]{:S(2)}) collective-permute-start(bf16[64,1024]{1,0:T(8,128)(2,1)S(1)} %get-tuple-element.104), channel_id=1, source_target_pairs={{0,1},{1,2},{2,3},{3,0},{4,5},{5,6},{6,7},{7,4},{8,9},{9,10},{10,1... | collective-permute-start | bytes 393224 | tf_op jit(solution)/shard_map/ppermute | solution.py:480
  113.4 16.1 %collective-permute-start.17 = (bf16[64,1024]{1,0:T(8,128)(2,1)S(1)}, bf16[64,1024]{1,0:T(8,128)(2,1)S(1)}, u32[]{:S(2)}, u32[]{:S(2)}) collective-permute-start(bf16[64,1024]{1,0:T(8,128)(2,1)S(1)} %get-tuple-element.103), channel_id=1, source_target_pairs={{0,2},{1,3},{2,0},{3,1},{4,6},{5,7},{6,4},{7,5},{8,10},{9,11},{10,... | collective-permute-start | bytes 393224 | tf_op jit(solution)/shard_map/ppermute | solution.py:480
  115.9 13.6 %collective-permute-start.18 = (bf16[64,1024]{1,0:T(8,128)(2,1)S(1)}, bf16[64,1024]{1,0:T(8,128)(2,1)S(1)}, u32[]{:S(2)}, u32[]{:S(2)}) collective-permute-start(bf16[64,1024]{1,0:T(8,128)(2,1)S(1)} %get-tuple-element.102), channel_id=1, source_target_pairs={{0,3},{1,0},{2,1},{3,2},{4,7},{5,4},{6,5},{7,6},{8,11},{9,8},{10,9... | collective-permute-start | bytes 393224 | tf_op jit(solution)/shard_map/ppermute | solution.py:480
  120.8 9.3 %collective-permute-start.22 = (bf16[64,1024]{1,0:T(8,128)(2,1)S(1)}, bf16[64,1024]{1,0:T(8,128)(2,1)S(1)}, u32[]{:S(2)}, u32[]{:S(2)}) collective-permute-start(bf16[64,1024]{1,0:T(8,128)(2,1)S(1)} %get-tuple-element.99), channel_id=1, source_target_pairs={{0,1},{1,2},{2,3},{3,0},{4,5},{5,6},{6,7},{7,4},{8,9},{9,10},{10,1... | collective-permute-start | bytes 393224 | tf_op jit(solution)/shard_map/ppermute | solution.py:480
  121.0 15.8 %collective-permute-start.23 = (bf16[64,1024]{1,0:T(8,128)(2,1)S(1)}, bf16[64,1024]{1,0:T(8,128)(2,1)S(1)}, u32[]{:S(2)}, u32[]{:S(2)}) collective-permute-start(bf16[64,1024]{1,0:T(8,128)(2,1)S(1)} %get-tuple-element.101), channel_id=1, source_target_pairs={{0,2},{1,3},{2,0},{3,1},{4,6},{5,7},{6,4},{7,5},{8,10},{9,11},{10,... | collective-permute-start | bytes 393224 | tf_op jit(solution)/shard_map/ppermute | solution.py:480
  122.4 14.4 %collective-permute-start.24 = (bf16[64,1024]{1,0:T(8,128)(2,1)S(1)}, bf16[64,1024]{1,0:T(8,128)(2,1)S(1)}, u32[]{:S(2)}, u32[]{:S(2)}) collective-permute-start(bf16[64,1024]{1,0:T(8,128)(2,1)S(1)} %get-tuple-element.100), channel_id=1, source_target_pairs={{0,3},{1,0},{2,1},{3,2},{4,7},{5,4},{6,5},{7,6},{8,11},{9,8},{10,9... | collective-permute-start | bytes 393224 | tf_op jit(solution)/shard_map/ppermute | solution.py:480

commit v10 on v9

--- a/solution.py
+++ b/solution.py
@@ -17,6 +17,7 @@
 BF = jnp.bfloat16
 F32 = jnp.float32
 NEG = -1e30
+COPY = pl.CostEstimate(flops=1000, bytes_accessed=8 << 20, transcendentals=0)
 LIGHT = pl.CostEstimate(flops=1000, bytes_accessed=1000, transcendentals=0)
 
 
@@ -39,10 +40,8 @@
     return (onehot, cached * page_len + tok_index - first_pos)
 
 
-def pick_kernel(n_dp, cap, me_ref, asked_ref, pool_ref, *rest):
-    n_out = len(rest) - 3
-    outs, (buf, sem_in, sem_out) = rest[:n_out], rest[n_out:]
-    lanes = outs[0].shape[-1]
+def pick_kernel(n_dp, cap, group, me_ref, asked_ref, pool_ref, out, buf, sem_in, sem_out):
+    part = pl.ds(group * out.shape[-1], out.shape[-1])
     me = me_ref[0]
     slots = asked_ref.shape[2]
 
@@ -54,7 +53,7 @@
             @pl.when(hit)
             def _():
                 pltpu.make_async_copy(
-                    pool_ref.at[asked_ref[g, 1, p]], buf.at[g, count], sem_in.at[g]
+                    pool_ref.at[asked_ref[g, 1, p], :, :, part], buf.at[g, count], sem_in.at[g]
                 ).start()
 
             count = count + hit.astype(jnp.int32)
@@ -63,33 +62,31 @@
     lax.fori_loop(0, n_dp, find, 0)
     done = []
     for g in range(n_dp):
-        pltpu.make_async_copy(pool_ref.at[pl.ds(0, cap)], buf.at[g], sem_in.at[g]).wait()
-        for a in range(n_out):
-            copy = pltpu.make_async_copy(
-                buf.at[g, :, :, :, pl.ds(a * lanes, lanes)], outs[a].at[g], sem_out.at[a, g]
-            )
-            copy.start()
-            done.append(copy)
+        pltpu.make_async_copy(
+            pool_ref.at[pl.ds(0, cap), :, :, part], buf.at[g], sem_in.at[g]
+        ).wait()
+        copy = pltpu.make_async_copy(buf.at[g], out.at[g], sem_out.at[g])
+        copy.start()
+        done.append(copy)
     for copy in done:
         copy.wait()
 
 
-def pick(me, asked, pool, n_dp, cap, lanes):
+def pick(group, me, asked, pool, n_dp, cap, lanes):
     smem = pl.BlockSpec(memory_space=pltpu.SMEM)
     hbm = pl.BlockSpec(memory_space=pl.ANY)
-    n_out = pool.shape[-1] // lanes
-    shape = (n_dp, cap) + pool.shape[1:-1]
+    shape = (n_dp, cap) + pool.shape[1:-1] + (lanes,)
     return pl.pallas_call(
-        functools.partial(pick_kernel, n_dp, cap),
-        out_shape=[jax.ShapeDtypeStruct(shape + (lanes,), pool.dtype)] * n_out,
+        functools.partial(pick_kernel, n_dp, cap, group),
+        out_shape=jax.ShapeDtypeStruct(shape, pool.dtype),
         in_specs=[smem, smem, hbm],
-        out_specs=[hbm] * n_out,
+        out_specs=hbm,
         scratch_shapes=[
-            pltpu.VMEM(shape + pool.shape[-1:], pool.dtype),
+            pltpu.VMEM(shape, pool.dtype),
             pltpu.SemaphoreType.DMA((n_dp,)),
-            pltpu.SemaphoreType.DMA((n_out, n_dp)),
+            pltpu.SemaphoreType.DMA((n_dp,)),
         ],
-        cost_estimate=LIGHT,
+        cost_estimate=LIGHT if group == 0 else COPY,
         name="pick_pages",
     )(me, asked, pool)
 
@@ -450,30 +447,26 @@
 
 
 def partial_kernel(n_chunk, n_block, *refs):
-    toks, refs = refs[:n_chunk], refs[n_chunk:]
     blocks, refs = refs[:n_block], refs[n_block:]
     w_ref, outs = refs[0], refs[1:]
     rows = outs[0].shape[0]
     for c in range(n_chunk):
         part = jnp.concatenate([b[c * rows : (c + 1) * rows, :] for b in blocks], axis=1)
-        outs[c][...] = toks[c][...].astype(F32) + jnp.dot(
-            part, w_ref[...], preferred_element_type=F32
-        )
-
-
-def partial(toks, blocks, weight):
-    n_chunk = len(toks)
+        outs[c][...] = jnp.dot(part, w_ref[...], preferred_element_type=F32)
+
+
+def partial(n_chunk, blocks, weight):
     vmem = pl.BlockSpec(memory_space=pltpu.VMEM)
-    out = jax.ShapeDtypeStruct(toks[0].shape, F32)
+    out = jax.ShapeDtypeStruct((blocks[0].shape[0] // n_chunk, weight.shape[1]), F32)
     return pl.pallas_call(
         functools.partial(partial_kernel, n_chunk, len(blocks)),
         out_shape=[out] * n_chunk,
-        in_specs=[vmem] * (n_chunk + len(blocks) + 1),
+        in_specs=[vmem] * (len(blocks) + 1),
         out_specs=[vmem] * n_chunk,
         compiler_params=pltpu.CompilerParams(vmem_limit_bytes=24 << 20),
         cost_estimate=LIGHT,
         name="partial",
-    )(*toks, *blocks, weight)
+    )(*blocks, weight)
 
 
 def shift(value, axis, n, k):
@@ -546,13 +539,15 @@
     payload = jnp.concatenate([down_part, adapter_up.reshape(n_loc * span, width), names], axis=0)
     gathered = lax.all_gather(payload, "dp", axis=0)
     asked = gathered[:, 2 * n_loc * span : 2 * n_loc * span + 2, : page_table.shape[1]]
-    picked = pick(me, asked.astype(jnp.int32), cache_pool, n_dp, cap, lanes)
-    send = lax.optimization_barrier((picked[0], toks[1:-1]))[0]
+    asked = asked.astype(jnp.int32)
+    send = pick(0, me, asked, cache_pool, n_dp, cap, lanes)
+    send = lax.optimization_barrier((send, toks[1:-1]))[0]
     fetched = [lax.all_to_all(send, "dp", split_axis=0, concat_axis=0, tiled=True)]
 
     own_half = lax.dynamic_slice_in_dim(w_out, (dp % 2) * (width // 2), width // 2, 0)
     gathered, lengths_b = lax.optimization_barrier((gathered, lengths, send))[:2]
     down_named, up_named = named(owner_table, adapter_ids, gathered, n_loc, span)
+    later = lax.optimization_barrier((asked, down_named))[0]
     downs = [down_named] + [shift(down_named, "tensor", n_tp, k) for k in far_first]
 
     _, position = token_layout(lengths_b[0], page_counts[0], page_len, tok_total)
@@ -567,7 +562,8 @@
     own_half = lax.optimization_barrier((own_half, downs[1:]))[0]
     halves = [shift(own_half, "tensor", n_tp, k) for k in far_first]
     for a in range(1, n_group):
-        send = lax.optimization_barrier((picked[a], fetched[-1], query, halves[:1]))[0]
+        send = pick(a, me, later, cache_pool, n_dp, cap, lanes)
+        send = lax.optimization_barrier((send, fetched[-1], query, halves[:1]))[0]
         fetched.append(lax.all_to_all(send, "dp", split_axis=0, concat_axis=0, tiled=True))
     fetched = [f.reshape(slots, 2 * page_len, lanes) for f in fetched]
 
@@ -597,9 +593,7 @@
         w_whole = whole_weight(w_out, halves, dp, n_dp, n_group)
     last = attended(n_group - 1, query, True)
     early, last, w_whole = lax.optimization_barrier((early, last, w_whole))
-    bases = [tok.reshape(n_tp * sub, d_model) for tok in all_tokens]
-    for a in range(n_group - 1):
-        bases = partial(bases, early[a], w_whole[a])
+    bases = [partial(n_chunk, early[a], w_whole[a]) for a in range(n_group - 1)]
     outs = []
     pieces = None
     late = []
@@ -612,7 +606,10 @@
         blocks = late[c]
         if pieces is not None:
             blocks = lax.optimization_barrier((blocks, pieces))[0]
-        residual = bases[c].astype(F32) + mixed(blocks, n_group - 1)
+        residual = all_tokens[c].reshape(n_tp * sub, d_model).astype(F32)
+        for part in bases:
+            residual = residual + part[c]
+        residual = residual + mixed(blocks, n_group - 1)
         ffn_in = normalize(residual, ffn_gain).astype(BF)
         gate_up = jnp.einsum("td,kdf->ktf", ffn_in, w_gateup, preferred_element_type=F32)
         hidden = (jax.nn.silu(gate_up[0]) * gate_up[1]).astype(BF)

time: 138 us -> 147 us (1.065)
  Pallas kernels: 34.5 us -> 39.8 us
  other arithmetic: 8.55 us -> 11.6 us
  local copies, waits for them, and re-layouts: 6.36 us -> 3.57 us
  matrix products: 6.72 us -> 8.85 us
  waiting for transfers between devices: 20.9 us -> 23 us
  starting transfers between devices: 50.2 us -> 48.7 us
    ppermute x24, waiting for transfers between devices: 19 us -> 23 us  [shift(): return lax.ppermute(value, axis, [(i, (i + k) % n) for i in range(n)])]
    unnamed x42 -> x36, local copies, waits for them, and re-layouts: 3.56 us -> 0.08 us
    pallas_call x1 -> x2, Pallas kernels: 4.53 us -> 7.7 us  [pick(): pl.pallas_call(functools.partial(pick_kernel, n_dp, cap, group), out_shap...]
    convert_element_type x2, other arithmetic: 0.17 us -> 2.32 us  [per_device(): outs.append(total.astype(BF))]
    pallas_call x2, Pallas kernels: 19.4 us -> 21.6 us  [attend(): pl.pallas_call(functools.partial(attend_kernel, group, per, n_chunk), gri...]
    dot_general x2, matrix products: 1.66 us -> 3.65 us  [per_device(): jnp.dot(hidden, w_down, preferred_element_type=F32)]
    all_to_all x2, waiting for transfers between devices: 1.85 us -> 0.01 us  [per_device(): lax.all_to_all(send, 'dp', split_axis=0, concat_axis=0, tiled=True)]
  transfers between devices with their start and end apart: 27 -> 27, of which waited for: 7 -> 9; matrix products, arithmetic and copies ran while one was open for 13% -> 12% of each run, Pallas kernels for 25% -> 27%
where the time goes in v10:
time: 147 us; the launch traced here: 146 us
  starting transfers between devices  48.7 us (33%)
  Pallas kernels  39.8 us (27%)
  waiting for transfers between devices  23 us (16%)
  other arithmetic  11.6 us (8%)
  blocking collectives  9.99 us (7%)
  matrix products  8.85 us (6%)
  local copies, waits for them, and re-layouts  3.57 us (2%)
    ppermute x24, starting transfers between devices, shift(): return lax.ppermute(value, axis, [(i, (i + k) % n) for i in range(n)])  40 us
    ppermute x24, waiting for transfers between devices, shift(): return lax.ppermute(value, axis, [(i, (i + k) % n) for i in range(n)])  23 us
    pallas_call x2, Pallas kernels, attend(): pl.pallas_call(functools.partial(attend_kernel, group, per, n_chunk), gri...  21.6 us
    all_gather x1, blocking collectives, per_device(): gathered = lax.all_gather(payload, 'dp', axis=0)  9.99 us
    all_to_all x2, starting transfers between devices, per_device(): lax.all_to_all(send, 'dp', split_axis=0, concat_axis=0, tiled=True)  8.74 us
    pallas_call x2, Pallas kernels, pick(): pl.pallas_call(functools.partial(pick_kernel, n_dp, cap, group), out_shap...  7.7 us
    pallas_call x1, Pallas kernels, project(): pl.pallas_call(functools.partial(project_kernel, n_tp, cap, pool_dev, n_c...  6.55 us
    dot_general x2, matrix products, per_device(): jnp.dot(hidden, w_down, preferred_element_type=F32)  3.65 us
  transfers between devices with their start and end apart: 27, of which 9 were waited for; matrix products, arithmetic and copies ran while one was open for 12% of the time, Pallas kernels for 27%

profile of v10, /device:TPU:0, one launch (start us, length us, event | category | flops | bytes accessed | tf_op | source)
XLA Modules:
  0.0 146.0 jit_solution(4235530473498349435)
XLA Ops:
  0.0 3.0 %collective-permute-start = (bf16[128,1024]{1,0:T(8,128)(2,1)}, bf16[128,1024]{1,0:T(8,128)(2,1)}, u32[]{:S(2)}, u32[]{:S(2)}) collective-permute-start(bf16[128,1024]{1,0:T(8,128)(2,1)} %rest_5_.1), channel_id=1, source_target_pairs={{0,1},{1,2},{2,3},{3,0},{4,5},{5,6},{6,7},{7,4},{8,9},{9,10},{10,1... | collective-permute-start | bytes 786440 | tf_op jit(solution)/shard_map/ppermute | solution.py:473
  3.0 2.6 %collective-permute-start.1 = (bf16[128,1024]{1,0:T(8,128)(2,1)}, bf16[128,1024]{1,0:T(8,128)(2,1)}, u32[]{:S(2)}, u32[]{:S(2)}) collective-permute-start(bf16[128,1024]{1,0:T(8,128)(2,1)} %rest_5_.1), channel_id=1, source_target_pairs={{0,2},{1,3},{2,0},{3,1},{4,6},{5,7},{6,4},{7,5},{8,10},{9,11},{10,... | collective-permute-start | bytes 786440 | tf_op jit(solution)/shard_map/ppermute | solution.py:473
  5.6 0.7 fusion.55
  6.3 0.8 constant_dynamic-slice_fusion.1
  7.1 0.8 pad_maximum_fusion.4
  7.8 10.0 %all-gather = bf16[1152,256]{1,0:T(8,128)(2,1)S(1)} all-gather(bf16[144,256]{1,0:T(8,128)(2,1)S(1)} %pad_maximum_fusion.4), channel_id=2, replica_groups=mesh['dp'=8,'tensor'=4] {'dp'}, dimensions={0}, use_global_device_ids=true | all-gather | bytes 663552 | tf_op jit(solution)/shard_map/all_gather | solution.py:540
  17.8 0.6 slice_convert_fusion.asked_ref
  18.5 3.8 %pick_pages.2 = bf16[8,4,128,2,128]{4,3,2,1,0:T(2,128)(2,1)} custom-call(s32[1]{0:T(128)} %bitcast.4.me_ref, s32[8,2,32]{2,1,0:T(2,128)} %slice_convert_fusion.asked_ref, bf16[32,128,2,256]{3,2,1,0:T(2,128)(2,1)} %pool_ref.3), custom_call_target="tpu_custom_call" | custom-call | flops 1000 | bytes 1000 | tf_op jit(solution)/shard_map/pick_pages/pallas_call | solution.py:79
  22.3 0.6 collective-permute-done.1.rest_7_
  22.9 4.4 %all-to-all-start = ((bf16[8,4,128,2,128]{4,3,2,1,0:T(2,128)(2,1)}), bf16[8,4,128,2,128]{4,3,2,1,0:T(2,128)(2,1)}, u32[]{:S(2)}, u32[]{:S(2)}) async-start(bf16[8,4,128,2,128]{4,3,2,1,0:T(2,128)(2,1)} %pick_pages.2), calls=%async_computation | async-start | bytes 4194304 | tf_op jit(solution)/shard_map/all_to_all | solution.py:545
  27.3 1.7 %collective-permute-start.2 = (bf16[128,1024]{1,0:T(8,128)(2,1)S(1)}, bf16[128,1024]{1,0:T(8,128)(2,1)}, u32[]{:S(2)}, u32[]{:S(2)}) collective-permute-start(bf16[128,1024]{1,0:T(8,128)(2,1)S(1)} %copy-done.9), channel_id=1, source_target_pairs={{0,3},{1,0},{2,1},{3,2},{4,7},{5,4},{6,5},{7,6},{8,11},{9,8},{10,9... | collective-permute-start | bytes 786440 | tf_op jit(solution)/shard_map/ppermute | solution.py:473
  29.0 0.6 reshape.112.rest_0_
  29.6 0.9 fusion.62
  30.5 2.2 %named_adapters.1 = (bf16[128,256]{1,0:T(8,128)(2,1)}, bf16[128,256]{1,0:T(8,128)(2,1)}) custom-call(s32[16]{0:T(128)} %table_ref.2, s32[1,4]{1,0:T(1,128)} %ids_ref.1, bf16[8,144,256]{2,1,0:T(8,128)(2,1)} %bitcast.103), custom_call_target="tpu_custom_call" | custom-call | flops 1000 | bytes 1000 | tf_op jit(solution)/shard_map/named_adapters/pallas_call | solution.py:123
  32.7 0.4 collective-permute-start.3
  33.2 0.2 collective-permute-start.4
  33.4 3.2 %collective-permute-start.5 = (bf16[128,256]{1,0:T(8,128)(2,1)}, bf16[128,256]{1,0:T(8,128)(2,1)S(1)}, u32[]{:S(2)}, u32[]{:S(2)}) collective-permute-start(bf16[128,256]{1,0:T(8,128)(2,1)} %get-tuple-element.47.rest_9_), channel_id=1, source_target_pairs={{0,3},{1,0},{2,1},{3,2},{4,7},{5,4},{6,5},{7,6},{8,11},{9,8},{10,9... | collective-permute-start | bytes 196616 | tf_op jit(solution)/shard_map/ppermute | solution.py:473
  36.6 0.2 reduce-window.4
  36.9 0.1 select_reduce_fusion.1
  37.0 2.8 %collective-permute-done.3.rest_10_ = bf16[128,256]{1,0:T(8,128)(2,1)S(1)} collective-permute-done((bf16[128,256]{1,0:T(8,128)(2,1)}, bf16[128,256]{1,0:T(8,128)(2,1)S(1)}, u32[]{:S(2)}, u32[]{:S(2)}) %collective-permute-start.3) | collective-permute-done | bytes 65568 | tf_op jit(solution)/shard_map/ppermute | solution.py:473
  39.7 1.8 %collective-permute-done.4.rest_11_ = bf16[128,256]{1,0:T(8,128)(2,1)S(1)} collective-permute-done((bf16[128,256]{1,0:T(8,128)(2,1)}, bf16[128,256]{1,0:T(8,128)(2,1)S(1)}, u32[]{:S(2)}, u32[]{:S(2)}) %collective-permute-start.4) | collective-permute-done | bytes 65568 | tf_op jit(solution)/shard_map/ppermute | solution.py:473
  41.6 1.4 collective-permute-start.6
  42.9 3.9 %pick_pages.3 = bf16[8,4,128,2,128]{4,3,2,1,0:T(2,128)(2,1)} custom-call(s32[1]{0:T(128)} %bitcast.4.me_ref, s32[8,2,32]{2,1,0:T(2,128)} %slice_convert_fusion.asked_ref, bf16[32,128,2,256]{3,2,1,0:T(2,128)(2,1)} %pool_ref.3), custom_call_target="tpu_custom_call" | custom-call | flops 1000 | bytes 8388608 | tf_op jit(solution)/shard_map/pick_pages/pallas_call | solution.py:79
  46.9 1.8 %fusion.16 = (f32[512,128]{1,0:T(8,128)}, f32[512,128]{1,0:T(8,128)}) fusion(f32[128]{0:T(128)S(1)} %get-tuple-element.118, f32[128]{0:T(128)S(1)} %get-tuple-element.119, f32[512]{0:T(512)S(1)} %fusion.49), kind=kLoop, calls=%fused_computation.29 | loop fusion | flops 131072 | bytes 527360 | tf_op jit(solution)/shard_map/mul | solution.py:560
  48.7 6.6 %project.1 = (bf16[512,256]{1,0:T(8,128)(2,1)}, bf16[512,256]{1,0:T(8,128)(2,1)}, bf16[512,256]{1,0:T(8,128)(2,1)}, s32[32]{0:T(128)}, bf16[4,64,1024]{2,1,0:T(8,128)(2,1)}, /*index=5*/bf16[4,64,1024]{2,1,0:T(8,128)(2,1)}) custom-call(s32[1]{0:T(128)} %bitcast.tp_ref, s32[1,4]{1,0:T(1,128)} %lens_ref.5, s32[1,32]{1,0:T(1,128)} %table_ref.3, ...), custom_call_target="tpu_custom_call" | custom-call | flops 1000 | bytes 1000 | tf_op jit(solution)/shard_map/project/pallas_call | solution.py:247
  55.3 4.4 %all-to-all-start.1 = ((bf16[8,4,128,2,128]{4,3,2,1,0:T(2,128)(2,1)}), bf16[8,4,128,2,128]{4,3,2,1,0:T(2,128)(2,1)}, u32[]{:S(2)}, u32[]{:S(2)}) async-start(bf16[8,4,128,2,128]{4,3,2,1,0:T(2,128)(2,1)} %pick_pages.3), calls=%async_computation.1 | async-start | bytes 4194304 | tf_op jit(solution)/shard_map/all_to_all | solution.py:567
  59.7 2.7 %collective-permute-start.7 = (bf16[128,1024]{1,0:T(8,128)(2,1)S(1)}, bf16[128,1024]{1,0:T(8,128)(2,1)S(1)}, u32[]{:S(2)}, u32[]{:S(2)}) collective-permute-start(bf16[128,1024]{1,0:T(8,128)(2,1)S(1)} %get-tuple-element.53), channel_id=1, source_target_pairs={{0,2},{1,3},{2,0},{3,1},{4,6},{5,7},{6,4},{7,5},{8,10},{9,11},{10,... | collective-permute-start | bytes 786440 | tf_op jit(solution)/shard_map/ppermute | solution.py:473
  62.4 0.1 collective-permute-start.8
  62.5 10.8 %attend.2.refs_0_ = bf16[512,128]{1,0:T(8,128)(2,1)} custom-call(s32[1,4]{1,0:T(1,128)} %lens_ref.5, s32[1,4]{1,0:T(1,128)} %counts_ref.3, s32[32]{0:T(128)} %get-tuple-element.49.pos_ref, f32[2,4]{1,0:T(2,128)} %bias_ref.3, bf16[512,256]{1,0:T(8,128)(2,1)} %get-tuple-element.58.q_ref, bf16[512,256]{1,0:T(8,128)(2,1)} %get-tuple-element.51.kn_ref, ...), custom_call_target="tpu_custom_call" | custom-call | flops 1000 | bytes 1000 | tf_op jit(solution)/shard_map/attend/pallas_call | solution.py:424
  73.3 1.4 collective-permute-done.7
  74.7 1.4 collective-permute-done.8
  76.1 1.0 pad_maximum_fusion.2
  77.1 4.9 %collective-permute-start.9 = (bf16[512,128]{1,0:T(8,128)(2,1)}, bf16[512,128]{1,0:T(8,128)(2,1)S(1)}, u32[]{:S(2)}, u32[]{:S(2)}) collective-permute-start(bf16[512,128]{1,0:T(8,128)(2,1)} %attend.2.refs_0_), channel_id=1, source_target_pairs={{0,1},{1,2},{2,3},{3,0},{4,5},{5,6},{6,7},{7,4},{8,9},{9,10},{10,1... | collective-permute-start | bytes 393224 | tf_op jit(solution)/shard_map/ppermute | solution.py:473
  82.0 2.4 %collective-permute-start.10 = (bf16[512,128]{1,0:T(8,128)(2,1)}, bf16[512,128]{1,0:T(8,128)(2,1)S(1)}, u32[]{:S(2)}, u32[]{:S(2)}) collective-permute-start(bf16[512,128]{1,0:T(8,128)(2,1)} %attend.2.refs_0_), channel_id=1, source_target_pairs={{0,2},{1,3},{2,0},{3,1},{4,6},{5,7},{6,4},{7,5},{8,10},{9,11},{10,... | collective-permute-start | bytes 393224 | tf_op jit(solution)/shard_map/ppermute | solution.py:473
  84.4 1.2 broadcast_select_fusion.2
  85.7 1.0 pad_maximum_fusion.refs_4_
  86.7 1.1 pad_maximum_fusion.1
  87.8 10.8 %attend.3 = (bf16[256,128]{1,0:T(8,128)(2,1)}, bf16[256,128]{1,0:T(8,128)(2,1)}) custom-call(s32[1,4]{1,0:T(1,128)} %lens_ref.5, s32[1,4]{1,0:T(1,128)} %counts_ref.3, s32[32]{0:T(128)} %get-tuple-element.49.pos_ref, f32[2,4]{1,0:T(2,128)} %bias_ref.3, bf16[512,256]{1,0:T(8,128)(2,1)} %get-tuple-element.58.q_ref, bf16[512,256]{1,0:T(8,128)(2,1)} %get-tuple-element.51.kn_ref, ...), custom_call_target="tpu_custom_call" | custom-call | flops 1000 | bytes 1000 | tf_op jit(solution)/shard_map/attend/pallas_call | solution.py:424
  98.6 2.1 %collective-permute-start.15 = (bf16[256,128]{1,0:T(8,128)(2,1)}, bf16[256,128]{1,0:T(8,128)(2,1)}, u32[]{:S(2)}, u32[]{:S(2)}) collective-permute-start(bf16[256,128]{1,0:T(8,128)(2,1)} %get-tuple-element.71), channel_id=1, source_target_pairs={{0,3},{1,0},{2,1},{3,2},{4,7},{5,4},{6,5},{7,6},{8,11},{9,8},{10,9... | collective-permute-start | bytes 196616 | tf_op jit(solution)/shard_map/ppermute | solution.py:473
  100.7 1.4 collective-permute-start.14
  102.2 1.8 %partial.1 = (f32[256,1024]{1,0:T(8,128)S(1)}, f32[256,1024]{1,0:T(8,128)S(1)}) custom-call(bf16[512,128]{1,0:T(8,128)(2,1)S(1)} %copy-done.1, bf16[512,128]{1,0:T(8,128)(2,1)S(1)} %collective-permute-done.9.refs_1_, bf16[512,128]{1,0:T(8,128)(2,1)S(1)} %collective-permute-done.10.refs_2_, bf16[512,128]{1,0:T(8,128)(2,1)} %collective-permute-done.11.refs_3_, ...), custom_call_target="tpu_custom_call" | custom-call | flops 1000 | bytes 1000 | tf_op jit(solution)/shard_map/partial/pallas_call | solution.py:461
  104.0 2.0 %collective-permute-start.19 = (bf16[256,128]{1,0:T(8,128)(2,1)}, bf16[256,128]{1,0:T(8,128)(2,1)S(1)}, u32[]{:S(2)}, u32[]{:S(2)}) collective-permute-start(bf16[256,128]{1,0:T(8,128)(2,1)} %get-tuple-element.77), channel_id=1, source_target_pairs={{0,1},{1,2},{2,3},{3,0},{4,5},{5,6},{6,7},{7,4},{8,9},{9,10},{10,1... | collective-permute-start | bytes 196616 | tf_op jit(solution)/shard_map/ppermute | solution.py:473
  106.0 2.3 %collective-permute-start.20 = (bf16[256,128]{1,0:T(8,128)(2,1)}, bf16[256,128]{1,0:T(8,128)(2,1)S(1)}, u32[]{:S(2)}, u32[]{:S(2)}) collective-permute-start(bf16[256,128]{1,0:T(8,128)(2,1)} %get-tuple-element.77), channel_id=1, source_target_pairs={{0,2},{1,3},{2,0},{3,1},{4,6},{5,7},{6,4},{7,5},{8,10},{9,11},{10,... | collective-permute-start | bytes 196616 | tf_op jit(solution)/shard_map/ppermute | solution.py:473
  108.3 0.1 collective-permute-start.21
  108.5 2.3 %collective-permute-done.14 = bf16[256,128]{1,0:T(8,128)(2,1)} collective-permute-done((bf16[256,128]{1,0:T(8,128)(2,1)}, bf16[256,128]{1,0:T(8,128)(2,1)}, u32[]{:S(2)}, u32[]{:S(2)}) %collective-permute-start.14) | collective-permute-done | bytes 65568 | tf_op jit(solution)/shard_map/ppermute | solution.py:473
  110.7 2.0 %multiply_reduce_fusion.1 = (f32[256]{0:T(256)S(1)}, f32[256,1024]{1,0:T(8,128)S(1)}) fusion(bf16[512,1024]{1,0:T(8,128)(2,1)} %pad_maximum_fusion.1, bf16[256,128]{1,0:T(8,128)(2,1)} %collective-permute-done.15, bf16[256,128]{1,0:T(8,128)(2,1)} %collective-permute-done.14, bf16[256,128]{1,0:T(8,128)(2,1)} %collective-permute-done.13, ...), kind=kOutput, calls=%fused_computation.17 | convolution fusion | flops 270794496 | bytes 3933184 | tf_op jit(solution)/shard_map/dot_general | solution.py:572
  112.8 1.3 convolution_bitcast_fusion.1
  114.1 0.2 fusion.61
  114.4 1.8 %fusion.63 = (bf16[4,64,1024]{2,1,0:T(8,128)(2,1)S(1)}, f32[4,64,1024]{2,1,0:T(8,128)}) fusion(bf16[1024,1024]{1,0:T(8,128)(2,1)S(1)} %copy-done, f32[4,64,1024]{2,1,0:T(8,128)S(1)} %bitcast.105, f32[4,64,1024]{2,1,0:T(8,128)S(1)} %bitcast.104), kind=kOutput, calls=%fused_computation.114 | convolution fusion | flops 538705920 | bytes 5767168 | tf_op jit(solution)/shard_map/dot_general | solution.py:616
  116.3 0.5 multiply_reduce_fusion
  116.9 1.3 convolution_bitcast_fusion
  118.2 0.2 fusion.60
  118.4 1.8 %fusion.64 = (bf16[4,64,1024]{2,1,0:T(8,128)(2,1)S(1)}, f32[4,64,1024]{2,1,0:T(8,128)}) fusion(bf16[1024,1024]{1,0:T(8,128)(2,1)S(1)} %copy-done, f32[4,64,1024]{2,1,0:T(8,128)S(1)} %bitcast.107, f32[4,64,1024]{2,1,0:T(8,128)S(1)} %bitcast.106), kind=kOutput, calls=%fused_computation.115 | convolution fusion | flops 538705920 | bytes 5767168 | tf_op jit(solution)/shard_map/dot_general | solution.py:616
  120.3 0.7 dynamic-slice_bitcast_fusion.2
  121.0 1.1 collective-permute-start.23
  122.1 0.9 collective-permute-start.22
  123.0 2.9 %collective-permute-start.18 = (bf16[64,1024]{1,0:T(8,128)(2,1)S(1)}, bf16[64,1024]{1,0:T(8,128)(2,1)S(1)}, u32[]{:S(2)}, u32[]{:S(2)}) collective-permute-start(bf16[64,1024]{1,0:T(8,128)(2,1)S(1)} %get-tuple-element.100), channel_id=1, source_target_pairs={{0,3},{1,0},{2,1},{3,2},{4,7},{5,4},{6,5},{7,6},{8,11},{9,8},{10,9... | collective-permute-start | bytes 393224 | tf_op jit(solution)/shard_map/ppermute | solution.py:473
  126.0 3.3 %collective-permute-done.24 = bf16[64,1024]{1,0:T(8,128)(2,1)} collective-permute-done((bf16[64,1024]{1,0:T(8,128)(2,1)}, bf16[64,1024]{1,0:T(8,128)(2,1)}, u32[]{:S(2)}, u32[]{:S(2)}) %collective-permute-start.24) | collective-permute-done | bytes 131104 | tf_op jit(solution)/shard_map/ppermute | solution.py:473
  129.3 4.3 %collective-permute-start.16 = (bf16[64,1024]{1,0:T(8,128)(2,1)S(1)}, bf16[64,1024]{1,0:T(8,128)(2,1)S(1)}, u32[]{:S(2)}, u32[]{:S(2)}) collective-permute-start(bf16[64,1024]{1,0:T(8,128)(2,1)S(1)} %get-tuple-element.102), channel_id=1, source_target_pairs={{0,1},{1,2},{2,3},{3,0},{4,5},{5,6},{6,7},{7,4},{8,9},{9,10},{10,1... | collective-permute-start | bytes 393224 | tf_op jit(solution)/shard_map/ppermute | solution.py:473
  133.6 6.6 %collective-permute-done.23 = bf16[64,1024]{1,0:T(8,128)(2,1)} collective-permute-done((bf16[64,1024]{1,0:T(8,128)(2,1)}, bf16[64,1024]{1,0:T(8,128)(2,1)}, u32[]{:S(2)}, u32[]{:S(2)}) %collective-permute-start.23) | collective-permute-done | bytes 131104 | tf_op jit(solution)/shard_map/ppermute | solution.py:473
  140.1 1.3 fusion.39
  141.4 2.8 %collective-permute-done.17 = bf16[64,1024]{1,0:T(8,128)(2,1)S(1)} collective-permute-done((bf16[64,1024]{1,0:T(8,128)(2,1)S(1)}, bf16[64,1024]{1,0:T(8,128)(2,1)S(1)}, u32[]{:S(2)}, u32[]{:S(2)}) %collective-permute-start.17) | collective-permute-done | bytes 131104 | tf_op jit(solution)/shard_map/ppermute | solution.py:473
  144.2 1.0 fusion.42
  145.3 0.7 pad_maximum_fusion.3
  (68 shorter events, 0.4 us)
Async XLA Ops:
  0.0 114.3 %copy-start = (bf16[1024,1024]{1,0:T(8,128)(2,1)S(1)}, bf16[1024,1024]{1,0:T(8,128)(2,1)}, u32[]{:S(2)}) copy-start(bf16[1024,1024]{1,0:T(8,128)(2,1)} %param.22) | copy-start | bytes 6291460
  0.0 22.3 %collective-permute-start = (bf16[128,1024]{1,0:T(8,128)(2,1)}, bf16[128,1024]{1,0:T(8,128)(2,1)}, u32[]{:S(2)}, u32[]{:S(2)}) collective-permute-start(bf16[128,1024]{1,0:T(8,128)(2,1)} %rest_5_.1), channel_id=1, source_target_pairs={{0,1},{1,2},{2,3},{3,0},{4,5},{5,6},{6,7},{7,4},{8,9},{9,10},{10,1... | collective-permute-start | bytes 786440 | tf_op jit(solution)/shard_map/ppermute | solution.py:473
  3.0 19.9 %collective-permute-start.1 = (bf16[128,1024]{1,0:T(8,128)(2,1)}, bf16[128,1024]{1,0:T(8,128)(2,1)}, u32[]{:S(2)}, u32[]{:S(2)}) collective-permute-start(bf16[128,1024]{1,0:T(8,128)(2,1)} %rest_5_.1), channel_id=1, source_target_pairs={{0,2},{1,3},{2,0},{3,1},{4,6},{5,7},{6,4},{7,5},{8,10},{9,11},{10,... | collective-permute-start | bytes 786440 | tf_op jit(solution)/shard_map/ppermute | solution.py:473
  17.8 4.5 %copy-start.5 = (bf16[1152,256]{1,0:T(8,128)(2,1)}, bf16[1152,256]{1,0:T(8,128)(2,1)S(1)}, u32[]{:S(2)}) copy-start(bf16[1152,256]{1,0:T(8,128)(2,1)S(1)} %all-gather) | copy-start | bytes 1769476
  22.3 5.0 %copy-start.9 = (bf16[128,1024]{1,0:T(8,128)(2,1)S(1)}, bf16[128,1024]{1,0:T(8,128)(2,1)}, u32[]{:S(2)}) copy-start(bf16[128,1024]{1,0:T(8,128)(2,1)} %rest_5_.1) | copy-start | bytes 786436
  22.3 6.7 %copy-start.16 = (bf16[1024]{0:T(1024)(128)(2,1)S(1)}, bf16[1024]{0:T(1024)(128)(2,1)}, u32[]{:S(2)}) copy-start(bf16[1024]{0:T(1024)(128)(2,1)} %param.17) | copy-start | bytes 6148
  22.3 7.3 %copy-start.6 = (bf16[256,1024]{1,0:T(8,128)(2,1)S(1)}, bf16[256,1024]{1,0:T(8,128)(2,1)}, u32[]{:S(2)}) copy-start(bf16[256,1024]{1,0:T(8,128)(2,1)} %param.20) | copy-start | bytes 1572868
  22.9 32.4 %all-to-all-start = ((bf16[8,4,128,2,128]{4,3,2,1,0:T(2,128)(2,1)}), bf16[8,4,128,2,128]{4,3,2,1,0:T(2,128)(2,1)}, u32[]{:S(2)}, u32[]{:S(2)}) async-start(bf16[8,4,128,2,128]{4,3,2,1,0:T(2,128)(2,1)} %pick_pages.2), calls=%async_computation | async-start | bytes 4194304 | tf_op jit(solution)/shard_map/all_to_all | solution.py:545
  27.3 9.3 %copy-start.15 = (s32[1,4]{1,0:T(1,128)S(1)}, s32[1,4]{1,0:T(1,128)}, u32[]{:S(2)}) copy-start(s32[1,4]{1,0:T(1,128)} %lens_ref.5) | copy-start | bytes 52
  27.3 9.6 %copy-start.14 = (s32[1,4]{1,0:T(1,128)S(1)}, s32[1,4]{1,0:T(1,128)}, u32[]{:S(2)}) copy-start(s32[1,4]{1,0:T(1,128)} %counts_ref.3) | copy-start | bytes 52
  27.3 21.4 %collective-permute-start.2 = (bf16[128,1024]{1,0:T(8,128)(2,1)S(1)}, bf16[128,1024]{1,0:T(8,128)(2,1)}, u32[]{:S(2)}, u32[]{:S(2)}) collective-permute-start(bf16[128,1024]{1,0:T(8,128)(2,1)S(1)} %copy-done.9), channel_id=1, source_target_pairs={{0,3},{1,0},{2,1},{3,2},{4,7},{5,4},{6,5},{7,6},{8,11},{9,8},{10,9... | collective-permute-start | bytes 786440 | tf_op jit(solution)/shard_map/ppermute | solution.py:473
  32.7 7.0 %collective-permute-start.3 = (bf16[128,256]{1,0:T(8,128)(2,1)}, bf16[128,256]{1,0:T(8,128)(2,1)S(1)}, u32[]{:S(2)}, u32[]{:S(2)}) collective-permute-start(bf16[128,256]{1,0:T(8,128)(2,1)} %get-tuple-element.47.rest_9_), channel_id=1, source_target_pairs={{0,1},{1,2},{2,3},{3,0},{4,5},{5,6},{6,7},{7,4},{8,9},{9,10},{10,1... | collective-permute-start | bytes 196616 | tf_op jit(solution)/shard_map/ppermute | solution.py:473
  33.2 8.4 %collective-permute-start.4 = (bf16[128,256]{1,0:T(8,128)(2,1)}, bf16[128,256]{1,0:T(8,128)(2,1)S(1)}, u32[]{:S(2)}, u32[]{:S(2)}) collective-permute-start(bf16[128,256]{1,0:T(8,128)(2,1)} %get-tuple-element.47.rest_9_), channel_id=1, source_target_pairs={{0,2},{1,3},{2,0},{3,1},{4,6},{5,7},{6,4},{7,5},{8,10},{9,11},{10,... | collective-permute-start | bytes 196616 | tf_op jit(solution)/shard_map/ppermute | solution.py:473
  33.4 8.2 %collective-permute-start.5 = (bf16[128,256]{1,0:T(8,128)(2,1)}, bf16[128,256]{1,0:T(8,128)(2,1)S(1)}, u32[]{:S(2)}, u32[]{:S(2)}) collective-permute-start(bf16[128,256]{1,0:T(8,128)(2,1)} %get-tuple-element.47.rest_9_), channel_id=1, source_target_pairs={{0,3},{1,0},{2,1},{3,2},{4,7},{5,4},{6,5},{7,6},{8,11},{9,8},{10,9... | collective-permute-start | bytes 196616 | tf_op jit(solution)/shard_map/ppermute | solution.py:473
  39.7 7.1 %copy-start.11 = (bf16[128,256]{1,0:T(8,128)(2,1)}, bf16[128,256]{1,0:T(8,128)(2,1)S(1)}, u32[]{:S(2)}) copy-start(bf16[128,256]{1,0:T(8,128)(2,1)S(1)} %collective-permute-done.3.rest_10_) | copy-start | bytes 196612
  41.6 5.3 %copy-start.12 = (bf16[128,256]{1,0:T(8,128)(2,1)}, bf16[128,256]{1,0:T(8,128)(2,1)S(1)}, u32[]{:S(2)}) copy-start(bf16[128,256]{1,0:T(8,128)(2,1)S(1)} %collective-permute-done.4.rest_11_) | copy-start | bytes 196612
  41.6 5.3 %copy-start.13 = (bf16[128,256]{1,0:T(8,128)(2,1)}, bf16[128,256]{1,0:T(8,128)(2,1)S(1)}, u32[]{:S(2)}) copy-start(bf16[128,256]{1,0:T(8,128)(2,1)S(1)} %collective-permute-done.5.rest_12_) | copy-start | bytes 196612
  41.6 13.7 %collective-permute-start.6 = (bf16[128,1024]{1,0:T(8,128)(2,1)S(1)}, bf16[128,1024]{1,0:T(8,128)(2,1)S(1)}, u32[]{:S(2)}, u32[]{:S(2)}) collective-permute-start(bf16[128,1024]{1,0:T(8,128)(2,1)S(1)} %get-tuple-element.53), channel_id=1, source_target_pairs={{0,1},{1,2},{2,3},{3,0},{4,5},{5,6},{6,7},{7,4},{8,9},{9,10},{10,1... | collective-permute-start | bytes 786440 | tf_op jit(solution)/shard_map/ppermute | solution.py:473
  55.3 32.5 %all-to-all-start.1 = ((bf16[8,4,128,2,128]{4,3,2,1,0:T(2,128)(2,1)}), bf16[8,4,128,2,128]{4,3,2,1,0:T(2,128)(2,1)}, u32[]{:S(2)}, u32[]{:S(2)}) async-start(bf16[8,4,128,2,128]{4,3,2,1,0:T(2,128)(2,1)} %pick_pages.3), calls=%async_computation.1 | async-start | bytes 4194304 | tf_op jit(solution)/shard_map/all_to_all | solution.py:567
  59.7 15.1 %collective-permute-start.7 = (bf16[128,1024]{1,0:T(8,128)(2,1)S(1)}, bf16[128,1024]{1,0:T(8,128)(2,1)S(1)}, u32[]{:S(2)}, u32[]{:S(2)}) collective-permute-start(bf16[128,1024]{1,0:T(8,128)(2,1)S(1)} %get-tuple-element.53), channel_id=1, source_target_pairs={{0,2},{1,3},{2,0},{3,1},{4,6},{5,7},{6,4},{7,5},{8,10},{9,11},{10,... | collective-permute-start | bytes 786440 | tf_op jit(solution)/shard_map/ppermute | solution.py:473
  62.4 13.8 %collective-permute-start.8 = (bf16[128,1024]{1,0:T(8,128)(2,1)S(1)}, bf16[128,1024]{1,0:T(8,128)(2,1)S(1)}, u32[]{:S(2)}, u32[]{:S(2)}) collective-permute-start(bf16[128,1024]{1,0:T(8,128)(2,1)S(1)} %get-tuple-element.53), channel_id=1, source_target_pairs={{0,3},{1,0},{2,1},{3,2},{4,7},{5,4},{6,5},{7,6},{8,11},{9,8},{10,9... | collective-permute-start | bytes 786440 | tf_op jit(solution)/shard_map/ppermute | solution.py:473
  77.1 7.3 %collective-permute-start.12 = (bf16[3,128,1024]{2,1,0:T(8,128)(2,1)}, bf16[3,128,1024]{2,1,0:T(8,128)(2,1)}, u32[]{:S(2)}, u32[]{:S(2)}) collective-permute-start(bf16[3,128,1024]{2,1,0:T(8,128)(2,1)} %pad_maximum_fusion.2), channel_id=1, source_target_pairs={{0,4},{4,0},{8,12},{12,8},{16,20},{20,16},{24,28},{28,24},{1,5},{5... | collective-permute-start | bytes 2359304 | tf_op jit(solution)/shard_map/ppermute | solution.py:477
  77.1 9.5 %copy-start.7 = (bf16[128,1024]{1,0:T(8,128)(2,1)S(1)}, bf16[128,1024]{1,0:T(8,128)(2,1)}, u32[]{:S(2)}) copy-start(bf16[128,1024]{1,0:T(8,128)(2,1)} %get-tuple-element.103) | copy-start | bytes 786436
  77.1 21.4 %collective-permute-start.9 = (bf16[512,128]{1,0:T(8,128)(2,1)}, bf16[512,128]{1,0:T(8,128)(2,1)S(1)}, u32[]{:S(2)}, u32[]{:S(2)}) collective-permute-start(bf16[512,128]{1,0:T(8,128)(2,1)} %attend.2.refs_0_), channel_id=1, source_target_pairs={{0,1},{1,2},{2,3},{3,0},{4,5},{5,6},{6,7},{7,4},{8,9},{9,10},{10,1... | collective-permute-start | bytes 393224 | tf_op jit(solution)/shard_map/ppermute | solution.py:473
  82.0 16.6 %collective-permute-start.10 = (bf16[512,128]{1,0:T(8,128)(2,1)}, bf16[512,128]{1,0:T(8,128)(2,1)S(1)}, u32[]{:S(2)}, u32[]{:S(2)}) collective-permute-start(bf16[512,128]{1,0:T(8,128)(2,1)} %attend.2.refs_0_), channel_id=1, source_target_pairs={{0,2},{1,3},{2,0},{3,1},{4,6},{5,7},{6,4},{7,5},{8,10},{9,11},{10,... | collective-permute-start | bytes 393224 | tf_op jit(solution)/shard_map/ppermute | solution.py:473
  84.4 14.1 %collective-permute-start.11 = (bf16[512,128]{1,0:T(8,128)(2,1)}, bf16[512,128]{1,0:T(8,128)(2,1)}, u32[]{:S(2)}, u32[]{:S(2)}) collective-permute-start(bf16[512,128]{1,0:T(8,128)(2,1)} %attend.2.refs_0_), channel_id=1, source_target_pairs={{0,3},{1,0},{2,1},{3,2},{4,7},{5,4},{6,5},{7,6},{8,11},{9,8},{10,9... | collective-permute-start | bytes 393224 | tf_op jit(solution)/shard_map/ppermute | solution.py:473
  86.7 15.5 %copy-start.17 = (bf16[1024]{0:T(1024)(128)(2,1)S(1)}, bf16[1024]{0:T(1024)(128)(2,1)}, u32[]{:S(2)}) copy-start(bf16[1024]{0:T(1024)(128)(2,1)} %param.18) | copy-start | bytes 6148
  86.7 15.5 %copy-start.1 = (bf16[512,128]{1,0:T(8,128)(2,1)S(1)}, bf16[512,128]{1,0:T(8,128)(2,1)}, u32[]{:S(2)}) copy-start(bf16[512,128]{1,0:T(8,128)(2,1)} %attend.2.refs_0_) | copy-start | bytes 393220
  98.6 9.8 %collective-permute-start.15 = (bf16[256,128]{1,0:T(8,128)(2,1)}, bf16[256,128]{1,0:T(8,128)(2,1)}, u32[]{:S(2)}, u32[]{:S(2)}) collective-permute-start(bf16[256,128]{1,0:T(8,128)(2,1)} %get-tuple-element.71), channel_id=1, source_target_pairs={{0,3},{1,0},{2,1},{3,2},{4,7},{5,4},{6,5},{7,6},{8,11},{9,8},{10,9... | collective-permute-start | bytes 196616 | tf_op jit(solution)/shard_map/ppermute | solution.py:473
  100.7 10.0 %collective-permute-start.14 = (bf16[256,128]{1,0:T(8,128)(2,1)}, bf16[256,128]{1,0:T(8,128)(2,1)}, u32[]{:S(2)}, u32[]{:S(2)}) collective-permute-start(bf16[256,128]{1,0:T(8,128)(2,1)} %get-tuple-element.71), channel_id=1, source_target_pairs={{0,2},{1,3},{2,0},{3,1},{4,6},{5,7},{6,4},{7,5},{8,10},{9,11},{10,... | collective-permute-start | bytes 196616 | tf_op jit(solution)/shard_map/ppermute | solution.py:473
  102.1 8.6 %collective-permute-start.13 = (bf16[256,128]{1,0:T(8,128)(2,1)}, bf16[256,128]{1,0:T(8,128)(2,1)}, u32[]{:S(2)}, u32[]{:S(2)}) collective-permute-start(bf16[256,128]{1,0:T(8,128)(2,1)} %get-tuple-element.71), channel_id=1, source_target_pairs={{0,1},{1,2},{2,3},{3,0},{4,5},{5,6},{6,7},{7,4},{8,9},{9,10},{10,1... | collective-permute-start | bytes 196616 | tf_op jit(solution)/shard_map/ppermute | solution.py:473
  102.2 10.6 %copy-start.2 = (bf16[2,1024,1024]{2,1,0:T(8,128)(2,1)S(1)}, bf16[2,1024,1024]{2,1,0:T(8,128)(2,1)}, u32[]{:S(2)}) copy-start(bf16[2,1024,1024]{2,1,0:T(8,128)(2,1)} %param.21) | copy-start | bytes 12582916
  104.0 12.3 %collective-permute-start.19 = (bf16[256,128]{1,0:T(8,128)(2,1)}, bf16[256,128]{1,0:T(8,128)(2,1)S(1)}, u32[]{:S(2)}, u32[]{:S(2)}) collective-permute-start(bf16[256,128]{1,0:T(8,128)(2,1)} %get-tuple-element.77), channel_id=1, source_target_pairs={{0,1},{1,2},{2,3},{3,0},{4,5},{5,6},{6,7},{7,4},{8,9},{9,10},{10,1... | collective-permute-start | bytes 196616 | tf_op jit(solution)/shard_map/ppermute | solution.py:473
  106.0 10.2 %collective-permute-start.20 = (bf16[256,128]{1,0:T(8,128)(2,1)}, bf16[256,128]{1,0:T(8,128)(2,1)S(1)}, u32[]{:S(2)}, u32[]{:S(2)}) collective-permute-start(bf16[256,128]{1,0:T(8,128)(2,1)} %get-tuple-element.77), channel_id=1, source_target_pairs={{0,2},{1,3},{2,0},{3,1},{4,6},{5,7},{6,4},{7,5},{8,10},{9,11},{10,... | collective-permute-start | bytes 196616 | tf_op jit(solution)/shard_map/ppermute | solution.py:473
  108.3 7.9 %collective-permute-start.21 = (bf16[256,128]{1,0:T(8,128)(2,1)}, bf16[256,128]{1,0:T(8,128)(2,1)S(1)}, u32[]{:S(2)}, u32[]{:S(2)}) collective-permute-start(bf16[256,128]{1,0:T(8,128)(2,1)} %get-tuple-element.77), channel_id=1, source_target_pairs={{0,3},{1,0},{2,1},{3,2},{4,7},{5,4},{6,5},{7,6},{8,11},{9,8},{10,9... | collective-permute-start | bytes 196616 | tf_op jit(solution)/shard_map/ppermute | solution.py:473
  114.3 1.9 %copy-start.3 = (bf16[512,1024]{1,0:T(8,128)(2,1)S(1)}, bf16[512,1024]{1,0:T(8,128)(2,1)}, u32[]{:S(2)}) copy-start(bf16[512,1024]{1,0:T(8,128)(2,1)} %pad_maximum_fusion.1) | copy-start | bytes 3145732
  114.4 1.9 %copy-start.8 = (bf16[4,64,1024]{2,1,0:T(8,128)(2,1)S(1)}, bf16[4,64,1024]{2,1,0:T(8,128)(2,1)}, u32[]{:S(2)}) copy-start(bf16[4,64,1024]{2,1,0:T(8,128)(2,1)} %get-tuple-element.73) | copy-start | bytes 1572868
  114.4 1.9 %copy-start.10 = (bf16[256,128]{1,0:T(8,128)(2,1)S(1)}, bf16[256,128]{1,0:T(8,128)(2,1)}, u32[]{:S(2)}) copy-start(bf16[256,128]{1,0:T(8,128)(2,1)} %get-tuple-element.77) | copy-start | bytes 196612
  116.8 1.3 copy-start.4
  121.0 8.3 %collective-permute-start.24 = (bf16[64,1024]{1,0:T(8,128)(2,1)}, bf16[64,1024]{1,0:T(8,128)(2,1)}, u32[]{:S(2)}, u32[]{:S(2)}) collective-permute-start(bf16[64,1024]{1,0:T(8,128)(2,1)} %get-tuple-element.98), channel_id=1, source_target_pairs={{0,3},{1,0},{2,1},{3,2},{4,7},{5,4},{6,5},{7,6},{8,11},{9,8},{10,9... | collective-permute-start | bytes 393224 | tf_op jit(solution)/shard_map/ppermute | solution.py:473
  121.0 19.1 %collective-permute-start.23 = (bf16[64,1024]{1,0:T(8,128)(2,1)}, bf16[64,1024]{1,0:T(8,128)(2,1)}, u32[]{:S(2)}, u32[]{:S(2)}) collective-permute-start(bf16[64,1024]{1,0:T(8,128)(2,1)} %get-tuple-element.99), channel_id=1, source_target_pairs={{0,2},{1,3},{2,0},{3,1},{4,6},{5,7},{6,4},{7,5},{8,10},{9,11},{10,... | collective-permute-start | bytes 393224 | tf_op jit(solution)/shard_map/ppermute | solution.py:473
  122.1 18.0 %collective-permute-start.22 = (bf16[64,1024]{1,0:T(8,128)(2,1)}, bf16[64,1024]{1,0:T(8,128)(2,1)}, u32[]{:S(2)}, u32[]{:S(2)}) collective-permute-start(bf16[64,1024]{1,0:T(8,128)(2,1)} %get-tuple-element.97), channel_id=1, source_target_pairs={{0,1},{1,2},{2,3},{3,0},{4,5},{5,6},{6,7},{7,4},{8,9},{9,10},{10,1... | collective-permute-start | bytes 393224 | tf_op jit(solution)/shard_map/ppermute | solution.py:473
  123.0 18.4 %collective-permute-start.18 = (bf16[64,1024]{1,0:T(8,128)(2,1)S(1)}, bf16[64,1024]{1,0:T(8,128)(2,1)S(1)}, u32[]{:S(2)}, u32[]{:S(2)}) collective-permute-start(bf16[64,1024]{1,0:T(8,128)(2,1)S(1)} %get-tuple-element.100), channel_id=1, source_target_pairs={{0,3},{1,0},{2,1},{3,2},{4,7},{5,4},{6,5},{7,6},{8,11},{9,8},{10,9... | collective-permute-start | bytes 393224 | tf_op jit(solution)/shard_map/ppermute | solution.py:473
  126.0 18.3 %collective-permute-start.17 = (bf16[64,1024]{1,0:T(8,128)(2,1)S(1)}, bf16[64,1024]{1,0:T(8,128)(2,1)S(1)}, u32[]{:S(2)}, u32[]{:S(2)}) collective-permute-start(bf16[64,1024]{1,0:T(8,128)(2,1)S(1)} %get-tuple-element.101), channel_id=1, source_target_pairs={{0,2},{1,3},{2,0},{3,1},{4,6},{5,7},{6,4},{7,5},{8,10},{9,11},{10,... | collective-permute-start | bytes 393224 | tf_op jit(solution)/shard_map/ppermute | solution.py:473
  129.3 15.0 %collective-permute-start.16 = (bf16[64,1024]{1,0:T(8,128)(2,1)S(1)}, bf16[64,1024]{1,0:T(8,128)(2,1)S(1)}, u32[]{:S(2)}, u32[]{:S(2)}) collective-permute-start(bf16[64,1024]{1,0:T(8,128)(2,1)S(1)} %get-tuple-element.102), channel_id=1, source_target_pairs={{0,1},{1,2},{2,3},{3,0},{4,5},{5,6},{6,7},{7,4},{8,9},{9,10},{10,1... | collective-permute-start | bytes 393224 | tf_op jit(solution)/shard_map/ppermute | solution.py:473

commit v11 on v9

--- a/solution.py
+++ b/solution.py
@@ -450,30 +450,26 @@
 
 
 def partial_kernel(n_chunk, n_block, *refs):
-    toks, refs = refs[:n_chunk], refs[n_chunk:]
     blocks, refs = refs[:n_block], refs[n_block:]
     w_ref, outs = refs[0], refs[1:]
     rows = outs[0].shape[0]
     for c in range(n_chunk):
         part = jnp.concatenate([b[c * rows : (c + 1) * rows, :] for b in blocks], axis=1)
-        outs[c][...] = toks[c][...].astype(F32) + jnp.dot(
-            part, w_ref[...], preferred_element_type=F32
-        )
-
-
-def partial(toks, blocks, weight):
-    n_chunk = len(toks)
+        outs[c][...] = jnp.dot(part, w_ref[...], preferred_element_type=F32)
+
+
+def partial(n_chunk, blocks, weight):
     vmem = pl.BlockSpec(memory_space=pltpu.VMEM)
-    out = jax.ShapeDtypeStruct(toks[0].shape, F32)
+    out = jax.ShapeDtypeStruct((blocks[0].shape[0] // n_chunk, weight.shape[1]), F32)
     return pl.pallas_call(
         functools.partial(partial_kernel, n_chunk, len(blocks)),
         out_shape=[out] * n_chunk,
-        in_specs=[vmem] * (n_chunk + len(blocks) + 1),
+        in_specs=[vmem] * (len(blocks) + 1),
         out_specs=[vmem] * n_chunk,
         compiler_params=pltpu.CompilerParams(vmem_limit_bytes=24 << 20),
         cost_estimate=LIGHT,
         name="partial",
-    )(*toks, *blocks, weight)
+    )(*blocks, weight)
 
 
 def shift(value, axis, n, k):
@@ -597,9 +593,7 @@
         w_whole = whole_weight(w_out, halves, dp, n_dp, n_group)
     last = attended(n_group - 1, query, True)
     early, last, w_whole = lax.optimization_barrier((early, last, w_whole))
-    bases = [tok.reshape(n_tp * sub, d_model) for tok in all_tokens]
-    for a in range(n_group - 1):
-        bases = partial(bases, early[a], w_whole[a])
+    bases = [partial(n_chunk, early[a], w_whole[a]) for a in range(n_group - 1)]
     outs = []
     pieces = None
     late = []
@@ -612,7 +606,10 @@
         blocks = late[c]
         if pieces is not None:
             blocks = lax.optimization_barrier((blocks, pieces))[0]
-        residual = bases[c].astype(F32) + mixed(blocks, n_group - 1)
+        residual = all_tokens[c].reshape(n_tp * sub, d_model).astype(F32)
+        for part in bases:
+            residual = residual + part[c]
+        residual = residual + mixed(blocks, n_group - 1)
         ffn_in = normalize(residual, ffn_gain).astype(BF)
         gate_up = jnp.einsum("td,kdf->ktf", ffn_in, w_gateup, preferred_element_type=F32)
         hidden = (jax.nn.silu(gate_up[0]) * gate_up[1]).astype(BF)

time: 138 us -> 138 us (level); the launches traced: 138 us -> 136 us
  local copies, waits for them, and re-layouts: 6.36 us -> 4.05 us
    unnamed x42 -> x38, local copies, waits for them, and re-layouts: 3.56 us -> 1.49 us
  transfers between devices with their start and end apart: 27 -> 27, of which waited for: 7 -> 7; matrix products, arithmetic and copies ran while one was open for 13% -> 13% of each run, Pallas kernels for 25% -> 26%
where the time goes in v11:
time: 138 us; the launch traced here: 136 us
  starting transfers between devices  50.2 us (36%)
  Pallas kernels  34.6 us (25%)
  waiting for transfers between devices  21 us (15%)
  blocking collectives  9.99 us (7%)
  other arithmetic  8.54 us (6%)
  matrix products  6.87 us (5%)
  local copies, waits for them, and re-layouts  4.05 us (3%)
    ppermute x24, starting transfers between devices, shift(): return lax.ppermute(value, axis, [(i, (i + k) % n) for i in range(n)])  41.3 us
    pallas_call x2, Pallas kernels, attend(): pl.pallas_call(functools.partial(attend_kernel, group, per, n_chunk), gri...  19.4 us
    ppermute x24, waiting for transfers between devices, shift(): return lax.ppermute(value, axis, [(i, (i + k) % n) for i in range(n)])  18.3 us
    all_gather x1, blocking collectives, per_device(): gathered = lax.all_gather(payload, 'dp', axis=0)  9.99 us
    all_to_all x2, starting transfers between devices, per_device(): lax.all_to_all(send, 'dp', split_axis=0, concat_axis=0, tiled=True)  8.85 us
    pallas_call x1, Pallas kernels, project(): pl.pallas_call(functools.partial(project_kernel, n_tp, cap, pool_dev, n_c...  6.57 us
    pallas_call x1, Pallas kernels, pick(): pl.pallas_call(functools.partial(pick_kernel, n_dp, cap), out_shape=[jax....  4.56 us
  transfers between devices with their start and end apart: 27, of which 7 were waited for; matrix products, arithmetic and copies ran while one was open for 13% of the time, Pallas kernels for 26%

profile of v11, /device:TPU:0, one launch (start us, length us, event | category | flops | bytes accessed | tf_op | source)
XLA Modules:
  0.0 135.5 jit_solution(12441556793649004136)
XLA Ops:
  0.0 3.0 %collective-permute-start = (bf16[128,1024]{1,0:T(8,128)(2,1)}, bf16[128,1024]{1,0:T(8,128)(2,1)S(1)}, u32[]{:S(2)}, u32[]{:S(2)}) collective-permute-start(bf16[128,1024]{1,0:T(8,128)(2,1)} %rest_5_.1), channel_id=1, source_target_pairs={{0,1},{1,2},{2,3},{3,0},{4,5},{5,6},{6,7},{7,4},{8,9},{9,10},{10,1... | collective-permute-start | bytes 786440 | tf_op jit(solution)/shard_map/ppermute | solution.py:476
  3.0 2.6 %collective-permute-start.1 = (bf16[128,1024]{1,0:T(8,128)(2,1)}, bf16[128,1024]{1,0:T(8,128)(2,1)S(1)}, u32[]{:S(2)}, u32[]{:S(2)}) collective-permute-start(bf16[128,1024]{1,0:T(8,128)(2,1)} %rest_5_.1), channel_id=1, source_target_pairs={{0,2},{1,3},{2,0},{3,1},{4,6},{5,7},{6,4},{7,5},{8,10},{9,11},{10,... | collective-permute-start | bytes 786440 | tf_op jit(solution)/shard_map/ppermute | solution.py:476
  5.6 0.7 fusion.55
  6.3 0.8 constant_dynamic-slice_fusion.1
  7.1 0.8 pad_maximum_fusion.4
  7.8 10.0 %all-gather = bf16[1152,256]{1,0:T(8,128)(2,1)S(1)} all-gather(bf16[144,256]{1,0:T(8,128)(2,1)S(1)} %pad_maximum_fusion.4), channel_id=2, replica_groups=mesh['dp'=8,'tensor'=4] {'dp'}, dimensions={0}, use_global_device_ids=true | all-gather | bytes 663552 | tf_op jit(solution)/shard_map/all_gather | solution.py:543
  17.8 0.6 slice_convert_fusion.asked_ref
  18.5 4.6 %pick_pages.1 = (bf16[8,4,128,2,128]{4,3,2,1,0:T(2,128)(2,1)}, bf16[8,4,128,2,128]{4,3,2,1,0:T(2,128)(2,1)}) custom-call(s32[1]{0:T(128)} %bitcast.4.me_ref, s32[8,2,32]{2,1,0:T(2,128)} %slice_convert_fusion.asked_ref, bf16[32,128,2,256]{3,2,1,0:T(2,128)(2,1)} %pool_ref.1), custom_call_target="tpu_custom_call" | custom-call | flops 1000 | bytes 1000 | tf_op jit(solution)/shard_map/pick_pages/pallas_call | solution.py:82
  23.1 0.7 copy-done.9
  23.8 0.7 copy-done.10
  24.5 4.5 %all-to-all-start = ((bf16[8,4,128,2,128]{4,3,2,1,0:T(2,128)(2,1)}), bf16[8,4,128,2,128]{4,3,2,1,0:T(2,128)(2,1)}, u32[]{:S(2)}, u32[]{:S(2)}) async-start(bf16[8,4,128,2,128]{4,3,2,1,0:T(2,128)(2,1)} %get-tuple-element.45), calls=%async_computation | async-start | bytes 4194304 | tf_op jit(solution)/shard_map/all_to_all | solution.py:547
  29.0 1.4 %collective-permute-start.2 = (bf16[128,1024]{1,0:T(8,128)(2,1)S(1)}, bf16[128,1024]{1,0:T(8,128)(2,1)}, u32[]{:S(2)}, u32[]{:S(2)}) collective-permute-start(bf16[128,1024]{1,0:T(8,128)(2,1)S(1)} %copy-done.8), channel_id=1, source_target_pairs={{0,3},{1,0},{2,1},{3,2},{4,7},{5,4},{6,5},{7,6},{8,11},{9,8},{10,9... | collective-permute-start | bytes 786440 | tf_op jit(solution)/shard_map/ppermute | solution.py:476
  30.4 0.6 reshape.112.rest_0_
  31.0 0.8 fusion.62
  31.8 2.2 %named_adapters.1 = (bf16[128,256]{1,0:T(8,128)(2,1)}, bf16[128,256]{1,0:T(8,128)(2,1)}) custom-call(s32[16]{0:T(128)} %table_ref.2, s32[1,4]{1,0:T(1,128)} %ids_ref.1, bf16[8,144,256]{2,1,0:T(8,128)(2,1)} %bitcast.103), custom_call_target="tpu_custom_call" | custom-call | flops 1000 | bytes 1000 | tf_op jit(solution)/shard_map/named_adapters/pallas_call | solution.py:126
  34.0 0.7 collective-permute-start.3
  34.8 0.3 collective-permute-start.4
  35.1 2.8 %collective-permute-start.5 = (bf16[128,256]{1,0:T(8,128)(2,1)}, bf16[128,256]{1,0:T(8,128)(2,1)S(1)}, u32[]{:S(2)}, u32[]{:S(2)}) collective-permute-start(bf16[128,256]{1,0:T(8,128)(2,1)} %get-tuple-element.49.rest_9_), channel_id=1, source_target_pairs={{0,3},{1,0},{2,1},{3,2},{4,7},{5,4},{6,5},{7,6},{8,11},{9,8},{10,9... | collective-permute-start | bytes 196616 | tf_op jit(solution)/shard_map/ppermute | solution.py:476
  37.9 0.2 reduce-window.4
  38.1 0.1 convert_reduce_fusion
  38.2 0.1 select_reduce_fusion.1
  38.3 2.8 %collective-permute-done.3.rest_10_ = bf16[128,256]{1,0:T(8,128)(2,1)S(1)} collective-permute-done((bf16[128,256]{1,0:T(8,128)(2,1)}, bf16[128,256]{1,0:T(8,128)(2,1)S(1)}, u32[]{:S(2)}, u32[]{:S(2)}) %collective-permute-start.3) | collective-permute-done | bytes 65568 | tf_op jit(solution)/shard_map/ppermute | solution.py:476
  41.1 2.0 %collective-permute-done.4.rest_11_ = bf16[128,256]{1,0:T(8,128)(2,1)S(1)} collective-permute-done((bf16[128,256]{1,0:T(8,128)(2,1)}, bf16[128,256]{1,0:T(8,128)(2,1)S(1)}, u32[]{:S(2)}, u32[]{:S(2)}) %collective-permute-start.4) | collective-permute-done | bytes 65568 | tf_op jit(solution)/shard_map/ppermute | solution.py:476
  43.1 1.3 collective-permute-start.6
  44.5 1.8 %fusion.16 = (f32[512,128]{1,0:T(8,128)}, f32[512,128]{1,0:T(8,128)}) fusion(f32[128]{0:T(128)S(1)} %get-tuple-element.120, f32[128]{0:T(128)S(1)} %get-tuple-element.121, f32[512]{0:T(512)S(1)} %fusion.49), kind=kLoop, calls=%fused_computation.29 | loop fusion | flops 131072 | bytes 527360 | tf_op jit(solution)/shard_map/mul | solution.py:561
  46.3 6.6 %project.1 = (bf16[512,256]{1,0:T(8,128)(2,1)}, bf16[512,256]{1,0:T(8,128)(2,1)}, bf16[512,256]{1,0:T(8,128)(2,1)}, s32[32]{0:T(128)}, bf16[4,64,1024]{2,1,0:T(8,128)(2,1)}, /*index=5*/bf16[4,64,1024]{2,1,0:T(8,128)(2,1)}) custom-call(s32[1]{0:T(128)} %bitcast.tp_ref, s32[1,4]{1,0:T(1,128)} %lens_ref.5, s32[1,32]{1,0:T(1,128)} %table_ref.3, ...), custom_call_target="tpu_custom_call" | custom-call | flops 1000 | bytes 1000 | tf_op jit(solution)/shard_map/project/pallas_call | solution.py:250
  52.9 0.1 collective-permute-done.6
  53.0 2.7 %all-to-all-done = bf16[8,4,128,2,128]{4,3,2,1,0:T(2,128)(2,1)} async-done(((bf16[8,4,128,2,128]{4,3,2,1,0:T(2,128)(2,1)}), bf16[8,4,128,2,128]{4,3,2,1,0:T(2,128)(2,1)}, u32[]{:S(2)}, u32[]{:S(2)}) %all-to-all-start) | async-done | bytes 2097184 | tf_op jit(solution)/shard_map/all_to_all | solution.py:547
  55.6 4.4 %all-to-all-start.1 = ((bf16[8,4,128,2,128]{4,3,2,1,0:T(2,128)(2,1)}), bf16[8,4,128,2,128]{4,3,2,1,0:T(2,128)(2,1)}, u32[]{:S(2)}, u32[]{:S(2)}) async-start(bf16[8,4,128,2,128]{4,3,2,1,0:T(2,128)(2,1)} %get-tuple-element.62), calls=%async_computation.1 | async-start | bytes 4194304 | tf_op jit(solution)/shard_map/all_to_all | solution.py:567
  60.0 0.4 collective-permute-start.7
  60.4 2.2 %collective-permute-start.8 = (bf16[128,1024]{1,0:T(8,128)(2,1)S(1)}, bf16[128,1024]{1,0:T(8,128)(2,1)S(1)}, u32[]{:S(2)}, u32[]{:S(2)}) collective-permute-start(bf16[128,1024]{1,0:T(8,128)(2,1)S(1)} %get-tuple-element.55), channel_id=1, source_target_pairs={{0,3},{1,0},{2,1},{3,2},{4,7},{5,4},{6,5},{7,6},{8,11},{9,8},{10,9... | collective-permute-start | bytes 786440 | tf_op jit(solution)/shard_map/ppermute | solution.py:476
  62.7 9.7 %attend.2.refs_0_ = bf16[512,128]{1,0:T(8,128)(2,1)} custom-call(s32[1,4]{1,0:T(1,128)} %lens_ref.5, s32[1,4]{1,0:T(1,128)} %counts_ref.3, s32[32]{0:T(128)} %get-tuple-element.51.pos_ref, f32[2,4]{1,0:T(2,128)} %bias_ref.3, bf16[512,256]{1,0:T(8,128)(2,1)} %get-tuple-element.60.q_ref, bf16[512,256]{1,0:T(8,128)(2,1)} %get-tuple-element.53.kn_ref, ...), custom_call_target="tpu_custom_call" | custom-call | flops 1000 | bytes 1000 | tf_op jit(solution)/shard_map/attend/pallas_call | solution.py:427
  72.4 2.5 %collective-permute-done.7 = bf16[128,1024]{1,0:T(8,128)(2,1)S(1)} collective-permute-done((bf16[128,1024]{1,0:T(8,128)(2,1)S(1)}, bf16[128,1024]{1,0:T(8,128)(2,1)S(1)}, u32[]{:S(2)}, u32[]{:S(2)}) %collective-permute-start.7) | collective-permute-done | bytes 262176 | tf_op jit(solution)/shard_map/ppermute | solution.py:476
  74.8 1.0 pad_maximum_fusion.2
  75.8 5.2 %collective-permute-start.10 = (bf16[512,128]{1,0:T(8,128)(2,1)}, bf16[512,128]{1,0:T(8,128)(2,1)S(1)}, u32[]{:S(2)}, u32[]{:S(2)}) collective-permute-start(bf16[512,128]{1,0:T(8,128)(2,1)} %attend.2.refs_0_), channel_id=1, source_target_pairs={{0,2},{1,3},{2,0},{3,1},{4,6},{5,7},{6,4},{7,5},{8,10},{9,11},{10,... | collective-permute-start | bytes 393224 | tf_op jit(solution)/shard_map/ppermute | solution.py:476
  81.0 3.5 %collective-permute-start.11 = (bf16[512,128]{1,0:T(8,128)(2,1)}, bf16[512,128]{1,0:T(8,128)(2,1)S(1)}, u32[]{:S(2)}, u32[]{:S(2)}) collective-permute-start(bf16[512,128]{1,0:T(8,128)(2,1)} %attend.2.refs_0_), channel_id=1, source_target_pairs={{0,3},{1,0},{2,1},{3,2},{4,7},{5,4},{6,5},{7,6},{8,11},{9,8},{10,9... | collective-permute-start | bytes 393224 | tf_op jit(solution)/shard_map/ppermute | solution.py:476
  84.5 1.2 broadcast_select_fusion.2
  85.7 1.1 pad_maximum_fusion.1
  86.8 0.1 pad_maximum_fusion.refs_4_
  86.9 9.7 %attend.3 = (bf16[256,128]{1,0:T(8,128)(2,1)}, bf16[256,128]{1,0:T(8,128)(2,1)}) custom-call(s32[1,4]{1,0:T(1,128)} %lens_ref.5, s32[1,4]{1,0:T(1,128)} %counts_ref.3, s32[32]{0:T(128)} %get-tuple-element.51.pos_ref, f32[2,4]{1,0:T(2,128)} %bias_ref.3, bf16[512,256]{1,0:T(8,128)(2,1)} %get-tuple-element.60.q_ref, bf16[512,256]{1,0:T(8,128)(2,1)} %get-tuple-element.53.kn_ref, ...), custom_call_target="tpu_custom_call" | custom-call | flops 1000 | bytes 1000 | tf_op jit(solution)/shard_map/attend/pallas_call | solution.py:427
  96.6 1.3 collective-permute-start.13
  97.9 3.1 %collective-permute-start.14 = (bf16[256,128]{1,0:T(8,128)(2,1)}, bf16[256,128]{1,0:T(8,128)(2,1)}, u32[]{:S(2)}, u32[]{:S(2)}) collective-permute-start(bf16[256,128]{1,0:T(8,128)(2,1)} %get-tuple-element.73), channel_id=1, source_target_pairs={{0,2},{1,3},{2,0},{3,1},{4,6},{5,7},{6,4},{7,5},{8,10},{9,11},{10,... | collective-permute-start | bytes 196616 | tf_op jit(solution)/shard_map/ppermute | solution.py:476
  101.1 1.8 %partial.1 = (f32[256,1024]{1,0:T(8,128)S(1)}, f32[256,1024]{1,0:T(8,128)S(1)}) custom-call(bf16[512,128]{1,0:T(8,128)(2,1)S(1)} %copy-done.1, bf16[512,128]{1,0:T(8,128)(2,1)} %collective-permute-done.9.refs_1_, bf16[512,128]{1,0:T(8,128)(2,1)S(1)} %collective-permute-done.10.refs_2_, bf16[512,128]{1,0:T(8,128)(2,1)S(1)} %collective-permute-done.11.refs_3_, ...), custom_call_target="tpu_custom_call" | custom-call | flops 1000 | bytes 1000 | tf_op jit(solution)/shard_map/partial/pallas_call | solution.py:464
  102.8 2.0 %collective-permute-start.19 = (bf16[256,128]{1,0:T(8,128)(2,1)}, bf16[256,128]{1,0:T(8,128)(2,1)S(1)}, u32[]{:S(2)}, u32[]{:S(2)}) collective-permute-start(bf16[256,128]{1,0:T(8,128)(2,1)} %get-tuple-element.79), channel_id=1, source_target_pairs={{0,1},{1,2},{2,3},{3,0},{4,5},{5,6},{6,7},{7,4},{8,9},{9,10},{10,1... | collective-permute-start | bytes 196616 | tf_op jit(solution)/shard_map/ppermute | solution.py:476
  104.9 2.4 %collective-permute-start.21 = (bf16[256,128]{1,0:T(8,128)(2,1)}, bf16[256,128]{1,0:T(8,128)(2,1)S(1)}, u32[]{:S(2)}, u32[]{:S(2)}) collective-permute-start(bf16[256,128]{1,0:T(8,128)(2,1)} %get-tuple-element.79), channel_id=1, source_target_pairs={{0,3},{1,0},{2,1},{3,2},{4,7},{5,4},{6,5},{7,6},{8,11},{9,8},{10,9... | collective-permute-start | bytes 196616 | tf_op jit(solution)/shard_map/ppermute | solution.py:476
  107.3 2.0 %multiply_reduce_fusion.1 = (f32[256]{0:T(256)S(1)}, f32[256,1024]{1,0:T(8,128)S(1)}) fusion(bf16[512,1024]{1,0:T(8,128)(2,1)} %pad_maximum_fusion.1, bf16[256,128]{1,0:T(8,128)(2,1)} %collective-permute-done.15, bf16[256,128]{1,0:T(8,128)(2,1)} %collective-permute-done.14, bf16[256,128]{1,0:T(8,128)(2,1)} %collective-permute-done.13, ...), kind=kOutput, calls=%fused_computation.17 | convolution fusion | flops 270794496 | bytes 3933184 | tf_op jit(solution)/shard_map/dot_general | solution.py:572
  109.4 1.3 convolution_bitcast_fusion.1
  110.7 0.2 fusion.61
  111.0 0.8 fusion.63
  111.9 1.5 %collective-permute-start.16 = (bf16[64,1024]{1,0:T(8,128)(2,1)S(1)}, bf16[64,1024]{1,0:T(8,128)(2,1)S(1)}, u32[]{:S(2)}, u32[]{:S(2)}) collective-permute-start(bf16[64,1024]{1,0:T(8,128)(2,1)S(1)} %get-tuple-element.104), channel_id=1, source_target_pairs={{0,1},{1,2},{2,3},{3,0},{4,5},{5,6},{6,7},{7,4},{8,9},{9,10},{10,1... | collective-permute-start | bytes 393224 | tf_op jit(solution)/shard_map/ppermute | solution.py:476
  113.4 1.0 collective-permute-start.17
  114.4 1.8 %collective-permute-start.18 = (bf16[64,1024]{1,0:T(8,128)(2,1)S(1)}, bf16[64,1024]{1,0:T(8,128)(2,1)S(1)}, u32[]{:S(2)}, u32[]{:S(2)}) collective-permute-start(bf16[64,1024]{1,0:T(8,128)(2,1)S(1)} %get-tuple-element.102), channel_id=1, source_target_pairs={{0,3},{1,0},{2,1},{3,2},{4,7},{5,4},{6,5},{7,6},{8,11},{9,8},{10,9... | collective-permute-start | bytes 393224 | tf_op jit(solution)/shard_map/ppermute | solution.py:476
  116.3 0.5 multiply_reduce_fusion
  116.9 1.3 convolution_bitcast_fusion
  118.2 0.1 fusion.60
  118.3 0.8 fusion.64
  119.2 0.3 collective-permute-start.22
  119.5 1.9 %collective-permute-start.23 = (bf16[64,1024]{1,0:T(8,128)(2,1)S(1)}, bf16[64,1024]{1,0:T(8,128)(2,1)S(1)}, u32[]{:S(2)}, u32[]{:S(2)}) collective-permute-start(bf16[64,1024]{1,0:T(8,128)(2,1)S(1)} %get-tuple-element.101), channel_id=1, source_target_pairs={{0,2},{1,3},{2,0},{3,1},{4,6},{5,7},{6,4},{7,5},{8,10},{9,11},{10,... | collective-permute-start | bytes 393224 | tf_op jit(solution)/shard_map/ppermute | solution.py:476
  121.4 2.3 %collective-permute-start.24 = (bf16[64,1024]{1,0:T(8,128)(2,1)S(1)}, bf16[64,1024]{1,0:T(8,128)(2,1)S(1)}, u32[]{:S(2)}, u32[]{:S(2)}) collective-permute-start(bf16[64,1024]{1,0:T(8,128)(2,1)S(1)} %get-tuple-element.100), channel_id=1, source_target_pairs={{0,3},{1,0},{2,1},{3,2},{4,7},{5,4},{6,5},{7,6},{8,11},{9,8},{10,9... | collective-permute-start | bytes 393224 | tf_op jit(solution)/shard_map/ppermute | solution.py:476
  123.7 4.2 %collective-permute-done.17 = bf16[64,1024]{1,0:T(8,128)(2,1)S(1)} collective-permute-done((bf16[64,1024]{1,0:T(8,128)(2,1)S(1)}, bf16[64,1024]{1,0:T(8,128)(2,1)S(1)}, u32[]{:S(2)}, u32[]{:S(2)}) %collective-permute-start.17) | collective-permute-done | bytes 131104 | tf_op jit(solution)/shard_map/ppermute | solution.py:476
  127.9 0.1 fusion.42
  128.0 6.8 %collective-permute-done.23 = bf16[64,1024]{1,0:T(8,128)(2,1)S(1)} collective-permute-done((bf16[64,1024]{1,0:T(8,128)(2,1)S(1)}, bf16[64,1024]{1,0:T(8,128)(2,1)S(1)}, u32[]{:S(2)}, u32[]{:S(2)}) %collective-permute-start.23) | collective-permute-done | bytes 131104 | tf_op jit(solution)/shard_map/ppermute | solution.py:476
  134.7 0.1 fusion.39
  134.8 0.7 pad_maximum_fusion.3
  (69 shorter events, 0.3 us)
Async XLA Ops:
  0.0 111.0 %copy-start = (bf16[1024,1024]{1,0:T(8,128)(2,1)S(1)}, bf16[1024,1024]{1,0:T(8,128)(2,1)}, u32[]{:S(2)}) copy-start(bf16[1024,1024]{1,0:T(8,128)(2,1)} %param.22) | copy-start | bytes 6291460
  0.0 23.0 %collective-permute-start = (bf16[128,1024]{1,0:T(8,128)(2,1)}, bf16[128,1024]{1,0:T(8,128)(2,1)S(1)}, u32[]{:S(2)}, u32[]{:S(2)}) collective-permute-start(bf16[128,1024]{1,0:T(8,128)(2,1)} %rest_5_.1), channel_id=1, source_target_pairs={{0,1},{1,2},{2,3},{3,0},{4,5},{5,6},{6,7},{7,4},{8,9},{9,10},{10,1... | collective-permute-start | bytes 786440 | tf_op jit(solution)/shard_map/ppermute | solution.py:476
  3.0 20.0 %collective-permute-start.1 = (bf16[128,1024]{1,0:T(8,128)(2,1)}, bf16[128,1024]{1,0:T(8,128)(2,1)S(1)}, u32[]{:S(2)}, u32[]{:S(2)}) collective-permute-start(bf16[128,1024]{1,0:T(8,128)(2,1)} %rest_5_.1), channel_id=1, source_target_pairs={{0,2},{1,3},{2,0},{3,1},{4,6},{5,7},{6,4},{7,5},{8,10},{9,11},{10,... | collective-permute-start | bytes 786440 | tf_op jit(solution)/shard_map/ppermute | solution.py:476
  17.8 5.2 %copy-start.4 = (bf16[1152,256]{1,0:T(8,128)(2,1)}, bf16[1152,256]{1,0:T(8,128)(2,1)S(1)}, u32[]{:S(2)}) copy-start(bf16[1152,256]{1,0:T(8,128)(2,1)S(1)} %all-gather) | copy-start | bytes 1769476
  23.0 0.7 copy-start.9
  23.8 0.7 copy-start.10
  24.5 4.5 %copy-start.8 = (bf16[128,1024]{1,0:T(8,128)(2,1)S(1)}, bf16[128,1024]{1,0:T(8,128)(2,1)}, u32[]{:S(2)}) copy-start(bf16[128,1024]{1,0:T(8,128)(2,1)} %rest_5_.1) | copy-start | bytes 786436
  24.5 5.9 %copy-start.17 = (bf16[1024]{0:T(1024)(128)(2,1)S(1)}, bf16[1024]{0:T(1024)(128)(2,1)}, u32[]{:S(2)}) copy-start(bf16[1024]{0:T(1024)(128)(2,1)} %param.17) | copy-start | bytes 6148
  24.5 6.5 %copy-start.5 = (bf16[256,1024]{1,0:T(8,128)(2,1)S(1)}, bf16[256,1024]{1,0:T(8,128)(2,1)}, u32[]{:S(2)}) copy-start(bf16[256,1024]{1,0:T(8,128)(2,1)} %param.20) | copy-start | bytes 1572868
  24.5 31.1 %all-to-all-start = ((bf16[8,4,128,2,128]{4,3,2,1,0:T(2,128)(2,1)}), bf16[8,4,128,2,128]{4,3,2,1,0:T(2,128)(2,1)}, u32[]{:S(2)}, u32[]{:S(2)}) async-start(bf16[8,4,128,2,128]{4,3,2,1,0:T(2,128)(2,1)} %get-tuple-element.45), calls=%async_computation | async-start | bytes 4194304 | tf_op jit(solution)/shard_map/all_to_all | solution.py:547
  29.0 8.9 %copy-start.16 = (s32[1,4]{1,0:T(1,128)S(1)}, s32[1,4]{1,0:T(1,128)}, u32[]{:S(2)}) copy-start(s32[1,4]{1,0:T(1,128)} %lens_ref.5) | copy-start | bytes 52
  29.0 9.2 %copy-start.15 = (s32[1,4]{1,0:T(1,128)S(1)}, s32[1,4]{1,0:T(1,128)}, u32[]{:S(2)}) copy-start(s32[1,4]{1,0:T(1,128)} %counts_ref.3) | copy-start | bytes 52
  29.0 17.3 %collective-permute-start.2 = (bf16[128,1024]{1,0:T(8,128)(2,1)S(1)}, bf16[128,1024]{1,0:T(8,128)(2,1)}, u32[]{:S(2)}, u32[]{:S(2)}) collective-permute-start(bf16[128,1024]{1,0:T(8,128)(2,1)S(1)} %copy-done.8), channel_id=1, source_target_pairs={{0,3},{1,0},{2,1},{3,2},{4,7},{5,4},{6,5},{7,6},{8,11},{9,8},{10,9... | collective-permute-start | bytes 786440 | tf_op jit(solution)/shard_map/ppermute | solution.py:476
  34.0 7.1 %collective-permute-start.3 = (bf16[128,256]{1,0:T(8,128)(2,1)}, bf16[128,256]{1,0:T(8,128)(2,1)S(1)}, u32[]{:S(2)}, u32[]{:S(2)}) collective-permute-start(bf16[128,256]{1,0:T(8,128)(2,1)} %get-tuple-element.49.rest_9_), channel_id=1, source_target_pairs={{0,1},{1,2},{2,3},{3,0},{4,5},{5,6},{6,7},{7,4},{8,9},{9,10},{10,1... | collective-permute-start | bytes 196616 | tf_op jit(solution)/shard_map/ppermute | solution.py:476
  34.8 8.3 %collective-permute-start.4 = (bf16[128,256]{1,0:T(8,128)(2,1)}, bf16[128,256]{1,0:T(8,128)(2,1)S(1)}, u32[]{:S(2)}, u32[]{:S(2)}) collective-permute-start(bf16[128,256]{1,0:T(8,128)(2,1)} %get-tuple-element.49.rest_9_), channel_id=1, source_target_pairs={{0,2},{1,3},{2,0},{3,1},{4,6},{5,7},{6,4},{7,5},{8,10},{9,11},{10,... | collective-permute-start | bytes 196616 | tf_op jit(solution)/shard_map/ppermute | solution.py:476
  35.1 8.0 %collective-permute-start.5 = (bf16[128,256]{1,0:T(8,128)(2,1)}, bf16[128,256]{1,0:T(8,128)(2,1)S(1)}, u32[]{:S(2)}, u32[]{:S(2)}) collective-permute-start(bf16[128,256]{1,0:T(8,128)(2,1)} %get-tuple-element.49.rest_9_), channel_id=1, source_target_pairs={{0,3},{1,0},{2,1},{3,2},{4,7},{5,4},{6,5},{7,6},{8,11},{9,8},{10,9... | collective-permute-start | bytes 196616 | tf_op jit(solution)/shard_map/ppermute | solution.py:476
  41.1 5.2 %copy-start.12 = (bf16[128,256]{1,0:T(8,128)(2,1)}, bf16[128,256]{1,0:T(8,128)(2,1)S(1)}, u32[]{:S(2)}) copy-start(bf16[128,256]{1,0:T(8,128)(2,1)S(1)} %collective-permute-done.3.rest_10_) | copy-start | bytes 196612
  43.1 3.2 %copy-start.13 = (bf16[128,256]{1,0:T(8,128)(2,1)}, bf16[128,256]{1,0:T(8,128)(2,1)S(1)}, u32[]{:S(2)}) copy-start(bf16[128,256]{1,0:T(8,128)(2,1)S(1)} %collective-permute-done.4.rest_11_) | copy-start | bytes 196612
  43.1 3.2 %copy-start.14 = (bf16[128,256]{1,0:T(8,128)(2,1)}, bf16[128,256]{1,0:T(8,128)(2,1)S(1)}, u32[]{:S(2)}) copy-start(bf16[128,256]{1,0:T(8,128)(2,1)S(1)} %collective-permute-done.5.rest_12_) | copy-start | bytes 196612
  43.1 9.8 %collective-permute-start.6 = (bf16[128,1024]{1,0:T(8,128)(2,1)S(1)}, bf16[128,1024]{1,0:T(8,128)(2,1)S(1)}, u32[]{:S(2)}, u32[]{:S(2)}) collective-permute-start(bf16[128,1024]{1,0:T(8,128)(2,1)S(1)} %get-tuple-element.55), channel_id=1, source_target_pairs={{0,1},{1,2},{2,3},{3,0},{4,5},{5,6},{6,7},{7,4},{8,9},{9,10},{10,1... | collective-permute-start | bytes 786440 | tf_op jit(solution)/shard_map/ppermute | solution.py:476
  55.6 31.2 %all-to-all-start.1 = ((bf16[8,4,128,2,128]{4,3,2,1,0:T(2,128)(2,1)}), bf16[8,4,128,2,128]{4,3,2,1,0:T(2,128)(2,1)}, u32[]{:S(2)}, u32[]{:S(2)}) async-start(bf16[8,4,128,2,128]{4,3,2,1,0:T(2,128)(2,1)} %get-tuple-element.62), calls=%async_computation.1 | async-start | bytes 4194304 | tf_op jit(solution)/shard_map/all_to_all | solution.py:567
  60.0 14.8 %collective-permute-start.7 = (bf16[128,1024]{1,0:T(8,128)(2,1)S(1)}, bf16[128,1024]{1,0:T(8,128)(2,1)S(1)}, u32[]{:S(2)}, u32[]{:S(2)}) collective-permute-start(bf16[128,1024]{1,0:T(8,128)(2,1)S(1)} %get-tuple-element.55), channel_id=1, source_target_pairs={{0,2},{1,3},{2,0},{3,1},{4,6},{5,7},{6,4},{7,5},{8,10},{9,11},{10,... | collective-permute-start | bytes 786440 | tf_op jit(solution)/shard_map/ppermute | solution.py:476
  60.4 14.4 %collective-permute-start.8 = (bf16[128,1024]{1,0:T(8,128)(2,1)S(1)}, bf16[128,1024]{1,0:T(8,128)(2,1)S(1)}, u32[]{:S(2)}, u32[]{:S(2)}) collective-permute-start(bf16[128,1024]{1,0:T(8,128)(2,1)S(1)} %get-tuple-element.55), channel_id=1, source_target_pairs={{0,3},{1,0},{2,1},{3,2},{4,7},{5,4},{6,5},{7,6},{8,11},{9,8},{10,9... | collective-permute-start | bytes 786440 | tf_op jit(solution)/shard_map/ppermute | solution.py:476
  75.8 8.7 %collective-permute-start.12 = (bf16[3,128,1024]{2,1,0:T(8,128)(2,1)}, bf16[3,128,1024]{2,1,0:T(8,128)(2,1)}, u32[]{:S(2)}, u32[]{:S(2)}) collective-permute-start(bf16[3,128,1024]{2,1,0:T(8,128)(2,1)} %pad_maximum_fusion.2), channel_id=1, source_target_pairs={{0,4},{4,0},{8,12},{12,8},{16,20},{20,16},{24,28},{28,24},{1,5},{5... | collective-permute-start | bytes 2359304 | tf_op jit(solution)/shard_map/ppermute | solution.py:480
  75.8 10.9 %copy-start.6 = (bf16[128,1024]{1,0:T(8,128)(2,1)S(1)}, bf16[128,1024]{1,0:T(8,128)(2,1)}, u32[]{:S(2)}) copy-start(bf16[128,1024]{1,0:T(8,128)(2,1)} %get-tuple-element.107) | copy-start | bytes 786436
  75.8 20.7 %collective-permute-start.10 = (bf16[512,128]{1,0:T(8,128)(2,1)}, bf16[512,128]{1,0:T(8,128)(2,1)S(1)}, u32[]{:S(2)}, u32[]{:S(2)}) collective-permute-start(bf16[512,128]{1,0:T(8,128)(2,1)} %attend.2.refs_0_), channel_id=1, source_target_pairs={{0,2},{1,3},{2,0},{3,1},{4,6},{5,7},{6,4},{7,5},{8,10},{9,11},{10,... | collective-permute-start | bytes 393224 | tf_op jit(solution)/shard_map/ppermute | solution.py:476
  81.0 15.6 %collective-permute-start.11 = (bf16[512,128]{1,0:T(8,128)(2,1)}, bf16[512,128]{1,0:T(8,128)(2,1)S(1)}, u32[]{:S(2)}, u32[]{:S(2)}) collective-permute-start(bf16[512,128]{1,0:T(8,128)(2,1)} %attend.2.refs_0_), channel_id=1, source_target_pairs={{0,3},{1,0},{2,1},{3,2},{4,7},{5,4},{6,5},{7,6},{8,11},{9,8},{10,9... | collective-permute-start | bytes 393224 | tf_op jit(solution)/shard_map/ppermute | solution.py:476
  84.5 12.1 %collective-permute-start.9 = (bf16[512,128]{1,0:T(8,128)(2,1)}, bf16[512,128]{1,0:T(8,128)(2,1)}, u32[]{:S(2)}, u32[]{:S(2)}) collective-permute-start(bf16[512,128]{1,0:T(8,128)(2,1)} %attend.2.refs_0_), channel_id=1, source_target_pairs={{0,1},{1,2},{2,3},{3,0},{4,5},{5,6},{6,7},{7,4},{8,9},{9,10},{10,1... | collective-permute-start | bytes 393224 | tf_op jit(solution)/shard_map/ppermute | solution.py:476
  86.8 14.3 %copy-start.18 = (bf16[1024]{0:T(1024)(128)(2,1)S(1)}, bf16[1024]{0:T(1024)(128)(2,1)}, u32[]{:S(2)}) copy-start(bf16[1024]{0:T(1024)(128)(2,1)} %param.18) | copy-start | bytes 6148
  86.8 14.3 %copy-start.1 = (bf16[512,128]{1,0:T(8,128)(2,1)S(1)}, bf16[512,128]{1,0:T(8,128)(2,1)}, u32[]{:S(2)}) copy-start(bf16[512,128]{1,0:T(8,128)(2,1)} %attend.2.refs_0_) | copy-start | bytes 393220
  96.6 8.3 %collective-permute-start.13 = (bf16[256,128]{1,0:T(8,128)(2,1)}, bf16[256,128]{1,0:T(8,128)(2,1)}, u32[]{:S(2)}, u32[]{:S(2)}) collective-permute-start(bf16[256,128]{1,0:T(8,128)(2,1)} %get-tuple-element.73), channel_id=1, source_target_pairs={{0,1},{1,2},{2,3},{3,0},{4,5},{5,6},{6,7},{7,4},{8,9},{9,10},{10,1... | collective-permute-start | bytes 196616 | tf_op jit(solution)/shard_map/ppermute | solution.py:476
  97.9 9.5 %collective-permute-start.14 = (bf16[256,128]{1,0:T(8,128)(2,1)}, bf16[256,128]{1,0:T(8,128)(2,1)}, u32[]{:S(2)}, u32[]{:S(2)}) collective-permute-start(bf16[256,128]{1,0:T(8,128)(2,1)} %get-tuple-element.73), channel_id=1, source_target_pairs={{0,2},{1,3},{2,0},{3,1},{4,6},{5,7},{6,4},{7,5},{8,10},{9,11},{10,... | collective-permute-start | bytes 196616 | tf_op jit(solution)/shard_map/ppermute | solution.py:476
  101.0 6.3 %collective-permute-start.15 = (bf16[256,128]{1,0:T(8,128)(2,1)}, bf16[256,128]{1,0:T(8,128)(2,1)}, u32[]{:S(2)}, u32[]{:S(2)}) collective-permute-start(bf16[256,128]{1,0:T(8,128)(2,1)} %get-tuple-element.73), channel_id=1, source_target_pairs={{0,3},{1,0},{2,1},{3,2},{4,7},{5,4},{6,5},{7,6},{8,11},{9,8},{10,9... | collective-permute-start | bytes 196616 | tf_op jit(solution)/shard_map/ppermute | solution.py:476
  101.1 8.3 %copy-start.2 = (bf16[2,1024,1024]{2,1,0:T(8,128)(2,1)S(1)}, bf16[2,1024,1024]{2,1,0:T(8,128)(2,1)}, u32[]{:S(2)}) copy-start(bf16[2,1024,1024]{2,1,0:T(8,128)(2,1)} %param.21) | copy-start | bytes 12582916
  102.8 11.6 %collective-permute-start.19 = (bf16[256,128]{1,0:T(8,128)(2,1)}, bf16[256,128]{1,0:T(8,128)(2,1)S(1)}, u32[]{:S(2)}, u32[]{:S(2)}) collective-permute-start(bf16[256,128]{1,0:T(8,128)(2,1)} %get-tuple-element.79), channel_id=1, source_target_pairs={{0,1},{1,2},{2,3},{3,0},{4,5},{5,6},{6,7},{7,4},{8,9},{9,10},{10,1... | collective-permute-start | bytes 196616 | tf_op jit(solution)/shard_map/ppermute | solution.py:476
  104.9 11.4 %collective-permute-start.20 = (bf16[256,128]{1,0:T(8,128)(2,1)}, bf16[256,128]{1,0:T(8,128)(2,1)S(1)}, u32[]{:S(2)}, u32[]{:S(2)}) collective-permute-start(bf16[256,128]{1,0:T(8,128)(2,1)} %get-tuple-element.79), channel_id=1, source_target_pairs={{0,2},{1,3},{2,0},{3,1},{4,6},{5,7},{6,4},{7,5},{8,10},{9,11},{10,... | collective-permute-start | bytes 196616 | tf_op jit(solution)/shard_map/ppermute | solution.py:476
  104.9 11.4 %collective-permute-start.21 = (bf16[256,128]{1,0:T(8,128)(2,1)}, bf16[256,128]{1,0:T(8,128)(2,1)S(1)}, u32[]{:S(2)}, u32[]{:S(2)}) collective-permute-start(bf16[256,128]{1,0:T(8,128)(2,1)} %get-tuple-element.79), channel_id=1, source_target_pairs={{0,3},{1,0},{2,1},{3,2},{4,7},{5,4},{6,5},{7,6},{8,11},{9,8},{10,9... | collective-permute-start | bytes 196616 | tf_op jit(solution)/shard_map/ppermute | solution.py:476
  111.0 5.3 %copy-start.3 = (bf16[512,1024]{1,0:T(8,128)(2,1)S(1)}, bf16[512,1024]{1,0:T(8,128)(2,1)}, u32[]{:S(2)}) copy-start(bf16[512,1024]{1,0:T(8,128)(2,1)} %pad_maximum_fusion.1) | copy-start | bytes 3145732
  111.0 5.3 %copy-start.7 = (bf16[4,64,1024]{2,1,0:T(8,128)(2,1)S(1)}, bf16[4,64,1024]{2,1,0:T(8,128)(2,1)}, u32[]{:S(2)}) copy-start(bf16[4,64,1024]{2,1,0:T(8,128)(2,1)} %get-tuple-element.75) | copy-start | bytes 1572868
  111.0 5.3 %copy-start.11 = (bf16[256,128]{1,0:T(8,128)(2,1)S(1)}, bf16[256,128]{1,0:T(8,128)(2,1)}, u32[]{:S(2)}) copy-start(bf16[256,128]{1,0:T(8,128)(2,1)} %get-tuple-element.79) | copy-start | bytes 196612
  111.9 9.5 %collective-permute-start.16 = (bf16[64,1024]{1,0:T(8,128)(2,1)S(1)}, bf16[64,1024]{1,0:T(8,128)(2,1)S(1)}, u32[]{:S(2)}, u32[]{:S(2)}) collective-permute-start(bf16[64,1024]{1,0:T(8,128)(2,1)S(1)} %get-tuple-element.104), channel_id=1, source_target_pairs={{0,1},{1,2},{2,3},{3,0},{4,5},{5,6},{6,7},{7,4},{8,9},{9,10},{10,1... | collective-permute-start | bytes 393224 | tf_op jit(solution)/shard_map/ppermute | solution.py:476
  113.4 14.5 %collective-permute-start.17 = (bf16[64,1024]{1,0:T(8,128)(2,1)S(1)}, bf16[64,1024]{1,0:T(8,128)(2,1)S(1)}, u32[]{:S(2)}, u32[]{:S(2)}) collective-permute-start(bf16[64,1024]{1,0:T(8,128)(2,1)S(1)} %get-tuple-element.103), channel_id=1, source_target_pairs={{0,2},{1,3},{2,0},{3,1},{4,6},{5,7},{6,4},{7,5},{8,10},{9,11},{10,... | collective-permute-start | bytes 393224 | tf_op jit(solution)/shard_map/ppermute | solution.py:476
  114.4 13.4 %collective-permute-start.18 = (bf16[64,1024]{1,0:T(8,128)(2,1)S(1)}, bf16[64,1024]{1,0:T(8,128)(2,1)S(1)}, u32[]{:S(2)}, u32[]{:S(2)}) collective-permute-start(bf16[64,1024]{1,0:T(8,128)(2,1)S(1)} %get-tuple-element.102), channel_id=1, source_target_pairs={{0,3},{1,0},{2,1},{3,2},{4,7},{5,4},{6,5},{7,6},{8,11},{9,8},{10,9... | collective-permute-start | bytes 393224 | tf_op jit(solution)/shard_map/ppermute | solution.py:476
  119.2 8.7 %collective-permute-start.22 = (bf16[64,1024]{1,0:T(8,128)(2,1)S(1)}, bf16[64,1024]{1,0:T(8,128)(2,1)S(1)}, u32[]{:S(2)}, u32[]{:S(2)}) collective-permute-start(bf16[64,1024]{1,0:T(8,128)(2,1)S(1)} %get-tuple-element.99), channel_id=1, source_target_pairs={{0,1},{1,2},{2,3},{3,0},{4,5},{5,6},{6,7},{7,4},{8,9},{9,10},{10,1... | collective-permute-start | bytes 393224 | tf_op jit(solution)/shard_map/ppermute | solution.py:476
  119.5 15.3 %collective-permute-start.23 = (bf16[64,1024]{1,0:T(8,128)(2,1)S(1)}, bf16[64,1024]{1,0:T(8,128)(2,1)S(1)}, u32[]{:S(2)}, u32[]{:S(2)}) collective-permute-start(bf16[64,1024]{1,0:T(8,128)(2,1)S(1)} %get-tuple-element.101), channel_id=1, source_target_pairs={{0,2},{1,3},{2,0},{3,1},{4,6},{5,7},{6,4},{7,5},{8,10},{9,11},{10,... | collective-permute-start | bytes 393224 | tf_op jit(solution)/shard_map/ppermute | solution.py:476
  121.4 13.4 %collective-permute-start.24 = (bf16[64,1024]{1,0:T(8,128)(2,1)S(1)}, bf16[64,1024]{1,0:T(8,128)(2,1)S(1)}, u32[]{:S(2)}, u32[]{:S(2)}) collective-permute-start(bf16[64,1024]{1,0:T(8,128)(2,1)S(1)} %get-tuple-element.100), channel_id=1, source_target_pairs={{0,3},{1,0},{2,1},{3,2},{4,7},{5,4},{6,5},{7,6},{8,11},{9,8},{10,9... | collective-permute-start | bytes 393224 | tf_op jit(solution)/shard_map/ppermute | solution.py:476
